TPU v7x, 32 devices: a whole 2x2x4 slice. The times are simulated.
32 devices in a mesh: seq: 8 (over z, y), head: 4 (over x, core).
Axes of the slice: x: 2, y: 2, z: 4, core: 2. Of those that a mesh axis runs over, the one named last changes fastest.
Arguments:
- layer_input: bfloat16 [8192, 2048], P('seq'), may hold values from -6 to 6
- output_grad: bfloat16 [8192, 2048], P('seq'), may hold values from -6 to 6
- loss_mask: int32 [8192], P('seq'), may hold values 0 or 1
- proj_weight: bfloat16 [2048, 3, 2048], P(None, None, 'head'), may hold values from -0.125 to 0.125
- out_weight: bfloat16 [2048, 2048], P('head'), may hold values from -0.125 to 0.125
- norm_gain: bfloat16 [2048], P('head'), may hold values from 0.099609375 to 1.8984375
Outputs:
- input_grad: bfloat16 [8192, 2048], P(('seq', 'head'))
- proj_weight_grad: float32 [2048, 3, 2048], P('seq', None, 'head')
- out_weight_grad: float32 [2048, 2048], P('head', 'seq')
All inputs are finite; a program needn't handle non-finite values. No bound on the sum of `loss_mask` on one device may be relied on, other than what follows from the above.
Results may differ from a plain program's by a relative error of at most 0.018.
Values may be sent and summed in bfloat16 or wider, within the bound.
No kernel may reach another device: no remote copies, remote signals or barrier semaphores. Data moves between devices by JAX's collectives and lax.ppermute only.
A program may use at most 128 MiB of HBM per device.

v0:
```python
import jax
import jax.numpy as jnp
from jax import lax
from jax.sharding import PartitionSpec as P

D = 2048
HD = 128
BLOCK = 1024


epsilon = 1e-06


def add_before(position, carry, piece):
    index = jnp.arange(piece.shape[0], dtype=jnp.int32)
    keep = (index < position)[:, None, None, None]
    return carry + jnp.sum(jnp.where(keep, piece, 0.0), 0)


def add_after(position, carry, piece):
    index = jnp.arange(piece.shape[0], dtype=jnp.int32)
    keep = (index > position)[:, None, None, None]
    return carry + jnp.sum(jnp.where(keep, piece, 0.0), 0)


def per_device(layer_input, output_grad, loss_mask, proj_weight, out_weight, norm_gain):
    count = layer_input.shape[0]
    blocks = count // BLOCK
    width_dev = proj_weight.shape[2]
    heads_dev = width_dev // HD
    position = lax.axis_index("seq")
    flat_weight = proj_weight.reshape(D, 3 * width_dev)
    projected = jnp.dot(layer_input, flat_weight, preferred_element_type=jnp.float32).astype(
        jnp.bfloat16
    )
    projected = projected.reshape(count, 3, width_dev)
    query_rows = projected[:, 0].reshape(blocks, BLOCK, heads_dev, HD)
    key_rows = projected[:, 1].reshape(blocks, BLOCK, heads_dev, HD)
    value_rows = projected[:, 2].reshape(blocks, BLOCK, heads_dev, HD)
    block_state = jnp.einsum(
        "nbhi,nbhj->nhij", key_rows, value_rows, preferred_element_type=jnp.float32
    )
    shard_state = jnp.sum(block_state, 0)
    zero_state = jnp.zeros_like(shard_state)
    earlier = add_before(
        position,
        zero_state,
        lax.all_gather(shard_state[None].astype(jnp.bfloat16), "seq", axis=0, tiled=True).astype(
            jnp.float32
        ),
    )
    state = (earlier[None] + jnp.cumsum(block_state, 0)).astype(jnp.bfloat16)
    attended = jnp.einsum("nbhi,nhij->nbhj", query_rows, state, preferred_element_type=jnp.float32)
    scale = lax.rsqrt(jnp.mean(attended * attended, -1, keepdims=True) + epsilon)
    gain = norm_gain.astype(jnp.float32).reshape(heads_dev, HD)
    normed = (attended * scale * gain).astype(jnp.bfloat16).reshape(count, width_dev)
    masked_grad = output_grad * loss_mask[:, None].astype(jnp.bfloat16)
    out_terms = jnp.dot(normed.T, masked_grad, preferred_element_type=jnp.float32)
    out_weight_grad = lax.psum_scatter(
        out_terms.astype(jnp.bfloat16), "seq", scatter_dimension=1, tiled=True
    ).astype(jnp.float32)
    normed_grad = lax.dot_general(
        masked_grad, out_weight, (((1,), (1,)), ((), ())), preferred_element_type=jnp.float32
    )
    scaled = normed_grad.reshape(blocks, BLOCK, heads_dev, HD) * gain
    inner_mean = jnp.mean(scaled * attended, -1, keepdims=True)
    attended_grad = (scale * scaled - attended * scale**3 * inner_mean).astype(jnp.bfloat16)
    block_grad = jnp.einsum(
        "nbhi,nbhj->nhij", query_rows, attended_grad, preferred_element_type=jnp.float32
    )
    shard_grad = jnp.sum(block_grad, 0)
    later = add_after(
        position,
        zero_state,
        lax.all_gather(shard_grad[None].astype(jnp.bfloat16), "seq", axis=0, tiled=True).astype(
            jnp.float32
        ),
    )
    local_suffix = jnp.flip(jnp.cumsum(jnp.flip(block_grad, 0), 0), 0)
    state_grad = (later[None] + local_suffix).astype(jnp.bfloat16)
    query_grad = jnp.einsum(
        "nbhj,nhij->nbhi", attended_grad, state, preferred_element_type=jnp.float32
    )
    key_grad = jnp.einsum(
        "nbhj,nhij->nbhi", value_rows, state_grad, preferred_element_type=jnp.float32
    )
    value_grad = jnp.einsum(
        "nbhi,nhij->nbhj", key_rows, state_grad, preferred_element_type=jnp.float32
    )
    projected_grad = jnp.stack(
        [
            query_grad.reshape(count, width_dev),
            key_grad.reshape(count, width_dev),
            value_grad.reshape(count, width_dev),
        ],
        1,
    ).astype(jnp.bfloat16)
    flat_grad = projected_grad.reshape(count, 3 * width_dev)
    proj_weight_grad = lax.psum_scatter(
        jnp.dot(layer_input.T, flat_grad, preferred_element_type=jnp.float32).astype(jnp.bfloat16),
        "seq",
        scatter_dimension=0,
        tiled=True,
    ).astype(jnp.float32)
    proj_weight_grad = proj_weight_grad.reshape(D // lax.axis_size("seq"), 3, width_dev)
    summed = lax.psum_scatter(
        lax.dot_general(
            flat_grad, flat_weight, (((1,), (1,)), ((), ())), preferred_element_type=jnp.float32
        ).astype(jnp.bfloat16),
        "head",
        scatter_dimension=0,
        tiled=True,
    )
    return (summed, proj_weight_grad, out_weight_grad)


def solution(mesh):
    in_specs = (
        P("seq", None),
        P("seq", None),
        P("seq"),
        P(None, None, "head"),
        P("head", None),
        P("head"),
    )
    out_specs = (P(("seq", "head"), None), P("seq", None, "head"), P("head", "seq"))
    return jax.shard_map(
        per_device, mesh=mesh, in_specs=in_specs, out_specs=out_specs, check_vma=False
    )
```

profile of v0, /device:TPU:0, one launch (start us, length us, event | category | flops | bytes accessed | tf_op | source)
XLA Modules:
  0.0 368.9 jit_solution(7344549703378429225)
XLA Ops:
  7.2 8.9 %copy.35 = bf16[2048,3,512]{0,2,1:T(8,128)(2,1)} copy(bf16[2048,3,512]{2,0,1:T(8,128)(2,1)} %param.9) | data formatting | bytes 12582912 | tf_op args[3]
  16.2 11.3 %convolution_convert_fusion.1 = bf16[1024,1536]{1,0:T(8,128)(2,1)} fusion(bf16[1024,2048]{1,0:T(8,128)(2,1)} %param.6, bf16[2048,1536]{0,1:T(8,128)(2,1)} %bitcast.89), kind=kOutput, calls=%fused_computation.4 | convolution fusion | flops 6444023808 | bytes 13631488 | tf_op jit(solution)/shard_map/dot_general | solution.py:33
  27.5 4.7 %copy.36 = bf16[1024,1536]{0,1:T(8,128)(2,1)} copy(bf16[1024,1536]{1,0:T(8,128)(2,1)} %convolution_convert_fusion.1) | data formatting | bytes 6291456 | tf_op jit(solution)/shard_map/convert_element_type | solution.py:33
  32.1 2.2 fusion.20
  36.5 6.0 %fusion.3 = f32[1024,512]{0,1:T(8,128)} fusion(bf16[512,2048]{1,0:T(8,128)(2,1)S(1)} %copy-done, bf16[1024,2048]{1,0:T(8,128)(2,1)} %param.7, bf16[1024]{0:T(1024)(128)(2,1)S(1)} %convert_element_type.72), kind=kOutput, calls=%fused_computation.7 | convolution fusion | flops 2149580800 | bytes 8390656 | tf_op jit(solution)/shard_map/dot_general | solution.py:62
  42.5 36.9 %all-gather.5.cloned.1.call-done = bf16[32,128,128]{2,1,0:T(8,128)(2,1)} async-done(((bf16[4,128,128]{2,1,0:T(8,128)(2,1)}), bf16[32,128,128]{2,1,0:T(8,128)(2,1)}) %all-gather.5.cloned.1.call-update) | async-done | bytes 1048592 | tf_op jit(solution)/shard_map/all_gather | solution.py:48
  79.4 1.5 fusion.9
  81.0 2.4 fusion.10
  84.2 1.1 fusion.22
  85.4 5.9 %fusion.5 = bf16[512,2048]{1,0:T(8,128)(2,1)} fusion(bf16[1024,512]{0,1:T(8,128)(2,1)S(1)} %bitcast.96, bf16[1024,2048]{1,0:T(8,128)(2,1)} %param.7, bf16[1024]{0:T(1024)(128)(2,1)S(1)} %convert_element_type.72), kind=kOutput, calls=%fused_computation.9 | convolution fusion | flops 2150629376 | bytes 7342080 | tf_op jit(solution)/shard_map/dot_general | solution.py:58
  92.0 1.3 copy.45
  93.4 31.0 %all-gather.7.cloned.1.call-done = bf16[32,128,128]{2,1,0:T(8,128)(2,1)} async-done(((bf16[4,128,128]{2,1,0:T(8,128)(2,1)}), bf16[32,128,128]{2,1,0:T(8,128)(2,1)}) %all-gather.7.cloned.1.call-update) | async-done | bytes 1048592 | tf_op jit(solution)/shard_map/all_gather | solution.py:75
  124.4 1.6 fusion.8
  126.5 1.3 copy.47
  129.1 3.6 maximum_convert_fusion
  132.7 4.7 %copy.48 = bf16[1024,3,512]{0,2,1:T(8,128)(2,1)} copy(bf16[1024,3,512]{2,0,1:T(8,128)(2,1)} %maximum_convert_fusion) | data formatting | bytes 6291456 | tf_op jit(solution)/shard_map/convert_element_type | solution.py:97
  137.4 11.2 %fusion = bf16[2048,1536]{0,1:T(8,128)(2,1)} fusion(bf16[1024,1536]{0,1:T(8,128)(2,1)} %bitcast.93, bf16[1024,2048]{1,0:T(8,128)(2,1)} %param.6), kind=kOutput, calls=%fused_computation.2 | convolution fusion | flops 6445596672 | bytes 13631488 | tf_op jit(solution)/shard_map/dot_general | solution.py:100
  148.7 1.2 copy-done.8
  150.2 11.1 %bitcast_convert_fusion = bf16[1024,2048]{1,0:T(8,128)(2,1)} fusion(bf16[2048,3,512]{2,0,1:T(8,128)(2,1)} %param.9, bf16[1024,1,512]{2,0,1:T(8,128)(2,1)S(1)} %copy-done.8, bf16[1024,1,512]{2,0,1:T(8,128)(2,1)S(1)} %copy-done.10, bf16[1024,1,512]{2,0,1:T(8,128)(2,1)S(1)} %copy-done.7), kind=kOutput, calls=%fused_computation | convolution fusion | flops 6447693824 | bytes 13631488 | tf_op jit(solution)/shard_map/dot_general | solution.py:107
  161.3 33.6 %reduce-scatter.8.cloned.1.call-done = bf16[512,256]{1,0:T(8,128)(2,1)} async-done(((bf16[512,2048]{1,0:T(8,128)(2,1)}), bf16[512,256]{1,0:T(8,128)(2,1)}) %reduce-scatter.8.cloned.1.call-update) | async-done | bytes 262160 | tf_op jit(solution)/shard_map/reduce_scatter | solution.py:59
  194.9 1.8 convert_element_type.85
  196.6 119.1 %reduce-scatter.6.cloned.1.call-done = bf16[256,1536]{0,1:T(8,128)(2,1)} async-done(((bf16[2048,1536]{0,1:T(8,128)(2,1)}), bf16[256,1536]{0,1:T(8,128)(2,1)}) %reduce-scatter.6.cloned.1.call-update) | async-done | bytes 786448 | tf_op jit(solution)/shard_map/reduce_scatter | solution.py:99
  315.8 2.6 copy.49
  318.3 44.1 %reduce-scatter.4.cloned.1.call-done = bf16[256,2048]{1,0:T(8,128)(2,1)} async-done(((bf16[1024,2048]{1,0:T(8,128)(2,1)}), bf16[256,2048]{1,0:T(8,128)(2,1)}) %reduce-scatter.4.cloned.1.call-update) | async-done | bytes 1048592 | tf_op jit(solution)/shard_map/reduce_scatter | solution.py:106
  (48 shorter events, 5.8 us)
Async XLA Ops:
  7.2 29.4 %copy-start = (bf16[512,2048]{1,0:T(8,128)(2,1)S(1)}, bf16[512,2048]{1,0:T(8,128)(2,1)}, u32[]{:S(2)}) copy-start(bf16[512,2048]{1,0:T(8,128)(2,1)} %param.10) | copy-start | bytes 6291460
  7.2 72.2 %all-gather.5.cloned.1.call-start = ((), (), s32[]{:S(2)}) async-start(), calls=%async_computation.6 | async-start | bytes 1179648 | tf_op jit(solution)/shard_map/all_gather | solution.py:48
  32.1 4.3 %copy-start.11 = (s32[1024]{0:T(1024)S(1)}, s32[1024]{0:T(1024)}, u32[]{:S(2)}) copy-start(s32[1024]{0:T(1024)} %param.8) | copy-start | bytes 12292
  32.1 4.4 %copy-start.12 = (bf16[512]{0:T(512)(128)(2,1)S(1)}, bf16[512]{0:T(512)(128)(2,1)}, u32[]{:S(2)}) copy-start(bf16[512]{0:T(512)(128)(2,1)} %param.11) | copy-start | bytes 3076
  34.3 1.0 copy-start.2
  34.3 2.1 copy-start.4
  36.4 88.0 %all-gather.7.cloned.1.call-start = ((), (), s32[]{:S(2)}) async-start(), calls=%async_computation.7 | async-start | bytes 1179648 | tf_op jit(solution)/shard_map/all_gather | solution.py:75
  80.9 2.5 copy-start.6
  85.3 109.5 %reduce-scatter.8.cloned.1.call-start = ((), (), s32[]{:S(2)}) async-start(), calls=%async_computation.5 | async-start | bytes 2359296 | tf_op jit(solution)/shard_map/reduce_scatter | solution.py:59
  91.3 224.4 %reduce-scatter.6.cloned.1.call-start = ((), (), s32[]{:S(2)}) async-start(), calls=%async_computation.4 | async-start | bytes 7077888 | tf_op jit(solution)/shard_map/reduce_scatter | solution.py:99
  91.6 34.5 %copy-start.5 = (bf16[1024,1,512]{0,2,1:T(8,128)(2,1)S(1)}, bf16[1024,1,512]{0,2,1:T(8,128)(2,1)}, u32[]{:S(2)}) copy-start(bf16[1024,1,512]{0,2,1:T(8,128)(2,1)} %copy-done.4) | copy-start | bytes 3145732
  124.4 3.5 copy-start.3
  127.9 1.2 copy-start.7
  129.1 3.6 copy-start.9
  148.6 1.2 copy-start.8
  148.6 1.6 copy-start.10
  148.6 213.8 %reduce-scatter.4.cloned.1.call-start = ((), (), s32[]{:S(2)}) async-start(), calls=%async_computation.3 | async-start | bytes 5242880 | tf_op jit(solution)/shard_map/reduce_scatter | solution.py:106
  161.2 201.2 %copy-start.1 = (bf16[512,2048]{1,0:T(8,128)(2,1)S(1)}, bf16[512,2048]{1,0:T(8,128)(2,1)}, u32[]{:S(2)}) copy-start(bf16[512,2048]{1,0:T(8,128)(2,1)} %param.10) | copy-start | bytes 6291460
Sparse Core Ops, SparseCore 0:
  36.5 42.8 all-gather.4
  85.5 38.8 all-gather.6
  127.9 66.8 reduce-scatter.7
  198.3 117.3 reduce-scatter.5
  318.7 43.6 reduce-scatter.3
where the time goes:
time: 370 us; the launch traced here: 369 us
  waiting for transfers between devices  265 us (72%)
  matrix products  51.4 us (14%)
  local copies, waits for them, and re-layouts  29 us (8%)
  between operations  14 us (4%)
  other arithmetic  9.31 us (3%)
    reduce_scatter x1, waiting for transfers between devices, per_device(): lax.psum_scatter(jnp.dot(layer_input.T, flat_grad, preferred_element_type...  119 us
    reduce_scatter x1, waiting for transfers between devices, per_device(): lax.psum_scatter(lax.dot_general(flat_grad, flat_weight, (((1,), (1,)), (...  44.1 us
    all_gather x1, waiting for transfers between devices, per_device(): lax.all_gather(shard_state[None].astype(jnp.bfloat16), 'seq', axis=0, til...  36.9 us
    reduce_scatter x1, waiting for transfers between devices, per_device(): lax.psum_scatter(out_terms.astype(jnp.bfloat16), 'seq', scatter_dimension...  33.6 us
    all_gather x1, waiting for transfers between devices, per_device(): lax.all_gather(shard_grad[None].astype(jnp.bfloat16), 'seq', axis=0, tile...  31 us
    unnamed x28, local copies, waits for them, and re-layouts  14.2 us
    dot_general x1, matrix products, per_device(): jnp.dot(layer_input, flat_weight, preferred_element_type=jnp.float32)  11.3 us
    dot_general x1, matrix products, per_device(): jnp.dot(layer_input.T, flat_grad, preferred_element_type=jnp.float32)  11.2 us
  transfers between devices with their start and end apart: 5, of which 5 were waited for; matrix products, arithmetic and copies ran while one was open for 14% of the time, Pallas kernels for 0%

commit v1 on v0

v1 whole, which is shorter than its diff:
```python
import functools

import jax
import jax.numpy as jnp
from jax import lax
from jax.experimental import pallas as pl
from jax.experimental.pallas import tpu as pltpu
from jax.sharding import PartitionSpec as P

D = 2048
HD = 128
BLOCK = 1024
epsilon = 1e-06
f32 = jnp.float32
bf16 = jnp.bfloat16
VMEM_LIMIT = 48 * 1024 * 1024


def params():
    return pltpu.CompilerParams(vmem_limit_bytes=VMEM_LIMIT)


def dot(a, b):
    return lax.dot_general(a, b, (((1,), (0,)), ((), ())), preferred_element_type=f32)


def dot_t(a, b):
    return lax.dot_general(a, b, (((1,), (1,)), ((), ())), preferred_element_type=f32)


def exchange(arr, axis, bit):
    count = lax.axis_size(axis)
    return lax.ppermute(arr, axis, [(i, i ^ (1 << bit)) for i in range(count)])


def slot_order(stage_bits):
    order = [0]
    for bit in reversed(stage_bits):
        order = order + [slot | (1 << bit) for slot in order]
    return order


def state_kernel(key_ref, value_ref, state_ref, key_t_ref, value_t_ref):
    key_t = key_ref[...].T
    key_t_ref[...] = key_t
    value_t_ref[...] = value_ref[...].T
    state_ref[0] = dot(key_t, value_ref[...])


def block_states(keys, values):
    count, width = keys.shape
    heads = width // HD
    column = pl.BlockSpec((count, HD), lambda h: (0, h))
    row = pl.BlockSpec((HD, count), lambda h: (h, 0))
    return pl.pallas_call(
        state_kernel,
        grid=(heads,),
        in_specs=[column, column],
        out_specs=[pl.BlockSpec((1, HD, HD), lambda h: (h, 0, 0)), row, row],
        out_shape=[
            jax.ShapeDtypeStruct((heads, HD, HD), f32),
            jax.ShapeDtypeStruct((width, count), bf16),
            jax.ShapeDtypeStruct((width, count), bf16),
        ],
        compiler_params=params(),
        cost_estimate=pl.CostEstimate(
            flops=2 * count * width * HD, bytes_accessed=8 * count * width, transcendentals=0
        ),
        name="block_states",
    )(keys, values)


def terms_kernel(count_left, block_ref, *refs):
    left, right, out = refs[:count_left], refs[count_left], refs[count_left + 1]
    rows = left[0].shape[0]
    for index, ref in enumerate(left):
        out[0, index * rows : (index + 1) * rows, :] = dot(ref[...], right[...]).astype(bf16)


def gradient_terms(lefts, right, position, slots):
    rows, count = lefts[0].shape
    width = right.shape[1] // lax.axis_size("seq")
    total = rows * len(lefts)
    blocks = position ^ jnp.array(slots, jnp.int32)
    if width % 128:
        picked = jnp.take(right.reshape(count, -1, width), blocks, axis=1)
        left = jnp.concatenate(lefts, 0)
        return jnp.einsum("at,tnb->nab", left, picked, preferred_element_type=f32).astype(bf16)
    return pl.pallas_call(
        functools.partial(terms_kernel, len(lefts)),
        grid_spec=pltpu.PrefetchScalarGridSpec(
            num_scalar_prefetch=1,
            grid=(len(slots),),
            in_specs=[pl.BlockSpec((rows, count), lambda i, b: (0, 0)) for _ in lefts]
            + [pl.BlockSpec((count, width), lambda i, b: (0, b[i]))],
            out_specs=pl.BlockSpec((1, total, width), lambda i, b: (i, 0, 0)),
        ),
        out_shape=jax.ShapeDtypeStruct((len(slots), total, width), bf16),
        compiler_params=params(),
        cost_estimate=pl.CostEstimate(
            flops=2 * count * total * width * len(slots),
            bytes_accessed=2 * len(slots) * width * (count + total) + 2 * total * count,
            transcendentals=0,
        ),
        name="gradient_terms",
    )(blocks, *lefts, right)


def middle_kernel(query_ref, grad_ref, mask_ref, gain_ref, state_ref, normed_t_ref, query_grad_ref, query_grad_t_ref, block_grad_ref):
    query = query_ref[...]
    state = state_ref[0]
    mask = mask_ref[...]
    gain = gain_ref[...].astype(f32)
    attended = dot(query, state)
    scale = lax.rsqrt(jnp.mean(attended * attended, -1, keepdims=True) + epsilon)
    unit = attended * scale
    normed_t_ref[...] = (unit * gain * mask).astype(bf16).T
    scaled = grad_ref[...] * mask * gain
    inner = jnp.mean(scaled * attended, -1, keepdims=True)
    attended_grad = (scale * scaled - attended * (scale * scale * scale) * inner).astype(bf16)
    attended_grad_t = attended_grad.T
    block_grad_ref[0] = dot(attended_grad_t, query)
    query_grad_ref[...] = dot_t(attended_grad, state).astype(bf16)
    query_grad_t_ref[...] = dot(state, attended_grad_t).astype(bf16)


def middle(queries, normed_grad, mask, gain, state):
    count, width = queries.shape
    heads = width // HD
    column = pl.BlockSpec((count, HD), lambda h: (0, h))
    row = pl.BlockSpec((HD, count), lambda h: (h, 0))
    square = pl.BlockSpec((1, HD, HD), lambda h: (h, 0, 0))
    return pl.pallas_call(
        middle_kernel,
        grid=(heads,),
        in_specs=[
            column,
            column,
            pl.BlockSpec((count, 1), lambda h: (0, 0)),
            pl.BlockSpec((1, HD), lambda h: (0, h)),
            square,
        ],
        out_specs=[row, column, row, square],
        out_shape=[
            jax.ShapeDtypeStruct((width, count), bf16),
            jax.ShapeDtypeStruct((count, width), bf16),
            jax.ShapeDtypeStruct((width, count), bf16),
            jax.ShapeDtypeStruct((heads, HD, HD), f32),
        ],
        compiler_params=params(),
        cost_estimate=pl.CostEstimate(
            flops=8 * count * width * HD, bytes_accessed=12 * count * width, transcendentals=count
        ),
        name="norm_backward",
    )(queries, normed_grad, mask, gain, state)


def late_kernel(heads, mine_ref, other_ref, own_keep_ref, own_send_ref, got_keep_ref, got_send_ref, keep_ref, send_ref):
    width = heads * HD
    for own, got, out in ((own_keep_ref, got_keep_ref, keep_ref), (own_send_ref, got_send_ref, send_ref)):
        for h in range(heads):
            lo, hi = h * HD, (h + 1) * HD
            key = lax.dot_general(mine_ref[h], own[0, lo:hi, :], (((0,), (0,)), ((), ())), preferred_element_type=f32)
            key += lax.dot_general(other_ref[h], got[0, lo:hi, :], (((0,), (0,)), ((), ())), preferred_element_type=f32)
            out[0, lo:hi, :] = key.astype(bf16)
            value = dot(mine_ref[h], own[0, width + lo : width + hi, :])
            value += dot(other_ref[h], got[0, width + lo : width + hi, :])
            out[0, width + lo : width + hi, :] = value.astype(bf16)


def late_terms(mine, other, own, got):
    slots, total, width = own.shape
    heads = mine.shape[0]
    half = slots // 2
    square = pl.BlockSpec((heads, HD, HD), lambda i: (0, 0, 0))
    low = pl.BlockSpec((1, total, width), lambda i: (i, 0, 0))
    high = pl.BlockSpec((1, total, width), lambda i: (i + half, 0, 0))
    out = jax.ShapeDtypeStruct((half, total, width), bf16)
    return pl.pallas_call(
        functools.partial(late_kernel, heads),
        grid=(half,),
        in_specs=[square, square, low, high, low, high],
        out_specs=[low, low],
        out_shape=[out, out],
        compiler_params=params(),
        cost_estimate=pl.CostEstimate(
            flops=4 * slots * total * width * HD, bytes_accessed=6 * slots * total * width, transcendentals=0
        ),
        name="late_terms",
    )(mine, other, own, own, got, got)


def key_value_kernel(key_ref, value_ref, grad_ref, key_grad_ref, value_grad_ref):
    key_grad_ref[...] = dot(value_ref[...], grad_ref[0]).astype(bf16)
    value_grad_ref[...] = dot_t(key_ref[...], grad_ref[0]).astype(bf16)


def key_value_grads(keys, values, state_grad_t):
    count, width = keys.shape
    column = pl.BlockSpec((count, HD), lambda h: (0, h))
    out = jax.ShapeDtypeStruct((count, width), bf16)
    return pl.pallas_call(
        key_value_kernel,
        grid=(width // HD,),
        in_specs=[column, column, pl.BlockSpec((1, HD, HD), lambda h: (h, 0, 0))],
        out_specs=[column, column],
        out_shape=[out, out],
        compiler_params=params(),
        cost_estimate=pl.CostEstimate(
            flops=4 * count * width * HD, bytes_accessed=8 * count * width, transcendentals=0
        ),
        name="key_value_grads",
    )(keys, values, state_grad_t)


def halving(keep, send, axis, stage_bits):
    for bit in stage_bits:
        got = exchange(send, axis, bit)
        total = keep.astype(f32) + got.astype(f32)
        half = total.shape[0] // 2
        if half:
            keep, send = total[:half].astype(bf16), total[half:].astype(bf16)
    return total[0]


def per_device(layer_input, output_grad, loss_mask, proj_weight, out_weight, norm_gain):
    count = layer_input.shape[0]
    width_dev = proj_weight.shape[2]
    heads_dev = width_dev // HD
    position = lax.axis_index("seq")
    seq_bits = lax.axis_size("seq").bit_length() - 1
    head_bits = lax.axis_size("head").bit_length() - 1
    stages = list(range(seq_bits))
    swapped = [1, 0] + stages[2:] if seq_bits > 1 else stages
    order = slot_order(stages)
    half = len(order) // 2
    w_query, w_key, w_value = (proj_weight[:, i, :] for i in range(3))

    def project(weight):
        return jnp.dot(layer_input, weight, preferred_element_type=f32).astype(bf16)

    keys, values = project(w_key), project(w_value)
    own_state, keys_t, values_t = block_states(keys, values)

    before, total = jnp.zeros_like(own_state), own_state
    for bit in stages:
        got = exchange(total.astype(bf16), "seq", bit).astype(f32)
        before = before + jnp.where((position >> bit) & 1, got, 0.0)
        total = total + got
    state = (before + own_state).astype(bf16)

    early_send = gradient_terms([values_t, keys_t], layer_input, position, order[half:])
    early_got = exchange(early_send, "seq", stages[0])
    early_keep = gradient_terms([values_t, keys_t], layer_input, position, order[:half])

    queries = project(w_query)
    normed_grad = dot_t(output_grad, out_weight)
    mask = loss_mask.astype(f32)[:, None]
    normed_t, query_grad, query_grad_t, own_grad = middle(
        queries, normed_grad, mask, norm_gain[None, :], state
    )

    after, total, partner = jnp.zeros_like(own_grad), own_grad, None
    for bit in stages:
        got = exchange(total.astype(bf16), "seq", bit).astype(f32)
        if partner is None:
            partner = got
        else:
            after = after + jnp.where((position >> bit) & 1, 0.0, got)
        total = total + got
    upper = (position & 1) == 1
    pair = own_grad + partner
    state_grad = (after + jnp.where(upper, own_grad, pair)).astype(bf16)
    partner_state_grad = (after + jnp.where(upper, pair, partner)).astype(bf16)

    out_send = gradient_terms([normed_t], output_grad, position, order[half:])
    out_keep = gradient_terms([normed_t], output_grad, position, order[:half])
    out_weight_grad = halving(out_keep, out_send, "seq", stages)

    query_order = slot_order(swapped)
    query_send = gradient_terms([query_grad_t], layer_input, position, query_order[half:])
    query_keep = gradient_terms([query_grad_t], layer_input, position, query_order[:half])
    query_part = halving(query_keep, query_send, "seq", swapped)

    late_keep, late_send = late_terms(state_grad, partner_state_grad, early_keep, early_got)
    late_part = halving(late_keep, late_send, "seq", stages[1:])

    key_grad, value_grad = key_value_grads(keys, values, state_grad)
    place = lax.axis_index("head")
    token_order = slot_order(list(range(head_bits)))
    rows = count // len(token_order)

    def pick(grad):
        return [lax.dynamic_slice_in_dim(grad, (place ^ slot) * rows, rows, 0) for slot in token_order]

    half_tokens = len(token_order) // 2
    picked = [pick(grad) for grad in (query_grad, key_grad, value_grad)]

    def input_terms(lo, hi):
        part = 0.0
        for grad, weight in zip(picked, (w_query, w_key, w_value)):
            part = part + dot_t(jnp.concatenate(grad[lo:hi], 0), weight)
        return part.astype(bf16).reshape(hi - lo, rows, D)

    input_send = input_terms(half_tokens, 2 * half_tokens)
    input_keep = input_terms(0, half_tokens)
    input_grad = halving(input_keep, input_send, "head", list(range(head_bits))).astype(bf16)

    proj_weight_grad = jnp.stack(
        [query_part.T, late_part[:width_dev].T, late_part[width_dev:].T], 1
    )
    return (input_grad, proj_weight_grad, out_weight_grad)


def solution(mesh):
    in_specs = (
        P("seq", None),
        P("seq", None),
        P("seq"),
        P(None, None, "head"),
        P("head", None),
        P("head"),
    )
    out_specs = (P(("seq", "head"), None), P("seq", None, "head"), P("head", "seq"))
    return jax.shard_map(
        per_device, mesh=mesh, in_specs=in_specs, out_specs=out_specs, check_vma=False
    )
```

time: 370 us -> 213 us (0.58)
  waiting for transfers between devices: 265 us -> 84.8 us
  Pallas kernels: 0 us -> 39.2 us
  starting transfers between devices: 0.39 us -> 21.6 us
  local copies, waits for them, and re-layouts: 29 us -> 10.1 us
  between operations: 14 us -> 1.11 us
  matrix products: 51.4 us -> 41.6 us
  other arithmetic: 9.31 us -> 13.2 us
    reduce_scatter x3 -> x0, waiting for transfers between devices: 197 us -> none  [the longest x1 119 us: per_device(): lax.psum_scatter(jnp.dot(layer_input.T, flat_grad, preferred_element_type...]
    ppermute x0 -> x17, waiting for transfers between devices: none -> 84.8 us  [exchange(): return lax.ppermute(arr, axis, [(i, i ^ 1 << bit) for i in range(count)])]
    all_gather x2 -> x0, waiting for transfers between devices: 67.9 us -> none  [the longest x1 36.9 us: per_device(): lax.all_gather(shard_state[None].astype(jnp.bfloat16), 'seq', axis=0, til...]
    pallas_call x0 -> x10, Pallas kernels: none -> 39.2 us  [the longest x6 27.1 us: gradient_terms(): pl.pallas_call(functools.partial(terms_kernel, len(lefts)), grid_spec=plt...]
    ppermute x0 -> x17, starting transfers between devices: none -> 21.6 us  [exchange(): return lax.ppermute(arr, axis, [(i, i ^ 1 << bit) for i in range(count)])]
    dot_general x11 -> x10, matrix products: 51.4 us -> 41.6 us  [the longest x7 27.1 us: dot_t(): lax.dot_general(a, b, (((1,), (1,)), ((), ())), preferred_element_type=f32)]
    convert_element_type x2 -> x0, local copies, waits for them, and re-layouts: 9.37 us -> none  [the longest x1 4.71 us: per_device(): projected_grad = jnp.stack([query_grad.reshape(count, width_dev), key_gra...]
    unnamed x28 -> x47, local copies, waits for them, and re-layouts: 14.2 us -> 6.68 us
  transfers between devices with their start and end apart: 5 -> 17, of which waited for: 5 -> 6; matrix products, arithmetic and copies ran while one was open for 14% -> 23% of each run, Pallas kernels for 0% -> 18%
where the time goes in v1:
time: 213 us; the launch traced here: 212 us
  waiting for transfers between devices  84.8 us (40%)
  matrix products  41.6 us (20%)
  Pallas kernels  39.2 us (18%)
  starting transfers between devices  21.6 us (10%)
  other arithmetic  13.2 us (6%)
  local copies, waits for them, and re-layouts  10.1 us (5%)
    ppermute x17, waiting for transfers between devices, exchange(): return lax.ppermute(arr, axis, [(i, i ^ 1 << bit) for i in range(count)])  84.8 us
    pallas_call x6, Pallas kernels, gradient_terms(): pl.pallas_call(functools.partial(terms_kernel, len(lefts)), grid_spec=plt...  27.1 us
    dot_general x7, matrix products, dot_t(): lax.dot_general(a, b, (((1,), (1,)), ((), ())), preferred_element_type=f32)  27.1 us
    ppermute x17, starting transfers between devices, exchange(): return lax.ppermute(arr, axis, [(i, i ^ 1 << bit) for i in range(count)])  21.6 us
    dot_general x3, matrix products, project(): return jnp.dot(layer_input, weight, preferred_element_type=f32).astype(bf16)  14.5 us
    unnamed x47, local copies, waits for them, and re-layouts  6.68 us
    another operation x6, other arithmetic  5.96 us
    pallas_call x1, Pallas kernels, middle(): pl.pallas_call(middle_kernel, grid=(heads,), in_specs=[column, column, pl...  5.55 us
  transfers between devices with their start and end apart: 17, of which 6 were waited for; matrix products, arithmetic and copies ran while one was open for 23% of the time, Pallas kernels for 18%

profile of v1, /device:TPU:0, one launch (start us, length us, event | category | flops | bytes accessed | tf_op | source)
XLA Modules:
  0.0 211.6 jit_solution(5009863501559686905)
XLA Ops:
  0.7 5.3 %fusion.29.key_ref = bf16[1024,512]{1,0:T(8,128)(2,1)S(1)} fusion(bf16[1024,2048]{1,0:T(8,128)(2,1)} %refs_2_.3, bf16[2048,3,512]{2,0,1:T(8,128)(2,1)} %param.15), kind=kOutput, calls=%fused_computation.35 | convolution fusion | flops 2148007936 | bytes 7340032 | tf_op jit(solution)/shard_map/dot_general | solution.py:240
  6.0 4.3 %fusion.32.value_ref = bf16[1024,512]{1,0:T(8,128)(2,1)S(1)} fusion(bf16[1024,2048]{1,0:T(8,128)(2,1)S(1)} %copy-done.11, bf16[2048,3,512]{2,0,1:T(8,128)(2,1)} %param.15), kind=kOutput, calls=%fused_computation.36 | convolution fusion | flops 2148007936 | bytes 7340032 | tf_op jit(solution)/shard_map/dot_general | solution.py:240
  13.7 3.0 %collective-permute-start = (bf16[4,128,128]{2,1,0:T(8,128)(2,1)}, bf16[4,128,128]{2,1,0:T(8,128)(2,1)S(1)}, u32[]{:S(2)}, u32[]{:S(2)}) collective-permute-start(bf16[4,128,128]{2,1,0:T(8,128)(2,1)} %convert_element_type.148), channel_id=1, source_target_pairs={{0,4},{4,0},{8,12},{12,8},{16,20},{20,16},{24,28},{28,24},{1,5},{5... | collective-permute-start | bytes 393224 | tf_op jit(solution)/shard_map/ppermute | solution.py:33
  17.9 6.1 %gradient_terms.9 = bf16[4,1024,256]{2,1,0:T(8,128)(2,1)} custom-call(s32[4]{0:T(128)S(1)} %broadcast_xor_fusion.block_ref, bf16[512,1024]{1,0:T(8,128)(2,1)S(1)} %copy-done.3, bf16[512,1024]{1,0:T(8,128)(2,1)S(1)} %get-tuple-element.21.refs_1_, bf16[1024,2048]{1,0:T(8,128)(2,1)} %refs_2_.3), custom_call_target="tpu_custom_call" | custom-call | flops 2147483648 | bytes 6291456 | tf_op jit(solution)/shard_map/gradient_terms/pallas_call | solution.py:89
  24.0 4.9 %fusion.26.query_ref = bf16[1024,512]{1,0:T(8,128)(2,1)} fusion(bf16[1024,2048]{1,0:T(8,128)(2,1)S(1)} %copy-done.12, bf16[2048,3,512]{2,0,1:T(8,128)(2,1)} %param.15), kind=kOutput, calls=%fused_computation.34 | convolution fusion | flops 2148007936 | bytes 7340032 | tf_op jit(solution)/shard_map/dot_general | solution.py:240
  30.7 5.9 %fusion.71.grad_ref = f32[1024,512]{1,0:T(8,128)} fusion(bf16[1024,2048]{1,0:T(8,128)(2,1)} %refs_1_.7, bf16[512,2048]{1,0:T(8,128)(2,1)S(1)} %copy-done), kind=kOutput, calls=%fused_computation.105 | convolution fusion | flops 2147483648 | bytes 8388608 | tf_op jit(solution)/shard_map/dot_general | solution.py:28
  39.4 2.9 %collective-permute-done.1 = bf16[4,128,128]{2,1,0:T(8,128)(2,1)S(1)} collective-permute-done((bf16[4,128,128]{2,1,0:T(8,128)(2,1)S(1)}, bf16[4,128,128]{2,1,0:T(8,128)(2,1)S(1)}, u32[]{:S(2)}, u32[]{:S(2)}) %collective-permute-start.1) | collective-permute-done | bytes 131104 | tf_op jit(solution)/shard_map/ppermute | solution.py:33
  42.4 3.1 %collective-permute-start.2 = (bf16[4,128,128]{2,1,0:T(8,128)(2,1)S(1)}, bf16[4,128,128]{2,1,0:T(8,128)(2,1)S(1)}, u32[]{:S(2)}, u32[]{:S(2)}) collective-permute-start(bf16[4,128,128]{2,1,0:T(8,128)(2,1)S(1)} %fusion.58), channel_id=1, source_target_pairs={{0,16},{4,20},{8,24},{12,28},{16,0},{20,4},{24,8},{28,12},{1,17},{... | collective-permute-start | bytes 393224 | tf_op jit(solution)/shard_map/ppermute | solution.py:33
  46.7 4.8 %gradient_terms.8.own_keep_ref.own_send_ref = bf16[4,1024,256]{2,1,0:T(8,128)(2,1)S(1)} custom-call(s32[4]{0:T(128)S(1)} %broadcast_xor_fusion.1.block_ref, bf16[512,1024]{1,0:T(8,128)(2,1)S(1)} %copy-done.4, bf16[512,1024]{1,0:T(8,128)(2,1)S(1)} %get-tuple-element.21.refs_1_, bf16[1024,2048]{1,0:T(8,128)(2,1)} %refs_2_.3), custom_call_target="tpu_custom_call" | custom-call | flops 2147483648 | bytes 6291456 | tf_op jit(solution)/shard_map/gradient_terms/pallas_call | solution.py:89
  51.7 5.5 %norm_backward.1 = (bf16[512,1024]{1,0:T(8,128)(2,1)S(1)}, bf16[1024,512]{1,0:T(8,128)(2,1)S(1)}, bf16[512,1024]{1,0:T(8,128)(2,1)S(1)}, f32[4,128,128]{2,1,0:T(8,128)S(1)}) custom-call(bf16[1024,512]{1,0:T(8,128)(2,1)S(1)} %copy-done.10, f32[1024,512]{1,0:T(8,128)} %fusion.71.grad_ref, f32[1024,1]{1,0:T(8,128)S(1)} %copy-done.9, ...), custom_call_target="tpu_custom_call" | custom-call | flops 536870912 | bytes 6291456 | tf_op jit(solution)/shard_map/norm_backward/pallas_call | solution.py:133
  57.2 4.0 %gradient_terms.11 = bf16[4,512,256]{2,1,0:T(8,128)(2,1)S(1)} custom-call(s32[4]{0:T(128)S(1)} %broadcast_xor_fusion.block_ref, bf16[512,1024]{1,0:T(8,128)(2,1)S(1)} %get-tuple-element.24.refs_0_, bf16[1024,2048]{1,0:T(8,128)(2,1)} %refs_1_.7), custom_call_target="tpu_custom_call" | custom-call | flops 1073741824 | bytes 4194304 | tf_op jit(solution)/shard_map/gradient_terms/pallas_call | solution.py:89
  62.9 4.0 %gradient_terms.7 = bf16[4,512,256]{2,1,0:T(8,128)(2,1)S(1)} custom-call(s32[4]{0:T(128)S(1)} %broadcast_xor_fusion.2.block_ref, bf16[512,1024]{1,0:T(8,128)(2,1)S(1)} %get-tuple-element.19.refs_0_, bf16[1024,2048]{1,0:T(8,128)(2,1)} %refs_2_.3), custom_call_target="tpu_custom_call" | custom-call | flops 1073741824 | bytes 4194304 | tf_op jit(solution)/shard_map/gradient_terms/pallas_call | solution.py:89
  69.2 27.4 %collective-permute-done.3 = bf16[4,128,128]{2,1,0:T(8,128)(2,1)S(1)} collective-permute-done((bf16[4,128,128]{2,1,0:T(8,128)(2,1)S(1)}, bf16[4,128,128]{2,1,0:T(8,128)(2,1)S(1)}, u32[]{:S(2)}, u32[]{:S(2)}) %collective-permute-start.3) | collective-permute-done | bytes 131104 | tf_op jit(solution)/shard_map/ppermute | solution.py:33
  98.3 2.9 %fusion.13 = f32[512,2048]{1,0:T(8,128)S(1)} fusion(bf16[2048,3,512]{2,0,1:T(8,128)(2,1)} %param.15, bf16[256,512]{1,0:T(8,128)(2,1)S(1)} %get-tuple-element.43, bf16[256,512]{1,0:T(8,128)(2,1)S(1)} %get-tuple-element.44), kind=kOutput, calls=%fused_computation.16 | convolution fusion | flops 1074790400 | bytes 6815744 | tf_op jit(solution)/shard_map/dot_general | solution.py:28
  101.2 4.0 %gradient_terms.10 = bf16[4,512,256]{2,1,0:T(8,128)(2,1)S(1)} custom-call(s32[4]{0:T(128)S(1)} %broadcast_xor_fusion.1.block_ref, bf16[512,1024]{1,0:T(8,128)(2,1)S(1)} %get-tuple-element.24.refs_0_, bf16[1024,2048]{1,0:T(8,128)(2,1)} %refs_1_.7), custom_call_target="tpu_custom_call" | custom-call | flops 1073741824 | bytes 4194304 | tf_op jit(solution)/shard_map/gradient_terms/pallas_call | solution.py:89
  107.9 4.9 %fusion.11 = f32[512,2048]{1,0:T(8,128)} fusion(bf16[2048,3,512]{2,0,1:T(8,128)(2,1)} %param.15, bf16[256,512]{1,0:T(8,128)(2,1)S(1)} %get-tuple-element.42, bf16[256,512]{1,0:T(8,128)(2,1)S(1)} %get-tuple-element.41), kind=kOutput, calls=%fused_computation.14 | convolution fusion | flops 1074790400 | bytes 6815744 | tf_op jit(solution)/shard_map/dot_general | solution.py:28
  112.8 4.1 %gradient_terms.6 = bf16[4,512,256]{2,1,0:T(8,128)(2,1)S(1)} custom-call(s32[4]{0:T(128)S(1)} %broadcast_xor_fusion.3.block_ref, bf16[512,1024]{1,0:T(8,128)(2,1)S(1)} %get-tuple-element.19.refs_0_, bf16[1024,2048]{1,0:T(8,128)(2,1)} %refs_2_.3), custom_call_target="tpu_custom_call" | custom-call | flops 1073741824 | bytes 4194304 | tf_op jit(solution)/shard_map/gradient_terms/pallas_call | solution.py:89
  119.4 3.1 %fusion.5 = f32[512,2048]{1,0:T(8,128)S(1)} fusion(bf16[2048,3,512]{2,0,1:T(8,128)(2,1)} %param.15, bf16[256,512]{1,0:T(8,128)(2,1)S(1)} %get-tuple-element.49, bf16[256,512]{1,0:T(8,128)(2,1)S(1)} %get-tuple-element.50), kind=kOutput, calls=%fused_computation.8 | convolution fusion | flops 1074790400 | bytes 6815744 | tf_op jit(solution)/shard_map/dot_general | solution.py:28
  122.4 4.3 %add_convert_fusion = bf16[512,2048]{1,0:T(8,128)(2,1)} fusion(f32[512,2048]{1,0:T(8,128)S(1)} %copy-done.14, f32[512,2048]{1,0:T(8,128)S(1)} %fusion.5, bf16[2048,3,512]{2,0,1:T(8,128)(2,1)} %param.15, bf16[256,512]{1,0:T(8,128)(2,1)S(1)} %get-tuple-element.34, bf16[256,512]{1,0:T(8,128)(2,1)S(1)} %get-tuple-element.33), kind=kOutput, calls=%fused_computation.2 | convolution fusion | flops 1077936128 | bytes 13107200 | tf_op jit(solution)/shard_map/dot_general | solution.py:28
  139.0 3.1 %add_convert_fusion.1 = bf16[512,2048]{1,0:T(8,128)(2,1)S(1)} fusion(f32[512,2048]{1,0:T(8,128)S(1)} %fusion.13, f32[512,2048]{1,0:T(8,128)S(1)} %fusion.7, bf16[2048,3,512]{2,0,1:T(8,128)(2,1)} %param.15, bf16[256,512]{1,0:T(8,128)(2,1)S(1)} %get-tuple-element.35, bf16[256,512]{1,0:T(8,128)(2,1)S(1)} %get-tuple-element.36), kind=kOutput, calls=%fused_computation.3 | convolution fusion | flops 1077936128 | bytes 13107200 | tf_op jit(solution)/shard_map/dot_general | solution.py:28
  142.2 3.8 %collective-permute-done.15 = bf16[2,512,256]{2,1,0:T(8,128)(2,1)S(1)} collective-permute-done((bf16[2,512,256]{2,1,0:T(8,128)(2,1)S(1)}, bf16[2,512,256]{2,1,0:T(8,128)(2,1)S(1)}, u32[]{:S(2)}, u32[]{:S(2)}) %collective-permute-start.15) | collective-permute-done | bytes 524320 | tf_op jit(solution)/shard_map/ppermute | solution.py:33
  149.4 29.9 %collective-permute-done.12 = bf16[2,1024,256]{2,1,0:T(8,128)(2,1)S(1)} collective-permute-done((bf16[2,1024,256]{2,1,0:T(8,128)(2,1)S(1)}, bf16[2,1024,256]{2,1,0:T(8,128)(2,1)S(1)}, u32[]{:S(2)}, u32[]{:S(2)}) %collective-permute-start.12) | collective-permute-done | bytes 1048608 | tf_op jit(solution)/shard_map/ppermute | solution.py:33
  185.7 18.7 %collective-permute-done.13 = bf16[1,1024,256]{2,1,0:T(8,128)(2,1)S(1)} collective-permute-done((bf16[1,1024,256]{2,1,0:T(8,128)(2,1)S(1)}, bf16[1,1024,256]{2,1,0:T(8,128)(2,1)S(1)}, u32[]{:S(2)}, u32[]{:S(2)}) %collective-permute-start.13) | collective-permute-done | bytes 524320 | tf_op jit(solution)/shard_map/ppermute | solution.py:33
  205.9 3.2 %copy.17 = f32[256,3,512]{2,0,1:T(8,128)} copy(f32[256,3,512]{0,2,1:T(8,128)} %pad_maximum_fusion) | data formatting | bytes 3145728
  (112 shorter events, 47.1 us)
Async XLA Ops:
  0.6 30.0 %copy-start = (bf16[512,2048]{1,0:T(8,128)(2,1)S(1)}, bf16[512,2048]{1,0:T(8,128)(2,1)}, u32[]{:S(2)}) copy-start(bf16[512,2048]{1,0:T(8,128)(2,1)} %param.16) | copy-start | bytes 6291460
  10.3 6.3 %copy-start.22 = (s32[4]{0:T(128)S(1)}, s32[4]{0:T(128)}, u32[]{:S(2)}) copy-start(s32[4]{0:T(128)} %constant.38.clone) | copy-start | bytes 52
  13.7 23.5 %collective-permute-start = (bf16[4,128,128]{2,1,0:T(8,128)(2,1)}, bf16[4,128,128]{2,1,0:T(8,128)(2,1)S(1)}, u32[]{:S(2)}, u32[]{:S(2)}) collective-permute-start(bf16[4,128,128]{2,1,0:T(8,128)(2,1)} %convert_element_type.148), channel_id=1, source_target_pairs={{0,4},{4,0},{8,12},{12,8},{16,20},{20,16},{24,28},{28,24},{1,5},{5... | collective-permute-start | bytes 393224 | tf_op jit(solution)/shard_map/ppermute | solution.py:33
  17.9 6.1 %copy-start.12 = (bf16[1024,2048]{1,0:T(8,128)(2,1)S(1)}, bf16[1024,2048]{1,0:T(8,128)(2,1)}, u32[]{:S(2)}) copy-start(bf16[1024,2048]{1,0:T(8,128)(2,1)} %refs_2_.3) | copy-start | bytes 12582916
  24.0 6.0 %copy-start.20 = (bf16[512]{0:T(512)(128)(2,1)S(1)}, bf16[512]{0:T(512)(128)(2,1)}, u32[]{:S(2)}) copy-start(bf16[512]{0:T(512)(128)(2,1)} %param.17) | copy-start | bytes 3076
  24.0 110.7 %collective-permute-start.11 = (bf16[4,1024,256]{2,1,0:T(8,128)(2,1)}, bf16[4,1024,256]{2,1,0:T(8,128)(2,1)}, u32[]{:S(2)}, u32[]{:S(2)}) collective-permute-start(bf16[4,1024,256]{2,1,0:T(8,128)(2,1)} %gradient_terms.9), channel_id=1, source_target_pairs={{0,4},{4,0},{8,12},{12,8},{16,20},{20,16},{24,28},{28,24},{1,5},{5... | collective-permute-start | bytes 6291464 | tf_op jit(solution)/shard_map/ppermute | solution.py:33
  30.6 8.7 %copy-start.21 = (s32[4]{0:T(128)S(1)}, s32[4]{0:T(128)}, u32[]{:S(2)}) copy-start(s32[4]{0:T(128)} %constant.41.clone) | copy-start | bytes 52
  37.3 5.1 %collective-permute-start.1 = (bf16[4,128,128]{2,1,0:T(8,128)(2,1)S(1)}, bf16[4,128,128]{2,1,0:T(8,128)(2,1)S(1)}, u32[]{:S(2)}, u32[]{:S(2)}) collective-permute-start(bf16[4,128,128]{2,1,0:T(8,128)(2,1)S(1)} %fusion.64), channel_id=1, source_target_pairs={{0,8},{4,12},{8,0},{12,4},{16,24},{20,28},{24,16},{28,20},{1,9},{5... | collective-permute-start | bytes 393224 | tf_op jit(solution)/shard_map/ppermute | solution.py:33
  42.4 9.2 %collective-permute-start.2 = (bf16[4,128,128]{2,1,0:T(8,128)(2,1)S(1)}, bf16[4,128,128]{2,1,0:T(8,128)(2,1)S(1)}, u32[]{:S(2)}, u32[]{:S(2)}) collective-permute-start(bf16[4,128,128]{2,1,0:T(8,128)(2,1)S(1)} %fusion.58), channel_id=1, source_target_pairs={{0,16},{4,20},{8,24},{12,28},{16,0},{20,4},{24,8},{28,12},{1,17},{... | collective-permute-start | bytes 393224 | tf_op jit(solution)/shard_map/ppermute | solution.py:33
  61.3 68.4 %collective-permute-start.14 = (bf16[4,512,256]{2,1,0:T(8,128)(2,1)S(1)}, bf16[4,512,256]{2,1,0:T(8,128)(2,1)}, u32[]{:S(2)}, u32[]{:S(2)}) collective-permute-start(bf16[4,512,256]{2,1,0:T(8,128)(2,1)S(1)} %gradient_terms.11), channel_id=1, source_target_pairs={{0,4},{4,0},{8,12},{12,8},{16,20},{20,16},{24,28},{28,24},{1,5},{5... | collective-permute-start | bytes 3145736 | tf_op jit(solution)/shard_map/ppermute | solution.py:33
  66.9 64.9 %collective-permute-start.8 = (bf16[4,512,256]{2,1,0:T(8,128)(2,1)S(1)}, bf16[4,512,256]{2,1,0:T(8,128)(2,1)}, u32[]{:S(2)}, u32[]{:S(2)}) collective-permute-start(bf16[4,512,256]{2,1,0:T(8,128)(2,1)S(1)} %gradient_terms.7), channel_id=1, source_target_pairs={{0,8},{4,12},{8,0},{12,4},{16,24},{20,28},{24,16},{28,20},{1,9},{5... | collective-permute-start | bytes 3145736 | tf_op jit(solution)/shard_map/ppermute | solution.py:33
  68.5 28.1 %collective-permute-start.3 = (bf16[4,128,128]{2,1,0:T(8,128)(2,1)S(1)}, bf16[4,128,128]{2,1,0:T(8,128)(2,1)S(1)}, u32[]{:S(2)}, u32[]{:S(2)}) collective-permute-start(bf16[4,128,128]{2,1,0:T(8,128)(2,1)S(1)} %convert_element_type.155), channel_id=1, source_target_pairs={{0,4},{4,0},{8,12},{12,8},{16,20},{20,16},{24,28},{28,24},{1,5},{5... | collective-permute-start | bytes 393224 | tf_op jit(solution)/shard_map/ppermute | solution.py:33
  96.6 8.6 %collective-permute-start.4 = (bf16[4,128,128]{2,1,0:T(8,128)(2,1)S(1)}, bf16[4,128,128]{2,1,0:T(8,128)(2,1)S(1)}, u32[]{:S(2)}, u32[]{:S(2)}) collective-permute-start(bf16[4,128,128]{2,1,0:T(8,128)(2,1)S(1)} %fusion.63), channel_id=1, source_target_pairs={{0,8},{4,12},{8,0},{12,4},{16,24},{20,28},{24,16},{28,20},{1,9},{5... | collective-permute-start | bytes 393224 | tf_op jit(solution)/shard_map/ppermute | solution.py:33
  105.3 11.6 %collective-permute-start.5 = (bf16[4,128,128]{2,1,0:T(8,128)(2,1)S(1)}, bf16[4,128,128]{2,1,0:T(8,128)(2,1)S(1)}, u32[]{:S(2)}, u32[]{:S(2)}) collective-permute-start(bf16[4,128,128]{2,1,0:T(8,128)(2,1)S(1)} %fusion.62), channel_id=1, source_target_pairs={{0,16},{4,20},{8,24},{12,28},{16,0},{20,4},{24,8},{28,12},{1,17},{... | collective-permute-start | bytes 393224 | tf_op jit(solution)/shard_map/ppermute | solution.py:33
  126.8 53.0 %collective-permute-start.6 = (bf16[2,256,2048]{2,1,0:T(8,128)(2,1)}, bf16[2,256,2048]{2,1,0:T(8,128)(2,1)}, u32[]{:S(2)}, u32[]{:S(2)}) collective-permute-start(bf16[2,256,2048]{2,1,0:T(8,128)(2,1)} %bitcast.5), channel_id=1, source_target_pairs={{0,1},{1,0},{2,3},{3,2},{4,5},{5,4},{6,7},{7,6},{8,9},{9,8},{10,11... | collective-permute-start | bytes 6291464 | tf_op jit(solution)/shard_map/ppermute | solution.py:33
  131.2 14.8 %collective-permute-start.15 = (bf16[2,512,256]{2,1,0:T(8,128)(2,1)S(1)}, bf16[2,512,256]{2,1,0:T(8,128)(2,1)S(1)}, u32[]{:S(2)}, u32[]{:S(2)}) collective-permute-start(bf16[2,512,256]{2,1,0:T(8,128)(2,1)S(1)} %slice.99), channel_id=1, source_target_pairs={{0,8},{4,12},{8,0},{12,4},{16,24},{20,28},{24,16},{28,20},{1,9},{5... | collective-permute-start | bytes 1572872 | tf_op jit(solution)/shard_map/ppermute | solution.py:33
  134.2 14.3 %collective-permute-start.9 = (bf16[2,512,256]{2,1,0:T(8,128)(2,1)}, bf16[2,512,256]{2,1,0:T(8,128)(2,1)S(1)}, u32[]{:S(2)}, u32[]{:S(2)}) collective-permute-start(bf16[2,512,256]{2,1,0:T(8,128)(2,1)} %slice.91), channel_id=1, source_target_pairs={{0,4},{4,0},{8,12},{12,8},{16,20},{20,16},{24,28},{28,24},{1,5},{5... | collective-permute-start | bytes 1572872 | tf_op jit(solution)/shard_map/ppermute | solution.py:33
  137.4 42.0 %collective-permute-start.12 = (bf16[2,1024,256]{2,1,0:T(8,128)(2,1)S(1)}, bf16[2,1024,256]{2,1,0:T(8,128)(2,1)S(1)}, u32[]{:S(2)}, u32[]{:S(2)}) collective-permute-start(bf16[2,1024,256]{2,1,0:T(8,128)(2,1)S(1)} %get-tuple-element.23), channel_id=1, source_target_pairs={{0,8},{4,12},{8,0},{12,4},{16,24},{20,28},{24,16},{28,20},{1,9},{5... | collective-permute-start | bytes 3145736 | tf_op jit(solution)/shard_map/ppermute | solution.py:33
  139.0 7.0 %copy-start.16 = (bf16[4,512,256]{2,1,0:T(8,128)(2,1)S(1)}, bf16[4,512,256]{2,1,0:T(8,128)(2,1)}, u32[]{:S(2)}) copy-start(bf16[4,512,256]{2,1,0:T(8,128)(2,1)} %copy-done.15) | copy-start | bytes 3145732
  142.2 6.3 %copy-start.18 = (bf16[4,512,256]{2,1,0:T(8,128)(2,1)S(1)}, bf16[4,512,256]{2,1,0:T(8,128)(2,1)}, u32[]{:S(2)}) copy-start(bf16[4,512,256]{2,1,0:T(8,128)(2,1)} %copy-done.17) | copy-start | bytes 3145732
  146.2 38.6 %collective-permute-start.16 = (bf16[1,512,256]{2,1,0:T(8,128)(2,1)S(1)}, bf16[1,512,256]{2,1,0:T(8,128)(2,1)S(1)}, u32[]{:S(2)}, u32[]{:S(2)}) collective-permute-start(bf16[1,512,256]{2,1,0:T(8,128)(2,1)S(1)} %slice.101), channel_id=1, source_target_pairs={{0,16},{4,20},{8,24},{12,28},{16,0},{20,4},{24,8},{28,12},{1,17},{... | collective-permute-start | bytes 786440 | tf_op jit(solution)/shard_map/ppermute | solution.py:33
  148.7 36.9 %collective-permute-start.10 = (bf16[1,512,256]{2,1,0:T(8,128)(2,1)S(1)}, bf16[1,512,256]{2,1,0:T(8,128)(2,1)S(1)}, u32[]{:S(2)}, u32[]{:S(2)}) collective-permute-start(bf16[1,512,256]{2,1,0:T(8,128)(2,1)S(1)} %slice.93), channel_id=1, source_target_pairs={{0,16},{4,20},{8,24},{12,28},{16,0},{20,4},{24,8},{28,12},{1,17},{... | collective-permute-start | bytes 786440 | tf_op jit(solution)/shard_map/ppermute | solution.py:33
  179.7 24.7 %collective-permute-start.13 = (bf16[1,1024,256]{2,1,0:T(8,128)(2,1)S(1)}, bf16[1,1024,256]{2,1,0:T(8,128)(2,1)S(1)}, u32[]{:S(2)}, u32[]{:S(2)}) collective-permute-start(bf16[1,1024,256]{2,1,0:T(8,128)(2,1)S(1)} %slice.95), channel_id=1, source_target_pairs={{0,16},{4,20},{8,24},{12,28},{16,0},{20,4},{24,8},{28,12},{1,17},{... | collective-permute-start | bytes 1572872 | tf_op jit(solution)/shard_map/ppermute | solution.py:33
  183.3 25.8 %collective-permute-start.7 = (bf16[1,256,2048]{2,1,0:T(8,128)(2,1)}, bf16[1,256,2048]{2,1,0:T(8,128)(2,1)S(1)}, u32[]{:S(2)}, u32[]{:S(2)}) collective-permute-start(bf16[1,256,2048]{2,1,0:T(8,128)(2,1)} %slice.89), channel_id=1, source_target_pairs={{0,2},{1,3},{2,0},{3,1},{4,6},{5,7},{6,4},{7,5},{8,10},{9,11},{10,... | collective-permute-start | bytes 3145736 | tf_op jit(solution)/shard_map/ppermute | solution.py:33
  (16 other events, 56.8 us)

commit v2 on v1

v2 whole, which is shorter than its diff:
```python
import functools

import jax
import jax.numpy as jnp
from jax import lax
from jax.experimental import pallas as pl
from jax.experimental.pallas import tpu as pltpu
from jax.sharding import PartitionSpec as P

D = 2048
HD = 128
BLOCK = 1024
epsilon = 1e-06
f32 = jnp.float32
bf16 = jnp.bfloat16
VMEM_LIMIT = 48 * 1024 * 1024


def params():
    return pltpu.CompilerParams(vmem_limit_bytes=VMEM_LIMIT)


def dot(a, b):
    return lax.dot_general(a, b, (((1,), (0,)), ((), ())), preferred_element_type=f32)


def dot_t(a, b):
    return lax.dot_general(a, b, (((1,), (1,)), ((), ())), preferred_element_type=f32)


def exchange(arr, axis, bit):
    count = lax.axis_size(axis)
    return lax.ppermute(arr, axis, [(i, i ^ (1 << bit)) for i in range(count)])


def slot_order(stage_bits):
    order = [0]
    for bit in reversed(stage_bits):
        order = order + [slot | (1 << bit) for slot in order]
    return order


def state_kernel(key_ref, value_ref, state_ref, key_t_ref, value_t_ref):
    key_t = key_ref[...].T
    key_t_ref[...] = key_t
    value_t_ref[...] = value_ref[...].T
    state_ref[0] = dot(key_t, value_ref[...])


def block_states(keys, values):
    count, width = keys.shape
    heads = width // HD
    column = pl.BlockSpec((count, HD), lambda h: (0, h))
    row = pl.BlockSpec((HD, count), lambda h: (h, 0))
    return pl.pallas_call(
        state_kernel,
        grid=(heads,),
        in_specs=[column, column],
        out_specs=[pl.BlockSpec((1, HD, HD), lambda h: (h, 0, 0)), row, row],
        out_shape=[
            jax.ShapeDtypeStruct((heads, HD, HD), f32),
            jax.ShapeDtypeStruct((width, count), bf16),
            jax.ShapeDtypeStruct((width, count), bf16),
        ],
        compiler_params=params(),
        cost_estimate=pl.CostEstimate(
            flops=2 * count * width * HD, bytes_accessed=8 * count * width, transcendentals=0
        ),
        name="block_states",
    )(keys, values)


def terms_kernel(count_left, slots, block_ref, *refs):
    lefts, right = refs[:count_left], refs[count_left]
    out, held, sems = refs[count_left + 1 :]
    width = out.shape[2]
    copies = []
    for index in range(slots):
        start = pl.multiple_of(block_ref[index] * width, width)
        copy = pltpu.make_async_copy(right.at[:, pl.ds(start, width)], held.at[index], sems.at[index])
        copy.start()
        copies.append(copy)
    for index in range(slots):
        copies[index].wait()
        low = 0
        for ref in lefts:
            high = low + ref.shape[0]
            out[index, low:high, :] = dot(ref[...], held[index]).astype(bf16)
            low = high


def gradient_terms(lefts, right, position, slots):
    rows, count = lefts[0].shape
    width = right.shape[1] // lax.axis_size("seq")
    total = rows * len(lefts)
    number = len(slots)
    blocks = position ^ jnp.array(slots, jnp.int32)
    if width % 128:
        picked = jnp.take(right.reshape(count, -1, width), blocks, axis=1)
        left = jnp.concatenate(lefts, 0)
        return jnp.einsum("at,tnb->nab", left, picked, preferred_element_type=f32).astype(bf16)
    vmem = pl.BlockSpec(memory_space=pltpu.VMEM)
    return pl.pallas_call(
        functools.partial(terms_kernel, len(lefts), number),
        in_specs=[pl.BlockSpec(memory_space=pltpu.SMEM)]
        + [vmem] * len(lefts)
        + [pl.BlockSpec(memory_space=pl.ANY)],
        out_specs=vmem,
        out_shape=jax.ShapeDtypeStruct((number, total, width), bf16),
        scratch_shapes=[pltpu.VMEM((number, count, width), bf16), pltpu.SemaphoreType.DMA((number,))],
        compiler_params=params(),
        cost_estimate=pl.CostEstimate(
            flops=2 * count * total * width * number,
            bytes_accessed=2 * number * width * (count + total) + 2 * total * count,
            transcendentals=0,
        ),
        name="gradient_terms",
    )(blocks, *lefts, right)


def middle_kernel(query_ref, grad_ref, mask_ref, gain_ref, state_ref, normed_t_ref, query_grad_ref, query_grad_t_ref, block_grad_ref):
    query = query_ref[...]
    state = state_ref[0]
    mask = mask_ref[...]
    gain = gain_ref[...].astype(f32)
    attended = dot(query, state)
    scale = lax.rsqrt(jnp.mean(attended * attended, -1, keepdims=True) + epsilon)
    unit = attended * scale
    normed_t_ref[...] = (unit * gain * mask).astype(bf16).T
    scaled = grad_ref[...] * mask * gain
    inner = jnp.mean(scaled * attended, -1, keepdims=True)
    attended_grad = (scale * scaled - attended * (scale * scale * scale) * inner).astype(bf16)
    attended_grad_t = attended_grad.T
    block_grad_ref[0] = dot(attended_grad_t, query)
    query_grad_ref[...] = dot_t(attended_grad, state).astype(bf16)
    query_grad_t_ref[...] = dot(state, attended_grad_t).astype(bf16)


def middle(queries, normed_grad, mask, gain, state):
    count, width = queries.shape
    heads = width // HD
    column = pl.BlockSpec((count, HD), lambda h: (0, h))
    row = pl.BlockSpec((HD, count), lambda h: (h, 0))
    square = pl.BlockSpec((1, HD, HD), lambda h: (h, 0, 0))
    return pl.pallas_call(
        middle_kernel,
        grid=(heads,),
        in_specs=[
            column,
            column,
            pl.BlockSpec((count, 1), lambda h: (0, 0)),
            pl.BlockSpec((1, HD), lambda h: (0, h)),
            square,
        ],
        out_specs=[row, column, row, square],
        out_shape=[
            jax.ShapeDtypeStruct((width, count), bf16),
            jax.ShapeDtypeStruct((count, width), bf16),
            jax.ShapeDtypeStruct((width, count), bf16),
            jax.ShapeDtypeStruct((heads, HD, HD), f32),
        ],
        compiler_params=params(),
        cost_estimate=pl.CostEstimate(
            flops=8 * count * width * HD, bytes_accessed=12 * count * width, transcendentals=count
        ),
        name="norm_backward",
    )(queries, normed_grad, mask, gain, state)


def late_kernel(flip, mine_ref, other_ref, own_keep_ref, own_send_ref, got_keep_ref, got_send_ref, keep_ref, send_ref):
    side = 0 if flip else 1

    def times(state, block):
        return lax.dot_general(state, block, (((side,), (0,)), ((), ())), preferred_element_type=f32)

    for own, got, out in ((own_keep_ref, got_keep_ref, keep_ref), (own_send_ref, got_send_ref, send_ref)):
        for h in range(mine_ref.shape[0]):
            rows = slice(h * HD, (h + 1) * HD)
            out[0, rows, :] = (times(mine_ref[h], own[0, rows, :]) + times(other_ref[h], got[0, rows, :])).astype(bf16)


def late_terms(flip, mine, other, own, got):
    slots, total, width = own.shape
    heads = mine.shape[0]
    half = slots // 2
    square = pl.BlockSpec((heads, HD, HD), lambda i: (0, 0, 0))
    low = pl.BlockSpec((1, total, width), lambda i: (i, 0, 0))
    high = pl.BlockSpec((1, total, width), lambda i: (i + half, 0, 0))
    out = jax.ShapeDtypeStruct((half, total, width), bf16)
    return pl.pallas_call(
        functools.partial(late_kernel, flip),
        grid=(half,),
        in_specs=[square, square, low, high, low, high],
        out_specs=[low, low],
        out_shape=[out, out],
        compiler_params=params(),
        cost_estimate=pl.CostEstimate(
            flops=4 * slots * total * width * HD, bytes_accessed=6 * slots * total * width, transcendentals=0
        ),
        name="late_terms",
    )(mine, other, own, own, got, got)


def key_value_kernel(key_ref, value_ref, grad_ref, key_grad_ref, value_grad_ref):
    key_grad_ref[...] = dot(value_ref[...], grad_ref[0]).astype(bf16)
    value_grad_ref[...] = dot_t(key_ref[...], grad_ref[0]).astype(bf16)


def key_value_grads(keys, values, state_grad_t):
    count, width = keys.shape
    column = pl.BlockSpec((count, HD), lambda h: (0, h))
    out = jax.ShapeDtypeStruct((count, width), bf16)
    return pl.pallas_call(
        key_value_kernel,
        grid=(width // HD,),
        in_specs=[column, column, pl.BlockSpec((1, HD, HD), lambda h: (h, 0, 0))],
        out_specs=[column, column],
        out_shape=[out, out],
        compiler_params=params(),
        cost_estimate=pl.CostEstimate(
            flops=4 * count * width * HD, bytes_accessed=8 * count * width, transcendentals=0
        ),
        name="key_value_grads",
    )(keys, values, state_grad_t)


def input_kernel(slots, block_ref, query_ref, key_ref, value_ref, weight_ref, out_ref):
    rows = out_ref.shape[1]
    for index in range(slots):
        start = pl.multiple_of(block_ref[index] * rows, rows)
        total = dot_t(query_ref[pl.ds(start, rows), :], weight_ref[0])
        total += dot_t(key_ref[pl.ds(start, rows), :], weight_ref[1])
        total += dot_t(value_ref[pl.ds(start, rows), :], weight_ref[2])
        out_ref[index] = total.astype(bf16)


def input_terms(grads, weight, place, slots, tile=512):
    count, width = grads[0].shape
    rows = count // lax.axis_size("head")
    number = len(slots)
    full = pl.BlockSpec((count, width), lambda i, b: (0, 0))
    return pl.pallas_call(
        functools.partial(input_kernel, number),
        grid_spec=pltpu.PrefetchScalarGridSpec(
            num_scalar_prefetch=1,
            grid=(D // tile,),
            in_specs=[full, full, full, pl.BlockSpec((3, tile, width), lambda i, b: (0, i, 0))],
            out_specs=pl.BlockSpec((number, rows, tile), lambda i, b: (0, 0, i)),
        ),
        out_shape=jax.ShapeDtypeStruct((number, rows, D), bf16),
        compiler_params=params(),
        cost_estimate=pl.CostEstimate(
            flops=6 * number * rows * width * D,
            bytes_accessed=6 * D * width + 6 * count * width + 2 * number * rows * D,
            transcendentals=0,
        ),
        name="input_terms",
    )(place ^ jnp.array(slots, jnp.int32), *grads, weight)


def finish_kernel(*refs):
    out = refs[-1]
    for index in range(3):
        keep, got = refs[2 * index], refs[2 * index + 1]
        out[index] = (keep[...].astype(f32) + got[...].astype(f32)).T


def finish(pairs):
    rows, width = pairs[0].shape
    return pl.pallas_call(
        finish_kernel,
        out_shape=jax.ShapeDtypeStruct((3, width, rows), f32),
        compiler_params=params(),
        name="finish",
    )(*pairs)


def after(value, *others):
    return lax.optimization_barrier((value,) + others)[0]


def split_sum(keep, got):
    total = keep.astype(f32) + got.astype(f32)
    half = total.shape[0] // 2
    return total[:half].astype(bf16), total[half:].astype(bf16)


def halving(keep, send, axis, stage_bits):
    for bit in stage_bits[:-1]:
        keep, send = split_sum(keep, exchange(send, axis, bit))
    return keep[0], exchange(send, axis, stage_bits[-1])[0]


def per_device(layer_input, output_grad, loss_mask, proj_weight, out_weight, norm_gain):
    count = layer_input.shape[0]
    position = lax.axis_index("seq")
    seq_bits = lax.axis_size("seq").bit_length() - 1
    head_bits = lax.axis_size("head").bit_length() - 1
    stages = list(range(seq_bits))
    swapped = [1, 0] + stages[2:]
    bits = [(position >> bit) & 1 == 1 for bit in stages]
    order, order_swapped = slot_order(stages), slot_order(swapped)
    half = len(order) // 2
    weights = jnp.transpose(proj_weight, (1, 0, 2))

    def project(rows, index):
        return jnp.dot(rows, weights[index], preferred_element_type=f32).astype(bf16)

    def terms(lefts, right, slots):
        return gradient_terms(lefts, right, position, slots)

    keys, values = project(layer_input, 1), project(layer_input, 2)
    own_state, keys_t, values_t = block_states(keys, values)
    mask = loss_mask.astype(f32)[:, None]

    got = exchange(own_state.astype(bf16), "seq", 0)
    value_send = terms([values_t], after(layer_input, own_state), order[half:])
    got = after(got, value_send)
    before = jnp.where(bits[0], got.astype(f32), 0.0)
    total = own_state + got.astype(f32)
    value_got = exchange(after(value_send, total), "seq", 0)

    got = exchange(total.astype(bf16), "seq", 1)
    queries = project(after(layer_input, total), 0)
    got = after(got, queries)
    before = before + jnp.where(bits[1], got.astype(f32), 0.0)
    total = total + got.astype(f32)

    for bit in stages[2:]:
        got = exchange(total.astype(bf16), "seq", bit)
        if bit == 2:
            key_send = terms([keys_t], after(layer_input, total), order_swapped[half:])
            key_got = exchange(key_send, "seq", 1)
            normed_grad = dot_t(after(output_grad, key_send), out_weight)
            got = after(got, normed_grad)
        before = before + jnp.where(bits[bit], got.astype(f32), 0.0)
        total = total + got.astype(f32)
    state = (before + own_state).astype(bf16)

    normed_t, query_grad, query_grad_t, own_grad = middle(
        queries, normed_grad, mask, norm_gain[None, :], state
    )

    got = exchange(own_grad.astype(bf16), "seq", 0)
    out_send = terms([normed_t], after(output_grad, own_grad), order[half:])
    out_keep = terms([normed_t], after(output_grad, out_send), order[:half])
    got = after(got, out_keep).astype(f32)
    total = own_grad + got
    mine, mate = jnp.where(bits[0], own_grad, total), jnp.where(bits[0], total, got)
    out_send = after(out_send, total)
    out_got = exchange(out_send, "seq", 0)

    got = exchange(jnp.stack([total, mine]).astype(bf16), "seq", 1)
    query_send = terms([query_grad_t], after(layer_input, total), order[half:])
    query_keep = terms([query_grad_t], after(layer_input, query_send), order[:half])
    got = after(got, query_keep).astype(f32)
    later = jnp.where(bits[1], 0.0, got[0])
    mine, mate = mine + later, mate + later
    other = got[1] + jnp.where(bits[1], total, 0.0)
    total = total + got[0]
    query_got = exchange(after(query_send, total), "seq", 0)

    for bit in stages[2:]:
        got = exchange(total.astype(bf16), "seq", bit)
        if bit == 2:
            value_keep = terms([values_t], after(layer_input, total), order[:half])
            key_keep = terms([keys_t], after(layer_input, value_keep), order_swapped[:half])
            got = after(got, key_keep)
        got = got.astype(f32)
        later = jnp.where(bits[bit], 0.0, got)
        mine, mate, other = mine + later, mate + later, other + later
        total = total + got
    state_grad, mate_grad, other_grad = mine.astype(bf16), mate.astype(bf16), other.astype(bf16)

    value_half = late_terms(True, state_grad, mate_grad, value_keep, value_got)
    value_pair = halving(*value_half, "seq", stages[1:])
    key_half = late_terms(False, state_grad, other_grad, after(key_keep, value_half[0]), key_got)
    key_pair = halving(*key_half, "seq", swapped[1:])

    key_grad, value_grad = key_value_grads(keys, values, after(state_grad, key_half[0]))
    place = lax.axis_index("head")
    head_stages = list(range(head_bits))
    token_order = slot_order(head_stages)
    middle_slot = len(token_order) // 2
    grads = (query_grad, key_grad, value_grad)
    input_send = input_terms(grads, weights, place, token_order[middle_slot:])
    input_keep = input_terms(grads, after(weights, input_send), place, token_order[:middle_slot])
    keep, got = halving(input_keep, input_send, "head", head_stages)
    input_grad = (keep.astype(f32) + got.astype(f32)).astype(bf16)

    keep, send = split_sum(out_keep, out_got)
    keep, got = halving(keep, send, "seq", stages[1:])
    out_weight_grad = keep.astype(f32) + got.astype(f32)

    keep, send = split_sum(query_keep, query_got)
    query_pair = halving(keep, send, "seq", stages[1:])
    proj_weight_grad = finish(query_pair + value_pair + key_pair)
    return (input_grad, jnp.transpose(proj_weight_grad, (1, 0, 2)), out_weight_grad)


def solution(mesh):
    in_specs = (
        P("seq", None),
        P("seq", None),
        P("seq"),
        P(None, None, "head"),
        P("head", None),
        P("head"),
    )
    out_specs = (P(("seq", "head"), None), P("seq", None, "head"), P("head", "seq"))
    return jax.shard_map(
        per_device, mesh=mesh, in_specs=in_specs, out_specs=out_specs, check_vma=False
    )
```

time: 213 us -> 175 us (0.82)
  waiting for transfers between devices: 84.8 us -> 49.3 us
  matrix products: 41.6 us -> 17.3 us
  Pallas kernels: 39.2 us -> 62.7 us
  starting transfers between devices: 21.6 us -> 26 us
  local copies, waits for them, and re-layouts: 10.1 us -> 7.13 us
  other arithmetic: 13.2 us -> 10.9 us
    ppermute x17 -> x20, waiting for transfers between devices: 84.8 us -> 49.3 us  [exchange(): return lax.ppermute(arr, axis, [(i, i ^ 1 << bit) for i in range(count)])]
    pallas_call x7 -> x13, Pallas kernels: 29.8 us -> 53.5 us  [the longest x8 36.6 us: gradient_terms(): pl.pallas_call(functools.partial(terms_kernel, len(lefts), number), in_sp...]
    dot_general x7 -> x1, matrix products: 27.1 us -> 3.72 us  [dot_t(): lax.dot_general(a, b, (((1,), (1,)), ((), ())), preferred_element_type=f32)]
    ppermute x17 -> x20, starting transfers between devices: 21.6 us -> 26 us  [exchange(): return lax.ppermute(arr, axis, [(i, i ^ 1 << bit) for i in range(count)])]
    another operation x8 -> x10, other arithmetic: 7.28 us -> 5.76 us
    unnamed x47 -> x48, local copies, waits for them, and re-layouts: 6.68 us -> 5.8 us
  transfers between devices with their start and end apart: 17 -> 20, of which waited for: 6 -> 5; matrix products, arithmetic and copies ran while one was open for 23% -> 10% of each run, Pallas kernels for 18% -> 35%
where the time goes in v2:
time: 175 us; the launch traced here: 174 us
  Pallas kernels  62.7 us (36%)
  waiting for transfers between devices  49.3 us (28%)
  starting transfers between devices  26 us (15%)
  matrix products  17.3 us (10%)
  other arithmetic  10.9 us (6%)
  local copies, waits for them, and re-layouts  7.13 us (4%)
    ppermute x20, waiting for transfers between devices, exchange(): return lax.ppermute(arr, axis, [(i, i ^ 1 << bit) for i in range(count)])  49.3 us
    pallas_call x8, Pallas kernels, gradient_terms(): pl.pallas_call(functools.partial(terms_kernel, len(lefts), number), in_sp...  36.6 us
    ppermute x20, starting transfers between devices, exchange(): return lax.ppermute(arr, axis, [(i, i ^ 1 << bit) for i in range(count)])  26 us
    dot_general x3, matrix products, project(): jnp.dot(rows, weights[index], preferred_element_type=f32).astype(bf16)  13.5 us
    pallas_call x2, Pallas kernels, input_terms(): pl.pallas_call(functools.partial(input_kernel, number), grid_spec=pltpu.P...  13.5 us
    unnamed x48, local copies, waits for them, and re-layouts  5.8 us
    pallas_call x1, Pallas kernels, middle(): pl.pallas_call(middle_kernel, grid=(heads,), in_specs=[column, column, pl...  5.73 us
    another operation x7, other arithmetic  5.65 us
  transfers between devices with their start and end apart: 20, of which 5 were waited for; matrix products, arithmetic and copies ran while one was open for 10% of the time, Pallas kernels for 35%

profile of v2, /device:TPU:0, one launch (start us, length us, event | category | flops | bytes accessed | tf_op | source)
XLA Modules:
  0.0 174.5 jit_solution(7302309264107892611)
XLA Ops:
  0.7 5.3 %fusion.3.key_ref = bf16[1024,512]{1,0:T(8,128)(2,1)S(1)} fusion(bf16[1024,2048]{1,0:T(8,128)(2,1)} %refs_1_.7, bf16[3,2048,512]{2,1,0:T(8,128)(2,1)} %bitcast.63), kind=kOutput, calls=%fused_computation.10 | convolution fusion | flops 2148007936 | bytes 7340032 | tf_op jit(solution)/shard_map/dot_general | solution.py:307
  6.0 4.3 %fusion.4.value_ref = bf16[1024,512]{1,0:T(8,128)(2,1)S(1)} fusion(bf16[1024,2048]{1,0:T(8,128)(2,1)S(1)} %copy-done.14, bf16[3,2048,512]{2,1,0:T(8,128)(2,1)} %bitcast.64), kind=kOutput, calls=%fused_computation.11 | convolution fusion | flops 2148007936 | bytes 7340032 | tf_op jit(solution)/shard_map/dot_general | solution.py:307
  13.6 3.0 %collective-permute-start = (bf16[4,128,128]{2,1,0:T(8,128)(2,1)}, bf16[4,128,128]{2,1,0:T(8,128)(2,1)}, u32[]{:S(2)}, u32[]{:S(2)}) collective-permute-start(bf16[4,128,128]{2,1,0:T(8,128)(2,1)} %convert_element_type.140), channel_id=1, source_target_pairs={{0,4},{4,0},{8,12},{12,8},{16,20},{20,16},{24,28},{28,24},{1,5},{5... | collective-permute-start | bytes 393224 | tf_op jit(solution)/shard_map/ppermute | solution.py:33
  18.9 4.7 %gradient_terms.8 = bf16[4,512,256]{2,1,0:T(8,128)(2,1)S(1)} custom-call(s32[4]{0:T(128)S(1)} %broadcast_xor_fusion.3.block_ref, bf16[512,1024]{1,0:T(8,128)(2,1)S(1)} %copy-done.3, bf16[1024,2048]{1,0:T(8,128)(2,1)} %refs_1_.7), custom_call_target="tpu_custom_call" | custom-call | flops 1073741824 | bytes 4194304 | tf_op jit(solution)/shard_map/gradient_terms/pallas_call | solution.py:103
  26.2 3.9 %fusion.5.query_ref = bf16[1024,512]{1,0:T(8,128)(2,1)S(1)} fusion(bf16[1024,2048]{1,0:T(8,128)(2,1)S(1)} %copy-done.15, bf16[3,2048,512]{2,1,0:T(8,128)(2,1)} %bitcast.65), kind=kOutput, calls=%fused_computation.12 | convolution fusion | flops 2148007936 | bytes 7340032 | tf_op jit(solution)/shard_map/dot_general | solution.py:307
  30.7 2.6 %collective-permute-start.2 = (bf16[4,128,128]{2,1,0:T(8,128)(2,1)S(1)}, bf16[4,128,128]{2,1,0:T(8,128)(2,1)S(1)}, u32[]{:S(2)}, u32[]{:S(2)}) collective-permute-start(bf16[4,128,128]{2,1,0:T(8,128)(2,1)S(1)} %convert_add_fusion.1), channel_id=1, source_target_pairs={{0,16},{4,20},{8,24},{12,28},{16,0},{20,4},{24,8},{28,12},{1,17},{... | collective-permute-start | bytes 393224 | tf_op jit(solution)/shard_map/ppermute | solution.py:33
  33.4 5.6 %gradient_terms.9 = bf16[4,512,256]{2,1,0:T(8,128)(2,1)} custom-call(s32[4]{0:T(128)S(1)} %broadcast_xor_fusion.2.block_ref, bf16[512,1024]{1,0:T(8,128)(2,1)S(1)} %get-tuple-element.43.refs_0_, bf16[1024,2048]{1,0:T(8,128)(2,1)} %refs_1_.7), custom_call_target="tpu_custom_call" | custom-call | flops 1073741824 | bytes 4194304 | tf_op jit(solution)/shard_map/gradient_terms/pallas_call | solution.py:103
  39.6 3.7 %fusion.23.grad_ref = f32[1024,512]{1,0:T(8,128)} fusion(bf16[1024,2048]{1,0:T(8,128)(2,1)S(1)} %copy-done.16, bf16[512,2048]{1,0:T(8,128)(2,1)S(1)} %copy-done), kind=kOutput, calls=%fused_computation.58 | convolution fusion | flops 2147483648 | bytes 8388608 | tf_op jit(solution)/shard_map/dot_general | solution.py:28
  44.3 5.7 %norm_backward.1 = (bf16[512,1024]{1,0:T(8,128)(2,1)S(1)}, bf16[1024,512]{1,0:T(8,128)(2,1)S(1)}, bf16[512,1024]{1,0:T(8,128)(2,1)S(1)}, f32[4,128,128]{2,1,0:T(8,128)S(1)}) custom-call(bf16[1024,512]{1,0:T(8,128)(2,1)S(1)} %fusion.5.query_ref, f32[1024,512]{1,0:T(8,128)} %fusion.23.grad_ref, f32[1024,1]{1,0:T(8,128)S(1)} %copy-done.9, ...), custom_call_target="tpu_custom_call" | custom-call | flops 536870912 | bytes 6291456 | tf_op jit(solution)/shard_map/norm_backward/pallas_call | solution.py:145
  52.6 4.4 %gradient_terms.10 = bf16[4,512,256]{2,1,0:T(8,128)(2,1)S(1)} custom-call(s32[4]{0:T(128)S(1)} %broadcast_xor_fusion.3.block_ref, bf16[512,1024]{1,0:T(8,128)(2,1)S(1)} %get-tuple-element.50.refs_0_, bf16[1024,2048]{1,0:T(8,128)(2,1)} %refs_1_.3), custom_call_target="tpu_custom_call" | custom-call | flops 1073741824 | bytes 4194304 | tf_op jit(solution)/shard_map/gradient_terms/pallas_call | solution.py:103
  57.0 4.4 %gradient_terms.11 = bf16[4,512,256]{2,1,0:T(8,128)(2,1)S(1)} custom-call(s32[4]{0:T(128)S(1)} %broadcast_xor_fusion.1.block_ref, bf16[512,1024]{1,0:T(8,128)(2,1)S(1)} %get-tuple-element.50.refs_0_, bf16[1024,2048]{1,0:T(8,128)(2,1)} %refs_1_.3), custom_call_target="tpu_custom_call" | custom-call | flops 1073741824 | bytes 4194304 | tf_op jit(solution)/shard_map/gradient_terms/pallas_call | solution.py:103
  63.7 4.4 %gradient_terms.12 = bf16[4,512,256]{2,1,0:T(8,128)(2,1)S(1)} custom-call(s32[4]{0:T(128)S(1)} %broadcast_xor_fusion.3.block_ref, bf16[512,1024]{1,0:T(8,128)(2,1)S(1)} %get-tuple-element.54.refs_0_, bf16[1024,2048]{1,0:T(8,128)(2,1)} %refs_1_.7), custom_call_target="tpu_custom_call" | custom-call | flops 1073741824 | bytes 4194304 | tf_op jit(solution)/shard_map/gradient_terms/pallas_call | solution.py:103
  68.1 4.4 %gradient_terms.13 = bf16[4,512,256]{2,1,0:T(8,128)(2,1)S(1)} custom-call(s32[4]{0:T(128)S(1)} %broadcast_xor_fusion.1.block_ref, bf16[512,1024]{1,0:T(8,128)(2,1)S(1)} %get-tuple-element.54.refs_0_, bf16[1024,2048]{1,0:T(8,128)(2,1)} %refs_1_.7), custom_call_target="tpu_custom_call" | custom-call | flops 1073741824 | bytes 4194304 | tf_op jit(solution)/shard_map/gradient_terms/pallas_call | solution.py:103
  73.7 4.4 %gradient_terms.14.own_keep_ref.own_send_ref = bf16[4,512,256]{2,1,0:T(8,128)(2,1)S(1)} custom-call(s32[4]{0:T(128)S(1)} %broadcast_xor_fusion.1.block_ref, bf16[512,1024]{1,0:T(8,128)(2,1)S(1)} %copy-done.4, bf16[1024,2048]{1,0:T(8,128)(2,1)} %refs_1_.7), custom_call_target="tpu_custom_call" | custom-call | flops 1073741824 | bytes 4194304 | tf_op jit(solution)/shard_map/gradient_terms/pallas_call | solution.py:103
  78.1 4.4 %gradient_terms.15.own_keep_ref.own_send_ref = bf16[4,512,256]{2,1,0:T(8,128)(2,1)S(1)} custom-call(s32[4]{0:T(128)S(1)} %broadcast_xor_fusion.block_ref, bf16[512,1024]{1,0:T(8,128)(2,1)S(1)} %get-tuple-element.43.refs_0_, bf16[1024,2048]{1,0:T(8,128)(2,1)} %refs_1_.7), custom_call_target="tpu_custom_call" | custom-call | flops 1073741824 | bytes 4194304 | tf_op jit(solution)/shard_map/gradient_terms/pallas_call | solution.py:103
  87.1 6.6 %input_terms.2 = bf16[2,256,2048]{2,1,0:T(8,128)(2,1)S(1)} custom-call(s32[2]{0:T(128)S(1)} %broadcast_xor_fusion.4.block_ref, bf16[1024,512]{1,0:T(8,128)(2,1)S(1)} %copy-done.11, bf16[1024,512]{1,0:T(8,128)(2,1)S(1)} %get-tuple-element.66.key_ref, bf16[1024,512]{1,0:T(8,128)(2,1)S(1)} %get-tuple-element.67.value_ref, bf16[3,2048,512]{2,1,0:T(8,128)(2,1)} %bitcast.66), custom_call_target="tpu_custom_call" | custom-call | flops 3221225472 | bytes 11534336 | tf_op jit(solution)/shard_map/input_terms/pallas_call | solution.py:242
  97.6 6.8 %input_terms.3 = bf16[2,256,2048]{2,1,0:T(8,128)(2,1)S(1)} custom-call(s32[2]{0:T(128)S(1)} %multiply_xor_fusion.block_ref, bf16[1024,512]{1,0:T(8,128)(2,1)S(1)} %copy-done.11, bf16[1024,512]{1,0:T(8,128)(2,1)S(1)} %get-tuple-element.66.key_ref, bf16[1024,512]{1,0:T(8,128)(2,1)S(1)} %copy-done.13, bf16[3,2048,512]{2,1,0:T(8,128)(2,1)} %bitcast.67), custom_call_target="tpu_custom_call" | custom-call | flops 3221225472 | bytes 11534336 | tf_op jit(solution)/shard_map/input_terms/pallas_call | solution.py:242
  107.6 2.7 %collective-permute-done.13 = bf16[2,512,256]{2,1,0:T(8,128)(2,1)} collective-permute-done((bf16[2,512,256]{2,1,0:T(8,128)(2,1)S(1)}, bf16[2,512,256]{2,1,0:T(8,128)(2,1)}, u32[]{:S(2)}, u32[]{:S(2)}) %collective-permute-start.13) | collective-permute-done | bytes 524320 | tf_op jit(solution)/shard_map/ppermute | solution.py:33
  113.5 6.4 %collective-permute-done.10 = bf16[4,512,256]{2,1,0:T(8,128)(2,1)S(1)} collective-permute-done((bf16[4,512,256]{2,1,0:T(8,128)(2,1)S(1)}, bf16[4,512,256]{2,1,0:T(8,128)(2,1)S(1)}, u32[]{:S(2)}, u32[]{:S(2)}) %collective-permute-start.10) | collective-permute-done | bytes 1048608 | tf_op jit(solution)/shard_map/ppermute | solution.py:33
  120.7 9.9 %collective-permute-done.15 = bf16[2,512,256]{2,1,0:T(8,128)(2,1)S(1)} collective-permute-done((bf16[2,512,256]{2,1,0:T(8,128)(2,1)S(1)}, bf16[2,512,256]{2,1,0:T(8,128)(2,1)S(1)}, u32[]{:S(2)}, u32[]{:S(2)}) %collective-permute-start.15) | collective-permute-done | bytes 524320 | tf_op jit(solution)/shard_map/ppermute | solution.py:33
  130.8 2.4 %add_convert_fusion = bf16[2,256,2048]{2,1,0:T(8,128)(2,1)S(1)} fusion(bf16[2,256,2048]{2,1,0:T(8,128)(2,1)} %collective-permute-done.8, bf16[2,256,2048]{2,1,0:T(8,128)(2,1)S(1)} %input_terms.3), kind=kLoop, calls=%fused_computation | loop fusion | flops 4194304 | bytes 6291456 | tf_op jit(solution)/shard_map/convert.13
  138.3 2.1 %collective-permute-start.12 = (bf16[1,512,256]{2,1,0:T(8,128)(2,1)S(1)}, bf16[1,512,256]{2,1,0:T(8,128)(2,1)S(1)}, u32[]{:S(2)}, u32[]{:S(2)}) collective-permute-start(bf16[1,512,256]{2,1,0:T(8,128)(2,1)S(1)} %get-tuple-element.84), channel_id=1, source_target_pairs={{0,16},{4,20},{8,24},{12,28},{16,0},{20,4},{24,8},{28,12},{1,17},{... | collective-permute-start | bytes 786440 | tf_op jit(solution)/shard_map/ppermute | solution.py:33
  140.4 26.5 %collective-permute-done.19 = bf16[1,512,256]{2,1,0:T(8,128)(2,1)S(1)} collective-permute-done((bf16[1,512,256]{2,1,0:T(8,128)(2,1)S(1)}, bf16[1,512,256]{2,1,0:T(8,128)(2,1)S(1)}, u32[]{:S(2)}, u32[]{:S(2)}) %collective-permute-start.19) | collective-permute-done | bytes 262176 | tf_op jit(solution)/shard_map/ppermute | solution.py:33
  167.7 3.8 %collective-permute-done.12 = bf16[1,512,256]{2,1,0:T(8,128)(2,1)S(1)} collective-permute-done((bf16[1,512,256]{2,1,0:T(8,128)(2,1)S(1)}, bf16[1,512,256]{2,1,0:T(8,128)(2,1)S(1)}, u32[]{:S(2)}, u32[]{:S(2)}) %collective-permute-start.12) | collective-permute-done | bytes 262176 | tf_op jit(solution)/shard_map/ppermute | solution.py:33
  (120 shorter events, 40.8 us)
Async XLA Ops:
  0.6 38.9 %copy-start = (bf16[512,2048]{1,0:T(8,128)(2,1)S(1)}, bf16[512,2048]{1,0:T(8,128)(2,1)}, u32[]{:S(2)}) copy-start(bf16[512,2048]{1,0:T(8,128)(2,1)} %param.20) | copy-start | bytes 6291460
  10.4 7.3 %copy-start.18 = (bf16[512]{0:T(512)(128)(2,1)S(1)}, bf16[512]{0:T(512)(128)(2,1)}, u32[]{:S(2)}) copy-start(bf16[512]{0:T(512)(128)(2,1)} %param.21) | copy-start | bytes 3076
  13.6 10.0 %collective-permute-start = (bf16[4,128,128]{2,1,0:T(8,128)(2,1)}, bf16[4,128,128]{2,1,0:T(8,128)(2,1)}, u32[]{:S(2)}, u32[]{:S(2)}) collective-permute-start(bf16[4,128,128]{2,1,0:T(8,128)(2,1)} %convert_element_type.140), channel_id=1, source_target_pairs={{0,4},{4,0},{8,12},{12,8},{16,20},{20,16},{24,28},{28,24},{1,5},{5... | collective-permute-start | bytes 393224 | tf_op jit(solution)/shard_map/ppermute | solution.py:33
  18.9 7.3 %copy-start.15 = (bf16[1024,2048]{1,0:T(8,128)(2,1)S(1)}, bf16[1024,2048]{1,0:T(8,128)(2,1)}, u32[]{:S(2)}) copy-start(bf16[1024,2048]{1,0:T(8,128)(2,1)} %refs_1_.7) | copy-start | bytes 12582916
  24.5 6.1 %collective-permute-start.1 = (bf16[4,128,128]{2,1,0:T(8,128)(2,1)S(1)}, bf16[4,128,128]{2,1,0:T(8,128)(2,1)S(1)}, u32[]{:S(2)}, u32[]{:S(2)}) collective-permute-start(bf16[4,128,128]{2,1,0:T(8,128)(2,1)S(1)} %get-tuple-element.75), channel_id=1, source_target_pairs={{0,8},{4,12},{8,0},{12,4},{16,24},{20,28},{24,16},{28,20},{1,9},{5... | collective-permute-start | bytes 393224 | tf_op jit(solution)/shard_map/ppermute | solution.py:33
  30.1 52.5 %collective-permute-start.6 = (bf16[4,512,256]{2,1,0:T(8,128)(2,1)S(1)}, bf16[4,512,256]{2,1,0:T(8,128)(2,1)S(1)}, u32[]{:S(2)}, u32[]{:S(2)}) collective-permute-start(bf16[4,512,256]{2,1,0:T(8,128)(2,1)S(1)} %gradient_terms.8), channel_id=1, source_target_pairs={{0,4},{4,0},{8,12},{12,8},{16,20},{20,16},{24,28},{28,24},{1,5},{5... | collective-permute-start | bytes 3145736 | tf_op jit(solution)/shard_map/ppermute | solution.py:33
  30.7 12.6 %collective-permute-start.2 = (bf16[4,128,128]{2,1,0:T(8,128)(2,1)S(1)}, bf16[4,128,128]{2,1,0:T(8,128)(2,1)S(1)}, u32[]{:S(2)}, u32[]{:S(2)}) collective-permute-start(bf16[4,128,128]{2,1,0:T(8,128)(2,1)S(1)} %convert_add_fusion.1), channel_id=1, source_target_pairs={{0,16},{4,20},{8,24},{12,28},{16,0},{20,4},{24,8},{28,12},{1,17},{... | collective-permute-start | bytes 393224 | tf_op jit(solution)/shard_map/ppermute | solution.py:33
  39.0 44.6 %collective-permute-start.7 = (bf16[4,512,256]{2,1,0:T(8,128)(2,1)}, bf16[4,512,256]{2,1,0:T(8,128)(2,1)S(1)}, u32[]{:S(2)}, u32[]{:S(2)}) collective-permute-start(bf16[4,512,256]{2,1,0:T(8,128)(2,1)} %gradient_terms.9), channel_id=1, source_target_pairs={{0,8},{4,12},{8,0},{12,4},{16,24},{20,28},{24,16},{28,20},{1,9},{5... | collective-permute-start | bytes 3145736 | tf_op jit(solution)/shard_map/ppermute | solution.py:33
  51.0 10.4 %collective-permute-start.3 = (bf16[4,128,128]{2,1,0:T(8,128)(2,1)S(1)}, bf16[4,128,128]{2,1,0:T(8,128)(2,1)S(1)}, u32[]{:S(2)}, u32[]{:S(2)}) collective-permute-start(bf16[4,128,128]{2,1,0:T(8,128)(2,1)S(1)} %convert_element_type.149), channel_id=1, source_target_pairs={{0,4},{4,0},{8,12},{12,8},{16,20},{20,16},{24,28},{28,24},{1,5},{5... | collective-permute-start | bytes 393224 | tf_op jit(solution)/shard_map/ppermute | solution.py:33
  61.5 10.9 %collective-permute-start.4 = (bf16[2,4,128,128]{3,2,1,0:T(8,128)(2,1)S(1)}, bf16[2,4,128,128]{3,2,1,0:T(8,128)(2,1)S(1)}, u32[]{:S(2)}, u32[]{:S(2)}) collective-permute-start(bf16[2,4,128,128]{3,2,1,0:T(8,128)(2,1)S(1)} %pad_maximum_fusion), channel_id=1, source_target_pairs={{0,8},{4,12},{8,0},{12,4},{16,24},{20,28},{24,16},{28,20},{1,9},{5... | collective-permute-start | bytes 786440 | tf_op jit(solution)/shard_map/ppermute | solution.py:33
  63.2 41.3 %collective-permute-start.17 = (bf16[4,512,256]{2,1,0:T(8,128)(2,1)S(1)}, bf16[4,512,256]{2,1,0:T(8,128)(2,1)}, u32[]{:S(2)}, u32[]{:S(2)}) collective-permute-start(bf16[4,512,256]{2,1,0:T(8,128)(2,1)S(1)} %gradient_terms.10), channel_id=1, source_target_pairs={{0,4},{4,0},{8,12},{12,8},{16,20},{20,16},{24,28},{28,24},{1,5},{5... | collective-permute-start | bytes 3145736 | tf_op jit(solution)/shard_map/ppermute | solution.py:33
  72.6 9.9 %collective-permute-start.5 = (bf16[4,128,128]{2,1,0:T(8,128)(2,1)S(1)}, bf16[4,128,128]{2,1,0:T(8,128)(2,1)S(1)}, u32[]{:S(2)}, u32[]{:S(2)}) collective-permute-start(bf16[4,128,128]{2,1,0:T(8,128)(2,1)S(1)} %fusion.17), channel_id=1, source_target_pairs={{0,16},{4,20},{8,24},{12,28},{16,0},{20,4},{24,8},{28,12},{1,17},{... | collective-permute-start | bytes 393224 | tf_op jit(solution)/shard_map/ppermute | solution.py:33
  87.1 6.6 %copy-start.12 = (bf16[1024,512]{1,0:T(8,128)(2,1)}, bf16[1024,512]{1,0:T(8,128)(2,1)S(1)}, u32[]{:S(2)}) copy-start(bf16[1024,512]{1,0:T(8,128)(2,1)S(1)} %get-tuple-element.67.value_ref) | copy-start | bytes 3145732
  93.7 37.0 %collective-permute-start.8 = (bf16[2,256,2048]{2,1,0:T(8,128)(2,1)S(1)}, bf16[2,256,2048]{2,1,0:T(8,128)(2,1)}, u32[]{:S(2)}, u32[]{:S(2)}) collective-permute-start(bf16[2,256,2048]{2,1,0:T(8,128)(2,1)S(1)} %input_terms.2), channel_id=1, source_target_pairs={{0,1},{1,0},{2,3},{3,2},{4,5},{5,4},{6,7},{7,6},{8,9},{9,8},{10,11... | collective-permute-start | bytes 6291464 | tf_op jit(solution)/shard_map/ppermute | solution.py:33
  93.8 26.0 %collective-permute-start.10 = (bf16[4,512,256]{2,1,0:T(8,128)(2,1)S(1)}, bf16[4,512,256]{2,1,0:T(8,128)(2,1)S(1)}, u32[]{:S(2)}, u32[]{:S(2)}) collective-permute-start(bf16[4,512,256]{2,1,0:T(8,128)(2,1)S(1)} %gradient_terms.12), channel_id=1, source_target_pairs={{0,4},{4,0},{8,12},{12,8},{16,20},{20,16},{24,28},{28,24},{1,5},{5... | collective-permute-start | bytes 3145736 | tf_op jit(solution)/shard_map/ppermute | solution.py:33
  95.4 14.9 %collective-permute-start.13 = (bf16[2,512,256]{2,1,0:T(8,128)(2,1)S(1)}, bf16[2,512,256]{2,1,0:T(8,128)(2,1)}, u32[]{:S(2)}, u32[]{:S(2)}) collective-permute-start(bf16[2,512,256]{2,1,0:T(8,128)(2,1)S(1)} %get-tuple-element.70), channel_id=1, source_target_pairs={{0,8},{4,12},{8,0},{12,4},{16,24},{20,28},{24,16},{28,20},{1,9},{5... | collective-permute-start | bytes 1572872 | tf_op jit(solution)/shard_map/ppermute | solution.py:33
  95.9 34.7 %collective-permute-start.15 = (bf16[2,512,256]{2,1,0:T(8,128)(2,1)S(1)}, bf16[2,512,256]{2,1,0:T(8,128)(2,1)S(1)}, u32[]{:S(2)}, u32[]{:S(2)}) collective-permute-start(bf16[2,512,256]{2,1,0:T(8,128)(2,1)S(1)} %get-tuple-element.71), channel_id=1, source_target_pairs={{0,4},{4,0},{8,12},{12,8},{16,20},{20,16},{24,28},{28,24},{1,5},{5... | collective-permute-start | bytes 1572872 | tf_op jit(solution)/shard_map/ppermute | solution.py:33
  106.0 30.8 %collective-permute-start.18 = (bf16[2,512,256]{2,1,0:T(8,128)(2,1)S(1)}, bf16[2,512,256]{2,1,0:T(8,128)(2,1)S(1)}, u32[]{:S(2)}, u32[]{:S(2)}) collective-permute-start(bf16[2,512,256]{2,1,0:T(8,128)(2,1)S(1)} %slice.107), channel_id=1, source_target_pairs={{0,8},{4,12},{8,0},{12,4},{16,24},{20,28},{24,16},{28,20},{1,9},{5... | collective-permute-start | bytes 1572872 | tf_op jit(solution)/shard_map/ppermute | solution.py:33
  111.5 56.2 %collective-permute-start.14 = (bf16[1,512,256]{2,1,0:T(8,128)(2,1)S(1)}, bf16[1,512,256]{2,1,0:T(8,128)(2,1)S(1)}, u32[]{:S(2)}, u32[]{:S(2)}) collective-permute-start(bf16[1,512,256]{2,1,0:T(8,128)(2,1)S(1)} %get-tuple-element.82), channel_id=1, source_target_pairs={{0,16},{4,20},{8,24},{12,28},{16,0},{20,4},{24,8},{28,12},{1,17},{... | collective-permute-start | bytes 786440 | tf_op jit(solution)/shard_map/ppermute | solution.py:33
  120.2 17.9 %collective-permute-start.11 = (bf16[2,512,256]{2,1,0:T(8,128)(2,1)S(1)}, bf16[2,512,256]{2,1,0:T(8,128)(2,1)S(1)}, u32[]{:S(2)}, u32[]{:S(2)}) collective-permute-start(bf16[2,512,256]{2,1,0:T(8,128)(2,1)S(1)} %slice.99), channel_id=1, source_target_pairs={{0,8},{4,12},{8,0},{12,4},{16,24},{20,28},{24,16},{28,20},{1,9},{5... | collective-permute-start | bytes 1572872 | tf_op jit(solution)/shard_map/ppermute | solution.py:33
  133.3 39.9 %collective-permute-start.9 = (bf16[1,256,2048]{2,1,0:T(8,128)(2,1)S(1)}, bf16[1,256,2048]{2,1,0:T(8,128)(2,1)S(1)}, u32[]{:S(2)}, u32[]{:S(2)}) collective-permute-start(bf16[1,256,2048]{2,1,0:T(8,128)(2,1)S(1)} %slice.97), channel_id=1, source_target_pairs={{0,2},{1,3},{2,0},{3,1},{4,6},{5,7},{6,4},{7,5},{8,10},{9,11},{10,... | collective-permute-start | bytes 3145736 | tf_op jit(solution)/shard_map/ppermute | solution.py:33
  134.9 32.9 %collective-permute-start.16 = (bf16[1,512,256]{2,1,0:T(8,128)(2,1)S(1)}, bf16[1,512,256]{2,1,0:T(8,128)(2,1)S(1)}, u32[]{:S(2)}, u32[]{:S(2)}) collective-permute-start(bf16[1,512,256]{2,1,0:T(8,128)(2,1)S(1)} %get-tuple-element.80), channel_id=1, source_target_pairs={{0,16},{4,20},{8,24},{12,28},{16,0},{20,4},{24,8},{28,12},{1,17},{... | collective-permute-start | bytes 786440 | tf_op jit(solution)/shard_map/ppermute | solution.py:33
  137.0 29.9 %collective-permute-start.19 = (bf16[1,512,256]{2,1,0:T(8,128)(2,1)S(1)}, bf16[1,512,256]{2,1,0:T(8,128)(2,1)S(1)}, u32[]{:S(2)}, u32[]{:S(2)}) collective-permute-start(bf16[1,512,256]{2,1,0:T(8,128)(2,1)S(1)} %slice.109), channel_id=1, source_target_pairs={{0,16},{4,20},{8,24},{12,28},{16,0},{20,4},{24,8},{28,12},{1,17},{... | collective-permute-start | bytes 786440 | tf_op jit(solution)/shard_map/ppermute | solution.py:33
  138.3 33.2 %collective-permute-start.12 = (bf16[1,512,256]{2,1,0:T(8,128)(2,1)S(1)}, bf16[1,512,256]{2,1,0:T(8,128)(2,1)S(1)}, u32[]{:S(2)}, u32[]{:S(2)}) collective-permute-start(bf16[1,512,256]{2,1,0:T(8,128)(2,1)S(1)} %get-tuple-element.84), channel_id=1, source_target_pairs={{0,16},{4,20},{8,24},{12,28},{16,0},{20,4},{24,8},{28,12},{1,17},{... | collective-permute-start | bytes 786440 | tf_op jit(solution)/shard_map/ppermute | solution.py:33
  (20 other events, 74.0 us)

commit v3 on v2

--- a/solution.py
+++ b/solution.py
@@ -13,11 +13,11 @@
 epsilon = 1e-06
 f32 = jnp.float32
 bf16 = jnp.bfloat16
-VMEM_LIMIT = 48 * 1024 * 1024
-
-
-def params():
-    return pltpu.CompilerParams(vmem_limit_bytes=VMEM_LIMIT)
+MIB = 1024 * 1024
+
+
+def params(mib=16):
+    return pltpu.CompilerParams(vmem_limit_bytes=mib * MIB)
 
 
 def dot(a, b):
@@ -70,52 +70,82 @@
     )(keys, values)
 
 
-def terms_kernel(count_left, slots, block_ref, *refs):
-    lefts, right = refs[:count_left], refs[count_left]
-    out, held, sems = refs[count_left + 1 :]
-    width = out.shape[2]
-    copies = []
-    for index in range(slots):
-        start = pl.multiple_of(block_ref[index] * width, width)
-        copy = pltpu.make_async_copy(right.at[:, pl.ds(start, width)], held.at[index], sems.at[index])
-        copy.start()
-        copies.append(copy)
-    for index in range(slots):
-        copies[index].wait()
-        low = 0
-        for ref in lefts:
-            high = low + ref.shape[0]
-            out[index, low:high, :] = dot(ref[...], held[index]).astype(bf16)
-            low = high
-
-
-def gradient_terms(lefts, right, position, slots):
-    rows, count = lefts[0].shape
+def terms_kernel(number, outputs, position_ref, *refs):
+    lefts, right, outs = refs[:number], refs[number], refs[number + 1 :]
+    width = outs[0].shape[2]
+    jobs = {}
+    for out, (left, low, high, slots) in zip(outs, outputs):
+        for index, slot in enumerate(slots):
+            jobs.setdefault((left, slot), []).append((low, high, out, index))
+    for (left, slot), parts in jobs.items():
+        start = pl.multiple_of((position_ref[0] ^ slot) * width, width)
+        product = dot(lefts[left][...], right[:, pl.ds(start, width)]).astype(bf16)
+        for low, high, out, index in parts:
+            out[index] = product[low:high]
+
+
+def gradient_terms(lefts, right, position, outputs):
+    count = right.shape[0]
     width = right.shape[1] // lax.axis_size("seq")
-    total = rows * len(lefts)
-    number = len(slots)
-    blocks = position ^ jnp.array(slots, jnp.int32)
     if width % 128:
-        picked = jnp.take(right.reshape(count, -1, width), blocks, axis=1)
-        left = jnp.concatenate(lefts, 0)
-        return jnp.einsum("at,tnb->nab", left, picked, preferred_element_type=f32).astype(bf16)
+        blocked = right.reshape(count, -1, width)
+        results = []
+        for left, low, high, slots in outputs:
+            picked = jnp.take(blocked, position ^ jnp.array(slots, jnp.int32), axis=1)
+            part = jnp.einsum("at,tnb->nab", lefts[left][low:high], picked, preferred_element_type=f32)
+            results.append(part.astype(bf16))
+        return results
+    shapes = [(len(slots), high - low, width) for _, low, high, slots in outputs]
+    size = sum(n * r * w for n, r, w in shapes)
     vmem = pl.BlockSpec(memory_space=pltpu.VMEM)
     return pl.pallas_call(
-        functools.partial(terms_kernel, len(lefts), number),
-        in_specs=[pl.BlockSpec(memory_space=pltpu.SMEM)]
-        + [vmem] * len(lefts)
-        + [pl.BlockSpec(memory_space=pl.ANY)],
-        out_specs=vmem,
-        out_shape=jax.ShapeDtypeStruct((number, total, width), bf16),
-        scratch_shapes=[pltpu.VMEM((number, count, width), bf16), pltpu.SemaphoreType.DMA((number,))],
-        compiler_params=params(),
-        cost_estimate=pl.CostEstimate(
-            flops=2 * count * total * width * number,
-            bytes_accessed=2 * number * width * (count + total) + 2 * total * count,
+        functools.partial(terms_kernel, len(lefts), outputs),
+        in_specs=[pl.BlockSpec(memory_space=pltpu.SMEM)] + [vmem] * (len(lefts) + 1),
+        out_specs=[vmem] * len(outputs),
+        out_shape=[jax.ShapeDtypeStruct(shape, bf16) for shape in shapes],
+        compiler_params=params(),
+        cost_estimate=pl.CostEstimate(
+            flops=2 * count * size,
+            bytes_accessed=2 * (size + right.size + sum(left.size for left in lefts)),
             transcendentals=0,
         ),
         name="gradient_terms",
-    )(blocks, *lefts, right)
+    )(position[None], *lefts, right)
+
+
+def sums_kernel(groups, merge, *refs):
+    ins, outs = refs[: 2 * groups], refs[2 * groups :]
+    low = 0
+    for index in range(groups):
+        keep, got = ins[2 * index], ins[2 * index + 1]
+        half, rows = keep.shape[0] // 2, keep.shape[1]
+        if merge:
+            kept, sent = (out.at[:, low : low + rows, :] for out in outs)
+            low += rows
+        else:
+            kept, sent = outs[2 * index], outs[2 * index + 1]
+        for slot in range(half):
+            kept[slot] = (keep[slot].astype(f32) + got[slot].astype(f32)).astype(bf16)
+            other = half + slot
+            sent[slot] = (keep[other].astype(f32) + got[other].astype(f32)).astype(bf16)
+
+
+def sums(pairs, merge=False):
+    slots, rows, width = pairs[0][0].shape
+    total = sum(keep.shape[1] for keep, _ in pairs) if merge else rows
+    shape = jax.ShapeDtypeStruct((slots // 2, total, width), bf16)
+    vmem = pl.BlockSpec(memory_space=pltpu.VMEM)
+    outs = 2 if merge else 2 * len(pairs)
+    size = sum(keep.size for keep, _ in pairs)
+    return pl.pallas_call(
+        functools.partial(sums_kernel, len(pairs), merge),
+        in_specs=[vmem] * (2 * len(pairs)),
+        out_specs=[vmem] * outs,
+        out_shape=[shape] * outs,
+        compiler_params=params(),
+        cost_estimate=pl.CostEstimate(flops=size, bytes_accessed=6 * size, transcendentals=0),
+        name="sums",
+    )(*[array for pair in pairs for array in pair])
 
 
 def middle_kernel(query_ref, grad_ref, mask_ref, gain_ref, state_ref, normed_t_ref, query_grad_ref, query_grad_t_ref, block_grad_ref):
@@ -224,38 +254,44 @@
     )(keys, values, state_grad_t)
 
 
-def input_kernel(slots, block_ref, query_ref, key_ref, value_ref, weight_ref, out_ref):
-    rows = out_ref.shape[1]
-    for index in range(slots):
-        start = pl.multiple_of(block_ref[index] * rows, rows)
-        total = dot_t(query_ref[pl.ds(start, rows), :], weight_ref[0])
-        total += dot_t(key_ref[pl.ds(start, rows), :], weight_ref[1])
-        total += dot_t(value_ref[pl.ds(start, rows), :], weight_ref[2])
-        out_ref[index] = total.astype(bf16)
-
-
-def input_terms(grads, weight, place, slots, tile=512):
+def input_kernel(order, place_ref, query_ref, key_ref, value_ref, weight_ref, keep_ref, send_ref, held_ref):
+    total = dot_t(query_ref[...], weight_ref[0])
+    total += dot_t(key_ref[...], weight_ref[1])
+    total += dot_t(value_ref[...], weight_ref[2])
+    held_ref[...] = total.astype(bf16).reshape(held_ref.shape)
+    half = len(order) // 2
+    for index in range(half):
+        keep_ref[index] = held_ref[place_ref[0] ^ order[index]]
+        send_ref[index] = held_ref[place_ref[0] ^ order[half + index]]
+
+
+def input_terms(grads, weight, place, order, chunk, chunks, tile=512):
     count, width = grads[0].shape
-    rows = count // lax.axis_size("head")
-    number = len(slots)
+    half = len(order) // 2
+    rows = count // len(order)
+    columns = D // chunks
+    first = chunk * columns // tile
     full = pl.BlockSpec((count, width), lambda i, b: (0, 0))
-    return pl.pallas_call(
-        functools.partial(input_kernel, number),
+    out = pl.BlockSpec((half, rows, tile), lambda i, b: (0, 0, i))
+    shape = jax.ShapeDtypeStruct((half, rows, columns), bf16)
+    return pl.pallas_call(
+        functools.partial(input_kernel, order),
         grid_spec=pltpu.PrefetchScalarGridSpec(
             num_scalar_prefetch=1,
-            grid=(D // tile,),
-            in_specs=[full, full, full, pl.BlockSpec((3, tile, width), lambda i, b: (0, i, 0))],
-            out_specs=pl.BlockSpec((number, rows, tile), lambda i, b: (0, 0, i)),
-        ),
-        out_shape=jax.ShapeDtypeStruct((number, rows, D), bf16),
-        compiler_params=params(),
-        cost_estimate=pl.CostEstimate(
-            flops=6 * number * rows * width * D,
-            bytes_accessed=6 * D * width + 6 * count * width + 2 * number * rows * D,
+            grid=(columns // tile,),
+            in_specs=[full, full, full, pl.BlockSpec((3, tile, width), lambda i, b: (0, first + i, 0))],
+            out_specs=[out, out],
+            scratch_shapes=[pltpu.VMEM((len(order), rows, tile), bf16)],
+        ),
+        out_shape=[shape, shape],
+        compiler_params=params(32),
+        cost_estimate=pl.CostEstimate(
+            flops=6 * count * width * columns,
+            bytes_accessed=6 * columns * width + 6 * count * width + 2 * count * columns,
             transcendentals=0,
         ),
         name="input_terms",
-    )(place ^ jnp.array(slots, jnp.int32), *grads, weight)
+    )(place[None], *grads, weight)
 
 
 def finish_kernel(*refs):
@@ -279,42 +315,38 @@
     return lax.optimization_barrier((value,) + others)[0]
 
 
-def split_sum(keep, got):
-    total = keep.astype(f32) + got.astype(f32)
-    half = total.shape[0] // 2
-    return total[:half].astype(bf16), total[half:].astype(bf16)
-
-
-def halving(keep, send, axis, stage_bits):
-    for bit in stage_bits[:-1]:
-        keep, send = split_sum(keep, exchange(send, axis, bit))
-    return keep[0], exchange(send, axis, stage_bits[-1])[0]
-
-
 def per_device(layer_input, output_grad, loss_mask, proj_weight, out_weight, norm_gain):
-    count = layer_input.shape[0]
+    width_dev = proj_weight.shape[2]
+    side = width_dev // 2
     position = lax.axis_index("seq")
+    place = lax.axis_index("head")
     seq_bits = lax.axis_size("seq").bit_length() - 1
     head_bits = lax.axis_size("head").bit_length() - 1
     stages = list(range(seq_bits))
-    swapped = [1, 0] + stages[2:]
     bits = [(position >> bit) & 1 == 1 for bit in stages]
-    order, order_swapped = slot_order(stages), slot_order(swapped)
+    order, swapped = slot_order(stages), slot_order([1, 0] + stages[2:])
     half = len(order) // 2
+    head_order = slot_order(list(range(head_bits)))
     weights = jnp.transpose(proj_weight, (1, 0, 2))
 
     def project(rows, index):
         return jnp.dot(rows, weights[index], preferred_element_type=f32).astype(bf16)
 
-    def terms(lefts, right, slots):
-        return gradient_terms(lefts, right, position, slots)
+    def one_term(left, right, slots):
+        return gradient_terms([left], right, position, [(0, 0, left.shape[0], slots)])[0]
+
+    def both_terms(left, right):
+        outputs = []
+        for low, slots in ((0, order), (side, swapped)):
+            outputs += [(0, low, low + side, slots[:half]), (0, low, low + side, slots[half:])]
+        return gradient_terms([left], right, position, outputs)
 
     keys, values = project(layer_input, 1), project(layer_input, 2)
     own_state, keys_t, values_t = block_states(keys, values)
     mask = loss_mask.astype(f32)[:, None]
 
     got = exchange(own_state.astype(bf16), "seq", 0)
-    value_send = terms([values_t], after(layer_input, own_state), order[half:])
+    value_send = one_term(values_t, after(layer_input, own_state), order[half:])
     got = after(got, value_send)
     before = jnp.where(bits[0], got.astype(f32), 0.0)
     total = own_state + got.astype(f32)
@@ -329,7 +361,7 @@
     for bit in stages[2:]:
         got = exchange(total.astype(bf16), "seq", bit)
         if bit == 2:
-            key_send = terms([keys_t], after(layer_input, total), order_swapped[half:])
+            key_send = one_term(keys_t, after(layer_input, total), swapped[half:])
             key_got = exchange(key_send, "seq", 1)
             normed_grad = dot_t(after(output_grad, key_send), out_weight)
             got = after(got, normed_grad)
@@ -342,30 +374,27 @@
     )
 
     got = exchange(own_grad.astype(bf16), "seq", 0)
-    out_send = terms([normed_t], after(output_grad, own_grad), order[half:])
-    out_keep = terms([normed_t], after(output_grad, out_send), order[:half])
-    got = after(got, out_keep).astype(f32)
+    out_terms = both_terms(normed_t, after(output_grad, own_grad))
+    got = after(got, *out_terms).astype(f32)
     total = own_grad + got
     mine, mate = jnp.where(bits[0], own_grad, total), jnp.where(bits[0], total, got)
-    out_send = after(out_send, total)
-    out_got = exchange(out_send, "seq", 0)
+    out_first_got = exchange(after(out_terms[1], total), "seq", 0)
 
     got = exchange(jnp.stack([total, mine]).astype(bf16), "seq", 1)
-    query_send = terms([query_grad_t], after(layer_input, total), order[half:])
-    query_keep = terms([query_grad_t], after(layer_input, query_send), order[:half])
-    got = after(got, query_keep).astype(f32)
+    query_terms = both_terms(query_grad_t, after(layer_input, total))
+    got = after(got, *query_terms, value_got).astype(f32)
     later = jnp.where(bits[1], 0.0, got[0])
     mine, mate = mine + later, mate + later
     other = got[1] + jnp.where(bits[1], total, 0.0)
     total = total + got[0]
-    query_got = exchange(after(query_send, total), "seq", 0)
 
     for bit in stages[2:]:
         got = exchange(total.astype(bf16), "seq", bit)
         if bit == 2:
-            value_keep = terms([values_t], after(layer_input, total), order[:half])
-            key_keep = terms([keys_t], after(layer_input, value_keep), order_swapped[:half])
-            got = after(got, key_keep)
+            out_second_got = exchange(after(out_terms[3], total), "seq", 1)
+            value_keep = one_term(values_t, after(layer_input, total), order[:half])
+            key_keep = one_term(keys_t, after(layer_input, value_keep), swapped[:half])
+            got = after(got, key_keep, key_got)
         got = got.astype(f32)
         later = jnp.where(bits[bit], 0.0, got)
         mine, mate, other = mine + later, mate + later, other + later
@@ -373,27 +402,67 @@
     state_grad, mate_grad, other_grad = mine.astype(bf16), mate.astype(bf16), other.astype(bf16)
 
     value_half = late_terms(True, state_grad, mate_grad, value_keep, value_got)
-    value_pair = halving(*value_half, "seq", stages[1:])
+    value_got = exchange(value_half[1], "seq", 1)
     key_half = late_terms(False, state_grad, other_grad, after(key_keep, value_half[0]), key_got)
-    key_pair = halving(*key_half, "seq", swapped[1:])
+    key_got = exchange(key_half[1], "seq", 0)
 
     key_grad, value_grad = key_value_grads(keys, values, after(state_grad, key_half[0]))
-    place = lax.axis_index("head")
-    head_stages = list(range(head_bits))
-    token_order = slot_order(head_stages)
-    middle_slot = len(token_order) // 2
     grads = (query_grad, key_grad, value_grad)
-    input_send = input_terms(grads, weights, place, token_order[middle_slot:])
-    input_keep = input_terms(grads, after(weights, input_send), place, token_order[:middle_slot])
-    keep, got = halving(input_keep, input_send, "head", head_stages)
-    input_grad = (keep.astype(f32) + got.astype(f32)).astype(bf16)
-
-    keep, send = split_sum(out_keep, out_got)
-    keep, got = halving(keep, send, "seq", stages[1:])
-    out_weight_grad = keep.astype(f32) + got.astype(f32)
-
-    keep, send = split_sum(query_keep, query_got)
-    query_pair = halving(keep, send, "seq", stages[1:])
+    input_keep, input_send, input_got = [None, None], [None, None], [None, None]
+    input_keep[0], input_send[0] = input_terms(grads, weights, place, head_order, 0, 2)
+    input_got[0] = exchange(input_send[0], "head", 0)
+
+    out_first_got, out_second_got = after((out_first_got, out_second_got), input_keep[0])
+    out_terms = sums([(out_terms[0], out_first_got), (out_terms[2], out_second_got)])
+    out_first_got = exchange(out_terms[1], "seq", 1)
+    out_second_got = exchange(out_terms[3], "seq", 0)
+
+    input_keep[1], input_send[1] = input_terms(
+        grads, after(weights, out_terms[0]), place, head_order, 1, 2
+    )
+    input_got[1] = exchange(input_send[1], "head", 0)
+
+    def rest(keep, send, bits_left):
+        for bit in bits_left[:-1]:
+            keep, send = sums([(keep, exchange(send, "seq", bit))])
+        return keep[0], exchange(send, "seq", bits_left[-1])[0]
+
+    key_got = after(key_got, input_keep[1])
+    key_half = sums([(key_half[0], key_got)])
+    key_pair = rest(*key_half, stages[2:])
+    query_first_got = exchange(after(query_terms[1], key_half[0]), "seq", 0)
+    query_second_got = exchange(after(query_terms[3], key_half[0]), "seq", 1)
+
+    def head_rest(keep, got):
+        for bit in range(1, head_bits):
+            keep, send = sums([(keep, got)])
+            got = exchange(send, "head", bit)
+        return keep[0], got[0]
+
+    first = head_rest(input_keep[0], after(input_got[0], key_half[0]))
+    second = head_rest(input_keep[1], after(input_got[1], first[0]))
+
+    value_half = sums([(value_half[0], after(value_got, second[0]))])
+    value_pair = rest(*value_half, stages[2:])
+
+    out_first_got, out_second_got = after((out_first_got, out_second_got), value_half[0])
+    out_half = sums([(out_terms[0], out_first_got), (out_terms[2], out_second_got)], merge=True)
+    out_pair = rest(*out_half, stages[2:])
+
+    query_first_got, query_second_got = after((query_first_got, query_second_got), out_half[0])
+    query_terms = sums([(query_terms[0], query_first_got), (query_terms[2], query_second_got)])
+    query_first_got = exchange(query_terms[1], "seq", 1)
+    query_second_got = exchange(query_terms[3], "seq", 0)
+
+    first, second = after((first, second), query_terms[0])
+    input_grad = jnp.concatenate(
+        [(keep.astype(f32) + got.astype(f32)).astype(bf16) for keep, got in (first, second)], 1
+    )
+    query_half = sums(
+        [(query_terms[0], query_first_got), (query_terms[2], query_second_got)], merge=True
+    )
+    query_pair = rest(*query_half, stages[2:])
+    out_weight_grad = out_pair[0].astype(f32) + out_pair[1].astype(f32)
     proj_weight_grad = finish(query_pair + value_pair + key_pair)
     return (input_grad, jnp.transpose(proj_weight_grad, (1, 0, 2)), out_weight_grad)
 

time: 175 us -> 175 us (level)
  waiting for transfers between devices: 49.3 us -> 78 us
  Pallas kernels: 62.7 us -> 36.2 us
  other arithmetic: 10.9 us -> 5.12 us
  local copies, waits for them, and re-layouts: 7.13 us -> 9.77 us
  starting transfers between devices: 26 us -> 28.6 us
    ppermute x20 -> x26, waiting for transfers between devices: 49.3 us -> 78 us  [exchange(): return lax.ppermute(arr, axis, [(i, i ^ 1 << bit) for i in range(count)])]
    pallas_call x10 -> x16, Pallas kernels: 50 us -> 22 us  [the longest x6 11.9 us: gradient_terms(): pl.pallas_call(functools.partial(terms_kernel, len(lefts), outputs), in_s...]
    another operation x7 -> x0, other arithmetic: 5.65 us -> none
    unnamed x48 -> x56, local copies, waits for them, and re-layouts: 5.8 us -> 8.74 us
    ppermute x20 -> x26, starting transfers between devices: 26 us -> 28.6 us  [exchange(): return lax.ppermute(arr, axis, [(i, i ^ 1 << bit) for i in range(count)])]
    pallas_call x2, Pallas kernels: 1.86 us -> 4.17 us  [late_terms(): pl.pallas_call(functools.partial(late_kernel, flip), grid=(half,), in_spe...]
  transfers between devices with their start and end apart: 20 -> 26, of which waited for: 5 -> 11; matrix products, arithmetic and copies ran while one was open for 10% -> 7% of each run, Pallas kernels for 35% -> 19%
where the time goes in v3:
time: 175 us
  waiting for transfers between devices  78 us (45%)
  Pallas kernels  36.2 us (21%)
  starting transfers between devices  28.6 us (16%)
  matrix products  15.9 us (9%)
  local copies, waits for them, and re-layouts  9.77 us (6%)
  other arithmetic  5.12 us (3%)
    ppermute x26, waiting for transfers between devices, exchange(): return lax.ppermute(arr, axis, [(i, i ^ 1 << bit) for i in range(count)])  78 us
    ppermute x26, starting transfers between devices, exchange(): return lax.ppermute(arr, axis, [(i, i ^ 1 << bit) for i in range(count)])  28.6 us
    dot_general x3, matrix products, project(): jnp.dot(rows, weights[index], preferred_element_type=f32).astype(bf16)  13.6 us
    pallas_call x6, Pallas kernels, gradient_terms(): pl.pallas_call(functools.partial(terms_kernel, len(lefts), outputs), in_s...  11.9 us
    unnamed x56, local copies, waits for them, and re-layouts  8.74 us
    pallas_call x2, Pallas kernels, input_terms(): pl.pallas_call(functools.partial(input_kernel, order), grid_spec=pltpu.Pr...  8.64 us
    pallas_call x1, Pallas kernels, middle(): pl.pallas_call(middle_kernel, grid=(heads,), in_specs=[column, column, pl...  4.99 us
    pallas_call x2, Pallas kernels, late_terms(): pl.pallas_call(functools.partial(late_kernel, flip), grid=(half,), in_spe...  4.17 us
  transfers between devices with their start and end apart: 26, of which 11 were waited for; matrix products, arithmetic and copies ran while one was open for 7% of the time, Pallas kernels for 19%

profile of v3, /device:TPU:0, one launch (start us, length us, event | category | flops | bytes accessed | tf_op | source)
XLA Modules:
  0.0 174.8 jit_solution(13765832190495333228)
XLA Ops:
  0.7 5.3 %fusion.4.value_ref = bf16[1024,512]{1,0:T(8,128)(2,1)S(1)} fusion(bf16[1024,2048]{1,0:T(8,128)(2,1)} %refs_1_.5, bf16[3,2048,512]{2,1,0:T(8,128)(2,1)} %bitcast.67), kind=kOutput, calls=%fused_computation.7 | convolution fusion | flops 2148007936 | bytes 7340032 | tf_op jit(solution)/shard_map/dot_general | solution.py:333
  6.1 4.3 %fusion.3.key_ref = bf16[1024,512]{1,0:T(8,128)(2,1)S(1)} fusion(bf16[1024,2048]{1,0:T(8,128)(2,1)S(1)} %copy-done.2, bf16[3,2048,512]{2,1,0:T(8,128)(2,1)} %bitcast.68), kind=kOutput, calls=%fused_computation.6 | convolution fusion | flops 2148007936 | bytes 7340032 | tf_op jit(solution)/shard_map/dot_general | solution.py:333
  13.6 3.0 %collective-permute-start = (bf16[4,128,128]{2,1,0:T(8,128)(2,1)}, bf16[4,128,128]{2,1,0:T(8,128)(2,1)S(1)}, u32[]{:S(2)}, u32[]{:S(2)}) collective-permute-start(bf16[4,128,128]{2,1,0:T(8,128)(2,1)} %convert_element_type.88), channel_id=1, source_target_pairs={{0,4},{4,0},{8,12},{12,8},{16,20},{20,16},{24,28},{28,24},{1,5},{5... | collective-permute-start | bytes 393224 | tf_op jit(solution)/shard_map/ppermute | solution.py:33
  17.6 2.2 %copy-done.3 = bf16[1024,2048]{1,0:T(8,128)(2,1)S(1)} copy-done((bf16[1024,2048]{1,0:T(8,128)(2,1)S(1)}, bf16[1024,2048]{1,0:T(8,128)(2,1)}, u32[]{:S(2)}) %copy-start.3) | copy-done | bytes 4194328
  21.0 2.3 %gradient_terms.6 = bf16[4,512,256]{2,1,0:T(8,128)(2,1)} custom-call(s32[1]{0:T(128)} %bitcast.4.position_ref, bf16[512,1024]{1,0:T(8,128)(2,1)S(1)} %copy-done.7, bf16[1024,2048]{1,0:T(8,128)(2,1)S(1)} %copy-done.3), custom_call_target="tpu_custom_call" | custom-call | flops 1073741824 | bytes 6291456 | tf_op jit(solution)/shard_map/gradient_terms/pallas_call | solution.py:101
  25.0 3.9 %fusion.5.query_ref = bf16[1024,512]{1,0:T(8,128)(2,1)S(1)} fusion(bf16[1024,2048]{1,0:T(8,128)(2,1)S(1)} %copy-done.4, bf16[3,2048,512]{2,1,0:T(8,128)(2,1)} %bitcast.69), kind=kOutput, calls=%fused_computation.8 | convolution fusion | flops 2148007936 | bytes 7340032 | tf_op jit(solution)/shard_map/dot_general | solution.py:333
  29.5 2.6 %collective-permute-start.2 = (bf16[4,128,128]{2,1,0:T(8,128)(2,1)S(1)}, bf16[4,128,128]{2,1,0:T(8,128)(2,1)S(1)}, u32[]{:S(2)}, u32[]{:S(2)}) collective-permute-start(bf16[4,128,128]{2,1,0:T(8,128)(2,1)S(1)} %convert_add_fusion.1), channel_id=1, source_target_pairs={{0,16},{4,20},{8,24},{12,28},{16,0},{20,4},{24,8},{28,12},{1,17},{... | collective-permute-start | bytes 393224 | tf_op jit(solution)/shard_map/ppermute | solution.py:33
  32.2 2.3 %gradient_terms.7 = bf16[4,512,256]{2,1,0:T(8,128)(2,1)} custom-call(s32[1]{0:T(128)} %bitcast.4.position_ref, bf16[512,1024]{1,0:T(8,128)(2,1)S(1)} %get-tuple-element.89.refs_0_, bf16[1024,2048]{1,0:T(8,128)(2,1)S(1)} %copy-done.4), custom_call_target="tpu_custom_call" | custom-call | flops 1073741824 | bytes 6291456 | tf_op jit(solution)/shard_map/gradient_terms/pallas_call | solution.py:101
  34.9 2.4 %fusion.19.grad_ref = f32[1024,512]{1,0:T(8,128)S(1)} fusion(bf16[1024,2048]{1,0:T(8,128)(2,1)S(1)} %copy-done.16, bf16[512,2048]{1,0:T(8,128)(2,1)S(1)} %copy-done), kind=kOutput, calls=%fused_computation.40 | convolution fusion | flops 2147483648 | bytes 8388608 | tf_op jit(solution)/shard_map/dot_general | solution.py:28
  37.7 5.0 %norm_backward.1 = (bf16[512,1024]{1,0:T(8,128)(2,1)S(1)}, bf16[1024,512]{1,0:T(8,128)(2,1)S(1)}, bf16[512,1024]{1,0:T(8,128)(2,1)S(1)}, f32[4,128,128]{2,1,0:T(8,128)S(1)}) custom-call(bf16[1024,512]{1,0:T(8,128)(2,1)S(1)} %fusion.5.query_ref, f32[1024,512]{1,0:T(8,128)S(1)} %fusion.19.grad_ref, f32[1024,1]{1,0:T(8,128)S(1)} %copy-done.13, ...), custom_call_target="tpu_custom_call" | custom-call | flops 536870912 | bytes 6291456 | tf_op jit(solution)/shard_map/norm_backward/pallas_call | solution.py:175
  44.5 2.4 %gradient_terms.8 = (bf16[4,256,256]{2,1,0:T(8,128)(2,1)S(1)}, bf16[4,256,256]{2,1,0:T(8,128)(2,1)S(1)}, bf16[4,256,256]{2,1,0:T(8,128)(2,1)S(1)}, bf16[4,256,256]{2,1,0:T(8,128)(2,1)S(1)}) custom-call(s32[1]{0:T(128)} %bitcast.4.position_ref, bf16[512,1024]{1,0:T(8,128)(2,1)S(1)} %get-tuple-element.96.refs_0_, bf16[1024,2048]{1,0:T(8,128)(2,1)S(1)} %copy-done.16), custom_call_target="tpu_custom_call" | custom-call | flops 2147483648 | bytes 7340032 | tf_op jit(solution)/shard_map/gradient_terms/pallas_call | solution.py:101
  47.7 8.7 %collective-permute-done.3 = bf16[4,128,128]{2,1,0:T(8,128)(2,1)S(1)} collective-permute-done((bf16[4,128,128]{2,1,0:T(8,128)(2,1)S(1)}, bf16[4,128,128]{2,1,0:T(8,128)(2,1)S(1)}, u32[]{:S(2)}, u32[]{:S(2)}) %collective-permute-start.3) | collective-permute-done | bytes 131104 | tf_op jit(solution)/shard_map/ppermute | solution.py:33
  58.0 2.2 %copy-done.5 = bf16[1024,2048]{1,0:T(8,128)(2,1)S(1)} copy-done((bf16[1024,2048]{1,0:T(8,128)(2,1)S(1)}, bf16[1024,2048]{1,0:T(8,128)(2,1)}, u32[]{:S(2)}) %copy-start.5) | copy-done | bytes 4194328
  61.4 2.4 %gradient_terms.9 = (bf16[4,256,256]{2,1,0:T(8,128)(2,1)S(1)}, bf16[4,256,256]{2,1,0:T(8,128)(2,1)S(1)}, bf16[4,256,256]{2,1,0:T(8,128)(2,1)S(1)}, bf16[4,256,256]{2,1,0:T(8,128)(2,1)S(1)}) custom-call(s32[1]{0:T(128)} %bitcast.4.position_ref, bf16[512,1024]{1,0:T(8,128)(2,1)S(1)} %copy-done.20, bf16[1024,2048]{1,0:T(8,128)(2,1)S(1)} %copy-done.5), custom_call_target="tpu_custom_call" | custom-call | flops 2147483648 | bytes 7340032 | tf_op jit(solution)/shard_map/gradient_terms/pallas_call | solution.py:101
  80.4 4.2 %input_terms.2 = (bf16[2,256,1024]{2,1,0:T(8,128)(2,1)S(1)}, bf16[2,256,1024]{2,1,0:T(8,128)(2,1)S(1)}) custom-call(s32[1]{0:T(128)} %bitcast.place_ref, bf16[1024,512]{1,0:T(8,128)(2,1)S(1)} %copy-done.18, bf16[1024,512]{1,0:T(8,128)(2,1)S(1)} %get-tuple-element.118.key_ref, bf16[1024,512]{1,0:T(8,128)(2,1)S(1)} %get-tuple-element.119.value_ref, ...), custom_call_target="tpu_custom_call" | custom-call | flops 3221225472 | bytes 8388608 | tf_op jit(solution)/shard_map/input_terms/pallas_call | solution.py:277
  85.0 4.4 %input_terms.3 = (bf16[2,256,1024]{2,1,0:T(8,128)(2,1)S(1)}, bf16[2,256,1024]{2,1,0:T(8,128)(2,1)S(1)}) custom-call(s32[1]{0:T(128)} %bitcast.place_ref, bf16[1024,512]{1,0:T(8,128)(2,1)S(1)} %copy-done.18, bf16[1024,512]{1,0:T(8,128)(2,1)S(1)} %get-tuple-element.118.key_ref, bf16[1024,512]{1,0:T(8,128)(2,1)S(1)} %get-tuple-element.119.value_ref, ...), custom_call_target="tpu_custom_call" | custom-call | flops 3221225472 | bytes 8388608 | tf_op jit(solution)/shard_map/input_terms/pallas_call | solution.py:277
  92.0 12.2 %collective-permute-done.9.refs_1_ = bf16[2,512,256]{2,1,0:T(8,128)(2,1)S(1)} collective-permute-done((bf16[2,512,256]{2,1,0:T(8,128)(2,1)S(1)}, bf16[2,512,256]{2,1,0:T(8,128)(2,1)S(1)}, u32[]{:S(2)}, u32[]{:S(2)}) %collective-permute-start.9) | collective-permute-done | bytes 524320 | tf_op jit(solution)/shard_map/ppermute | solution.py:33
  110.4 14.1 %collective-permute-done.17.refs_1_ = bf16[2,256,256]{2,1,0:T(8,128)(2,1)S(1)} collective-permute-done((bf16[2,256,256]{2,1,0:T(8,128)(2,1)S(1)}, bf16[2,256,256]{2,1,0:T(8,128)(2,1)S(1)}, u32[]{:S(2)}, u32[]{:S(2)}) %collective-permute-start.17) | collective-permute-done | bytes 262176 | tf_op jit(solution)/shard_map/ppermute | solution.py:33
  129.1 7.6 %collective-permute-done.20.refs_1_ = bf16[2,256,256]{2,1,0:T(8,128)(2,1)S(1)} collective-permute-done((bf16[2,256,256]{2,1,0:T(8,128)(2,1)S(1)}, bf16[2,256,256]{2,1,0:T(8,128)(2,1)S(1)}, u32[]{:S(2)}, u32[]{:S(2)}) %collective-permute-start.20) | collective-permute-done | bytes 262176 | tf_op jit(solution)/shard_map/ppermute | solution.py:33
  137.0 2.6 %collective-permute-start.23 = (bf16[1,512,256]{2,1,0:T(8,128)(2,1)S(1)}, bf16[1,512,256]{2,1,0:T(8,128)(2,1)S(1)}, u32[]{:S(2)}, u32[]{:S(2)}) collective-permute-start(bf16[1,512,256]{2,1,0:T(8,128)(2,1)S(1)} %get-tuple-element.162), channel_id=1, source_target_pairs={{0,16},{4,20},{8,24},{12,28},{16,0},{20,4},{24,8},{28,12},{1,17},{... | collective-permute-start | bytes 786440 | tf_op jit(solution)/shard_map/ppermute | solution.py:33
  139.8 15.1 %collective-permute-done.25 = bf16[1,512,256]{2,1,0:T(8,128)(2,1)S(1)} collective-permute-done((bf16[1,512,256]{2,1,0:T(8,128)(2,1)S(1)}, bf16[1,512,256]{2,1,0:T(8,128)(2,1)S(1)}, u32[]{:S(2)}, u32[]{:S(2)}) %collective-permute-start.25) | collective-permute-done | bytes 262176 | tf_op jit(solution)/shard_map/ppermute | solution.py:33
  157.2 6.1 %collective-permute-done.24 = bf16[1,512,256]{2,1,0:T(8,128)(2,1)S(1)} collective-permute-done((bf16[1,512,256]{2,1,0:T(8,128)(2,1)S(1)}, bf16[1,512,256]{2,1,0:T(8,128)(2,1)S(1)}, u32[]{:S(2)}, u32[]{:S(2)}) %collective-permute-start.24) | collective-permute-done | bytes 262176 | tf_op jit(solution)/shard_map/ppermute | solution.py:33
  163.3 5.6 %collective-permute-done.23 = bf16[1,512,256]{2,1,0:T(8,128)(2,1)S(1)} collective-permute-done((bf16[1,512,256]{2,1,0:T(8,128)(2,1)S(1)}, bf16[1,512,256]{2,1,0:T(8,128)(2,1)S(1)}, u32[]{:S(2)}, u32[]{:S(2)}) %collective-permute-start.23) | collective-permute-done | bytes 262176 | tf_op jit(solution)/shard_map/ppermute | solution.py:33
  168.9 4.3 %collective-permute-done.22 = bf16[1,512,256]{2,1,0:T(8,128)(2,1)S(1)} collective-permute-done((bf16[1,512,256]{2,1,0:T(8,128)(2,1)S(1)}, bf16[1,512,256]{2,1,0:T(8,128)(2,1)S(1)}, u32[]{:S(2)}, u32[]{:S(2)}) %collective-permute-start.22) | collective-permute-done | bytes 262176 | tf_op jit(solution)/shard_map/ppermute | solution.py:33
  (128 shorter events, 48.5 us)
Async XLA Ops:
  13.6 9.7 %collective-permute-start = (bf16[4,128,128]{2,1,0:T(8,128)(2,1)}, bf16[4,128,128]{2,1,0:T(8,128)(2,1)S(1)}, u32[]{:S(2)}, u32[]{:S(2)}) collective-permute-start(bf16[4,128,128]{2,1,0:T(8,128)(2,1)} %convert_element_type.88), channel_id=1, source_target_pairs={{0,4},{4,0},{8,12},{12,8},{16,20},{20,16},{24,28},{28,24},{1,5},{5... | collective-permute-start | bytes 393224 | tf_op jit(solution)/shard_map/ppermute | solution.py:33
  28.9 36.8 %collective-permute-start.5 = (bf16[4,512,256]{2,1,0:T(8,128)(2,1)}, bf16[4,512,256]{2,1,0:T(8,128)(2,1)}, u32[]{:S(2)}, u32[]{:S(2)}) collective-permute-start(bf16[4,512,256]{2,1,0:T(8,128)(2,1)} %gradient_terms.6), channel_id=1, source_target_pairs={{0,4},{4,0},{8,12},{12,8},{16,20},{20,16},{24,28},{28,24},{1,5},{5... | collective-permute-start | bytes 3145736 | tf_op jit(solution)/shard_map/ppermute | solution.py:33
  29.5 8.1 %collective-permute-start.2 = (bf16[4,128,128]{2,1,0:T(8,128)(2,1)S(1)}, bf16[4,128,128]{2,1,0:T(8,128)(2,1)S(1)}, u32[]{:S(2)}, u32[]{:S(2)}) collective-permute-start(bf16[4,128,128]{2,1,0:T(8,128)(2,1)S(1)} %convert_add_fusion.1), channel_id=1, source_target_pairs={{0,16},{4,20},{8,24},{12,28},{16,0},{20,4},{24,8},{28,12},{1,17},{... | collective-permute-start | bytes 393224 | tf_op jit(solution)/shard_map/ppermute | solution.py:33
  34.4 39.6 %collective-permute-start.7 = (bf16[4,512,256]{2,1,0:T(8,128)(2,1)}, bf16[4,512,256]{2,1,0:T(8,128)(2,1)}, u32[]{:S(2)}, u32[]{:S(2)}) collective-permute-start(bf16[4,512,256]{2,1,0:T(8,128)(2,1)} %gradient_terms.7), channel_id=1, source_target_pairs={{0,8},{4,12},{8,0},{12,4},{16,24},{20,28},{24,16},{28,20},{1,9},{5... | collective-permute-start | bytes 3145736 | tf_op jit(solution)/shard_map/ppermute | solution.py:33
  42.8 13.6 %collective-permute-start.3 = (bf16[4,128,128]{2,1,0:T(8,128)(2,1)S(1)}, bf16[4,128,128]{2,1,0:T(8,128)(2,1)S(1)}, u32[]{:S(2)}, u32[]{:S(2)}) collective-permute-start(bf16[4,128,128]{2,1,0:T(8,128)(2,1)S(1)} %convert_element_type.97), channel_id=1, source_target_pairs={{0,4},{4,0},{8,12},{12,8},{16,20},{20,16},{24,28},{28,24},{1,5},{5... | collective-permute-start | bytes 393224 | tf_op jit(solution)/shard_map/ppermute | solution.py:33
  57.2 8.5 %collective-permute-start.4 = (bf16[2,4,128,128]{3,2,1,0:T(8,128)(2,1)}, bf16[2,4,128,128]{3,2,1,0:T(8,128)(2,1)}, u32[]{:S(2)}, u32[]{:S(2)}) collective-permute-start(bf16[2,4,128,128]{3,2,1,0:T(8,128)(2,1)} %pad_maximum_fusion.1), channel_id=1, source_target_pairs={{0,8},{4,12},{8,0},{12,4},{16,24},{20,28},{24,16},{28,20},{1,9},{5... | collective-permute-start | bytes 786440 | tf_op jit(solution)/shard_map/ppermute | solution.py:33
  57.7 27.0 %collective-permute-start.10 = (bf16[4,256,256]{2,1,0:T(8,128)(2,1)}, bf16[4,256,256]{2,1,0:T(8,128)(2,1)S(1)}, u32[]{:S(2)}, u32[]{:S(2)}) collective-permute-start(bf16[4,256,256]{2,1,0:T(8,128)(2,1)} %copy-done.23), channel_id=1, source_target_pairs={{0,4},{4,0},{8,12},{12,8},{16,20},{20,16},{24,28},{28,24},{1,5},{5... | collective-permute-start | bytes 1572872 | tf_op jit(solution)/shard_map/ppermute | solution.py:33
  69.2 15.6 %collective-permute-start.11 = (bf16[4,256,256]{2,1,0:T(8,128)(2,1)S(1)}, bf16[4,256,256]{2,1,0:T(8,128)(2,1)S(1)}, u32[]{:S(2)}, u32[]{:S(2)}) collective-permute-start(bf16[4,256,256]{2,1,0:T(8,128)(2,1)S(1)} %copy-done.22), channel_id=1, source_target_pairs={{0,8},{4,12},{8,0},{12,4},{16,24},{20,28},{24,16},{28,20},{1,9},{5... | collective-permute-start | bytes 1572872 | tf_op jit(solution)/shard_map/ppermute | solution.py:33
  84.6 21.4 %collective-permute-start.8 = (bf16[2,256,1024]{2,1,0:T(8,128)(2,1)S(1)}, bf16[2,256,1024]{2,1,0:T(8,128)(2,1)S(1)}, u32[]{:S(2)}, u32[]{:S(2)}) collective-permute-start(bf16[2,256,1024]{2,1,0:T(8,128)(2,1)S(1)} %get-tuple-element.121), channel_id=1, source_target_pairs={{0,1},{1,0},{2,3},{3,2},{4,5},{5,4},{6,7},{7,6},{8,9},{9,8},{10,11... | collective-permute-start | bytes 3145736 | tf_op jit(solution)/shard_map/ppermute | solution.py:33
  89.4 18.7 %collective-permute-start.13 = (bf16[2,256,1024]{2,1,0:T(8,128)(2,1)S(1)}, bf16[2,256,1024]{2,1,0:T(8,128)(2,1)S(1)}, u32[]{:S(2)}, u32[]{:S(2)}) collective-permute-start(bf16[2,256,1024]{2,1,0:T(8,128)(2,1)S(1)} %get-tuple-element.135), channel_id=1, source_target_pairs={{0,1},{1,0},{2,3},{3,2},{4,5},{5,4},{6,7},{7,6},{8,9},{9,8},{10,11... | collective-permute-start | bytes 3145736 | tf_op jit(solution)/shard_map/ppermute | solution.py:33
  90.0 14.2 %collective-permute-start.9 = (bf16[2,512,256]{2,1,0:T(8,128)(2,1)S(1)}, bf16[2,512,256]{2,1,0:T(8,128)(2,1)S(1)}, u32[]{:S(2)}, u32[]{:S(2)}) collective-permute-start(bf16[2,512,256]{2,1,0:T(8,128)(2,1)S(1)} %get-tuple-element.122), channel_id=1, source_target_pairs={{0,4},{4,0},{8,12},{12,8},{16,20},{20,16},{24,28},{28,24},{1,5},{5... | collective-permute-start | bytes 1572872 | tf_op jit(solution)/shard_map/ppermute | solution.py:33
  92.0 16.9 %collective-permute-start.19 = (bf16[2,512,256]{2,1,0:T(8,128)(2,1)S(1)}, bf16[2,512,256]{2,1,0:T(8,128)(2,1)S(1)}, u32[]{:S(2)}, u32[]{:S(2)}) collective-permute-start(bf16[2,512,256]{2,1,0:T(8,128)(2,1)S(1)} %get-tuple-element.143), channel_id=1, source_target_pairs={{0,8},{4,12},{8,0},{12,4},{16,24},{20,28},{24,16},{28,20},{1,9},{5... | collective-permute-start | bytes 1572872 | tf_op jit(solution)/shard_map/ppermute | solution.py:33
  104.3 21.9 %collective-permute-start.15 = (bf16[4,256,256]{2,1,0:T(8,128)(2,1)S(1)}, bf16[4,256,256]{2,1,0:T(8,128)(2,1)S(1)}, u32[]{:S(2)}, u32[]{:S(2)}) collective-permute-start(bf16[4,256,256]{2,1,0:T(8,128)(2,1)S(1)} %get-tuple-element.139), channel_id=1, source_target_pairs={{0,4},{4,0},{8,12},{12,8},{16,20},{20,16},{24,28},{28,24},{1,5},{5... | collective-permute-start | bytes 1572872 | tf_op jit(solution)/shard_map/ppermute | solution.py:33
  106.1 20.1 %collective-permute-start.16 = (bf16[4,256,256]{2,1,0:T(8,128)(2,1)S(1)}, bf16[4,256,256]{2,1,0:T(8,128)(2,1)S(1)}, u32[]{:S(2)}, u32[]{:S(2)}) collective-permute-start(bf16[4,256,256]{2,1,0:T(8,128)(2,1)S(1)} %get-tuple-element.140), channel_id=1, source_target_pairs={{0,8},{4,12},{8,0},{12,4},{16,24},{20,28},{24,16},{28,20},{1,9},{5... | collective-permute-start | bytes 1572872 | tf_op jit(solution)/shard_map/ppermute | solution.py:33
  106.1 18.4 %collective-permute-start.17 = (bf16[2,256,256]{2,1,0:T(8,128)(2,1)S(1)}, bf16[2,256,256]{2,1,0:T(8,128)(2,1)S(1)}, u32[]{:S(2)}, u32[]{:S(2)}) collective-permute-start(bf16[2,256,256]{2,1,0:T(8,128)(2,1)S(1)} %get-tuple-element.141), channel_id=1, source_target_pairs={{0,8},{4,12},{8,0},{12,4},{16,24},{20,28},{24,16},{28,20},{1,9},{5... | collective-permute-start | bytes 786440 | tf_op jit(solution)/shard_map/ppermute | solution.py:33
  108.1 17.9 %collective-permute-start.18 = (bf16[2,256,256]{2,1,0:T(8,128)(2,1)S(1)}, bf16[2,256,256]{2,1,0:T(8,128)(2,1)S(1)}, u32[]{:S(2)}, u32[]{:S(2)}) collective-permute-start(bf16[2,256,256]{2,1,0:T(8,128)(2,1)S(1)} %get-tuple-element.142), channel_id=1, source_target_pairs={{0,4},{4,0},{8,12},{12,8},{16,20},{20,16},{24,28},{28,24},{1,5},{5... | collective-permute-start | bytes 786440 | tf_op jit(solution)/shard_map/ppermute | solution.py:33
  108.9 46.8 %collective-permute-start.12 = (bf16[1,256,1024]{2,1,0:T(8,128)(2,1)S(1)}, bf16[1,256,1024]{2,1,0:T(8,128)(2,1)S(1)}, u32[]{:S(2)}, u32[]{:S(2)}) collective-permute-start(bf16[1,256,1024]{2,1,0:T(8,128)(2,1)S(1)} %get-tuple-element.134), channel_id=1, source_target_pairs={{0,2},{1,3},{2,0},{3,1},{4,6},{5,7},{6,4},{7,5},{8,10},{9,11},{10,... | collective-permute-start | bytes 1572872 | tf_op jit(solution)/shard_map/ppermute | solution.py:33
  124.5 31.3 %collective-permute-start.14 = (bf16[1,256,1024]{2,1,0:T(8,128)(2,1)S(1)}, bf16[1,256,1024]{2,1,0:T(8,128)(2,1)S(1)}, u32[]{:S(2)}, u32[]{:S(2)}) collective-permute-start(bf16[1,256,1024]{2,1,0:T(8,128)(2,1)S(1)} %get-tuple-element.138), channel_id=1, source_target_pairs={{0,2},{1,3},{2,0},{3,1},{4,6},{5,7},{6,4},{7,5},{8,10},{9,11},{10,... | collective-permute-start | bytes 1572872 | tf_op jit(solution)/shard_map/ppermute | solution.py:33
  126.5 10.3 %collective-permute-start.20 = (bf16[2,256,256]{2,1,0:T(8,128)(2,1)S(1)}, bf16[2,256,256]{2,1,0:T(8,128)(2,1)S(1)}, u32[]{:S(2)}, u32[]{:S(2)}) collective-permute-start(bf16[2,256,256]{2,1,0:T(8,128)(2,1)S(1)} %get-tuple-element.157), channel_id=1, source_target_pairs={{0,8},{4,12},{8,0},{12,4},{16,24},{20,28},{24,16},{28,20},{1,9},{5... | collective-permute-start | bytes 786440 | tf_op jit(solution)/shard_map/ppermute | solution.py:33
  126.8 10.2 %collective-permute-start.21 = (bf16[2,256,256]{2,1,0:T(8,128)(2,1)S(1)}, bf16[2,256,256]{2,1,0:T(8,128)(2,1)S(1)}, u32[]{:S(2)}, u32[]{:S(2)}) collective-permute-start(bf16[2,256,256]{2,1,0:T(8,128)(2,1)S(1)} %get-tuple-element.159), channel_id=1, source_target_pairs={{0,4},{4,0},{8,12},{12,8},{16,20},{20,16},{24,28},{28,24},{1,5},{5... | collective-permute-start | bytes 786440 | tf_op jit(solution)/shard_map/ppermute | solution.py:33
  127.2 27.7 %collective-permute-start.25 = (bf16[1,512,256]{2,1,0:T(8,128)(2,1)S(1)}, bf16[1,512,256]{2,1,0:T(8,128)(2,1)S(1)}, u32[]{:S(2)}, u32[]{:S(2)}) collective-permute-start(bf16[1,512,256]{2,1,0:T(8,128)(2,1)S(1)} %get-tuple-element.164), channel_id=1, source_target_pairs={{0,16},{4,20},{8,24},{12,28},{16,0},{20,4},{24,8},{28,12},{1,17},{... | collective-permute-start | bytes 786440 | tf_op jit(solution)/shard_map/ppermute | solution.py:33
  136.7 26.6 %collective-permute-start.24 = (bf16[1,512,256]{2,1,0:T(8,128)(2,1)S(1)}, bf16[1,512,256]{2,1,0:T(8,128)(2,1)S(1)}, u32[]{:S(2)}, u32[]{:S(2)}) collective-permute-start(bf16[1,512,256]{2,1,0:T(8,128)(2,1)S(1)} %get-tuple-element.163), channel_id=1, source_target_pairs={{0,16},{4,20},{8,24},{12,28},{16,0},{20,4},{24,8},{28,12},{1,17},{... | collective-permute-start | bytes 786440 | tf_op jit(solution)/shard_map/ppermute | solution.py:33
  137.0 31.9 %collective-permute-start.23 = (bf16[1,512,256]{2,1,0:T(8,128)(2,1)S(1)}, bf16[1,512,256]{2,1,0:T(8,128)(2,1)S(1)}, u32[]{:S(2)}, u32[]{:S(2)}) collective-permute-start(bf16[1,512,256]{2,1,0:T(8,128)(2,1)S(1)} %get-tuple-element.162), channel_id=1, source_target_pairs={{0,16},{4,20},{8,24},{12,28},{16,0},{20,4},{24,8},{28,12},{1,17},{... | collective-permute-start | bytes 786440 | tf_op jit(solution)/shard_map/ppermute | solution.py:33
  154.9 18.3 %collective-permute-start.22 = (bf16[1,512,256]{2,1,0:T(8,128)(2,1)S(1)}, bf16[1,512,256]{2,1,0:T(8,128)(2,1)S(1)}, u32[]{:S(2)}, u32[]{:S(2)}) collective-permute-start(bf16[1,512,256]{2,1,0:T(8,128)(2,1)S(1)} %get-tuple-element.161), channel_id=1, source_target_pairs={{0,16},{4,20},{8,24},{12,28},{16,0},{20,4},{24,8},{28,12},{1,17},{... | collective-permute-start | bytes 786440 | tf_op jit(solution)/shard_map/ppermute | solution.py:33
  (30 other events, 210.4 us)

commit v4 on v3

v4 whole, which is shorter than its diff:
```python
import functools

import jax
import jax.numpy as jnp
from jax import lax
from jax.experimental import pallas as pl
from jax.experimental.pallas import tpu as pltpu
from jax.sharding import PartitionSpec as P

D = 2048
HD = 128
BLOCK = 1024
epsilon = 1e-06
f32 = jnp.float32
bf16 = jnp.bfloat16
MIB = 1024 * 1024
COST = pl.CostEstimate(flops=1000000, bytes_accessed=1, transcendentals=0)


def params(mib=16):
    return pltpu.CompilerParams(vmem_limit_bytes=mib * MIB)


def dot(a, b):
    return lax.dot_general(a, b, (((1,), (0,)), ((), ())), preferred_element_type=f32)


def dot_t(a, b):
    return lax.dot_general(a, b, (((1,), (1,)), ((), ())), preferred_element_type=f32)


def exchange(arr, axis, bit):
    count = lax.axis_size(axis)
    return lax.ppermute(arr, axis, [(i, i ^ (1 << bit)) for i in range(count)])


def slot_order(stage_bits):
    order = [0]
    for bit in reversed(stage_bits):
        order = order + [slot | (1 << bit) for slot in order]
    return order


def flip_kernel(value_ref, value_t_ref):
    value_t_ref[...] = value_ref[...].T


def flipped(values):
    count, width = values.shape
    return pl.pallas_call(
        flip_kernel,
        grid=(width // HD,),
        in_specs=[pl.BlockSpec((count, HD), lambda h: (0, h))],
        out_specs=pl.BlockSpec((HD, count), lambda h: (h, 0)),
        out_shape=jax.ShapeDtypeStruct((width, count), bf16),
        compiler_params=params(),
        cost_estimate=COST,
        name="flipped",
    )(values)


def state_kernel(key_ref, value_ref, state_ref, sent_ref, key_t_ref):
    key_t = key_ref[...].T
    key_t_ref[...] = key_t
    state = dot(key_t, value_ref[...])
    state_ref[0] = state
    sent_ref[0] = state.astype(bf16)


def block_states(keys, values):
    count, width = keys.shape
    heads = width // HD
    column = pl.BlockSpec((count, HD), lambda h: (0, h))
    square = pl.BlockSpec((1, HD, HD), lambda h: (h, 0, 0))
    return pl.pallas_call(
        state_kernel,
        grid=(heads,),
        in_specs=[column, column],
        out_specs=[square, square, pl.BlockSpec((HD, count), lambda h: (h, 0))],
        out_shape=[
            jax.ShapeDtypeStruct((heads, HD, HD), f32),
            jax.ShapeDtypeStruct((heads, HD, HD), bf16),
            jax.ShapeDtypeStruct((width, count), bf16),
        ],
        compiler_params=params(),
        cost_estimate=COST,
        name="block_states",
    )(keys, values)


def terms_kernel(number, outputs, position_ref, *refs):
    lefts, right, outs = refs[:number], refs[number], refs[number + 1 :]
    width = outs[0].shape[2]
    jobs = {}
    for out, (left, low, high, slots) in zip(outs, outputs):
        for index, slot in enumerate(slots):
            jobs.setdefault((left, slot), []).append((low, high, out, index))
    for (left, slot), parts in jobs.items():
        start = pl.multiple_of((position_ref[0] ^ slot) * width, width)
        product = dot(lefts[left][...], right[:, pl.ds(start, width)]).astype(bf16)
        for low, high, out, index in parts:
            out[index] = product[low:high]


def gradient_terms(lefts, right, position, outputs):
    count = right.shape[0]
    width = right.shape[1] // lax.axis_size("seq")
    if width % 128:
        blocked = right.reshape(count, -1, width)
        results = []
        for left, low, high, slots in outputs:
            picked = jnp.take(blocked, position ^ jnp.array(slots, jnp.int32), axis=1)
            part = jnp.einsum("at,tnb->nab", lefts[left][low:high], picked, preferred_element_type=f32)
            results.append(part.astype(bf16))
        return results
    shapes = [(len(slots), high - low, width) for _, low, high, slots in outputs]
    size = sum(n * r * w for n, r, w in shapes)
    vmem = pl.BlockSpec(memory_space=pltpu.VMEM)
    return pl.pallas_call(
        functools.partial(terms_kernel, len(lefts), outputs),
        in_specs=[pl.BlockSpec(memory_space=pltpu.SMEM)] + [vmem] * (len(lefts) + 1),
        out_specs=[vmem] * len(outputs),
        out_shape=[jax.ShapeDtypeStruct(shape, bf16) for shape in shapes],
        compiler_params=params(),
        cost_estimate=COST,
        name="gradient_terms",
    )(position[None], *lefts, right)


def sums_kernel(groups, merge, *refs):
    ins, outs = refs[: 2 * groups], refs[2 * groups :]
    low = 0
    for index in range(groups):
        keep, got = ins[2 * index], ins[2 * index + 1]
        half, rows = keep.shape[0] // 2, keep.shape[1]
        if merge:
            kept, sent = (out.at[:, low : low + rows, :] for out in outs)
            low += rows
        else:
            kept, sent = outs[2 * index], outs[2 * index + 1]
        for slot in range(half):
            kept[slot] = (keep[slot].astype(f32) + got[slot].astype(f32)).astype(bf16)
            other = half + slot
            sent[slot] = (keep[other].astype(f32) + got[other].astype(f32)).astype(bf16)


def sums(pairs, merge=False):
    slots, rows, width = pairs[0][0].shape
    total = sum(keep.shape[1] for keep, _ in pairs) if merge else rows
    shape = jax.ShapeDtypeStruct((slots // 2, total, width), bf16)
    vmem = pl.BlockSpec(memory_space=pltpu.VMEM)
    outs = 2 if merge else 2 * len(pairs)
    size = sum(keep.size for keep, _ in pairs)
    return pl.pallas_call(
        functools.partial(sums_kernel, len(pairs), merge),
        in_specs=[vmem] * (2 * len(pairs)),
        out_specs=[vmem] * outs,
        out_shape=[shape] * outs,
        compiler_params=params(),
        cost_estimate=COST,
        name="sums",
    )(*[array for pair in pairs for array in pair])


def middle_kernel(query_ref, grad_ref, mask_ref, gain_ref, state_ref, normed_t_ref, query_grad_ref, query_grad_t_ref, block_grad_ref, sent_ref):
    query = query_ref[...]
    state = state_ref[0]
    mask = mask_ref[...]
    gain = gain_ref[...].astype(f32)
    attended = dot(query, state)
    scale = lax.rsqrt(jnp.mean(attended * attended, -1, keepdims=True) + epsilon)
    unit = attended * scale
    normed_t_ref[...] = (unit * gain * mask).astype(bf16).T
    scaled = grad_ref[...] * mask * gain
    inner = jnp.mean(scaled * attended, -1, keepdims=True)
    attended_grad = (scale * scaled - attended * (scale * scale * scale) * inner).astype(bf16)
    attended_grad_t = attended_grad.T
    block_grad = dot(attended_grad_t, query)
    block_grad_ref[0] = block_grad
    sent_ref[0] = block_grad.astype(bf16)
    query_grad_ref[...] = dot_t(attended_grad, state).astype(bf16)
    query_grad_t_ref[...] = dot(state, attended_grad_t).astype(bf16)


def middle(queries, normed_grad, mask, gain, state):
    count, width = queries.shape
    heads = width // HD
    column = pl.BlockSpec((count, HD), lambda h: (0, h))
    row = pl.BlockSpec((HD, count), lambda h: (h, 0))
    square = pl.BlockSpec((1, HD, HD), lambda h: (h, 0, 0))
    return pl.pallas_call(
        middle_kernel,
        grid=(heads,),
        in_specs=[
            column,
            column,
            pl.BlockSpec((count, 1), lambda h: (0, 0)),
            pl.BlockSpec((1, HD), lambda h: (0, h)),
            square,
        ],
        out_specs=[row, column, row, square, square],
        out_shape=[
            jax.ShapeDtypeStruct((width, count), bf16),
            jax.ShapeDtypeStruct((count, width), bf16),
            jax.ShapeDtypeStruct((width, count), bf16),
            jax.ShapeDtypeStruct((heads, HD, HD), f32),
            jax.ShapeDtypeStruct((heads, HD, HD), bf16),
        ],
        compiler_params=params(),
        cost_estimate=COST,
        name="norm_backward",
    )(queries, normed_grad, mask, gain, state)


def late_kernel(mine_ref, mate_ref, other_ref, *refs):
    for side, state_ref, parts in ((0, mate_ref, refs[0:2] + refs[4:6]), (1, other_ref, refs[2:4] + refs[6:8])):
        own, got, keep, send = parts
        half = keep.shape[0]

        def times(state, block):
            return lax.dot_general(state, block, (((side,), (0,)), ((), ())), preferred_element_type=f32)

        for slot in range(2 * half):
            out = keep if slot < half else send
            for h in range(mine_ref.shape[0]):
                rows = slice(h * HD, (h + 1) * HD)
                total = times(mine_ref[h], own[slot, rows, :]) + times(state_ref[h], got[slot, rows, :])
                out[slot % half, rows, :] = total.astype(bf16)


def late_terms(mine, mate, other, value_keep, value_got, key_keep, key_got):
    slots, rows, width = value_keep.shape
    vmem = pl.BlockSpec(memory_space=pltpu.VMEM)
    shape = jax.ShapeDtypeStruct((slots // 2, rows, width), bf16)
    return pl.pallas_call(
        late_kernel,
        in_specs=[vmem] * 7,
        out_specs=[vmem] * 4,
        out_shape=[shape] * 4,
        compiler_params=params(),
        cost_estimate=COST,
        name="late_terms",
    )(mine, mate, other, value_keep, value_got, key_keep, key_got)


def key_value_kernel(key_ref, value_ref, grad_ref, key_grad_ref, value_grad_ref):
    key_grad_ref[...] = dot(value_ref[...], grad_ref[0]).astype(bf16)
    value_grad_ref[...] = dot_t(key_ref[...], grad_ref[0]).astype(bf16)


def key_value_grads(keys, values, state_grad_t):
    count, width = keys.shape
    column = pl.BlockSpec((count, HD), lambda h: (0, h))
    out = jax.ShapeDtypeStruct((count, width), bf16)
    return pl.pallas_call(
        key_value_kernel,
        grid=(width // HD,),
        in_specs=[column, column, pl.BlockSpec((1, HD, HD), lambda h: (h, 0, 0))],
        out_specs=[column, column],
        out_shape=[out, out],
        compiler_params=params(),
        cost_estimate=COST,
        name="key_value_grads",
    )(keys, values, state_grad_t)


def input_kernel(order, place_ref, query_ref, key_ref, value_ref, weight_ref, keep_ref, send_ref, held_ref):
    total = dot_t(query_ref[...], weight_ref[0])
    total += dot_t(key_ref[...], weight_ref[1])
    total += dot_t(value_ref[...], weight_ref[2])
    held_ref[...] = total.astype(bf16).reshape(held_ref.shape)
    half = len(order) // 2
    for index in range(half):
        keep_ref[index] = held_ref[place_ref[0] ^ order[index]]
        send_ref[index] = held_ref[place_ref[0] ^ order[half + index]]


def input_terms(grads, weight, place, order, chunk, chunks, tile=512):
    count, width = grads[0].shape
    half = len(order) // 2
    rows = count // len(order)
    columns = D // chunks
    first = chunk * columns // tile
    full = pl.BlockSpec((count, width), lambda i, b: (0, 0))
    out = pl.BlockSpec((half, rows, tile), lambda i, b: (0, 0, i))
    shape = jax.ShapeDtypeStruct((half, rows, columns), bf16)
    return pl.pallas_call(
        functools.partial(input_kernel, order),
        grid_spec=pltpu.PrefetchScalarGridSpec(
            num_scalar_prefetch=1,
            grid=(columns // tile,),
            in_specs=[full, full, full, pl.BlockSpec((3, tile, width), lambda i, b: (0, first + i, 0))],
            out_specs=[out, out],
            scratch_shapes=[pltpu.VMEM((len(order), rows, tile), bf16)],
        ),
        out_shape=[shape, shape],
        compiler_params=params(32),
        cost_estimate=COST,
        name="input_terms",
    )(place[None], *grads, weight)


def finish_kernel(*refs):
    out = refs[-1]
    for index in range(3):
        keep, got = refs[2 * index], refs[2 * index + 1]
        out[index] = (keep[...].astype(f32) + got[...].astype(f32)).T


def finish(pairs):
    rows, width = pairs[0].shape
    return pl.pallas_call(
        finish_kernel,
        out_shape=jax.ShapeDtypeStruct((3, width, rows), f32),
        compiler_params=params(),
        cost_estimate=COST,
        name="finish",
    )(*pairs)


def after(value, *others):
    return lax.optimization_barrier((value,) + others)[0]


def per_device(layer_input, output_grad, loss_mask, proj_weight, out_weight, norm_gain):
    position = lax.axis_index("seq")
    place = lax.axis_index("head")
    seq_bits = lax.axis_size("seq").bit_length() - 1
    head_bits = lax.axis_size("head").bit_length() - 1
    stages = list(range(seq_bits))
    bits = [(position >> bit) & 1 == 1 for bit in stages]
    order, swapped = slot_order(stages), slot_order([1, 0] + stages[2:])
    half = len(order) // 2
    head_order = slot_order(list(range(head_bits)))
    weights = jnp.transpose(proj_weight, (1, 0, 2))

    def project(rows, index):
        return jnp.dot(rows, weights[index], preferred_element_type=f32).astype(bf16)

    def terms(left, right, *parts):
        outputs = [(0, 0, left.shape[0], slots) for slots in parts]
        return gradient_terms([left], right, position, outputs)

    values = project(layer_input, 2)
    values_t = flipped(values)
    (value_send,) = terms(values_t, layer_input, order[half:])
    value_got = exchange(value_send, "seq", 0)
    keys = project(after(layer_input, value_send), 1)
    own_state, sent, keys_t = block_states(keys, values)
    mask = loss_mask.astype(f32)[:, None]

    before, total = jnp.zeros_like(own_state), own_state
    for bit in stages[1:]:
        got = exchange(sent, "seq", bit)
        if bit == 1:
            queries = project(after(layer_input, own_state), 0)
            got = after(got, queries)
        elif bit == 2:
            (key_send,) = terms(keys_t, after(layer_input, total), swapped[half:])
            normed_grad = dot_t(after(output_grad, key_send), out_weight)
            key_got = exchange(key_send, "seq", 1)
            got = after(got, normed_grad)
        before = before + jnp.where(bits[bit], got.astype(f32), 0.0)
        total = total + got.astype(f32)
        sent = total.astype(bf16)
    sent = (before + jnp.where(bits[0], 0.0, own_state)).astype(bf16)
    got = exchange(after(sent, value_got), "seq", 0)
    state = (before + got.astype(f32) + own_state).astype(bf16)

    normed_t, query_grad, query_grad_t, own_grad, sent = middle(
        queries, normed_grad, mask, norm_gain[None, :], state
    )

    got = exchange(sent, "seq", 0)
    out_keep, out_send = terms(normed_t, after(output_grad, own_grad), order[:half], order[half:])
    got = after(got, out_keep, key_got).astype(f32)
    total = own_grad + got
    mine, mate = jnp.where(bits[0], own_grad, total), jnp.where(bits[0], total, got)
    out_got = exchange(after(out_send, total), "seq", 0)

    got = exchange(jnp.stack([total, mine]).astype(bf16), "seq", 1)
    query_keep, query_send = terms(query_grad_t, after(layer_input, total), order[:half], order[half:])
    got = after(got, query_keep).astype(f32)
    later = jnp.where(bits[1], 0.0, got[0])
    mine, mate = mine + later, mate + later
    other = got[1] + jnp.where(bits[1], total, 0.0)
    total = total + got[0]
    query_got = exchange(after(query_send, total), "seq", 0)

    for bit in stages[2:]:
        got = exchange(total.astype(bf16), "seq", bit)
        if bit == 2:
            (value_keep,) = terms(values_t, after(layer_input, total), order[:half])
            (key_keep,) = terms(keys_t, after(layer_input, value_keep), swapped[:half])
            got = after(got, key_keep)
        got = got.astype(f32)
        later = jnp.where(bits[bit], 0.0, got)
        mine, mate, other = mine + later, mate + later, other + later
        total = total + got
    state_grad = mine.astype(bf16)

    value_keep, value_send, key_keep, key_send = late_terms(
        state_grad, mate.astype(bf16), other.astype(bf16), value_keep, value_got, key_keep, key_got
    )
    value_got = exchange(value_send, "seq", 1)
    key_got = exchange(key_send, "seq", 0)

    key_grad, value_grad = key_value_grads(keys, values, after(state_grad, value_keep))
    grads = (query_grad, key_grad, value_grad)
    input_keep, input_send = input_terms(grads, weights, place, head_order, 0, 1)

    def stage(keep, got, token, bit, axis="seq"):
        keep, send = sums([(keep, after(got, token))])
        return keep, exchange(send, axis, bit)

    def rest(keep, got, bits_left):
        for bit in bits_left:
            keep, got = stage(keep, got, keep, bit)
        return keep[0], got[0]

    out_keep, out_got = stage(out_keep, out_got, input_keep, 1)
    value_keep, value_got = stage(value_keep, value_got, out_keep, 2)
    input_got = exchange(after(input_send, value_keep), "head", 0)
    for bit in range(1, head_bits):
        input_keep, input_got = stage(input_keep, input_got, value_keep, bit, "head")
    query_keep, query_got = stage(query_keep, query_got, (input_keep, value_got), 1)
    out_keep, out_got = stage(out_keep, out_got, query_keep, 2)
    key_keep, key_got = stage(key_keep, key_got, out_keep, 2)
    query_keep, query_got = stage(query_keep, query_got, key_keep, 2)

    out_pair = rest(out_keep, out_got, stages[3:])
    value_pair = rest(value_keep, value_got, stages[3:])
    key_pair = rest(key_keep, key_got, stages[3:])
    query_pair = rest(query_keep, query_got, stages[3:])
    input_got = after(input_got, query_keep)
    input_grad = (input_keep[0].astype(f32) + input_got[0].astype(f32)).astype(bf16)
    out_weight_grad = out_pair[0].astype(f32) + out_pair[1].astype(f32)
    proj_weight_grad = finish(query_pair + value_pair + key_pair)
    return (input_grad, jnp.transpose(proj_weight_grad, (1, 0, 2)), out_weight_grad)


def solution(mesh):
    in_specs = (
        P("seq", None),
        P("seq", None),
        P("seq"),
        P(None, None, "head"),
        P("head", None),
        P("head"),
    )
    out_specs = (P(("seq", "head"), None), P("seq", None, "head"), P("head", "seq"))
    return jax.shard_map(
        per_device, mesh=mesh, in_specs=in_specs, out_specs=out_specs, check_vma=False
    )
```

time: 175 us -> 167 us (0.954)
  waiting for transfers between devices: 78 us -> 62.5 us
  local copies, waits for them, and re-layouts: 9.77 us -> 15.8 us
  Pallas kernels: 36.2 us -> 39.3 us
    ppermute x26 -> x20, waiting for transfers between devices: 78 us -> 62.5 us  [exchange(): return lax.ppermute(arr, axis, [(i, i ^ 1 << bit) for i in range(count)])]
    unnamed x56 -> x70, local copies, waits for them, and re-layouts: 8.74 us -> 14.8 us
    dot_general x3, matrix products: 13.6 us -> 10.9 us  [project(): jnp.dot(rows, weights[index], preferred_element_type=f32).astype(bf16)]
    pallas_call x8 -> x7, Pallas kernels: 1.45 us -> 3.82 us  [sums(): pl.pallas_call(functools.partial(sums_kernel, len(pairs), merge), in_spec...]
    convert_element_type x7 -> x5, other arithmetic: 2.34 us -> 3.67 us  [the longest x1 1.36 us: per_device(): (input_keep[0].astype(f32) + input_got[0].astype(f32)).astype(bf16)]
    ppermute x26 -> x20, starting transfers between devices: 28.6 us -> 27.3 us  [exchange(): return lax.ppermute(arr, axis, [(i, i ^ 1 << bit) for i in range(count)])]
    pallas_call x2 -> x1, Pallas kernels: 8.64 us -> 8.35 us  [input_terms(): pl.pallas_call(functools.partial(input_kernel, order), grid_spec=pltpu.Pr...]
  transfers between devices with their start and end apart: 26 -> 20, of which waited for: 11 -> 11; matrix products, arithmetic and copies ran while one was open for 7% -> 9% of each run, Pallas kernels for 19% -> 21%
where the time goes in v4:
time: 167 us; the launch traced here: 166 us
  waiting for transfers between devices  62.5 us (37%)
  Pallas kernels  39.3 us (24%)
  starting transfers between devices  27.3 us (16%)
  local copies, waits for them, and re-layouts  15.8 us (9%)
  matrix products  14.7 us (9%)
  other arithmetic  5.59 us (3%)
    ppermute x20, waiting for transfers between devices, exchange(): return lax.ppermute(arr, axis, [(i, i ^ 1 << bit) for i in range(count)])  62.5 us
    ppermute x20, starting transfers between devices, exchange(): return lax.ppermute(arr, axis, [(i, i ^ 1 << bit) for i in range(count)])  27.3 us
    unnamed x70, local copies, waits for them, and re-layouts  14.8 us
    pallas_call x6, Pallas kernels, gradient_terms(): pl.pallas_call(functools.partial(terms_kernel, len(lefts), outputs), in_s...  12.9 us
    dot_general x3, matrix products, project(): jnp.dot(rows, weights[index], preferred_element_type=f32).astype(bf16)  10.9 us
    pallas_call x1, Pallas kernels, input_terms(): pl.pallas_call(functools.partial(input_kernel, order), grid_spec=pltpu.Pr...  8.35 us
    pallas_call x1, Pallas kernels, middle(): pl.pallas_call(middle_kernel, grid=(heads,), in_specs=[column, column, pl...  4.95 us
    pallas_call x7, Pallas kernels, sums(): pl.pallas_call(functools.partial(sums_kernel, len(pairs), merge), in_spec...  3.82 us
  transfers between devices with their start and end apart: 20, of which 11 were waited for; matrix products, arithmetic and copies ran while one was open for 9% of the time, Pallas kernels for 21%

profile of v4, /device:TPU:0, one launch (start us, length us, event | category | flops | bytes accessed | tf_op | source)
XLA Modules:
  0.0 166.3 jit_solution(12427609932867216895)
XLA Ops:
  0.7 5.3 %fusion.3.value_ref = bf16[1024,512]{1,0:T(8,128)(2,1)S(1)} fusion(bf16[1024,2048]{1,0:T(8,128)(2,1)} %refs_1_.6, bf16[3,2048,512]{2,1,0:T(8,128)(2,1)} %bitcast.57), kind=kOutput, calls=%fused_computation.7 | convolution fusion | flops 2148007936 | bytes 7340032 | tf_op jit(solution)/shard_map/dot_general | solution.py:338
  9.1 3.0 %collective-permute-start.2 = (bf16[4,512,256]{2,1,0:T(8,128)(2,1)}, bf16[4,512,256]{2,1,0:T(8,128)(2,1)}, u32[]{:S(2)}, u32[]{:S(2)}) collective-permute-start(bf16[4,512,256]{2,1,0:T(8,128)(2,1)} %gradient_terms.6), channel_id=1, source_target_pairs={{0,4},{4,0},{8,12},{12,8},{16,20},{20,16},{24,28},{28,24},{1,5},{5... | collective-permute-start | bytes 3145736 | tf_op jit(solution)/shard_map/ppermute | solution.py:34
  12.0 2.3 %fusion.4.key_ref = bf16[1024,512]{1,0:T(8,128)(2,1)S(1)} fusion(bf16[1024,2048]{1,0:T(8,128)(2,1)S(1)} %copy-done.2, bf16[3,2048,512]{2,1,0:T(8,128)(2,1)S(1)} %bitcast.58), kind=kOutput, calls=%fused_computation.8 | convolution fusion | flops 2148007936 | bytes 7340032 | tf_op jit(solution)/shard_map/dot_general | solution.py:338
  18.5 3.3 %fusion.5.query_ref = bf16[1024,512]{1,0:T(8,128)(2,1)} fusion(bf16[1024,2048]{1,0:T(8,128)(2,1)S(1)} %copy-done.2, bf16[3,2048,512]{2,1,0:T(8,128)(2,1)S(1)} %bitcast.59), kind=kOutput, calls=%fused_computation.9 | convolution fusion | flops 2148007936 | bytes 7340032 | tf_op jit(solution)/shard_map/dot_general | solution.py:338
  23.0 2.7 %collective-permute-start.1 = (bf16[4,128,128]{2,1,0:T(8,128)(2,1)S(1)}, bf16[4,128,128]{2,1,0:T(8,128)(2,1)S(1)}, u32[]{:S(2)}, u32[]{:S(2)}) collective-permute-start(bf16[4,128,128]{2,1,0:T(8,128)(2,1)S(1)} %convert_add_fusion.1), channel_id=1, source_target_pairs={{0,16},{4,20},{8,24},{12,28},{16,0},{20,4},{24,8},{28,12},{1,17},{... | collective-permute-start | bytes 393224 | tf_op jit(solution)/shard_map/ppermute | solution.py:34
  29.1 2.3 %gradient_terms.7 = bf16[4,512,256]{2,1,0:T(8,128)(2,1)} custom-call(s32[1]{0:T(128)} %bitcast.1.position_ref, bf16[512,1024]{1,0:T(8,128)(2,1)S(1)} %copy-done.10, bf16[1024,2048]{1,0:T(8,128)(2,1)S(1)} %copy-done.3), custom_call_target="tpu_custom_call" | custom-call | flops 1000000 | bytes 1 | tf_op jit(solution)/shard_map/gradient_terms/pallas_call | solution.py:119
  32.9 3.7 %fusion.16.grad_ref = f32[1024,512]{1,0:T(8,128)} fusion(bf16[1024,2048]{1,0:T(8,128)(2,1)S(1)} %copy-done.12, bf16[512,2048]{1,0:T(8,128)(2,1)S(1)} %copy-done), kind=kOutput, calls=%fused_computation.35 | convolution fusion | flops 2147483648 | bytes 8388608 | tf_op jit(solution)/shard_map/dot_general | solution.py:29
  39.9 2.8 %collective-permute-done.3 = bf16[4,128,128]{2,1,0:T(8,128)(2,1)S(1)} collective-permute-done((bf16[4,128,128]{2,1,0:T(8,128)(2,1)S(1)}, bf16[4,128,128]{2,1,0:T(8,128)(2,1)S(1)}, u32[]{:S(2)}, u32[]{:S(2)}) %collective-permute-start.3) | collective-permute-done | bytes 131104 | tf_op jit(solution)/shard_map/ppermute | solution.py:34
  47.9 4.9 %norm_backward.1 = (bf16[512,1024]{1,0:T(8,128)(2,1)S(1)}, bf16[1024,512]{1,0:T(8,128)(2,1)S(1)}, bf16[512,1024]{1,0:T(8,128)(2,1)S(1)}, f32[4,128,128]{2,1,0:T(8,128)S(1)}, bf16[4,128,128]{2,1,0:T(8,128)(2,1)S(1)}) custom-call(bf16[1024,512]{1,0:T(8,128)(2,1)S(1)} %copy-done.20, f32[1024,512]{1,0:T(8,128)S(1)} %copy-done.16, f32[1024,1]{1,0:T(8,128)S(1)} %copy-done.17, ...), custom_call_target="tpu_custom_call" | custom-call | flops 1000000 | bytes 1 | tf_op jit(solution)/shard_map/norm_backward/pallas_call | solution.py:191
  54.9 3.4 %gradient_terms.8 = (bf16[4,512,256]{2,1,0:T(8,128)(2,1)S(1)}, bf16[4,512,256]{2,1,0:T(8,128)(2,1)}) custom-call(s32[1]{0:T(128)} %bitcast.1.position_ref, bf16[512,1024]{1,0:T(8,128)(2,1)S(1)} %get-tuple-element.76.refs_0_, bf16[1024,2048]{1,0:T(8,128)(2,1)S(1)} %copy-done.13), custom_call_target="tpu_custom_call" | custom-call | flops 1000000 | bytes 1 | tf_op jit(solution)/shard_map/gradient_terms/pallas_call | solution.py:119
  60.6 2.4 %gradient_terms.9 = (bf16[4,512,256]{2,1,0:T(8,128)(2,1)S(1)}, bf16[4,512,256]{2,1,0:T(8,128)(2,1)S(1)}) custom-call(s32[1]{0:T(128)} %bitcast.1.position_ref, bf16[512,1024]{1,0:T(8,128)(2,1)S(1)} %get-tuple-element.80.refs_0_, bf16[1024,2048]{1,0:T(8,128)(2,1)S(1)} %copy-done.4), custom_call_target="tpu_custom_call" | custom-call | flops 1000000 | bytes 1 | tf_op jit(solution)/shard_map/gradient_terms/pallas_call | solution.py:119
  63.0 3.1 %collective-permute-done.6 = bf16[2,4,128,128]{3,2,1,0:T(8,128)(2,1)S(1)} collective-permute-done((bf16[2,4,128,128]{3,2,1,0:T(8,128)(2,1)S(1)}, bf16[2,4,128,128]{3,2,1,0:T(8,128)(2,1)S(1)}, u32[]{:S(2)}, u32[]{:S(2)}) %collective-permute-start.6) | collective-permute-done | bytes 262176 | tf_op jit(solution)/shard_map/ppermute | solution.py:34
  69.1 3.9 %collective-permute-done.7 = bf16[4,128,128]{2,1,0:T(8,128)(2,1)S(1)} collective-permute-done((bf16[4,128,128]{2,1,0:T(8,128)(2,1)S(1)}, bf16[4,128,128]{2,1,0:T(8,128)(2,1)S(1)}, u32[]{:S(2)}, u32[]{:S(2)}) %collective-permute-start.7) | collective-permute-done | bytes 131104 | tf_op jit(solution)/shard_map/ppermute | solution.py:34
  73.2 3.6 %late_terms.1 = (bf16[2,512,256]{2,1,0:T(8,128)(2,1)S(1)}, bf16[2,512,256]{2,1,0:T(8,128)(2,1)}, bf16[2,512,256]{2,1,0:T(8,128)(2,1)S(1)}, bf16[2,512,256]{2,1,0:T(8,128)(2,1)S(1)}) custom-call(bf16[4,128,128]{2,1,0:T(8,128)(2,1)S(1)} %get-tuple-element.88.mine_ref.grad_ref, bf16[4,128,128]{2,1,0:T(8,128)(2,1)S(1)} %get-tuple-element.126.mate_ref, ...), custom_call_target="tpu_custom_call" | custom-call | flops 1000000 | bytes 1 | tf_op jit(solution)/shard_map/late_terms/pallas_call | solution.py:235
  81.1 2.8 %copy-done.8 = bf16[2048,3,512]{2,0,1:T(8,128)(2,1)S(1)} copy-done((bf16[2048,3,512]{2,0,1:T(8,128)(2,1)S(1)}, bf16[2048,3,512]{2,0,1:T(8,128)(2,1)}, u32[]{:S(2)}) %copy-start.8) | copy-done | bytes 6291480
  83.9 8.3 %input_terms.1 = (bf16[2,256,2048]{2,1,0:T(8,128)(2,1)S(1)}, bf16[2,256,2048]{2,1,0:T(8,128)(2,1)S(1)}) custom-call(s32[1]{0:T(128)} %bitcast.place_ref, bf16[1024,512]{1,0:T(8,128)(2,1)S(1)} %copy-done.19, bf16[1024,512]{1,0:T(8,128)(2,1)S(1)} %get-tuple-element.89.key_ref, bf16[1024,512]{1,0:T(8,128)(2,1)S(1)} %get-tuple-element.90.value_ref, ...), custom_call_target="tpu_custom_call" | custom-call | flops 1000000 | bytes 1 | tf_op jit(solution)/shard_map/input_terms/pallas_call | solution.py:287
  96.3 3.1 %collective-permute-start.13 = (bf16[1,512,256]{2,1,0:T(8,128)(2,1)S(1)}, bf16[1,512,256]{2,1,0:T(8,128)(2,1)S(1)}, u32[]{:S(2)}, u32[]{:S(2)}) collective-permute-start(bf16[1,512,256]{2,1,0:T(8,128)(2,1)S(1)} %get-tuple-element.106), channel_id=1, source_target_pairs={{0,16},{4,20},{8,24},{12,28},{16,0},{20,4},{24,8},{28,12},{1,17},{... | collective-permute-start | bytes 786440 | tf_op jit(solution)/shard_map/ppermute | solution.py:34
  104.5 7.3 %collective-permute-done.13 = bf16[1,512,256]{2,1,0:T(8,128)(2,1)S(1)} collective-permute-done((bf16[1,512,256]{2,1,0:T(8,128)(2,1)S(1)}, bf16[1,512,256]{2,1,0:T(8,128)(2,1)S(1)}, u32[]{:S(2)}, u32[]{:S(2)}) %collective-permute-start.13) | collective-permute-done | bytes 262176 | tf_op jit(solution)/shard_map/ppermute | solution.py:34
  111.8 9.4 %collective-permute-done.12.refs_1_ = bf16[4,512,256]{2,1,0:T(8,128)(2,1)S(1)} collective-permute-done((bf16[4,512,256]{2,1,0:T(8,128)(2,1)S(1)}, bf16[4,512,256]{2,1,0:T(8,128)(2,1)S(1)}, u32[]{:S(2)}, u32[]{:S(2)}) %collective-permute-start.12) | collective-permute-done | bytes 1048608 | tf_op jit(solution)/shard_map/ppermute | solution.py:34
  124.0 8.0 %collective-permute-done.15.refs_1_ = bf16[2,512,256]{2,1,0:T(8,128)(2,1)S(1)} collective-permute-done((bf16[2,512,256]{2,1,0:T(8,128)(2,1)S(1)}, bf16[2,512,256]{2,1,0:T(8,128)(2,1)S(1)}, u32[]{:S(2)}, u32[]{:S(2)}) %collective-permute-start.15) | collective-permute-done | bytes 524320 | tf_op jit(solution)/shard_map/ppermute | solution.py:34
  132.1 2.5 %collective-permute-start.18 = (bf16[1,512,256]{2,1,0:T(8,128)(2,1)S(1)}, bf16[1,512,256]{2,1,0:T(8,128)(2,1)S(1)}, u32[]{:S(2)}, u32[]{:S(2)}) collective-permute-start(bf16[1,512,256]{2,1,0:T(8,128)(2,1)S(1)} %get-tuple-element.121), channel_id=1, source_target_pairs={{0,16},{4,20},{8,24},{12,28},{16,0},{20,4},{24,8},{28,12},{1,17},{... | collective-permute-start | bytes 786440 | tf_op jit(solution)/shard_map/ppermute | solution.py:34
  134.6 7.2 %collective-permute-done.14.refs_1_ = bf16[2,512,256]{2,1,0:T(8,128)(2,1)S(1)} collective-permute-done((bf16[2,512,256]{2,1,0:T(8,128)(2,1)S(1)}, bf16[2,512,256]{2,1,0:T(8,128)(2,1)S(1)}, u32[]{:S(2)}, u32[]{:S(2)}) %collective-permute-start.14) | collective-permute-done | bytes 524320 | tf_op jit(solution)/shard_map/ppermute | solution.py:34
  143.1 15.3 %collective-permute-done.18 = bf16[1,512,256]{2,1,0:T(8,128)(2,1)S(1)} collective-permute-done((bf16[1,512,256]{2,1,0:T(8,128)(2,1)S(1)}, bf16[1,512,256]{2,1,0:T(8,128)(2,1)S(1)}, u32[]{:S(2)}, u32[]{:S(2)}) %collective-permute-start.18) | collective-permute-done | bytes 262176 | tf_op jit(solution)/shard_map/ppermute | solution.py:34
  158.4 4.9 %collective-permute-done.17 = bf16[1,512,256]{2,1,0:T(8,128)(2,1)S(1)} collective-permute-done((bf16[1,512,256]{2,1,0:T(8,128)(2,1)S(1)}, bf16[1,512,256]{2,1,0:T(8,128)(2,1)S(1)}, u32[]{:S(2)}, u32[]{:S(2)}) %collective-permute-start.17) | collective-permute-done | bytes 262176 | tf_op jit(solution)/shard_map/ppermute | solution.py:34
  (124 shorter events, 49.8 us)
Async XLA Ops:
  0.6 32.3 %copy-start = (bf16[512,2048]{1,0:T(8,128)(2,1)S(1)}, bf16[512,2048]{1,0:T(8,128)(2,1)}, u32[]{:S(2)}) copy-start(bf16[512,2048]{1,0:T(8,128)(2,1)} %param.10) | copy-start | bytes 6291460
  9.1 28.6 %collective-permute-start.2 = (bf16[4,512,256]{2,1,0:T(8,128)(2,1)}, bf16[4,512,256]{2,1,0:T(8,128)(2,1)}, u32[]{:S(2)}, u32[]{:S(2)}) collective-permute-start(bf16[4,512,256]{2,1,0:T(8,128)(2,1)} %gradient_terms.6), channel_id=1, source_target_pairs={{0,4},{4,0},{8,12},{12,8},{16,20},{20,16},{24,28},{28,24},{1,5},{5... | collective-permute-start | bytes 3145736 | tf_op jit(solution)/shard_map/ppermute | solution.py:34
  17.0 5.1 %collective-permute-start = (bf16[4,128,128]{2,1,0:T(8,128)(2,1)S(1)}, bf16[4,128,128]{2,1,0:T(8,128)(2,1)}, u32[]{:S(2)}, u32[]{:S(2)}) collective-permute-start(bf16[4,128,128]{2,1,0:T(8,128)(2,1)S(1)} %get-tuple-element.67), channel_id=1, source_target_pairs={{0,8},{4,12},{8,0},{12,4},{16,24},{20,28},{24,16},{28,20},{1,9},{5... | collective-permute-start | bytes 393224 | tf_op jit(solution)/shard_map/ppermute | solution.py:34
  23.0 13.7 %collective-permute-start.1 = (bf16[4,128,128]{2,1,0:T(8,128)(2,1)S(1)}, bf16[4,128,128]{2,1,0:T(8,128)(2,1)S(1)}, u32[]{:S(2)}, u32[]{:S(2)}) collective-permute-start(bf16[4,128,128]{2,1,0:T(8,128)(2,1)S(1)} %convert_add_fusion.1), channel_id=1, source_target_pairs={{0,16},{4,20},{8,24},{12,28},{16,0},{20,4},{24,8},{28,12},{1,17},{... | collective-permute-start | bytes 393224 | tf_op jit(solution)/shard_map/ppermute | solution.py:34
  31.4 27.0 %collective-permute-start.5 = (bf16[4,512,256]{2,1,0:T(8,128)(2,1)}, bf16[4,512,256]{2,1,0:T(8,128)(2,1)}, u32[]{:S(2)}, u32[]{:S(2)}) collective-permute-start(bf16[4,512,256]{2,1,0:T(8,128)(2,1)} %gradient_terms.7), channel_id=1, source_target_pairs={{0,8},{4,12},{8,0},{12,4},{16,24},{20,28},{24,16},{28,20},{1,9},{5... | collective-permute-start | bytes 3145736 | tf_op jit(solution)/shard_map/ppermute | solution.py:34
  37.7 5.0 %collective-permute-start.3 = (bf16[4,128,128]{2,1,0:T(8,128)(2,1)S(1)}, bf16[4,128,128]{2,1,0:T(8,128)(2,1)S(1)}, u32[]{:S(2)}, u32[]{:S(2)}) collective-permute-start(bf16[4,128,128]{2,1,0:T(8,128)(2,1)S(1)} %add_convert_fusion.3), channel_id=1, source_target_pairs={{0,4},{4,0},{8,12},{12,8},{16,20},{20,16},{24,28},{28,24},{1,5},{5... | collective-permute-start | bytes 393224 | tf_op jit(solution)/shard_map/ppermute | solution.py:34
  42.7 12.2 %copy-start.13 = (bf16[1024,2048]{1,0:T(8,128)(2,1)S(1)}, bf16[1024,2048]{1,0:T(8,128)(2,1)}, u32[]{:S(2)}) copy-start(bf16[1024,2048]{1,0:T(8,128)(2,1)} %refs_1_.3) | copy-start | bytes 12582916
  53.8 5.0 %collective-permute-start.4 = (bf16[4,128,128]{2,1,0:T(8,128)(2,1)S(1)}, bf16[4,128,128]{2,1,0:T(8,128)(2,1)S(1)}, u32[]{:S(2)}, u32[]{:S(2)}) collective-permute-start(bf16[4,128,128]{2,1,0:T(8,128)(2,1)S(1)} %get-tuple-element.75), channel_id=1, source_target_pairs={{0,4},{4,0},{8,12},{12,8},{16,20},{20,16},{24,28},{28,24},{1,5},{5... | collective-permute-start | bytes 393224 | tf_op jit(solution)/shard_map/ppermute | solution.py:34
  58.9 7.1 %collective-permute-start.6 = (bf16[2,4,128,128]{3,2,1,0:T(8,128)(2,1)S(1)}, bf16[2,4,128,128]{3,2,1,0:T(8,128)(2,1)S(1)}, u32[]{:S(2)}, u32[]{:S(2)}) collective-permute-start(bf16[2,4,128,128]{3,2,1,0:T(8,128)(2,1)S(1)} %pad_maximum_fusion), channel_id=1, source_target_pairs={{0,8},{4,12},{8,0},{12,4},{16,24},{20,28},{24,16},{28,20},{1,9},{5... | collective-permute-start | bytes 786440 | tf_op jit(solution)/shard_map/ppermute | solution.py:34
  59.4 32.9 %collective-permute-start.9 = (bf16[4,512,256]{2,1,0:T(8,128)(2,1)}, bf16[4,512,256]{2,1,0:T(8,128)(2,1)}, u32[]{:S(2)}, u32[]{:S(2)}) collective-permute-start(bf16[4,512,256]{2,1,0:T(8,128)(2,1)} %get-tuple-element.95), channel_id=1, source_target_pairs={{0,4},{4,0},{8,12},{12,8},{16,20},{20,16},{24,28},{28,24},{1,5},{5... | collective-permute-start | bytes 3145736 | tf_op jit(solution)/shard_map/ppermute | solution.py:34
  66.1 6.9 %collective-permute-start.7 = (bf16[4,128,128]{2,1,0:T(8,128)(2,1)S(1)}, bf16[4,128,128]{2,1,0:T(8,128)(2,1)S(1)}, u32[]{:S(2)}, u32[]{:S(2)}) collective-permute-start(bf16[4,128,128]{2,1,0:T(8,128)(2,1)S(1)} %fusion.14), channel_id=1, source_target_pairs={{0,16},{4,20},{8,24},{12,28},{16,0},{20,4},{24,8},{28,12},{1,17},{... | collective-permute-start | bytes 393224 | tf_op jit(solution)/shard_map/ppermute | solution.py:34
  79.2 14.7 %collective-permute-start.8 = (bf16[2,512,256]{2,1,0:T(8,128)(2,1)}, bf16[2,512,256]{2,1,0:T(8,128)(2,1)}, u32[]{:S(2)}, u32[]{:S(2)}) collective-permute-start(bf16[2,512,256]{2,1,0:T(8,128)(2,1)} %get-tuple-element.93), channel_id=1, source_target_pairs={{0,8},{4,12},{8,0},{12,4},{16,24},{20,28},{24,16},{28,20},{1,9},{5... | collective-permute-start | bytes 1572872 | tf_op jit(solution)/shard_map/ppermute | solution.py:34
  95.1 4.4 %collective-permute-start.10 = (bf16[2,256,2048]{2,1,0:T(8,128)(2,1)S(1)}, bf16[2,256,2048]{2,1,0:T(8,128)(2,1)S(1)}, u32[]{:S(2)}, u32[]{:S(2)}) collective-permute-start(bf16[2,256,2048]{2,1,0:T(8,128)(2,1)S(1)} %get-tuple-element.100), channel_id=1, source_target_pairs={{0,1},{1,0},{2,3},{3,2},{4,5},{5,4},{6,7},{7,6},{8,9},{9,8},{10,11... | collective-permute-start | bytes 6291464 | tf_op jit(solution)/shard_map/ppermute | solution.py:34
  95.2 26.0 %collective-permute-start.12 = (bf16[4,512,256]{2,1,0:T(8,128)(2,1)S(1)}, bf16[4,512,256]{2,1,0:T(8,128)(2,1)S(1)}, u32[]{:S(2)}, u32[]{:S(2)}) collective-permute-start(bf16[4,512,256]{2,1,0:T(8,128)(2,1)S(1)} %copy-done.30), channel_id=1, source_target_pairs={{0,4},{4,0},{8,12},{12,8},{16,20},{20,16},{24,28},{28,24},{1,5},{5... | collective-permute-start | bytes 3145736 | tf_op jit(solution)/shard_map/ppermute | solution.py:34
  96.3 24.8 %copy-start.22 = (bf16[4,512,256]{2,1,0:T(8,128)(2,1)S(1)}, bf16[4,512,256]{2,1,0:T(8,128)(2,1)}, u32[]{:S(2)}) copy-start(bf16[4,512,256]{2,1,0:T(8,128)(2,1)} %copy-done.21) | copy-start | bytes 3145732
  96.3 15.5 %collective-permute-start.13 = (bf16[1,512,256]{2,1,0:T(8,128)(2,1)S(1)}, bf16[1,512,256]{2,1,0:T(8,128)(2,1)S(1)}, u32[]{:S(2)}, u32[]{:S(2)}) collective-permute-start(bf16[1,512,256]{2,1,0:T(8,128)(2,1)S(1)} %get-tuple-element.106), channel_id=1, source_target_pairs={{0,16},{4,20},{8,24},{12,28},{16,0},{20,4},{24,8},{28,12},{1,17},{... | collective-permute-start | bytes 786440 | tf_op jit(solution)/shard_map/ppermute | solution.py:34
  99.9 32.0 %copy-start.26 = (bf16[2,512,256]{2,1,0:T(8,128)(2,1)S(1)}, bf16[2,512,256]{2,1,0:T(8,128)(2,1)}, u32[]{:S(2)}) copy-start(bf16[2,512,256]{2,1,0:T(8,128)(2,1)} %copy-done.25) | copy-start | bytes 1572868
  99.9 65.0 %collective-permute-start.11 = (bf16[1,256,2048]{2,1,0:T(8,128)(2,1)S(1)}, bf16[1,256,2048]{2,1,0:T(8,128)(2,1)S(1)}, u32[]{:S(2)}, u32[]{:S(2)}) collective-permute-start(bf16[1,256,2048]{2,1,0:T(8,128)(2,1)S(1)} %get-tuple-element.103), channel_id=1, source_target_pairs={{0,2},{1,3},{2,0},{3,1},{4,6},{5,7},{6,4},{7,5},{8,10},{9,11},{10,... | collective-permute-start | bytes 3145736 | tf_op jit(solution)/shard_map/ppermute | solution.py:34
  101.5 22.0 %collective-permute-start.16 = (bf16[2,512,256]{2,1,0:T(8,128)(2,1)S(1)}, bf16[2,512,256]{2,1,0:T(8,128)(2,1)S(1)}, u32[]{:S(2)}, u32[]{:S(2)}) collective-permute-start(bf16[2,512,256]{2,1,0:T(8,128)(2,1)S(1)} %get-tuple-element.112), channel_id=1, source_target_pairs={{0,8},{4,12},{8,0},{12,4},{16,24},{20,28},{24,16},{28,20},{1,9},{5... | collective-permute-start | bytes 1572872 | tf_op jit(solution)/shard_map/ppermute | solution.py:34
  103.3 28.7 %collective-permute-start.15 = (bf16[2,512,256]{2,1,0:T(8,128)(2,1)S(1)}, bf16[2,512,256]{2,1,0:T(8,128)(2,1)S(1)}, u32[]{:S(2)}, u32[]{:S(2)}) collective-permute-start(bf16[2,512,256]{2,1,0:T(8,128)(2,1)S(1)} %copy-done.32), channel_id=1, source_target_pairs={{0,4},{4,0},{8,12},{12,8},{16,20},{20,16},{24,28},{28,24},{1,5},{5... | collective-permute-start | bytes 1572872 | tf_op jit(solution)/shard_map/ppermute | solution.py:34
  121.4 20.4 %collective-permute-start.14 = (bf16[2,512,256]{2,1,0:T(8,128)(2,1)S(1)}, bf16[2,512,256]{2,1,0:T(8,128)(2,1)S(1)}, u32[]{:S(2)}, u32[]{:S(2)}) collective-permute-start(bf16[2,512,256]{2,1,0:T(8,128)(2,1)S(1)} %get-tuple-element.109), channel_id=1, source_target_pairs={{0,8},{4,12},{8,0},{12,4},{16,24},{20,28},{24,16},{28,20},{1,9},{5... | collective-permute-start | bytes 1572872 | tf_op jit(solution)/shard_map/ppermute | solution.py:34
  123.6 18.6 %collective-permute-start.19 = (bf16[1,512,256]{2,1,0:T(8,128)(2,1)S(1)}, bf16[1,512,256]{2,1,0:T(8,128)(2,1)S(1)}, u32[]{:S(2)}, u32[]{:S(2)}) collective-permute-start(bf16[1,512,256]{2,1,0:T(8,128)(2,1)S(1)} %get-tuple-element.122), channel_id=1, source_target_pairs={{0,16},{4,20},{8,24},{12,28},{16,0},{20,4},{24,8},{28,12},{1,17},{... | collective-permute-start | bytes 786440 | tf_op jit(solution)/shard_map/ppermute | solution.py:34
  132.1 26.3 %collective-permute-start.18 = (bf16[1,512,256]{2,1,0:T(8,128)(2,1)S(1)}, bf16[1,512,256]{2,1,0:T(8,128)(2,1)S(1)}, u32[]{:S(2)}, u32[]{:S(2)}) collective-permute-start(bf16[1,512,256]{2,1,0:T(8,128)(2,1)S(1)} %get-tuple-element.121), channel_id=1, source_target_pairs={{0,16},{4,20},{8,24},{12,28},{16,0},{20,4},{24,8},{28,12},{1,17},{... | collective-permute-start | bytes 786440 | tf_op jit(solution)/shard_map/ppermute | solution.py:34
  142.0 21.4 %collective-permute-start.17 = (bf16[1,512,256]{2,1,0:T(8,128)(2,1)S(1)}, bf16[1,512,256]{2,1,0:T(8,128)(2,1)S(1)}, u32[]{:S(2)}, u32[]{:S(2)}) collective-permute-start(bf16[1,512,256]{2,1,0:T(8,128)(2,1)S(1)} %get-tuple-element.120), channel_id=1, source_target_pairs={{0,16},{4,20},{8,24},{12,28},{16,0},{20,4},{24,8},{28,12},{1,17},{... | collective-permute-start | bytes 786440 | tf_op jit(solution)/shard_map/ppermute | solution.py:34
  (31 other events, 109.3 us)

commit v5 on v4

--- a/solution.py
+++ b/solution.py
@@ -102,14 +102,14 @@
             out[index] = product[low:high]
 
 
-def gradient_terms(lefts, right, position, outputs):
+def gradient_terms(lefts, right, info, outputs):
     count = right.shape[0]
     width = right.shape[1] // lax.axis_size("seq")
     if width % 128:
         blocked = right.reshape(count, -1, width)
         results = []
         for left, low, high, slots in outputs:
-            picked = jnp.take(blocked, position ^ jnp.array(slots, jnp.int32), axis=1)
+            picked = jnp.take(blocked, info[0] ^ jnp.array(slots, jnp.int32), axis=1)
             part = jnp.einsum("at,tnb->nab", lefts[left][low:high], picked, preferred_element_type=f32)
             results.append(part.astype(bf16))
         return results
@@ -124,7 +124,7 @@
         compiler_params=params(),
         cost_estimate=COST,
         name="gradient_terms",
-    )(position[None], *lefts, right)
+    )(info, *lefts, right)
 
 
 def sums_kernel(groups, merge, *refs):
@@ -162,10 +162,98 @@
     )(*[array for pair in pairs for array in pair])
 
 
-def middle_kernel(query_ref, grad_ref, mask_ref, gain_ref, state_ref, normed_t_ref, query_grad_ref, query_grad_t_ref, block_grad_ref, sent_ref):
+def flag(info_ref, bit):
+    return ((info_ref[0] >> bit) & 1).astype(f32)
+
+
+def small(kernel, info, arrays, shapes, name):
+    vmem = pl.BlockSpec(memory_space=pltpu.VMEM)
+    return pl.pallas_call(
+        kernel,
+        in_specs=[pl.BlockSpec(memory_space=pltpu.SMEM)] + [vmem] * len(arrays),
+        out_specs=[vmem] * len(shapes),
+        out_shape=[jax.ShapeDtypeStruct(shape, kind) for shape, kind in shapes],
+        compiler_params=params(),
+        cost_estimate=COST,
+        name=name,
+    )(info, *arrays)
+
+
+def prefix_kernel(bit, first, last, info_ref, *refs):
+    if first:
+        own_ref, got_ref, before_ref, total_ref, sent_ref = refs
+        before, total = 0.0, own_ref[...]
+    else:
+        own_ref, old_ref, sum_ref, got_ref, before_ref, total_ref, sent_ref = refs
+        before, total = old_ref[...], sum_ref[...]
+    got = got_ref[...].astype(f32)
+    before = before + got * flag(info_ref, bit)
+    total = total + got
+    before_ref[...] = before
+    total_ref[...] = total
+    sent = before + own_ref[...] * (1.0 - flag(info_ref, 0)) if last else total
+    sent_ref[...] = sent.astype(bf16)
+
+
+def prefix_step(info, bit, first, last, own, before, total, got):
+    arrays = [own, got] if first else [own, before, total, got]
+    shapes = [(own.shape, f32), (own.shape, f32), (own.shape, bf16)]
+    return small(functools.partial(prefix_kernel, bit, first, last), info, arrays, shapes, "prefix_step")
+
+
+def suffix_first_kernel(info_ref, own_ref, got_ref, total_ref, mine_ref, mate_ref, sent_ref):
+    upper = flag(info_ref, 0)
+    own, got = own_ref[...], got_ref[...].astype(f32)
+    total = own + got
+    mine = own + got * (1.0 - upper)
+    total_ref[...] = total
+    mine_ref[...] = mine
+    mate_ref[...] = got + own * upper
+    sent_ref[0] = total.astype(bf16)
+    sent_ref[1] = mine.astype(bf16)
+
+
+def suffix_first(info, own, got):
+    shape = own.shape
+    shapes = [(shape, f32), (shape, f32), (shape, f32), ((2,) + shape, bf16)]
+    return small(suffix_first_kernel, info, [own, got], shapes, "suffix_first")
+
+
+def suffix_kernel(bit, info_ref, *refs):
+    arrays, (total_ref, mine_ref, mate_ref, other_ref, sent_ref) = refs[:-5], refs[-5:]
+    upper = flag(info_ref, bit)
+    total = arrays[0][...]
+    if bit == 1:
+        got = arrays[3][0].astype(f32)
+        other = arrays[3][1].astype(f32) + total * upper
+        later = got * (1.0 - upper)
+    else:
+        got = arrays[4][...].astype(f32)
+        later = got * (1.0 - upper)
+        other = arrays[3][...] + later
+    total_ref[...] = total + got
+    mine_ref[...] = arrays[1][...] + later
+    mate_ref[...] = arrays[2][...] + later
+    other_ref[...] = other
+    sent_ref[...] = (total + got).astype(bf16)
+
+
+def suffix_step(info, bit, arrays):
+    shape = arrays[0].shape
+    shapes = [(shape, f32)] * 4 + [(shape, bf16)]
+    return small(functools.partial(suffix_kernel, bit), info, arrays, shapes, "suffix_step")
+
+
+def middle_kernel(query_ref, grad_ref, mask_ref, gain_ref, own_ref, before_ref, got_ref, normed_t_ref, query_grad_ref, query_grad_t_ref, block_grad_ref, sent_ref, held_ref):
+    mask_row = mask_ref[...].astype(f32)
+
+    @pl.when(pl.program_id(0) == 0)
+    def _():
+        held_ref[...] = jnp.broadcast_to(mask_row, held_ref.shape[::-1]).T
+
     query = query_ref[...]
-    state = state_ref[0]
-    mask = mask_ref[...]
+    state = (before_ref[0] + got_ref[0].astype(f32) + own_ref[0]).astype(bf16)
+    mask = held_ref[...]
     gain = gain_ref[...].astype(f32)
     attended = dot(query, state)
     scale = lax.rsqrt(jnp.mean(attended * attended, -1, keepdims=True) + epsilon)
@@ -182,7 +270,7 @@
     query_grad_t_ref[...] = dot(state, attended_grad_t).astype(bf16)
 
 
-def middle(queries, normed_grad, mask, gain, state):
+def middle(queries, normed_grad, mask, gain, own, before, got):
     count, width = queries.shape
     heads = width // HD
     column = pl.BlockSpec((count, HD), lambda h: (0, h))
@@ -194,8 +282,10 @@
         in_specs=[
             column,
             column,
-            pl.BlockSpec((count, 1), lambda h: (0, 0)),
+            pl.BlockSpec((1, count), lambda h: (0, 0)),
             pl.BlockSpec((1, HD), lambda h: (0, h)),
+            square,
+            square,
             square,
         ],
         out_specs=[row, column, row, square, square],
@@ -206,10 +296,13 @@
             jax.ShapeDtypeStruct((heads, HD, HD), f32),
             jax.ShapeDtypeStruct((heads, HD, HD), bf16),
         ],
-        compiler_params=params(),
-        cost_estimate=COST,
+        scratch_shapes=[pltpu.VMEM((count, HD), f32)],
+        compiler_params=params(),
+        cost_estimate=pl.CostEstimate(
+            flops=32 * count * width * HD, bytes_accessed=1, transcendentals=0
+        ),
         name="norm_backward",
-    )(queries, normed_grad, mask, gain, state)
+    )(queries, normed_grad, mask, gain, own, before, got)
 
 
 def late_kernel(mine_ref, mate_ref, other_ref, *refs):
@@ -224,7 +317,8 @@
             out = keep if slot < half else send
             for h in range(mine_ref.shape[0]):
                 rows = slice(h * HD, (h + 1) * HD)
-                total = times(mine_ref[h], own[slot, rows, :]) + times(state_ref[h], got[slot, rows, :])
+                total = times(mine_ref[h].astype(bf16), own[slot, rows, :])
+                total += times(state_ref[h].astype(bf16), got[slot, rows, :])
                 out[slot % half, rows, :] = total.astype(bf16)
 
 
@@ -244,8 +338,9 @@
 
 
 def key_value_kernel(key_ref, value_ref, grad_ref, key_grad_ref, value_grad_ref):
-    key_grad_ref[...] = dot(value_ref[...], grad_ref[0]).astype(bf16)
-    value_grad_ref[...] = dot_t(key_ref[...], grad_ref[0]).astype(bf16)
+    state_grad = grad_ref[0].astype(bf16)
+    key_grad_ref[...] = dot(value_ref[...], state_grad).astype(bf16)
+    value_grad_ref[...] = dot_t(key_ref[...], state_grad).astype(bf16)
 
 
 def key_value_grads(keys, values, state_grad_t):
@@ -271,11 +366,11 @@
     held_ref[...] = total.astype(bf16).reshape(held_ref.shape)
     half = len(order) // 2
     for index in range(half):
-        keep_ref[index] = held_ref[place_ref[0] ^ order[index]]
-        send_ref[index] = held_ref[place_ref[0] ^ order[half + index]]
-
-
-def input_terms(grads, weight, place, order, chunk, chunks, tile=512):
+        keep_ref[index] = held_ref[place_ref[1] ^ order[index]]
+        send_ref[index] = held_ref[place_ref[1] ^ order[half + index]]
+
+
+def input_terms(grads, weight, info, order, chunk, chunks, tile=512):
     count, width = grads[0].shape
     half = len(order) // 2
     rows = count // len(order)
@@ -294,10 +389,10 @@
             scratch_shapes=[pltpu.VMEM((len(order), rows, tile), bf16)],
         ),
         out_shape=[shape, shape],
-        compiler_params=params(32),
+        compiler_params=params(20),
         cost_estimate=COST,
         name="input_terms",
-    )(place[None], *grads, weight)
+    )(info, *grads, weight)
 
 
 def finish_kernel(*refs):
@@ -323,23 +418,26 @@
 
 
 def per_device(layer_input, output_grad, loss_mask, proj_weight, out_weight, norm_gain):
-    position = lax.axis_index("seq")
-    place = lax.axis_index("head")
+    count = layer_input.shape[0]
     seq_bits = lax.axis_size("seq").bit_length() - 1
     head_bits = lax.axis_size("head").bit_length() - 1
     stages = list(range(seq_bits))
-    bits = [(position >> bit) & 1 == 1 for bit in stages]
     order, swapped = slot_order(stages), slot_order([1, 0] + stages[2:])
     half = len(order) // 2
     head_order = slot_order(list(range(head_bits)))
+    info = jnp.stack([lax.axis_index("seq"), lax.axis_index("head")]).astype(jnp.int32)
+    layer_input, output_grad, loss_mask, proj_weight, norm_gain = after(
+        (layer_input, output_grad, loss_mask, proj_weight, norm_gain), info
+    )
     weights = jnp.transpose(proj_weight, (1, 0, 2))
+    mask = loss_mask.reshape(1, count)
 
     def project(rows, index):
         return jnp.dot(rows, weights[index], preferred_element_type=f32).astype(bf16)
 
     def terms(left, right, *parts):
         outputs = [(0, 0, left.shape[0], slots) for slots in parts]
-        return gradient_terms([left], right, position, outputs)
+        return gradient_terms([left], right, info, outputs)
 
     values = project(layer_input, 2)
     values_t = flipped(values)
@@ -347,9 +445,8 @@
     value_got = exchange(value_send, "seq", 0)
     keys = project(after(layer_input, value_send), 1)
     own_state, sent, keys_t = block_states(keys, values)
-    mask = loss_mask.astype(f32)[:, None]
-
-    before, total = jnp.zeros_like(own_state), own_state
+
+    before, total = None, own_state
     for bit in stages[1:]:
         got = exchange(sent, "seq", bit)
         if bit == 1:
@@ -357,57 +454,47 @@
             got = after(got, queries)
         elif bit == 2:
             (key_send,) = terms(keys_t, after(layer_input, total), swapped[half:])
-            normed_grad = dot_t(after(output_grad, key_send), out_weight)
             key_got = exchange(key_send, "seq", 1)
-            got = after(got, normed_grad)
-        before = before + jnp.where(bits[bit], got.astype(f32), 0.0)
-        total = total + got.astype(f32)
-        sent = total.astype(bf16)
-    sent = (before + jnp.where(bits[0], 0.0, own_state)).astype(bf16)
+            got = after(got, key_send)
+        before, total, sent = prefix_step(info, bit, bit == 1, bit == stages[-1], own_state, before, total, got)
     got = exchange(after(sent, value_got), "seq", 0)
-    state = (before + got.astype(f32) + own_state).astype(bf16)
+    normed_grad = dot_t(after(output_grad, sent), out_weight)
+    got = after(got, normed_grad)
 
     normed_t, query_grad, query_grad_t, own_grad, sent = middle(
-        queries, normed_grad, mask, norm_gain[None, :], state
+        queries, normed_grad, mask, norm_gain[None, :], own_state, before, got
     )
 
     got = exchange(sent, "seq", 0)
     out_keep, out_send = terms(normed_t, after(output_grad, own_grad), order[:half], order[half:])
-    got = after(got, out_keep, key_got).astype(f32)
-    total = own_grad + got
-    mine, mate = jnp.where(bits[0], own_grad, total), jnp.where(bits[0], total, got)
+    got = after(got, out_keep, key_got)
+    total, mine, mate, sent = suffix_first(info, own_grad, got)
     out_got = exchange(after(out_send, total), "seq", 0)
 
-    got = exchange(jnp.stack([total, mine]).astype(bf16), "seq", 1)
+    got = exchange(sent, "seq", 1)
     query_keep, query_send = terms(query_grad_t, after(layer_input, total), order[:half], order[half:])
-    got = after(got, query_keep).astype(f32)
-    later = jnp.where(bits[1], 0.0, got[0])
-    mine, mate = mine + later, mate + later
-    other = got[1] + jnp.where(bits[1], total, 0.0)
-    total = total + got[0]
-    query_got = exchange(after(query_send, total), "seq", 0)
+    got = after(got, query_keep)
+    suffix = suffix_step(info, 1, [total, mine, mate, got])
+    query_got = exchange(after(query_send, suffix[0]), "seq", 0)
 
     for bit in stages[2:]:
-        got = exchange(total.astype(bf16), "seq", bit)
+        got = exchange(suffix[4], "seq", bit)
         if bit == 2:
-            (value_keep,) = terms(values_t, after(layer_input, total), order[:half])
+            (value_keep,) = terms(values_t, after(layer_input, suffix[0]), order[:half])
             (key_keep,) = terms(keys_t, after(layer_input, value_keep), swapped[:half])
             got = after(got, key_keep)
-        got = got.astype(f32)
-        later = jnp.where(bits[bit], 0.0, got)
-        mine, mate, other = mine + later, mate + later, other + later
-        total = total + got
-    state_grad = mine.astype(bf16)
+        suffix = suffix_step(info, bit, list(suffix[:4]) + [got])
+    total, mine, mate, other, sent = suffix
 
     value_keep, value_send, key_keep, key_send = late_terms(
-        state_grad, mate.astype(bf16), other.astype(bf16), value_keep, value_got, key_keep, key_got
+        mine, mate, other, value_keep, value_got, key_keep, key_got
     )
     value_got = exchange(value_send, "seq", 1)
     key_got = exchange(key_send, "seq", 0)
 
-    key_grad, value_grad = key_value_grads(keys, values, after(state_grad, value_keep))
+    key_grad, value_grad = key_value_grads(keys, values, after(mine, value_keep))
     grads = (query_grad, key_grad, value_grad)
-    input_keep, input_send = input_terms(grads, weights, place, head_order, 0, 1)
+    first_keep, first_send = input_terms(grads, weights, info, head_order, 0, 2)
 
     def stage(keep, got, token, bit, axis="seq"):
         keep, send = sums([(keep, after(got, token))])
@@ -418,22 +505,30 @@
             keep, got = stage(keep, got, keep, bit)
         return keep[0], got[0]
 
-    out_keep, out_got = stage(out_keep, out_got, input_keep, 1)
-    value_keep, value_got = stage(value_keep, value_got, out_keep, 2)
-    input_got = exchange(after(input_send, value_keep), "head", 0)
+    out_keep, out_got = stage(out_keep, out_got, first_keep, 1)
+    second_keep, second_send = input_terms(grads, after(weights, out_keep), info, head_order, 1, 2)
+    value_keep, value_got = stage(value_keep, value_got, second_keep, 2)
+    first_got = exchange(after(first_send, value_keep), "head", 0)
+    second_got = exchange(after(second_send, value_keep), "head", 0)
     for bit in range(1, head_bits):
-        input_keep, input_got = stage(input_keep, input_got, value_keep, bit, "head")
-    query_keep, query_got = stage(query_keep, query_got, (input_keep, value_got), 1)
-    out_keep, out_got = stage(out_keep, out_got, query_keep, 2)
-    key_keep, key_got = stage(key_keep, key_got, out_keep, 2)
+        first_keep, first_got = stage(first_keep, first_got, out_got, bit, "head")
+        second_keep, second_got = stage(second_keep, second_got, first_keep, bit, "head")
+    out_keep, out_got = stage(out_keep, out_got, second_keep, 2)
+    query_keep, query_got = stage(query_keep, query_got, (out_keep, value_got), 1)
+    key_keep, key_got = stage(key_keep, key_got, (query_keep, out_got, first_got, second_got), 2)
     query_keep, query_got = stage(query_keep, query_got, key_keep, 2)
 
     out_pair = rest(out_keep, out_got, stages[3:])
     value_pair = rest(value_keep, value_got, stages[3:])
     key_pair = rest(key_keep, key_got, stages[3:])
     query_pair = rest(query_keep, query_got, stages[3:])
-    input_got = after(input_got, query_keep)
-    input_grad = (input_keep[0].astype(f32) + input_got[0].astype(f32)).astype(bf16)
+    input_grad = jnp.concatenate(
+        [
+            (keep[0].astype(f32) + got[0].astype(f32)).astype(bf16)
+            for keep, got in ((first_keep, first_got), (second_keep, second_got))
+        ],
+        1,
+    )
     out_weight_grad = out_pair[0].astype(f32) + out_pair[1].astype(f32)
     proj_weight_grad = finish(query_pair + value_pair + key_pair)
     return (input_grad, jnp.transpose(proj_weight_grad, (1, 0, 2)), out_weight_grad)

time: 167 us -> 154 us (0.922)
  local copies, waits for them, and re-layouts: 15.8 us -> 0.05 us
  starting transfers between devices: 27.3 us -> 33.6 us
  other arithmetic: 5.59 us -> 2.37 us
  matrix products: 14.7 us -> 12.4 us
    unnamed x70 -> x14, local copies, waits for them, and re-layouts: 14.8 us -> 0.04 us
    ppermute x20 -> x22, starting transfers between devices: 27.3 us -> 33.6 us  [exchange(): return lax.ppermute(arr, axis, [(i, i ^ 1 << bit) for i in range(count)])]
    pallas_call x0 -> x5, Pallas kernels: none -> 4.54 us  [small(): pl.pallas_call(kernel, in_specs=[pl.BlockSpec(memory_space=pltpu.SMEM)] +...]
    convert_element_type x6 -> x2, other arithmetic: 3.68 us -> 0.38 us  [per_device(): (keep[0].astype(f32) + got[0].astype(f32)).astype(bf16)]
    pallas_call x7 -> x8, Pallas kernels: 3.82 us -> 1.47 us  [sums(): pl.pallas_call(functools.partial(sums_kernel, len(pairs), merge), in_spec...]
    pallas_call x1, Pallas kernels: 3.57 us -> 1.32 us  [late_terms(): pl.pallas_call(late_kernel, in_specs=[vmem] * 7, out_specs=[vmem] * 4, ou...]
    pallas_call x1 -> x2, Pallas kernels: 8.35 us -> 9.71 us  [input_terms(): pl.pallas_call(functools.partial(input_kernel, order), grid_spec=pltpu.Pr...]
    ppermute x20 -> x22, waiting for transfers between devices: 62.5 us -> 63.6 us  [exchange(): return lax.ppermute(arr, axis, [(i, i ^ 1 << bit) for i in range(count)])]
  transfers between devices with their start and end apart: 20 -> 22, of which waited for: 11 -> 13; matrix products, arithmetic and copies ran while one was open for 9% -> 6% of each run, Pallas kernels for 21% -> 23%
where the time goes in v5:
time: 154 us; the launch traced here: 153 us
  waiting for transfers between devices  63.6 us (41%)
  Pallas kernels  40.5 us (26%)
  starting transfers between devices  33.6 us (22%)
  matrix products  12.4 us (8%)
  other arithmetic  2.37 us (2%)
    ppermute x22, waiting for transfers between devices, exchange(): return lax.ppermute(arr, axis, [(i, i ^ 1 << bit) for i in range(count)])  63.6 us
    ppermute x22, starting transfers between devices, exchange(): return lax.ppermute(arr, axis, [(i, i ^ 1 << bit) for i in range(count)])  33.6 us
    pallas_call x6, Pallas kernels, gradient_terms(): pl.pallas_call(functools.partial(terms_kernel, len(lefts), outputs), in_s...  13.1 us
    dot_general x3, matrix products, project(): jnp.dot(rows, weights[index], preferred_element_type=f32).astype(bf16)  9.96 us
    pallas_call x2, Pallas kernels, input_terms(): pl.pallas_call(functools.partial(input_kernel, order), grid_spec=pltpu.Pr...  9.71 us
    pallas_call x1, Pallas kernels, middle(): pl.pallas_call(middle_kernel, grid=(heads,), in_specs=[column, column, pl...  4.57 us
    pallas_call x5, Pallas kernels, small(): pl.pallas_call(kernel, in_specs=[pl.BlockSpec(memory_space=pltpu.SMEM)] +...  4.54 us
  transfers between devices with their start and end apart: 22, of which 13 were waited for; matrix products, arithmetic and copies ran while one was open for 6% of the time, Pallas kernels for 23%

profile of v5, /device:TPU:0, one launch (start us, length us, event | category | flops | bytes accessed | tf_op | source)
XLA Modules:
  0.0 153.4 jit_solution(5379378254740574382)
XLA Ops:
  0.7 5.3 %fusion.3.value_ref = bf16[1024,512]{1,0:T(8,128)(2,1)S(1)} fusion(bf16[1024,2048]{1,0:T(8,128)(2,1)} %refs_1_.5, bf16[3,2048,512]{2,1,0:T(8,128)(2,1)} %bitcast.37), kind=kOutput, calls=%fused_computation.6 | convolution fusion | flops 2148007936 | bytes 7340032 | tf_op jit(solution)/shard_map/dot_general | solution.py:436
  6.8 1.8 %gradient_terms.6 = bf16[4,512,256]{2,1,0:T(8,128)(2,1)S(1)} custom-call(s32[2]{0:T(128)S(1)} %pad_add_fusion.position_ref.info_ref.place_ref, bf16[512,1024]{1,0:T(8,128)(2,1)S(1)} %flipped.1.refs_0_, bf16[1024,2048]{1,0:T(8,128)(2,1)S(1)} %copy-done.2), custom_call_target="tpu_custom_call" | custom-call | flops 1000000 | bytes 1 | tf_op jit(solution)/shard_map/gradient_terms/pallas_call | solution.py:119
  8.6 3.0 %collective-permute-start.2 = (bf16[4,512,256]{2,1,0:T(8,128)(2,1)S(1)}, bf16[4,512,256]{2,1,0:T(8,128)(2,1)S(1)}, u32[]{:S(2)}, u32[]{:S(2)}) collective-permute-start(bf16[4,512,256]{2,1,0:T(8,128)(2,1)S(1)} %gradient_terms.6), channel_id=1, source_target_pairs={{0,4},{4,0},{8,12},{12,8},{16,20},{20,16},{24,28},{28,24},{1,5},{5... | collective-permute-start | bytes 3145736 | tf_op jit(solution)/shard_map/ppermute | solution.py:34
  11.7 2.3 %fusion.4.key_ref = bf16[1024,512]{1,0:T(8,128)(2,1)S(1)} fusion(bf16[1024,2048]{1,0:T(8,128)(2,1)S(1)} %copy-done.2, bf16[3,2048,512]{2,1,0:T(8,128)(2,1)S(1)} %bitcast.38), kind=kOutput, calls=%fused_computation.7 | convolution fusion | flops 2148007936 | bytes 7340032 | tf_op jit(solution)/shard_map/dot_general | solution.py:436
  17.2 2.3 %fusion.5.query_ref = bf16[1024,512]{1,0:T(8,128)(2,1)S(1)} fusion(bf16[1024,2048]{1,0:T(8,128)(2,1)S(1)} %copy-done.2, bf16[3,2048,512]{2,1,0:T(8,128)(2,1)S(1)} %bitcast.39), kind=kOutput, calls=%fused_computation.8 | convolution fusion | flops 2148007936 | bytes 7340032 | tf_op jit(solution)/shard_map/dot_general | solution.py:436
  21.2 2.7 %collective-permute-start.1 = (bf16[4,128,128]{2,1,0:T(8,128)(2,1)S(1)}, bf16[4,128,128]{2,1,0:T(8,128)(2,1)S(1)}, u32[]{:S(2)}, u32[]{:S(2)}) collective-permute-start(bf16[4,128,128]{2,1,0:T(8,128)(2,1)S(1)} %get-tuple-element.102), channel_id=1, source_target_pairs={{0,16},{4,20},{8,24},{12,28},{16,0},{20,4},{24,8},{28,12},{1,17},{... | collective-permute-start | bytes 393224 | tf_op jit(solution)/shard_map/ppermute | solution.py:34
  23.8 1.8 %gradient_terms.7 = bf16[4,512,256]{2,1,0:T(8,128)(2,1)S(1)} custom-call(s32[2]{0:T(128)S(1)} %pad_add_fusion.position_ref.info_ref.place_ref, bf16[512,1024]{1,0:T(8,128)(2,1)S(1)} %get-tuple-element.103.refs_0_, bf16[1024,2048]{1,0:T(8,128)(2,1)S(1)} %copy-done.2), custom_call_target="tpu_custom_call" | custom-call | flops 1000000 | bytes 1 | tf_op jit(solution)/shard_map/gradient_terms/pallas_call | solution.py:119
  29.9 5.0 %collective-permute-done.2.refs_1_ = bf16[4,512,256]{2,1,0:T(8,128)(2,1)S(1)} collective-permute-done((bf16[4,512,256]{2,1,0:T(8,128)(2,1)S(1)}, bf16[4,512,256]{2,1,0:T(8,128)(2,1)S(1)}, u32[]{:S(2)}, u32[]{:S(2)}) %collective-permute-start.2) | collective-permute-done | bytes 1048608 | tf_op jit(solution)/shard_map/ppermute | solution.py:34
  36.6 2.4 %fusion.8.grad_ref = f32[1024,512]{1,0:T(8,128)S(1)} fusion(bf16[1024,2048]{1,0:T(8,128)(2,1)S(1)} %copy-done.4, bf16[512,2048]{1,0:T(8,128)(2,1)S(1)} %copy-done), kind=kOutput, calls=%fused_computation.16 | convolution fusion | flops 2147483648 | bytes 8388608 | tf_op jit(solution)/shard_map/dot_general | solution.py:29
  39.8 4.6 %norm_backward.1 = (bf16[512,1024]{1,0:T(8,128)(2,1)S(1)}, bf16[1024,512]{1,0:T(8,128)(2,1)S(1)}, bf16[512,1024]{1,0:T(8,128)(2,1)S(1)}, f32[4,128,128]{2,1,0:T(8,128)S(1)}, bf16[4,128,128]{2,1,0:T(8,128)(2,1)S(1)}) custom-call(bf16[1024,512]{1,0:T(8,128)(2,1)S(1)} %fusion.5.query_ref, f32[1024,512]{1,0:T(8,128)S(1)} %fusion.8.grad_ref, ...), custom_call_target="tpu_custom_call" | custom-call | flops 2147483648 | bytes 1 | tf_op jit(solution)/shard_map/norm_backward/pallas_call | solution.py:279
  46.2 2.9 %gradient_terms.8 = (bf16[4,512,256]{2,1,0:T(8,128)(2,1)S(1)}, bf16[4,512,256]{2,1,0:T(8,128)(2,1)S(1)}) custom-call(s32[2]{0:T(128)S(1)} %pad_add_fusion.position_ref.info_ref.place_ref, bf16[512,1024]{1,0:T(8,128)(2,1)S(1)} %get-tuple-element.116.refs_0_, bf16[1024,2048]{1,0:T(8,128)(2,1)S(1)} %copy-done.4), custom_call_target="tpu_custom_call" | custom-call | flops 1000000 | bytes 1 | tf_op jit(solution)/shard_map/gradient_terms/pallas_call | solution.py:119
  53.5 2.9 %gradient_terms.9 = (bf16[4,512,256]{2,1,0:T(8,128)(2,1)S(1)}, bf16[4,512,256]{2,1,0:T(8,128)(2,1)S(1)}) custom-call(s32[2]{0:T(128)S(1)} %pad_add_fusion.position_ref.info_ref.place_ref, bf16[512,1024]{1,0:T(8,128)(2,1)S(1)} %get-tuple-element.124.refs_0_, bf16[1024,2048]{1,0:T(8,128)(2,1)S(1)} %copy-done.2), custom_call_target="tpu_custom_call" | custom-call | flops 1000000 | bytes 1 | tf_op jit(solution)/shard_map/gradient_terms/pallas_call | solution.py:119
  56.4 1.9 %collective-permute-done.6.refs_3_ = bf16[2,4,128,128]{3,2,1,0:T(8,128)(2,1)S(1)} collective-permute-done((bf16[2,4,128,128]{3,2,1,0:T(8,128)(2,1)S(1)}, bf16[2,4,128,128]{3,2,1,0:T(8,128)(2,1)S(1)}, u32[]{:S(2)}, u32[]{:S(2)}) %collective-permute-start.6) | collective-permute-done | bytes 262176 | tf_op jit(solution)/shard_map/ppermute | solution.py:34
  58.9 3.0 %collective-permute-start.7 = (bf16[4,128,128]{2,1,0:T(8,128)(2,1)S(1)}, bf16[4,128,128]{2,1,0:T(8,128)(2,1)S(1)}, u32[]{:S(2)}, u32[]{:S(2)}) collective-permute-start(bf16[4,128,128]{2,1,0:T(8,128)(2,1)S(1)} %get-tuple-element.132), channel_id=1, source_target_pairs={{0,16},{4,20},{8,24},{12,28},{16,0},{20,4},{24,8},{28,12},{1,17},{... | collective-permute-start | bytes 393224 | tf_op jit(solution)/shard_map/ppermute | solution.py:34
  69.8 1.9 %key_value_grads.1 = (bf16[1024,512]{1,0:T(8,128)(2,1)S(1)}, bf16[1024,512]{1,0:T(8,128)(2,1)S(1)}) custom-call(bf16[1024,512]{1,0:T(8,128)(2,1)S(1)} %fusion.4.key_ref, bf16[1024,512]{1,0:T(8,128)(2,1)S(1)} %fusion.3.value_ref, f32[4,128,128]{2,1,0:T(8,128)S(1)} %get-tuple-element.140.mine_ref.grad_ref), custom_call_target="tpu_custom_call" | custom-call | flops 1000000 | bytes 1 | tf_op jit(solution)/shard_map/key_value_grads/pallas_call | solution.py:350
  71.7 4.7 %input_terms.2 = (bf16[2,256,1024]{2,1,0:T(8,128)(2,1)S(1)}, bf16[2,256,1024]{2,1,0:T(8,128)(2,1)S(1)}) custom-call(s32[2]{0:T(128)S(1)} %pad_add_fusion.position_ref.info_ref.place_ref, bf16[1024,512]{1,0:T(8,128)(2,1)S(1)} %get-tuple-element.113.query_ref, bf16[1024,512]{1,0:T(8,128)(2,1)S(1)} %get-tuple-element.141.key_ref, ...), custom_call_target="tpu_custom_call" | custom-call | flops 1000000 | bytes 1 | tf_op jit(solution)/shard_map/input_terms/pallas_call | solution.py:382
  76.7 5.0 %input_terms.3 = (bf16[2,256,1024]{2,1,0:T(8,128)(2,1)S(1)}, bf16[2,256,1024]{2,1,0:T(8,128)(2,1)S(1)}) custom-call(s32[2]{0:T(128)S(1)} %pad_add_fusion.position_ref.info_ref.place_ref, bf16[1024,512]{1,0:T(8,128)(2,1)S(1)} %get-tuple-element.113.query_ref, bf16[1024,512]{1,0:T(8,128)(2,1)S(1)} %get-tuple-element.141.key_ref, ...), custom_call_target="tpu_custom_call" | custom-call | flops 1000000 | bytes 1 | tf_op jit(solution)/shard_map/input_terms/pallas_call | solution.py:382
  86.2 15.9 %collective-permute-done.11.refs_1_ = bf16[2,512,256]{2,1,0:T(8,128)(2,1)S(1)} collective-permute-done((bf16[2,512,256]{2,1,0:T(8,128)(2,1)S(1)}, bf16[2,512,256]{2,1,0:T(8,128)(2,1)S(1)}, u32[]{:S(2)}, u32[]{:S(2)}) %collective-permute-start.11) | collective-permute-done | bytes 524320 | tf_op jit(solution)/shard_map/ppermute | solution.py:34
  106.4 2.0 %collective-permute-done.15.refs_1_ = bf16[4,512,256]{2,1,0:T(8,128)(2,1)S(1)} collective-permute-done((bf16[4,512,256]{2,1,0:T(8,128)(2,1)S(1)}, bf16[4,512,256]{2,1,0:T(8,128)(2,1)S(1)}, u32[]{:S(2)}, u32[]{:S(2)}) %collective-permute-start.15) | collective-permute-done | bytes 1048608 | tf_op jit(solution)/shard_map/ppermute | solution.py:34
  109.9 2.2 %collective-permute-start.19 = (bf16[1,512,256]{2,1,0:T(8,128)(2,1)S(1)}, bf16[1,512,256]{2,1,0:T(8,128)(2,1)S(1)}, u32[]{:S(2)}, u32[]{:S(2)}) collective-permute-start(bf16[1,512,256]{2,1,0:T(8,128)(2,1)S(1)} %get-tuple-element.174), channel_id=1, source_target_pairs={{0,16},{4,20},{8,24},{12,28},{16,0},{20,4},{24,8},{28,12},{1,17},{... | collective-permute-start | bytes 786440 | tf_op jit(solution)/shard_map/ppermute | solution.py:34
  112.1 13.1 %collective-permute-done.19 = bf16[1,512,256]{2,1,0:T(8,128)(2,1)S(1)} collective-permute-done((bf16[1,512,256]{2,1,0:T(8,128)(2,1)S(1)}, bf16[1,512,256]{2,1,0:T(8,128)(2,1)S(1)}, u32[]{:S(2)}, u32[]{:S(2)}) %collective-permute-start.19) | collective-permute-done | bytes 262176 | tf_op jit(solution)/shard_map/ppermute | solution.py:34
  127.9 1.9 %collective-permute-start.20 = (bf16[1,512,256]{2,1,0:T(8,128)(2,1)S(1)}, bf16[1,512,256]{2,1,0:T(8,128)(2,1)S(1)}, u32[]{:S(2)}, u32[]{:S(2)}) collective-permute-start(bf16[1,512,256]{2,1,0:T(8,128)(2,1)S(1)} %get-tuple-element.179), channel_id=1, source_target_pairs={{0,16},{4,20},{8,24},{12,28},{16,0},{20,4},{24,8},{28,12},{1,17},{... | collective-permute-start | bytes 786440 | tf_op jit(solution)/shard_map/ppermute | solution.py:34
  132.4 16.1 %collective-permute-done.20 = bf16[1,512,256]{2,1,0:T(8,128)(2,1)S(1)} collective-permute-done((bf16[1,512,256]{2,1,0:T(8,128)(2,1)S(1)}, bf16[1,512,256]{2,1,0:T(8,128)(2,1)S(1)}, u32[]{:S(2)}, u32[]{:S(2)}) %collective-permute-start.20) | collective-permute-done | bytes 262176 | tf_op jit(solution)/shard_map/ppermute | solution.py:34
  148.5 3.3 %collective-permute-done.21 = bf16[1,512,256]{2,1,0:T(8,128)(2,1)S(1)} collective-permute-done((bf16[1,512,256]{2,1,0:T(8,128)(2,1)S(1)}, bf16[1,512,256]{2,1,0:T(8,128)(2,1)S(1)}, u32[]{:S(2)}, u32[]{:S(2)}) %collective-permute-start.21) | collective-permute-done | bytes 262176 | tf_op jit(solution)/shard_map/ppermute | solution.py:34
  (71 shorter events, 44.4 us)
Async XLA Ops:
  0.6 35.9 %copy-start = (bf16[512,2048]{1,0:T(8,128)(2,1)S(1)}, bf16[512,2048]{1,0:T(8,128)(2,1)}, u32[]{:S(2)}) copy-start(bf16[512,2048]{1,0:T(8,128)(2,1)} %param.10) | copy-start | bytes 6291460
  8.6 26.2 %collective-permute-start.2 = (bf16[4,512,256]{2,1,0:T(8,128)(2,1)S(1)}, bf16[4,512,256]{2,1,0:T(8,128)(2,1)S(1)}, u32[]{:S(2)}, u32[]{:S(2)}) collective-permute-start(bf16[4,512,256]{2,1,0:T(8,128)(2,1)S(1)} %gradient_terms.6), channel_id=1, source_target_pairs={{0,4},{4,0},{8,12},{12,8},{16,20},{20,16},{24,28},{28,24},{1,5},{5... | collective-permute-start | bytes 3145736 | tf_op jit(solution)/shard_map/ppermute | solution.py:34
  15.5 5.0 %collective-permute-start = (bf16[4,128,128]{2,1,0:T(8,128)(2,1)S(1)}, bf16[4,128,128]{2,1,0:T(8,128)(2,1)S(1)}, u32[]{:S(2)}, u32[]{:S(2)}) collective-permute-start(bf16[4,128,128]{2,1,0:T(8,128)(2,1)S(1)} %get-tuple-element.98), channel_id=1, source_target_pairs={{0,8},{4,12},{8,0},{12,4},{16,24},{20,28},{24,16},{28,20},{1,9},{5... | collective-permute-start | bytes 393224 | tf_op jit(solution)/shard_map/ppermute | solution.py:34
  21.2 7.4 %collective-permute-start.1 = (bf16[4,128,128]{2,1,0:T(8,128)(2,1)S(1)}, bf16[4,128,128]{2,1,0:T(8,128)(2,1)S(1)}, u32[]{:S(2)}, u32[]{:S(2)}) collective-permute-start(bf16[4,128,128]{2,1,0:T(8,128)(2,1)S(1)} %get-tuple-element.102), channel_id=1, source_target_pairs={{0,16},{4,20},{8,24},{12,28},{16,0},{20,4},{24,8},{28,12},{1,17},{... | collective-permute-start | bytes 393224 | tf_op jit(solution)/shard_map/ppermute | solution.py:34
  25.6 24.5 %collective-permute-start.5 = (bf16[4,512,256]{2,1,0:T(8,128)(2,1)S(1)}, bf16[4,512,256]{2,1,0:T(8,128)(2,1)S(1)}, u32[]{:S(2)}, u32[]{:S(2)}) collective-permute-start(bf16[4,512,256]{2,1,0:T(8,128)(2,1)S(1)} %gradient_terms.7), channel_id=1, source_target_pairs={{0,8},{4,12},{8,0},{12,4},{16,24},{20,28},{24,16},{28,20},{1,9},{5... | collective-permute-start | bytes 3145736 | tf_op jit(solution)/shard_map/ppermute | solution.py:34
  34.8 5.0 %collective-permute-start.3 = (bf16[4,128,128]{2,1,0:T(8,128)(2,1)S(1)}, bf16[4,128,128]{2,1,0:T(8,128)(2,1)S(1)}, u32[]{:S(2)}, u32[]{:S(2)}) collective-permute-start(bf16[4,128,128]{2,1,0:T(8,128)(2,1)S(1)} %get-tuple-element.111), channel_id=1, source_target_pairs={{0,4},{4,0},{8,12},{12,8},{16,20},{20,16},{24,28},{28,24},{1,5},{5... | collective-permute-start | bytes 393224 | tf_op jit(solution)/shard_map/ppermute | solution.py:34
  44.4 5.7 %collective-permute-start.4 = (bf16[4,128,128]{2,1,0:T(8,128)(2,1)S(1)}, bf16[4,128,128]{2,1,0:T(8,128)(2,1)S(1)}, u32[]{:S(2)}, u32[]{:S(2)}) collective-permute-start(bf16[4,128,128]{2,1,0:T(8,128)(2,1)S(1)} %get-tuple-element.115), channel_id=1, source_target_pairs={{0,4},{4,0},{8,12},{12,8},{16,20},{20,16},{24,28},{28,24},{1,5},{5... | collective-permute-start | bytes 393224 | tf_op jit(solution)/shard_map/ppermute | solution.py:34
  50.8 25.6 %collective-permute-start.9 = (bf16[4,512,256]{2,1,0:T(8,128)(2,1)S(1)}, bf16[4,512,256]{2,1,0:T(8,128)(2,1)S(1)}, u32[]{:S(2)}, u32[]{:S(2)}) collective-permute-start(bf16[4,512,256]{2,1,0:T(8,128)(2,1)S(1)} %get-tuple-element.147), channel_id=1, source_target_pairs={{0,4},{4,0},{8,12},{12,8},{16,20},{20,16},{24,28},{28,24},{1,5},{5... | collective-permute-start | bytes 3145736 | tf_op jit(solution)/shard_map/ppermute | solution.py:34
  51.9 6.4 %collective-permute-start.6 = (bf16[2,4,128,128]{3,2,1,0:T(8,128)(2,1)S(1)}, bf16[2,4,128,128]{3,2,1,0:T(8,128)(2,1)S(1)}, u32[]{:S(2)}, u32[]{:S(2)}) collective-permute-start(bf16[2,4,128,128]{3,2,1,0:T(8,128)(2,1)S(1)} %get-tuple-element.123), channel_id=1, source_target_pairs={{0,8},{4,12},{8,0},{12,4},{16,24},{20,28},{24,16},{28,20},{1,9},{5... | collective-permute-start | bytes 786440 | tf_op jit(solution)/shard_map/ppermute | solution.py:34
  58.9 7.4 %collective-permute-start.7 = (bf16[4,128,128]{2,1,0:T(8,128)(2,1)S(1)}, bf16[4,128,128]{2,1,0:T(8,128)(2,1)S(1)}, u32[]{:S(2)}, u32[]{:S(2)}) collective-permute-start(bf16[4,128,128]{2,1,0:T(8,128)(2,1)S(1)} %get-tuple-element.132), channel_id=1, source_target_pairs={{0,16},{4,20},{8,24},{12,28},{16,0},{20,4},{24,8},{28,12},{1,17},{... | collective-permute-start | bytes 393224 | tf_op jit(solution)/shard_map/ppermute | solution.py:34
  68.9 12.7 %collective-permute-start.8 = (bf16[2,512,256]{2,1,0:T(8,128)(2,1)S(1)}, bf16[2,512,256]{2,1,0:T(8,128)(2,1)S(1)}, u32[]{:S(2)}, u32[]{:S(2)}) collective-permute-start(bf16[2,512,256]{2,1,0:T(8,128)(2,1)S(1)} %get-tuple-element.145), channel_id=1, source_target_pairs={{0,8},{4,12},{8,0},{12,4},{16,24},{20,28},{24,16},{28,20},{1,9},{5... | collective-permute-start | bytes 1572872 | tf_op jit(solution)/shard_map/ppermute | solution.py:34
  81.8 21.9 %collective-permute-start.10 = (bf16[2,256,1024]{2,1,0:T(8,128)(2,1)S(1)}, bf16[2,256,1024]{2,1,0:T(8,128)(2,1)S(1)}, u32[]{:S(2)}, u32[]{:S(2)}) collective-permute-start(bf16[2,256,1024]{2,1,0:T(8,128)(2,1)S(1)} %get-tuple-element.154), channel_id=1, source_target_pairs={{0,1},{1,0},{2,3},{3,2},{4,5},{5,4},{6,7},{7,6},{8,9},{9,8},{10,11... | collective-permute-start | bytes 3145736 | tf_op jit(solution)/shard_map/ppermute | solution.py:34
  81.9 23.6 %collective-permute-start.13 = (bf16[2,256,1024]{2,1,0:T(8,128)(2,1)S(1)}, bf16[2,256,1024]{2,1,0:T(8,128)(2,1)S(1)}, u32[]{:S(2)}, u32[]{:S(2)}) collective-permute-start(bf16[2,256,1024]{2,1,0:T(8,128)(2,1)S(1)} %get-tuple-element.160), channel_id=1, source_target_pairs={{0,1},{1,0},{2,3},{3,2},{4,5},{5,4},{6,7},{7,6},{8,9},{9,8},{10,11... | collective-permute-start | bytes 3145736 | tf_op jit(solution)/shard_map/ppermute | solution.py:34
  82.4 26.0 %collective-permute-start.15 = (bf16[4,512,256]{2,1,0:T(8,128)(2,1)S(1)}, bf16[4,512,256]{2,1,0:T(8,128)(2,1)S(1)}, u32[]{:S(2)}, u32[]{:S(2)}) collective-permute-start(bf16[4,512,256]{2,1,0:T(8,128)(2,1)S(1)} %get-tuple-element.165), channel_id=1, source_target_pairs={{0,4},{4,0},{8,12},{12,8},{16,20},{20,16},{24,28},{28,24},{1,5},{5... | collective-permute-start | bytes 3145736 | tf_op jit(solution)/shard_map/ppermute | solution.py:34
  82.8 19.3 %collective-permute-start.11 = (bf16[2,512,256]{2,1,0:T(8,128)(2,1)S(1)}, bf16[2,512,256]{2,1,0:T(8,128)(2,1)S(1)}, u32[]{:S(2)}, u32[]{:S(2)}) collective-permute-start(bf16[2,512,256]{2,1,0:T(8,128)(2,1)S(1)} %get-tuple-element.155), channel_id=1, source_target_pairs={{0,8},{4,12},{8,0},{12,4},{16,24},{20,28},{24,16},{28,20},{1,9},{5... | collective-permute-start | bytes 1572872 | tf_op jit(solution)/shard_map/ppermute | solution.py:34
  84.6 21.8 %collective-permute-start.16 = (bf16[1,512,256]{2,1,0:T(8,128)(2,1)S(1)}, bf16[1,512,256]{2,1,0:T(8,128)(2,1)S(1)}, u32[]{:S(2)}, u32[]{:S(2)}) collective-permute-start(bf16[1,512,256]{2,1,0:T(8,128)(2,1)S(1)} %get-tuple-element.168), channel_id=1, source_target_pairs={{0,16},{4,20},{8,24},{12,28},{16,0},{20,4},{24,8},{28,12},{1,17},{... | collective-permute-start | bytes 786440 | tf_op jit(solution)/shard_map/ppermute | solution.py:34
  102.1 24.0 %collective-permute-start.18 = (bf16[2,512,256]{2,1,0:T(8,128)(2,1)S(1)}, bf16[2,512,256]{2,1,0:T(8,128)(2,1)S(1)}, u32[]{:S(2)}, u32[]{:S(2)}) collective-permute-start(bf16[2,512,256]{2,1,0:T(8,128)(2,1)S(1)} %get-tuple-element.173), channel_id=1, source_target_pairs={{0,4},{4,0},{8,12},{12,8},{16,20},{20,16},{24,28},{28,24},{1,5},{5... | collective-permute-start | bytes 1572872 | tf_op jit(solution)/shard_map/ppermute | solution.py:34
  103.9 22.3 %collective-permute-start.12 = (bf16[1,256,1024]{2,1,0:T(8,128)(2,1)S(1)}, bf16[1,256,1024]{2,1,0:T(8,128)(2,1)S(1)}, u32[]{:S(2)}, u32[]{:S(2)}) collective-permute-start(bf16[1,256,1024]{2,1,0:T(8,128)(2,1)S(1)} %get-tuple-element.158), channel_id=1, source_target_pairs={{0,2},{1,3},{2,0},{3,1},{4,6},{5,7},{6,4},{7,5},{8,10},{9,11},{10,... | collective-permute-start | bytes 1572872 | tf_op jit(solution)/shard_map/ppermute | solution.py:34
  105.8 21.8 %collective-permute-start.14 = (bf16[1,256,1024]{2,1,0:T(8,128)(2,1)S(1)}, bf16[1,256,1024]{2,1,0:T(8,128)(2,1)S(1)}, u32[]{:S(2)}, u32[]{:S(2)}) collective-permute-start(bf16[1,256,1024]{2,1,0:T(8,128)(2,1)S(1)} %get-tuple-element.163), channel_id=1, source_target_pairs={{0,2},{1,3},{2,0},{3,1},{4,6},{5,7},{6,4},{7,5},{8,10},{9,11},{10,... | collective-permute-start | bytes 1572872 | tf_op jit(solution)/shard_map/ppermute | solution.py:34
  108.6 19.2 %collective-permute-start.17 = (bf16[2,512,256]{2,1,0:T(8,128)(2,1)S(1)}, bf16[2,512,256]{2,1,0:T(8,128)(2,1)S(1)}, u32[]{:S(2)}, u32[]{:S(2)}) collective-permute-start(bf16[2,512,256]{2,1,0:T(8,128)(2,1)S(1)} %get-tuple-element.171), channel_id=1, source_target_pairs={{0,8},{4,12},{8,0},{12,4},{16,24},{20,28},{24,16},{28,20},{1,9},{5... | collective-permute-start | bytes 1572872 | tf_op jit(solution)/shard_map/ppermute | solution.py:34
  109.9 15.3 %collective-permute-start.19 = (bf16[1,512,256]{2,1,0:T(8,128)(2,1)S(1)}, bf16[1,512,256]{2,1,0:T(8,128)(2,1)S(1)}, u32[]{:S(2)}, u32[]{:S(2)}) collective-permute-start(bf16[1,512,256]{2,1,0:T(8,128)(2,1)S(1)} %get-tuple-element.174), channel_id=1, source_target_pairs={{0,16},{4,20},{8,24},{12,28},{16,0},{20,4},{24,8},{28,12},{1,17},{... | collective-permute-start | bytes 786440 | tf_op jit(solution)/shard_map/ppermute | solution.py:34
  127.9 20.6 %collective-permute-start.20 = (bf16[1,512,256]{2,1,0:T(8,128)(2,1)S(1)}, bf16[1,512,256]{2,1,0:T(8,128)(2,1)S(1)}, u32[]{:S(2)}, u32[]{:S(2)}) collective-permute-start(bf16[1,512,256]{2,1,0:T(8,128)(2,1)S(1)} %get-tuple-element.179), channel_id=1, source_target_pairs={{0,16},{4,20},{8,24},{12,28},{16,0},{20,4},{24,8},{28,12},{1,17},{... | collective-permute-start | bytes 786440 | tf_op jit(solution)/shard_map/ppermute | solution.py:34
  129.9 23.5 %copy-start.1 = (bf16[512,2048]{1,0:T(8,128)(2,1)S(1)}, bf16[512,2048]{1,0:T(8,128)(2,1)}, u32[]{:S(2)}) copy-start(bf16[512,2048]{1,0:T(8,128)(2,1)} %param.10) | copy-start | bytes 6291460
  129.9 21.9 %collective-permute-start.21 = (bf16[1,512,256]{2,1,0:T(8,128)(2,1)S(1)}, bf16[1,512,256]{2,1,0:T(8,128)(2,1)S(1)}, u32[]{:S(2)}, u32[]{:S(2)}) collective-permute-start(bf16[1,512,256]{2,1,0:T(8,128)(2,1)S(1)} %get-tuple-element.180), channel_id=1, source_target_pairs={{0,16},{4,20},{8,24},{12,28},{16,0},{20,4},{24,8},{28,12},{1,17},{... | collective-permute-start | bytes 786440 | tf_op jit(solution)/shard_map/ppermute | solution.py:34
  (5 other events, 46.5 us)

commit v6 on v5

--- a/solution.py
+++ b/solution.py
@@ -41,27 +41,10 @@
     return order
 
 
-def flip_kernel(value_ref, value_t_ref):
-    value_t_ref[...] = value_ref[...].T
-
-
-def flipped(values):
-    count, width = values.shape
-    return pl.pallas_call(
-        flip_kernel,
-        grid=(width // HD,),
-        in_specs=[pl.BlockSpec((count, HD), lambda h: (0, h))],
-        out_specs=pl.BlockSpec((HD, count), lambda h: (h, 0)),
-        out_shape=jax.ShapeDtypeStruct((width, count), bf16),
-        compiler_params=params(),
-        cost_estimate=COST,
-        name="flipped",
-    )(values)
-
-
-def state_kernel(key_ref, value_ref, state_ref, sent_ref, key_t_ref):
+def state_kernel(key_ref, value_ref, state_ref, sent_ref, key_t_ref, value_t_ref):
     key_t = key_ref[...].T
     key_t_ref[...] = key_t
+    value_t_ref[...] = value_ref[...].T
     state = dot(key_t, value_ref[...])
     state_ref[0] = state
     sent_ref[0] = state.astype(bf16)
@@ -71,15 +54,17 @@
     count, width = keys.shape
     heads = width // HD
     column = pl.BlockSpec((count, HD), lambda h: (0, h))
+    row = pl.BlockSpec((HD, count), lambda h: (h, 0))
     square = pl.BlockSpec((1, HD, HD), lambda h: (h, 0, 0))
     return pl.pallas_call(
         state_kernel,
         grid=(heads,),
         in_specs=[column, column],
-        out_specs=[square, square, pl.BlockSpec((HD, count), lambda h: (h, 0))],
+        out_specs=[square, square, row, row],
         out_shape=[
             jax.ShapeDtypeStruct((heads, HD, HD), f32),
             jax.ShapeDtypeStruct((heads, HD, HD), bf16),
+            jax.ShapeDtypeStruct((width, count), bf16),
             jax.ShapeDtypeStruct((width, count), bf16),
         ],
         compiler_params=params(),
@@ -179,26 +164,21 @@
     )(info, *arrays)
 
 
-def prefix_kernel(bit, first, last, info_ref, *refs):
-    if first:
-        own_ref, got_ref, before_ref, total_ref, sent_ref = refs
-        before, total = 0.0, own_ref[...]
-    else:
-        own_ref, old_ref, sum_ref, got_ref, before_ref, total_ref, sent_ref = refs
-        before, total = old_ref[...], sum_ref[...]
-    got = got_ref[...].astype(f32)
-    before = before + got * flag(info_ref, bit)
-    total = total + got
+def prefix_kernel(bit, info_ref, *refs):
+    before_ref, total_ref, sent_ref = refs[-3:]
+    total, got = refs[0][...], refs[1][...].astype(f32)
+    before = got * flag(info_ref, bit)
+    if bit:
+        before += refs[2][...]
     before_ref[...] = before
-    total_ref[...] = total
-    sent = before + own_ref[...] * (1.0 - flag(info_ref, 0)) if last else total
-    sent_ref[...] = sent.astype(bf16)
-
-
-def prefix_step(info, bit, first, last, own, before, total, got):
-    arrays = [own, got] if first else [own, before, total, got]
-    shapes = [(own.shape, f32), (own.shape, f32), (own.shape, bf16)]
-    return small(functools.partial(prefix_kernel, bit, first, last), info, arrays, shapes, "prefix_step")
+    total_ref[...] = total + got
+    sent_ref[...] = (total + got).astype(bf16)
+
+
+def prefix_step(info, bit, arrays):
+    shape = arrays[0].shape
+    shapes = [(shape, f32), (shape, f32), (shape, bf16)]
+    return small(functools.partial(prefix_kernel, bit), info, arrays, shapes, "prefix_step")
 
 
 def suffix_first_kernel(info_ref, own_ref, got_ref, total_ref, mine_ref, mate_ref, sent_ref):
@@ -244,7 +224,7 @@
     return small(functools.partial(suffix_kernel, bit), info, arrays, shapes, "suffix_step")
 
 
-def middle_kernel(query_ref, grad_ref, mask_ref, gain_ref, own_ref, before_ref, got_ref, normed_t_ref, query_grad_ref, query_grad_t_ref, block_grad_ref, sent_ref, held_ref):
+def middle_kernel(query_ref, grad_ref, mask_ref, gain_ref, own_ref, before_ref, normed_t_ref, query_grad_ref, query_grad_t_ref, block_grad_ref, sent_ref, held_ref):
     mask_row = mask_ref[...].astype(f32)
 
     @pl.when(pl.program_id(0) == 0)
@@ -252,7 +232,7 @@
         held_ref[...] = jnp.broadcast_to(mask_row, held_ref.shape[::-1]).T
 
     query = query_ref[...]
-    state = (before_ref[0] + got_ref[0].astype(f32) + own_ref[0]).astype(bf16)
+    state = (before_ref[0] + own_ref[0]).astype(bf16)
     mask = held_ref[...]
     gain = gain_ref[...].astype(f32)
     attended = dot(query, state)
@@ -270,7 +250,7 @@
     query_grad_t_ref[...] = dot(state, attended_grad_t).astype(bf16)
 
 
-def middle(queries, normed_grad, mask, gain, own, before, got):
+def middle(queries, normed_grad, mask, gain, own, before):
     count, width = queries.shape
     heads = width // HD
     column = pl.BlockSpec((count, HD), lambda h: (0, h))
@@ -284,7 +264,6 @@
             column,
             pl.BlockSpec((1, count), lambda h: (0, 0)),
             pl.BlockSpec((1, HD), lambda h: (0, h)),
-            square,
             square,
             square,
         ],
@@ -299,10 +278,10 @@
         scratch_shapes=[pltpu.VMEM((count, HD), f32)],
         compiler_params=params(),
         cost_estimate=pl.CostEstimate(
-            flops=32 * count * width * HD, bytes_accessed=1, transcendentals=0
+            flops=64 * count * width * HD, bytes_accessed=1, transcendentals=0
         ),
         name="norm_backward",
-    )(queries, normed_grad, mask, gain, own, before, got)
+    )(queries, normed_grad, mask, gain, own, before)
 
 
 def late_kernel(mine_ref, mate_ref, other_ref, *refs):
@@ -440,40 +419,39 @@
         return gradient_terms([left], right, info, outputs)
 
     values = project(layer_input, 2)
-    values_t = flipped(values)
-    (value_send,) = terms(values_t, layer_input, order[half:])
-    value_got = exchange(value_send, "seq", 0)
-    keys = project(after(layer_input, value_send), 1)
-    own_state, sent, keys_t = block_states(keys, values)
-
-    before, total = None, own_state
+    keys = project(after(layer_input, values), 1)
+    own_state, sent, keys_t, values_t = block_states(keys, values)
+
+    got = exchange(sent, "seq", 0)
+    (value_send,) = terms(values_t, after(layer_input, own_state), order[half:])
+    queries = project(after(layer_input, value_send), 0)
+    got = after(got, queries)
+    before, total, sent = prefix_step(info, 0, [own_state, got])
+    value_got = exchange(after(value_send, total), "seq", 0)
     for bit in stages[1:]:
         got = exchange(sent, "seq", bit)
         if bit == 1:
-            queries = project(after(layer_input, own_state), 0)
-            got = after(got, queries)
+            normed_grad = dot_t(after(output_grad, total), out_weight)
+            got = after(got, normed_grad)
         elif bit == 2:
             (key_send,) = terms(keys_t, after(layer_input, total), swapped[half:])
             key_got = exchange(key_send, "seq", 1)
             got = after(got, key_send)
-        before, total, sent = prefix_step(info, bit, bit == 1, bit == stages[-1], own_state, before, total, got)
-    got = exchange(after(sent, value_got), "seq", 0)
-    normed_grad = dot_t(after(output_grad, sent), out_weight)
-    got = after(got, normed_grad)
+        before, total, sent = prefix_step(info, bit, [total, got, before])
 
     normed_t, query_grad, query_grad_t, own_grad, sent = middle(
-        queries, normed_grad, mask, norm_gain[None, :], own_state, before, got
+        queries, normed_grad, mask, norm_gain[None, :], own_state, before
     )
 
     got = exchange(sent, "seq", 0)
     out_keep, out_send = terms(normed_t, after(output_grad, own_grad), order[:half], order[half:])
-    got = after(got, out_keep, key_got)
+    got = after(got, out_keep, value_got)
     total, mine, mate, sent = suffix_first(info, own_grad, got)
     out_got = exchange(after(out_send, total), "seq", 0)
 
     got = exchange(sent, "seq", 1)
     query_keep, query_send = terms(query_grad_t, after(layer_input, total), order[:half], order[half:])
-    got = after(got, query_keep)
+    got = after(got, query_keep, key_got)
     suffix = suffix_step(info, 1, [total, mine, mate, got])
     query_got = exchange(after(query_send, suffix[0]), "seq", 0)
 
@@ -510,13 +488,13 @@
     value_keep, value_got = stage(value_keep, value_got, second_keep, 2)
     first_got = exchange(after(first_send, value_keep), "head", 0)
     second_got = exchange(after(second_send, value_keep), "head", 0)
+    query_keep, query_got = stage(query_keep, query_got, value_keep, 1)
+    out_keep, out_got = stage(out_keep, out_got, (query_keep, value_got), 2)
     for bit in range(1, head_bits):
-        first_keep, first_got = stage(first_keep, first_got, out_got, bit, "head")
+        first_keep, first_got = stage(first_keep, first_got, out_keep, bit, "head")
         second_keep, second_got = stage(second_keep, second_got, first_keep, bit, "head")
-    out_keep, out_got = stage(out_keep, out_got, second_keep, 2)
-    query_keep, query_got = stage(query_keep, query_got, (out_keep, value_got), 1)
-    key_keep, key_got = stage(key_keep, key_got, (query_keep, out_got, first_got, second_got), 2)
-    query_keep, query_got = stage(query_keep, query_got, key_keep, 2)
+    key_keep, key_got = stage(key_keep, key_got, second_keep, 2)
+    query_keep, query_got = stage(query_keep, query_got, (key_keep, out_got), 2)
 
     out_pair = rest(out_keep, out_got, stages[3:])
     value_pair = rest(value_keep, value_got, stages[3:])

time: 154 us -> 150 us (0.974)
  starting transfers between devices: 33.6 us -> 28.2 us
    ppermute x22, starting transfers between devices: 33.6 us -> 28.2 us  [exchange(): return lax.ppermute(arr, axis, [(i, i ^ 1 << bit) for i in range(count)])]
    pallas_call x5 -> x6, Pallas kernels: 4.54 us -> 5.15 us  [small(): pl.pallas_call(kernel, in_specs=[pl.BlockSpec(memory_space=pltpu.SMEM)] +...]
  transfers between devices with their start and end apart: 22 -> 22, of which waited for: 13 -> 11; matrix products, arithmetic and copies ran while one was open for 6% -> 4% of each run, Pallas kernels for 23% -> 26%
where the time goes in v6:
time: 150 us
  waiting for transfers between devices  64.6 us (43%)
  Pallas kernels  40.4 us (27%)
  starting transfers between devices  28.2 us (19%)
  matrix products  12.3 us (8%)
  other arithmetic  2.36 us (2%)
    ppermute x22, waiting for transfers between devices, exchange(): return lax.ppermute(arr, axis, [(i, i ^ 1 << bit) for i in range(count)])  64.6 us
    ppermute x22, starting transfers between devices, exchange(): return lax.ppermute(arr, axis, [(i, i ^ 1 << bit) for i in range(count)])  28.2 us
    pallas_call x6, Pallas kernels, gradient_terms(): pl.pallas_call(functools.partial(terms_kernel, len(lefts), outputs), in_s...  13.1 us
    dot_general x3, matrix products, project(): jnp.dot(rows, weights[index], preferred_element_type=f32).astype(bf16)  9.96 us
    pallas_call x2, Pallas kernels, input_terms(): pl.pallas_call(functools.partial(input_kernel, order), grid_spec=pltpu.Pr...  9.72 us
    pallas_call x6, Pallas kernels, small(): pl.pallas_call(kernel, in_specs=[pl.BlockSpec(memory_space=pltpu.SMEM)] +...  5.15 us
    pallas_call x1, Pallas kernels, middle(): pl.pallas_call(middle_kernel, grid=(heads,), in_specs=[column, column, pl...  4.64 us
  transfers between devices with their start and end apart: 22, of which 11 were waited for; matrix products, arithmetic and copies ran while one was open for 4% of the time, Pallas kernels for 26%

profile of v6, /device:TPU:0, one launch (start us, length us, event | category | flops | bytes accessed | tf_op | source)
XLA Modules:
  0.0 149.6 jit_solution(7205059293594809322)
XLA Ops:
  0.7 5.3 %fusion.3.value_ref = bf16[1024,512]{1,0:T(8,128)(2,1)S(1)} fusion(bf16[1024,2048]{1,0:T(8,128)(2,1)} %refs_1_.5, bf16[3,2048,512]{2,1,0:T(8,128)(2,1)} %bitcast.37), kind=kOutput, calls=%fused_computation.6 | convolution fusion | flops 2148007936 | bytes 7340032 | tf_op jit(solution)/shard_map/dot_general | solution.py:415
  6.8 2.3 %fusion.4.key_ref = bf16[1024,512]{1,0:T(8,128)(2,1)S(1)} fusion(bf16[1024,2048]{1,0:T(8,128)(2,1)S(1)} %copy-done.2, bf16[3,2048,512]{2,1,0:T(8,128)(2,1)S(1)} %bitcast.38), kind=kOutput, calls=%fused_computation.7 | convolution fusion | flops 2148007936 | bytes 7340032 | tf_op jit(solution)/shard_map/dot_general | solution.py:415
  10.6 3.0 %collective-permute-start = (bf16[4,128,128]{2,1,0:T(8,128)(2,1)S(1)}, bf16[4,128,128]{2,1,0:T(8,128)(2,1)S(1)}, u32[]{:S(2)}, u32[]{:S(2)}) collective-permute-start(bf16[4,128,128]{2,1,0:T(8,128)(2,1)S(1)} %get-tuple-element.104), channel_id=1, source_target_pairs={{0,4},{4,0},{8,12},{12,8},{16,20},{20,16},{24,28},{28,24},{1,5},{5... | collective-permute-start | bytes 393224 | tf_op jit(solution)/shard_map/ppermute | solution.py:34
  15.5 2.3 %fusion.5.query_ref = bf16[1024,512]{1,0:T(8,128)(2,1)S(1)} fusion(bf16[1024,2048]{1,0:T(8,128)(2,1)S(1)} %copy-done.2, bf16[3,2048,512]{2,1,0:T(8,128)(2,1)S(1)} %bitcast.39), kind=kOutput, calls=%fused_computation.8 | convolution fusion | flops 2148007936 | bytes 7340032 | tf_op jit(solution)/shard_map/dot_general | solution.py:415
  21.1 2.4 %fusion.8.grad_ref = f32[1024,512]{1,0:T(8,128)S(1)} fusion(bf16[1024,2048]{1,0:T(8,128)(2,1)S(1)} %copy-done.4, bf16[512,2048]{1,0:T(8,128)(2,1)S(1)} %copy-done), kind=kOutput, calls=%fused_computation.16 | convolution fusion | flops 2147483648 | bytes 8388608 | tf_op jit(solution)/shard_map/dot_general | solution.py:29
  24.2 2.7 %collective-permute-start.2 = (bf16[4,128,128]{2,1,0:T(8,128)(2,1)S(1)}, bf16[4,128,128]{2,1,0:T(8,128)(2,1)S(1)}, u32[]{:S(2)}, u32[]{:S(2)}) collective-permute-start(bf16[4,128,128]{2,1,0:T(8,128)(2,1)S(1)} %get-tuple-element.114), channel_id=1, source_target_pairs={{0,16},{4,20},{8,24},{12,28},{16,0},{20,4},{24,8},{28,12},{1,17},{... | collective-permute-start | bytes 393224 | tf_op jit(solution)/shard_map/ppermute | solution.py:34
  32.6 4.6 %norm_backward.1 = (bf16[512,1024]{1,0:T(8,128)(2,1)S(1)}, bf16[1024,512]{1,0:T(8,128)(2,1)S(1)}, bf16[512,1024]{1,0:T(8,128)(2,1)S(1)}, f32[4,128,128]{2,1,0:T(8,128)S(1)}, bf16[4,128,128]{2,1,0:T(8,128)(2,1)S(1)}) custom-call(bf16[1024,512]{1,0:T(8,128)(2,1)S(1)} %fusion.5.query_ref, f32[1024,512]{1,0:T(8,128)S(1)} %fusion.8.grad_ref, ...), custom_call_target="tpu_custom_call" | custom-call | flops 4294967296 | bytes 1 | tf_op jit(solution)/shard_map/norm_backward/pallas_call | solution.py:259
  39.1 2.9 %gradient_terms.8 = (bf16[4,512,256]{2,1,0:T(8,128)(2,1)S(1)}, bf16[4,512,256]{2,1,0:T(8,128)(2,1)S(1)}) custom-call(s32[2]{0:T(128)S(1)} %pad_add_fusion.position_ref.info_ref.place_ref, bf16[512,1024]{1,0:T(8,128)(2,1)S(1)} %get-tuple-element.123.refs_0_, bf16[1024,2048]{1,0:T(8,128)(2,1)S(1)} %copy-done.4), custom_call_target="tpu_custom_call" | custom-call | flops 1000000 | bytes 1 | tf_op jit(solution)/shard_map/gradient_terms/pallas_call | solution.py:104
  42.0 5.2 %collective-permute-done.3.got_ref = bf16[4,128,128]{2,1,0:T(8,128)(2,1)S(1)} collective-permute-done((bf16[4,128,128]{2,1,0:T(8,128)(2,1)S(1)}, bf16[4,128,128]{2,1,0:T(8,128)(2,1)S(1)}, u32[]{:S(2)}, u32[]{:S(2)}) %collective-permute-start.3) | collective-permute-done | bytes 131104 | tf_op jit(solution)/shard_map/ppermute | solution.py:34
  48.9 2.9 %gradient_terms.9 = (bf16[4,512,256]{2,1,0:T(8,128)(2,1)S(1)}, bf16[4,512,256]{2,1,0:T(8,128)(2,1)S(1)}) custom-call(s32[2]{0:T(128)S(1)} %pad_add_fusion.position_ref.info_ref.place_ref, bf16[512,1024]{1,0:T(8,128)(2,1)S(1)} %get-tuple-element.132.refs_0_, bf16[1024,2048]{1,0:T(8,128)(2,1)S(1)} %copy-done.2), custom_call_target="tpu_custom_call" | custom-call | flops 1000000 | bytes 1 | tf_op jit(solution)/shard_map/gradient_terms/pallas_call | solution.py:104
  51.8 3.0 %collective-permute-done.6.refs_3_ = bf16[4,512,256]{2,1,0:T(8,128)(2,1)S(1)} collective-permute-done((bf16[4,512,256]{2,1,0:T(8,128)(2,1)S(1)}, bf16[4,512,256]{2,1,0:T(8,128)(2,1)S(1)}, u32[]{:S(2)}, u32[]{:S(2)}) %collective-permute-start.6) | collective-permute-done | bytes 1048608 | tf_op jit(solution)/shard_map/ppermute | solution.py:34
  54.8 3.6 %collective-permute-done.5.refs_3_ = bf16[2,4,128,128]{3,2,1,0:T(8,128)(2,1)S(1)} collective-permute-done((bf16[2,4,128,128]{3,2,1,0:T(8,128)(2,1)S(1)}, bf16[2,4,128,128]{3,2,1,0:T(8,128)(2,1)S(1)}, u32[]{:S(2)}, u32[]{:S(2)}) %collective-permute-start.5) | collective-permute-done | bytes 262176 | tf_op jit(solution)/shard_map/ppermute | solution.py:34
  63.9 2.6 %collective-permute-done.7.refs_4_ = bf16[4,128,128]{2,1,0:T(8,128)(2,1)S(1)} collective-permute-done((bf16[4,128,128]{2,1,0:T(8,128)(2,1)S(1)}, bf16[4,128,128]{2,1,0:T(8,128)(2,1)S(1)}, u32[]{:S(2)}, u32[]{:S(2)}) %collective-permute-start.7) | collective-permute-done | bytes 131104 | tf_op jit(solution)/shard_map/ppermute | solution.py:34
  70.9 1.9 %key_value_grads.1 = (bf16[1024,512]{1,0:T(8,128)(2,1)S(1)}, bf16[1024,512]{1,0:T(8,128)(2,1)S(1)}) custom-call(bf16[1024,512]{1,0:T(8,128)(2,1)S(1)} %fusion.4.key_ref, bf16[1024,512]{1,0:T(8,128)(2,1)S(1)} %fusion.3.value_ref, f32[4,128,128]{2,1,0:T(8,128)S(1)} %get-tuple-element.148.mine_ref.grad_ref), custom_call_target="tpu_custom_call" | custom-call | flops 1000000 | bytes 1 | tf_op jit(solution)/shard_map/key_value_grads/pallas_call | solution.py:329
  72.8 4.7 %input_terms.2 = (bf16[2,256,1024]{2,1,0:T(8,128)(2,1)S(1)}, bf16[2,256,1024]{2,1,0:T(8,128)(2,1)S(1)}) custom-call(s32[2]{0:T(128)S(1)} %pad_add_fusion.position_ref.info_ref.place_ref, bf16[1024,512]{1,0:T(8,128)(2,1)S(1)} %get-tuple-element.120.query_ref, bf16[1024,512]{1,0:T(8,128)(2,1)S(1)} %get-tuple-element.149.key_ref, ...), custom_call_target="tpu_custom_call" | custom-call | flops 1000000 | bytes 1 | tf_op jit(solution)/shard_map/input_terms/pallas_call | solution.py:361
  77.8 5.0 %input_terms.3 = (bf16[2,256,1024]{2,1,0:T(8,128)(2,1)S(1)}, bf16[2,256,1024]{2,1,0:T(8,128)(2,1)S(1)}) custom-call(s32[2]{0:T(128)S(1)} %pad_add_fusion.position_ref.info_ref.place_ref, bf16[1024,512]{1,0:T(8,128)(2,1)S(1)} %get-tuple-element.120.query_ref, bf16[1024,512]{1,0:T(8,128)(2,1)S(1)} %get-tuple-element.149.key_ref, ...), custom_call_target="tpu_custom_call" | custom-call | flops 1000000 | bytes 1 | tf_op jit(solution)/shard_map/input_terms/pallas_call | solution.py:361
  83.5 1.9 %collective-permute-start.11 = (bf16[2,512,256]{2,1,0:T(8,128)(2,1)S(1)}, bf16[2,512,256]{2,1,0:T(8,128)(2,1)S(1)}, u32[]{:S(2)}, u32[]{:S(2)}) collective-permute-start(bf16[2,512,256]{2,1,0:T(8,128)(2,1)S(1)} %get-tuple-element.163), channel_id=1, source_target_pairs={{0,8},{4,12},{8,0},{12,4},{16,24},{20,28},{24,16},{28,20},{1,9},{5... | collective-permute-start | bytes 1572872 | tf_op jit(solution)/shard_map/ppermute | solution.py:34
  85.7 8.2 %collective-permute-done.12.refs_1_ = bf16[4,512,256]{2,1,0:T(8,128)(2,1)S(1)} collective-permute-done((bf16[4,512,256]{2,1,0:T(8,128)(2,1)S(1)}, bf16[4,512,256]{2,1,0:T(8,128)(2,1)S(1)}, u32[]{:S(2)}, u32[]{:S(2)}) %collective-permute-start.12) | collective-permute-done | bytes 1048608 | tf_op jit(solution)/shard_map/ppermute | solution.py:34
  94.4 8.1 %collective-permute-done.13 = bf16[1,512,256]{2,1,0:T(8,128)(2,1)S(1)} collective-permute-done((bf16[1,512,256]{2,1,0:T(8,128)(2,1)S(1)}, bf16[1,512,256]{2,1,0:T(8,128)(2,1)S(1)}, u32[]{:S(2)}, u32[]{:S(2)}) %collective-permute-start.13) | collective-permute-done | bytes 262176 | tf_op jit(solution)/shard_map/ppermute | solution.py:34
  102.5 2.0 %collective-permute-start.17 = (bf16[2,512,256]{2,1,0:T(8,128)(2,1)S(1)}, bf16[2,512,256]{2,1,0:T(8,128)(2,1)S(1)}, u32[]{:S(2)}, u32[]{:S(2)}) collective-permute-start(bf16[2,512,256]{2,1,0:T(8,128)(2,1)S(1)} %get-tuple-element.179), channel_id=1, source_target_pairs={{0,8},{4,12},{8,0},{12,4},{16,24},{20,28},{24,16},{28,20},{1,9},{5... | collective-permute-start | bytes 1572872 | tf_op jit(solution)/shard_map/ppermute | solution.py:34
  108.3 12.4 %collective-permute-done.19 = bf16[1,512,256]{2,1,0:T(8,128)(2,1)S(1)} collective-permute-done((bf16[1,512,256]{2,1,0:T(8,128)(2,1)S(1)}, bf16[1,512,256]{2,1,0:T(8,128)(2,1)S(1)}, u32[]{:S(2)}, u32[]{:S(2)}) %collective-permute-start.19) | collective-permute-done | bytes 262176 | tf_op jit(solution)/shard_map/ppermute | solution.py:34
  121.6 2.7 %collective-permute-start.20 = (bf16[1,512,256]{2,1,0:T(8,128)(2,1)S(1)}, bf16[1,512,256]{2,1,0:T(8,128)(2,1)S(1)}, u32[]{:S(2)}, u32[]{:S(2)}) collective-permute-start(bf16[1,512,256]{2,1,0:T(8,128)(2,1)S(1)} %get-tuple-element.187), channel_id=1, source_target_pairs={{0,16},{4,20},{8,24},{12,28},{16,0},{20,4},{24,8},{28,12},{1,17},{... | collective-permute-start | bytes 786440 | tf_op jit(solution)/shard_map/ppermute | solution.py:34
  126.9 16.1 %collective-permute-done.20 = bf16[1,512,256]{2,1,0:T(8,128)(2,1)S(1)} collective-permute-done((bf16[1,512,256]{2,1,0:T(8,128)(2,1)S(1)}, bf16[1,512,256]{2,1,0:T(8,128)(2,1)S(1)}, u32[]{:S(2)}, u32[]{:S(2)}) %collective-permute-start.20) | collective-permute-done | bytes 262176 | tf_op jit(solution)/shard_map/ppermute | solution.py:34
  143.0 3.5 %collective-permute-done.21 = bf16[1,512,256]{2,1,0:T(8,128)(2,1)S(1)} collective-permute-done((bf16[1,512,256]{2,1,0:T(8,128)(2,1)S(1)}, bf16[1,512,256]{2,1,0:T(8,128)(2,1)S(1)}, u32[]{:S(2)}, u32[]{:S(2)}) %collective-permute-start.21) | collective-permute-done | bytes 262176 | tf_op jit(solution)/shard_map/ppermute | solution.py:34
  (71 shorter events, 39.1 us)
Async XLA Ops:
  0.6 20.5 %copy-start = (bf16[512,2048]{1,0:T(8,128)(2,1)S(1)}, bf16[512,2048]{1,0:T(8,128)(2,1)}, u32[]{:S(2)}) copy-start(bf16[512,2048]{1,0:T(8,128)(2,1)} %param.10) | copy-start | bytes 6291460
  10.6 7.2 %collective-permute-start = (bf16[4,128,128]{2,1,0:T(8,128)(2,1)S(1)}, bf16[4,128,128]{2,1,0:T(8,128)(2,1)S(1)}, u32[]{:S(2)}, u32[]{:S(2)}) collective-permute-start(bf16[4,128,128]{2,1,0:T(8,128)(2,1)S(1)} %get-tuple-element.104), channel_id=1, source_target_pairs={{0,4},{4,0},{8,12},{12,8},{16,20},{20,16},{24,28},{28,24},{1,5},{5... | collective-permute-start | bytes 393224 | tf_op jit(solution)/shard_map/ppermute | solution.py:34
  18.4 5.1 %collective-permute-start.1 = (bf16[4,128,128]{2,1,0:T(8,128)(2,1)S(1)}, bf16[4,128,128]{2,1,0:T(8,128)(2,1)S(1)}, u32[]{:S(2)}, u32[]{:S(2)}) collective-permute-start(bf16[4,128,128]{2,1,0:T(8,128)(2,1)S(1)} %get-tuple-element.110), channel_id=1, source_target_pairs={{0,8},{4,12},{8,0},{12,4},{16,24},{20,28},{24,16},{28,20},{1,9},{5... | collective-permute-start | bytes 393224 | tf_op jit(solution)/shard_map/ppermute | solution.py:34
  20.1 27.2 %collective-permute-start.4 = (bf16[4,512,256]{2,1,0:T(8,128)(2,1)S(1)}, bf16[4,512,256]{2,1,0:T(8,128)(2,1)S(1)}, u32[]{:S(2)}, u32[]{:S(2)}) collective-permute-start(bf16[4,512,256]{2,1,0:T(8,128)(2,1)S(1)} %gradient_terms.6), channel_id=1, source_target_pairs={{0,4},{4,0},{8,12},{12,8},{16,20},{20,16},{24,28},{28,24},{1,5},{5... | collective-permute-start | bytes 3145736 | tf_op jit(solution)/shard_map/ppermute | solution.py:34
  23.6 9.0 %copy-start.5 = (s32[1024]{0:T(1024)S(1)}, s32[1024]{0:T(1024)}, u32[]{:S(2)}) copy-start(s32[1024]{0:T(1024)} %param.8) | copy-start | bytes 12292
  24.2 7.1 %collective-permute-start.2 = (bf16[4,128,128]{2,1,0:T(8,128)(2,1)S(1)}, bf16[4,128,128]{2,1,0:T(8,128)(2,1)S(1)}, u32[]{:S(2)}, u32[]{:S(2)}) collective-permute-start(bf16[4,128,128]{2,1,0:T(8,128)(2,1)S(1)} %get-tuple-element.114), channel_id=1, source_target_pairs={{0,16},{4,20},{8,24},{12,28},{16,0},{20,4},{24,8},{28,12},{1,17},{... | collective-permute-start | bytes 393224 | tf_op jit(solution)/shard_map/ppermute | solution.py:34
  28.7 26.2 %collective-permute-start.6 = (bf16[4,512,256]{2,1,0:T(8,128)(2,1)S(1)}, bf16[4,512,256]{2,1,0:T(8,128)(2,1)S(1)}, u32[]{:S(2)}, u32[]{:S(2)}) collective-permute-start(bf16[4,512,256]{2,1,0:T(8,128)(2,1)S(1)} %gradient_terms.7), channel_id=1, source_target_pairs={{0,8},{4,12},{8,0},{12,4},{16,24},{20,28},{24,16},{28,20},{1,9},{5... | collective-permute-start | bytes 3145736 | tf_op jit(solution)/shard_map/ppermute | solution.py:34
  37.2 10.0 %collective-permute-start.3 = (bf16[4,128,128]{2,1,0:T(8,128)(2,1)S(1)}, bf16[4,128,128]{2,1,0:T(8,128)(2,1)S(1)}, u32[]{:S(2)}, u32[]{:S(2)}) collective-permute-start(bf16[4,128,128]{2,1,0:T(8,128)(2,1)S(1)} %get-tuple-element.122), channel_id=1, source_target_pairs={{0,4},{4,0},{8,12},{12,8},{16,20},{20,16},{24,28},{28,24},{1,5},{5... | collective-permute-start | bytes 393224 | tf_op jit(solution)/shard_map/ppermute | solution.py:34
  47.9 29.7 %collective-permute-start.9 = (bf16[4,512,256]{2,1,0:T(8,128)(2,1)S(1)}, bf16[4,512,256]{2,1,0:T(8,128)(2,1)S(1)}, u32[]{:S(2)}, u32[]{:S(2)}) collective-permute-start(bf16[4,512,256]{2,1,0:T(8,128)(2,1)S(1)} %get-tuple-element.155), channel_id=1, source_target_pairs={{0,4},{4,0},{8,12},{12,8},{16,20},{20,16},{24,28},{28,24},{1,5},{5... | collective-permute-start | bytes 3145736 | tf_op jit(solution)/shard_map/ppermute | solution.py:34
  48.5 10.0 %collective-permute-start.5 = (bf16[2,4,128,128]{3,2,1,0:T(8,128)(2,1)S(1)}, bf16[2,4,128,128]{3,2,1,0:T(8,128)(2,1)S(1)}, u32[]{:S(2)}, u32[]{:S(2)}) collective-permute-start(bf16[2,4,128,128]{3,2,1,0:T(8,128)(2,1)S(1)} %get-tuple-element.131), channel_id=1, source_target_pairs={{0,8},{4,12},{8,0},{12,4},{16,24},{20,28},{24,16},{28,20},{1,9},{5... | collective-permute-start | bytes 786440 | tf_op jit(solution)/shard_map/ppermute | solution.py:34
  59.1 7.3 %collective-permute-start.7 = (bf16[4,128,128]{2,1,0:T(8,128)(2,1)S(1)}, bf16[4,128,128]{2,1,0:T(8,128)(2,1)S(1)}, u32[]{:S(2)}, u32[]{:S(2)}) collective-permute-start(bf16[4,128,128]{2,1,0:T(8,128)(2,1)S(1)} %get-tuple-element.140), channel_id=1, source_target_pairs={{0,16},{4,20},{8,24},{12,28},{16,0},{20,4},{24,8},{28,12},{1,17},{... | collective-permute-start | bytes 393224 | tf_op jit(solution)/shard_map/ppermute | solution.py:34
  69.1 13.7 %collective-permute-start.8 = (bf16[2,512,256]{2,1,0:T(8,128)(2,1)S(1)}, bf16[2,512,256]{2,1,0:T(8,128)(2,1)S(1)}, u32[]{:S(2)}, u32[]{:S(2)}) collective-permute-start(bf16[2,512,256]{2,1,0:T(8,128)(2,1)S(1)} %get-tuple-element.153), channel_id=1, source_target_pairs={{0,8},{4,12},{8,0},{12,4},{16,24},{20,28},{24,16},{28,20},{1,9},{5... | collective-permute-start | bytes 1572872 | tf_op jit(solution)/shard_map/ppermute | solution.py:34
  69.3 24.6 %collective-permute-start.12 = (bf16[4,512,256]{2,1,0:T(8,128)(2,1)S(1)}, bf16[4,512,256]{2,1,0:T(8,128)(2,1)S(1)}, u32[]{:S(2)}, u32[]{:S(2)}) collective-permute-start(bf16[4,512,256]{2,1,0:T(8,128)(2,1)S(1)} %get-tuple-element.165), channel_id=1, source_target_pairs={{0,4},{4,0},{8,12},{12,8},{16,20},{20,16},{24,28},{28,24},{1,5},{5... | collective-permute-start | bytes 3145736 | tf_op jit(solution)/shard_map/ppermute | solution.py:34
  83.0 23.1 %collective-permute-start.10 = (bf16[2,256,1024]{2,1,0:T(8,128)(2,1)S(1)}, bf16[2,256,1024]{2,1,0:T(8,128)(2,1)S(1)}, u32[]{:S(2)}, u32[]{:S(2)}) collective-permute-start(bf16[2,256,1024]{2,1,0:T(8,128)(2,1)S(1)} %get-tuple-element.162), channel_id=1, source_target_pairs={{0,1},{1,0},{2,3},{3,2},{4,5},{5,4},{6,7},{7,6},{8,9},{9,8},{10,11... | collective-permute-start | bytes 3145736 | tf_op jit(solution)/shard_map/ppermute | solution.py:34
  83.0 24.9 %collective-permute-start.15 = (bf16[2,256,1024]{2,1,0:T(8,128)(2,1)S(1)}, bf16[2,256,1024]{2,1,0:T(8,128)(2,1)S(1)}, u32[]{:S(2)}, u32[]{:S(2)}) collective-permute-start(bf16[2,256,1024]{2,1,0:T(8,128)(2,1)S(1)} %get-tuple-element.175), channel_id=1, source_target_pairs={{0,1},{1,0},{2,3},{3,2},{4,5},{5,4},{6,7},{7,6},{8,9},{9,8},{10,11... | collective-permute-start | bytes 3145736 | tf_op jit(solution)/shard_map/ppermute | solution.py:34
  83.5 21.0 %collective-permute-start.11 = (bf16[2,512,256]{2,1,0:T(8,128)(2,1)S(1)}, bf16[2,512,256]{2,1,0:T(8,128)(2,1)S(1)}, u32[]{:S(2)}, u32[]{:S(2)}) collective-permute-start(bf16[2,512,256]{2,1,0:T(8,128)(2,1)S(1)} %get-tuple-element.163), channel_id=1, source_target_pairs={{0,8},{4,12},{8,0},{12,4},{16,24},{20,28},{24,16},{28,20},{1,9},{5... | collective-permute-start | bytes 1572872 | tf_op jit(solution)/shard_map/ppermute | solution.py:34
  85.5 17.0 %collective-permute-start.13 = (bf16[1,512,256]{2,1,0:T(8,128)(2,1)S(1)}, bf16[1,512,256]{2,1,0:T(8,128)(2,1)S(1)}, u32[]{:S(2)}, u32[]{:S(2)}) collective-permute-start(bf16[1,512,256]{2,1,0:T(8,128)(2,1)S(1)} %get-tuple-element.168), channel_id=1, source_target_pairs={{0,16},{4,20},{8,24},{12,28},{16,0},{20,4},{24,8},{28,12},{1,17},{... | collective-permute-start | bytes 786440 | tf_op jit(solution)/shard_map/ppermute | solution.py:34
  93.9 14.3 %collective-permute-start.18 = (bf16[2,512,256]{2,1,0:T(8,128)(2,1)S(1)}, bf16[2,512,256]{2,1,0:T(8,128)(2,1)S(1)}, u32[]{:S(2)}, u32[]{:S(2)}) collective-permute-start(bf16[2,512,256]{2,1,0:T(8,128)(2,1)S(1)} %get-tuple-element.181), channel_id=1, source_target_pairs={{0,4},{4,0},{8,12},{12,8},{16,20},{20,16},{24,28},{28,24},{1,5},{5... | collective-permute-start | bytes 1572872 | tf_op jit(solution)/shard_map/ppermute | solution.py:34
  102.5 18.9 %collective-permute-start.17 = (bf16[2,512,256]{2,1,0:T(8,128)(2,1)S(1)}, bf16[2,512,256]{2,1,0:T(8,128)(2,1)S(1)}, u32[]{:S(2)}, u32[]{:S(2)}) collective-permute-start(bf16[2,512,256]{2,1,0:T(8,128)(2,1)S(1)} %get-tuple-element.179), channel_id=1, source_target_pairs={{0,8},{4,12},{8,0},{12,4},{16,24},{20,28},{24,16},{28,20},{1,9},{5... | collective-permute-start | bytes 1572872 | tf_op jit(solution)/shard_map/ppermute | solution.py:34
  104.7 16.1 %collective-permute-start.19 = (bf16[1,512,256]{2,1,0:T(8,128)(2,1)S(1)}, bf16[1,512,256]{2,1,0:T(8,128)(2,1)S(1)}, u32[]{:S(2)}, u32[]{:S(2)}) collective-permute-start(bf16[1,512,256]{2,1,0:T(8,128)(2,1)S(1)} %get-tuple-element.184), channel_id=1, source_target_pairs={{0,16},{4,20},{8,24},{12,28},{16,0},{20,4},{24,8},{28,12},{1,17},{... | collective-permute-start | bytes 786440 | tf_op jit(solution)/shard_map/ppermute | solution.py:34
  106.4 41.8 %collective-permute-start.14 = (bf16[1,256,1024]{2,1,0:T(8,128)(2,1)S(1)}, bf16[1,256,1024]{2,1,0:T(8,128)(2,1)S(1)}, u32[]{:S(2)}, u32[]{:S(2)}) collective-permute-start(bf16[1,256,1024]{2,1,0:T(8,128)(2,1)S(1)} %get-tuple-element.173), channel_id=1, source_target_pairs={{0,2},{1,3},{2,0},{3,1},{4,6},{5,7},{6,4},{7,5},{8,10},{9,11},{10,... | collective-permute-start | bytes 1572872 | tf_op jit(solution)/shard_map/ppermute | solution.py:34
  121.6 21.4 %collective-permute-start.20 = (bf16[1,512,256]{2,1,0:T(8,128)(2,1)S(1)}, bf16[1,512,256]{2,1,0:T(8,128)(2,1)S(1)}, u32[]{:S(2)}, u32[]{:S(2)}) collective-permute-start(bf16[1,512,256]{2,1,0:T(8,128)(2,1)S(1)} %get-tuple-element.187), channel_id=1, source_target_pairs={{0,16},{4,20},{8,24},{12,28},{16,0},{20,4},{24,8},{28,12},{1,17},{... | collective-permute-start | bytes 786440 | tf_op jit(solution)/shard_map/ppermute | solution.py:34
  124.3 22.2 %collective-permute-start.21 = (bf16[1,512,256]{2,1,0:T(8,128)(2,1)S(1)}, bf16[1,512,256]{2,1,0:T(8,128)(2,1)S(1)}, u32[]{:S(2)}, u32[]{:S(2)}) collective-permute-start(bf16[1,512,256]{2,1,0:T(8,128)(2,1)S(1)} %get-tuple-element.188), channel_id=1, source_target_pairs={{0,16},{4,20},{8,24},{12,28},{16,0},{20,4},{24,8},{28,12},{1,17},{... | collective-permute-start | bytes 786440 | tf_op jit(solution)/shard_map/ppermute | solution.py:34
  124.6 23.7 %collective-permute-start.16 = (bf16[1,256,1024]{2,1,0:T(8,128)(2,1)S(1)}, bf16[1,256,1024]{2,1,0:T(8,128)(2,1)S(1)}, u32[]{:S(2)}, u32[]{:S(2)}) collective-permute-start(bf16[1,256,1024]{2,1,0:T(8,128)(2,1)S(1)} %get-tuple-element.178), channel_id=1, source_target_pairs={{0,2},{1,3},{2,0},{3,1},{4,6},{5,7},{6,4},{7,5},{8,10},{9,11},{10,... | collective-permute-start | bytes 1572872 | tf_op jit(solution)/shard_map/ppermute | solution.py:34
  (5 other events, 26.8 us)

commit v7 on v6

--- a/solution.py
+++ b/solution.py
@@ -41,36 +41,56 @@
     return order
 
 
-def state_kernel(key_ref, value_ref, state_ref, sent_ref, key_t_ref, value_t_ref):
-    key_t = key_ref[...].T
-    key_t_ref[...] = key_t
-    value_t_ref[...] = value_ref[...].T
-    state = dot(key_t, value_ref[...])
-    state_ref[0] = state
-    sent_ref[0] = state.astype(bf16)
-
-
-def block_states(keys, values):
-    count, width = keys.shape
+def states_kernel(rows_ref, weight_ref, key_ref, value_ref, state_ref, sent_ref, key_t_ref, value_t_ref):
+    heads = state_ref.shape[0]
+    product = dot(rows_ref[...], weight_ref[0]).astype(bf16)
+
+    @pl.when(pl.program_id(0) == 0)
+    def _():
+        value_ref[...] = product
+        for h in range(heads):
+            columns = slice(h * HD, (h + 1) * HD)
+            value_t_ref[columns, :] = value_ref[:, columns].T
+
+    @pl.when(pl.program_id(0) == 1)
+    def _():
+        key_ref[...] = product
+        for h in range(heads):
+            columns = slice(h * HD, (h + 1) * HD)
+            key_t = key_ref[:, columns].T
+            key_t_ref[columns, :] = key_t
+            state = dot(key_t, value_ref[:, columns])
+            state_ref[h] = state
+            sent_ref[h] = state.astype(bf16)
+
+
+def block_states(rows, weights):
+    count, depth = rows.shape
+    width = weights.shape[2]
     heads = width // HD
-    column = pl.BlockSpec((count, HD), lambda h: (0, h))
-    row = pl.BlockSpec((HD, count), lambda h: (h, 0))
-    square = pl.BlockSpec((1, HD, HD), lambda h: (h, 0, 0))
-    return pl.pallas_call(
-        state_kernel,
-        grid=(heads,),
-        in_specs=[column, column],
-        out_specs=[square, square, row, row],
+    full = pl.BlockSpec((count, width), lambda i: (0, 0))
+    full_t = pl.BlockSpec((width, count), lambda i: (0, 0))
+    squares = pl.BlockSpec((heads, HD, HD), lambda i: (0, 0, 0))
+    return pl.pallas_call(
+        states_kernel,
+        grid=(2,),
+        in_specs=[
+            pl.BlockSpec((count, depth), lambda i: (0, 0)),
+            pl.BlockSpec((1, depth, width), lambda i: (2 - i, 0, 0)),
+        ],
+        out_specs=[full, full, squares, squares, full_t, full_t],
         out_shape=[
+            jax.ShapeDtypeStruct((count, width), bf16),
+            jax.ShapeDtypeStruct((count, width), bf16),
             jax.ShapeDtypeStruct((heads, HD, HD), f32),
             jax.ShapeDtypeStruct((heads, HD, HD), bf16),
             jax.ShapeDtypeStruct((width, count), bf16),
             jax.ShapeDtypeStruct((width, count), bf16),
         ],
-        compiler_params=params(),
+        compiler_params=params(32),
         cost_estimate=COST,
         name="block_states",
-    )(keys, values)
+    )(rows, weights)
 
 
 def terms_kernel(number, outputs, position_ref, *refs):
@@ -162,6 +182,10 @@
         cost_estimate=COST,
         name=name,
     )(info, *arrays)
+
+
+def mark_kernel(info_ref, out_ref):
+    out_ref[...] = jnp.full(out_ref.shape, flag(info_ref, 0))
 
 
 def prefix_kernel(bit, info_ref, *refs):
@@ -374,22 +398,23 @@
     )(info, *grads, weight)
 
 
-def finish_kernel(*refs):
-    out = refs[-1]
-    for index in range(3):
-        keep, got = refs[2 * index], refs[2 * index + 1]
-        out[index] = (keep[...].astype(f32) + got[...].astype(f32)).T
-
-
-def finish(pairs):
-    rows, width = pairs[0].shape
+def finish_kernel(query_keep_ref, query_got_ref, late_keep_ref, late_got_ref, out_ref):
+    width = query_keep_ref.shape[0]
+    out_ref[0] = (query_keep_ref[...].astype(f32) + query_got_ref[...].astype(f32)).T
+    for index in range(2):
+        rows = slice(index * width, (index + 1) * width)
+        out_ref[1 + index] = (late_keep_ref[rows, :].astype(f32) + late_got_ref[rows, :].astype(f32)).T
+
+
+def finish(query_keep, query_got, late_keep, late_got):
+    rows, width = query_keep.shape
     return pl.pallas_call(
         finish_kernel,
         out_shape=jax.ShapeDtypeStruct((3, width, rows), f32),
         compiler_params=params(),
         cost_estimate=COST,
         name="finish",
-    )(*pairs)
+    )(query_keep, query_got, late_keep, late_got)
 
 
 def after(value, *others):
@@ -418,9 +443,7 @@
         outputs = [(0, 0, left.shape[0], slots) for slots in parts]
         return gradient_terms([left], right, info, outputs)
 
-    values = project(layer_input, 2)
-    keys = project(after(layer_input, values), 1)
-    own_state, sent, keys_t, values_t = block_states(keys, values)
+    keys, values, own_state, sent, keys_t, values_t = block_states(layer_input, weights)
 
     got = exchange(sent, "seq", 0)
     (value_send,) = terms(values_t, after(layer_input, own_state), order[half:])
@@ -432,11 +455,12 @@
         got = exchange(sent, "seq", bit)
         if bit == 1:
             normed_grad = dot_t(after(output_grad, total), out_weight)
-            got = after(got, normed_grad)
+            (key_send,) = terms(keys_t, after(layer_input, normed_grad), swapped[half:])
+            got = after(got, key_send)
         elif bit == 2:
-            (key_send,) = terms(keys_t, after(layer_input, total), swapped[half:])
-            key_got = exchange(key_send, "seq", 1)
-            got = after(got, key_send)
+            (mark,) = small(mark_kernel, after(info, total), [], [((8, 128), f32)], "mark")
+            key_got = exchange(after(key_send, mark), "seq", 1)
+            got = after(got, mark)
         before, total, sent = prefix_step(info, bit, [total, got, before])
 
     normed_t, query_grad, query_grad_t, own_grad, sent = middle(
@@ -472,7 +496,7 @@
 
     key_grad, value_grad = key_value_grads(keys, values, after(mine, value_keep))
     grads = (query_grad, key_grad, value_grad)
-    first_keep, first_send = input_terms(grads, weights, info, head_order, 0, 2)
+    input_keep, input_send = input_terms(grads, weights, info, head_order, 0, 1)
 
     def stage(keep, got, token, bit, axis="seq"):
         keep, send = sums([(keep, after(got, token))])
@@ -483,32 +507,23 @@
             keep, got = stage(keep, got, keep, bit)
         return keep[0], got[0]
 
-    out_keep, out_got = stage(out_keep, out_got, first_keep, 1)
-    second_keep, second_send = input_terms(grads, after(weights, out_keep), info, head_order, 1, 2)
-    value_keep, value_got = stage(value_keep, value_got, second_keep, 2)
-    first_got = exchange(after(first_send, value_keep), "head", 0)
-    second_got = exchange(after(second_send, value_keep), "head", 0)
-    query_keep, query_got = stage(query_keep, query_got, value_keep, 1)
-    out_keep, out_got = stage(out_keep, out_got, (query_keep, value_got), 2)
+    value_got, key_got = after((value_got, key_got), input_keep)
+    late_keep, late_send = sums([(value_keep, value_got), (key_keep, key_got)], merge=True)
+    late_got = exchange(late_send, "seq", 2)
+    out_keep, out_got = stage(out_keep, out_got, late_keep, 1)
+    input_got = exchange(after(input_send, out_keep), "head", 0)
     for bit in range(1, head_bits):
-        first_keep, first_got = stage(first_keep, first_got, out_keep, bit, "head")
-        second_keep, second_got = stage(second_keep, second_got, first_keep, bit, "head")
-    key_keep, key_got = stage(key_keep, key_got, second_keep, 2)
-    query_keep, query_got = stage(query_keep, query_got, (key_keep, out_got), 2)
+        input_keep, input_got = stage(input_keep, input_got, out_keep, bit, "head")
+    out_keep, out_got = stage(out_keep, out_got, (input_keep, late_got), 2)
+    query_keep, query_got = stage(query_keep, query_got, out_keep, 1)
+    query_keep, query_got = stage(query_keep, query_got, (query_keep, out_got, input_got), 2)
 
     out_pair = rest(out_keep, out_got, stages[3:])
-    value_pair = rest(value_keep, value_got, stages[3:])
-    key_pair = rest(key_keep, key_got, stages[3:])
+    late_pair = rest(late_keep, late_got, stages[3:])
     query_pair = rest(query_keep, query_got, stages[3:])
-    input_grad = jnp.concatenate(
-        [
-            (keep[0].astype(f32) + got[0].astype(f32)).astype(bf16)
-            for keep, got in ((first_keep, first_got), (second_keep, second_got))
-        ],
-        1,
-    )
+    input_grad = (input_keep[0].astype(f32) + input_got[0].astype(f32)).astype(bf16)
     out_weight_grad = out_pair[0].astype(f32) + out_pair[1].astype(f32)
-    proj_weight_grad = finish(query_pair + value_pair + key_pair)
+    proj_weight_grad = finish(*query_pair, *late_pair)
     return (input_grad, jnp.transpose(proj_weight_grad, (1, 0, 2)), out_weight_grad)
 
 

time: 150 us -> 147 us (0.980)
  matrix products: 12.3 us -> 4.71 us
  local copies, waits for them, and re-layouts: 0.74 us -> 5.14 us
  Pallas kernels: 40.4 us -> 43.7 us
  starting transfers between devices: 28.2 us -> 24.9 us
    dot_general x3 -> x1, matrix products: 9.96 us -> 2.32 us  [project(): jnp.dot(rows, weights[index], preferred_element_type=f32).astype(bf16)]
    unnamed x14, local copies, waits for them, and re-layouts: 0.74 us -> 5.14 us
    pallas_call x1, Pallas kernels: 1.53 us -> 5.57 us  [block_states(): pl.pallas_call(states_kernel, grid=(2,), in_specs=[pl.BlockSpec((count, d...]
    ppermute x22 -> x19, starting transfers between devices: 28.2 us -> 24.9 us  [exchange(): return lax.ppermute(arr, axis, [(i, i ^ 1 << bit) for i in range(count)])]
    pallas_call x2 -> x1, Pallas kernels: 9.72 us -> 8.9 us  [input_terms(): pl.pallas_call(functools.partial(input_kernel, order), grid_spec=pltpu.Pr...]
    ppermute x22 -> x19, waiting for transfers between devices: 64.6 us -> 64.9 us  [exchange(): return lax.ppermute(arr, axis, [(i, i ^ 1 << bit) for i in range(count)])]
  transfers between devices with their start and end apart: 22 -> 19, of which waited for: 11 -> 9; matrix products, arithmetic and copies ran while one was open for 4% -> 5% of each run, Pallas kernels for 26% -> 24%
where the time goes in v7:
time: 147 us
  waiting for transfers between devices  64.9 us (44%)
  Pallas kernels  43.7 us (30%)
  starting transfers between devices  24.9 us (17%)
  local copies, waits for them, and re-layouts  5.14 us (3%)
  matrix products  4.71 us (3%)
  other arithmetic  2.28 us (2%)
    ppermute x19, waiting for transfers between devices, exchange(): return lax.ppermute(arr, axis, [(i, i ^ 1 << bit) for i in range(count)])  64.9 us
    ppermute x19, starting transfers between devices, exchange(): return lax.ppermute(arr, axis, [(i, i ^ 1 << bit) for i in range(count)])  24.9 us
    pallas_call x6, Pallas kernels, gradient_terms(): pl.pallas_call(functools.partial(terms_kernel, len(lefts), outputs), in_s...  13.1 us
    pallas_call x1, Pallas kernels, input_terms(): pl.pallas_call(functools.partial(input_kernel, order), grid_spec=pltpu.Pr...  8.9 us
    pallas_call x1, Pallas kernels, block_states(): pl.pallas_call(states_kernel, grid=(2,), in_specs=[pl.BlockSpec((count, d...  5.57 us
    pallas_call x6, Pallas kernels, small(): pl.pallas_call(kernel, in_specs=[pl.BlockSpec(memory_space=pltpu.SMEM)] +...  5.15 us
    unnamed x14, local copies, waits for them, and re-layouts  5.14 us
    pallas_call x1, Pallas kernels, middle(): pl.pallas_call(middle_kernel, grid=(heads,), in_specs=[column, column, pl...  4.64 us
  transfers between devices with their start and end apart: 19, of which 9 were waited for; matrix products, arithmetic and copies ran while one was open for 5% of the time, Pallas kernels for 24%

profile of v7, /device:TPU:0, one launch (start us, length us, event | category | flops | bytes accessed | tf_op | source)
XLA Modules:
  0.0 146.5 jit_solution(8444893340017754796)
XLA Ops:
  0.7 2.3 %copy-done.2 = bf16[1024,2048]{1,0:T(8,128)(2,1)S(1)} copy-done((bf16[1024,2048]{1,0:T(8,128)(2,1)S(1)}, bf16[1024,2048]{1,0:T(8,128)(2,1)}, u32[]{:S(2)}) %copy-start.2) | copy-done | bytes 4194328
  3.1 2.8 %copy-done.3 = bf16[2048,3,512]{2,0,1:T(8,128)(2,1)S(1)} copy-done((bf16[2048,3,512]{2,0,1:T(8,128)(2,1)S(1)}, bf16[2048,3,512]{2,0,1:T(8,128)(2,1)}, u32[]{:S(2)}) %copy-start.3) | copy-done | bytes 6291480
  5.8 5.6 %block_states.1 = (bf16[1024,512]{1,0:T(8,128)(2,1)S(1)}, bf16[1024,512]{1,0:T(8,128)(2,1)S(1)}, f32[4,128,128]{2,1,0:T(8,128)S(1)}, bf16[4,128,128]{2,1,0:T(8,1...) custom-call(bf16[1024,2048]{1,0:T(8,128)(2,1)S(1)} %copy-done.2, ...), custom_call_target="tpu_custom_call" | custom-call | flops 1000000 | bytes 1 | tf_op jit(solution)/shard_map/block_states/pallas_call | solution.py:74
  11.4 3.0 %collective-permute-start = (bf16[4,128,128]{2,1,0:T(8,128)(2,1)S(1)}, bf16[4,128,128]{2,1,0:T(8,128)(2,1)S(1)}, u32[]{:S(2)}, u32[]{:S(2)}) collective-permute-start(bf16[4,128,128]{2,1,0:T(8,128)(2,1)S(1)} %get-tuple-element.97), channel_id=1, source_target_pairs={{0,4},{4,0},{8,12},{12,8},{16,20},{20,16},{24,28},{28,24},{1,5},{5... | collective-permute-start | bytes 393224 | tf_op jit(solution)/shard_map/ppermute | solution.py:34
  14.4 1.8 %gradient_terms.6 = bf16[4,512,256]{2,1,0:T(8,128)(2,1)S(1)} custom-call(s32[2]{0:T(128)S(1)} %pad_add_fusion.position_ref.info_ref.place_ref, bf16[512,1024]{1,0:T(8,128)(2,1)S(1)} %get-tuple-element.92.refs_0_, bf16[1024,2048]{1,0:T(8,128)(2,1)S(1)} %copy-done.2), custom_call_target="tpu_custom_call" | custom-call | flops 1000000 | bytes 1 | tf_op jit(solution)/shard_map/gradient_terms/pallas_call | solution.py:124
  16.3 2.3 %fusion.1.query_ref = bf16[1024,512]{1,0:T(8,128)(2,1)S(1)} fusion(bf16[1024,2048]{1,0:T(8,128)(2,1)S(1)} %copy-done.2, bf16[3,2048,512]{2,1,0:T(8,128)(2,1)S(1)} %bitcast.22), kind=kOutput, calls=%fused_computation.3 | convolution fusion | flops 2148007936 | bytes 7340032 | tf_op jit(solution)/shard_map/dot_general | solution.py:440
  21.9 2.4 %fusion.3.grad_ref = f32[1024,512]{1,0:T(8,128)S(1)} fusion(bf16[1024,2048]{1,0:T(8,128)(2,1)S(1)} %copy-done.4, bf16[512,2048]{1,0:T(8,128)(2,1)S(1)} %copy-done), kind=kOutput, calls=%fused_computation.7 | convolution fusion | flops 2147483648 | bytes 8388608 | tf_op jit(solution)/shard_map/dot_general | solution.py:29
  24.4 1.8 %gradient_terms.7 = bf16[4,512,256]{2,1,0:T(8,128)(2,1)S(1)} custom-call(s32[2]{0:T(128)S(1)} %pad_add_fusion.position_ref.info_ref.place_ref, bf16[512,1024]{1,0:T(8,128)(2,1)S(1)} %get-tuple-element.104.refs_0_, bf16[1024,2048]{1,0:T(8,128)(2,1)S(1)} %copy-done.2), custom_call_target="tpu_custom_call" | custom-call | flops 1000000 | bytes 1 | tf_op jit(solution)/shard_map/gradient_terms/pallas_call | solution.py:124
  26.8 2.7 %collective-permute-start.2 = (bf16[4,128,128]{2,1,0:T(8,128)(2,1)S(1)}, bf16[4,128,128]{2,1,0:T(8,128)(2,1)S(1)}, u32[]{:S(2)}, u32[]{:S(2)}) collective-permute-start(bf16[4,128,128]{2,1,0:T(8,128)(2,1)S(1)} %get-tuple-element.109), channel_id=1, source_target_pairs={{0,16},{4,20},{8,24},{12,28},{16,0},{20,4},{24,8},{28,12},{1,17},{... | collective-permute-start | bytes 393224 | tf_op jit(solution)/shard_map/ppermute | solution.py:34
  29.9 4.4 %collective-permute-done.2.refs_1_ = bf16[4,128,128]{2,1,0:T(8,128)(2,1)S(1)} collective-permute-done((bf16[4,128,128]{2,1,0:T(8,128)(2,1)S(1)}, bf16[4,128,128]{2,1,0:T(8,128)(2,1)S(1)}, u32[]{:S(2)}, u32[]{:S(2)}) %collective-permute-start.2) | collective-permute-done | bytes 131104 | tf_op jit(solution)/shard_map/ppermute | solution.py:34
  35.6 4.6 %norm_backward.1 = (bf16[512,1024]{1,0:T(8,128)(2,1)S(1)}, bf16[1024,512]{1,0:T(8,128)(2,1)S(1)}, bf16[512,1024]{1,0:T(8,128)(2,1)S(1)}, f32[4,128,128]{2,1,0:T(8,128)S(1)}, bf16[4,128,128]{2,1,0:T(8,128)(2,1)S(1)}) custom-call(bf16[1024,512]{1,0:T(8,128)(2,1)S(1)} %fusion.1.query_ref, f32[1024,512]{1,0:T(8,128)S(1)} %fusion.3.grad_ref, ...), custom_call_target="tpu_custom_call" | custom-call | flops 4294967296 | bytes 1 | tf_op jit(solution)/shard_map/norm_backward/pallas_call | solution.py:283
  41.9 2.9 %gradient_terms.8 = (bf16[4,512,256]{2,1,0:T(8,128)(2,1)S(1)}, bf16[4,512,256]{2,1,0:T(8,128)(2,1)S(1)}) custom-call(s32[2]{0:T(128)S(1)} %pad_add_fusion.position_ref.info_ref.place_ref, bf16[512,1024]{1,0:T(8,128)(2,1)S(1)} %get-tuple-element.119.refs_0_, bf16[1024,2048]{1,0:T(8,128)(2,1)S(1)} %copy-done.4), custom_call_target="tpu_custom_call" | custom-call | flops 1000000 | bytes 1 | tf_op jit(solution)/shard_map/gradient_terms/pallas_call | solution.py:124
  44.8 3.2 %collective-permute-done.3.got_ref = bf16[4,128,128]{2,1,0:T(8,128)(2,1)S(1)} collective-permute-done((bf16[4,128,128]{2,1,0:T(8,128)(2,1)S(1)}, bf16[4,128,128]{2,1,0:T(8,128)(2,1)S(1)}, u32[]{:S(2)}, u32[]{:S(2)}) %collective-permute-start.3) | collective-permute-done | bytes 131104 | tf_op jit(solution)/shard_map/ppermute | solution.py:34
  49.7 2.9 %gradient_terms.9 = (bf16[4,512,256]{2,1,0:T(8,128)(2,1)S(1)}, bf16[4,512,256]{2,1,0:T(8,128)(2,1)S(1)}) custom-call(s32[2]{0:T(128)S(1)} %pad_add_fusion.position_ref.info_ref.place_ref, bf16[512,1024]{1,0:T(8,128)(2,1)S(1)} %get-tuple-element.128.refs_0_, bf16[1024,2048]{1,0:T(8,128)(2,1)S(1)} %copy-done.2), custom_call_target="tpu_custom_call" | custom-call | flops 1000000 | bytes 1 | tf_op jit(solution)/shard_map/gradient_terms/pallas_call | solution.py:124
  52.6 3.7 %collective-permute-done.6.refs_3_ = bf16[4,512,256]{2,1,0:T(8,128)(2,1)S(1)} collective-permute-done((bf16[4,512,256]{2,1,0:T(8,128)(2,1)S(1)}, bf16[4,512,256]{2,1,0:T(8,128)(2,1)S(1)}, u32[]{:S(2)}, u32[]{:S(2)}) %collective-permute-start.6) | collective-permute-done | bytes 1048608 | tf_op jit(solution)/shard_map/ppermute | solution.py:34
  56.3 4.7 %collective-permute-done.5.refs_3_ = bf16[2,4,128,128]{3,2,1,0:T(8,128)(2,1)S(1)} collective-permute-done((bf16[2,4,128,128]{3,2,1,0:T(8,128)(2,1)S(1)}, bf16[2,4,128,128]{3,2,1,0:T(8,128)(2,1)S(1)}, u32[]{:S(2)}, u32[]{:S(2)}) %collective-permute-start.5) | collective-permute-done | bytes 262176 | tf_op jit(solution)/shard_map/ppermute | solution.py:34
  65.3 3.6 %collective-permute-done.7.refs_4_ = bf16[4,128,128]{2,1,0:T(8,128)(2,1)S(1)} collective-permute-done((bf16[4,128,128]{2,1,0:T(8,128)(2,1)S(1)}, bf16[4,128,128]{2,1,0:T(8,128)(2,1)S(1)}, u32[]{:S(2)}, u32[]{:S(2)}) %collective-permute-start.7) | collective-permute-done | bytes 131104 | tf_op jit(solution)/shard_map/ppermute | solution.py:34
  73.3 1.9 %key_value_grads.1 = (bf16[1024,512]{1,0:T(8,128)(2,1)S(1)}, bf16[1024,512]{1,0:T(8,128)(2,1)S(1)}) custom-call(bf16[1024,512]{1,0:T(8,128)(2,1)S(1)} %get-tuple-element.115.key_ref, bf16[1024,512]{1,0:T(8,128)(2,1)S(1)} %get-tuple-element.116.value_ref, f32[4,128,128]{2,1,0:T(8,128)S(1)} %get-tuple-element.145.mine_ref.grad_ref), custom_call_target="tpu_custom_call" | custom-call | flops 1000000 | bytes 1 | tf_op jit(solution)/shard_map/key_value_grads/pallas_call | solution.py:353
  75.2 8.9 %input_terms.1 = (bf16[2,256,2048]{2,1,0:T(8,128)(2,1)S(1)}, bf16[2,256,2048]{2,1,0:T(8,128)(2,1)S(1)}) custom-call(s32[2]{0:T(128)S(1)} %pad_add_fusion.position_ref.info_ref.place_ref, bf16[1024,512]{1,0:T(8,128)(2,1)S(1)} %get-tuple-element.114.query_ref, bf16[1024,512]{1,0:T(8,128)(2,1)S(1)} %get-tuple-element.146.key_ref, ...), custom_call_target="tpu_custom_call" | custom-call | flops 1000000 | bytes 1 | tf_op jit(solution)/shard_map/input_terms/pallas_call | solution.py:385
  85.3 2.7 %collective-permute-start.15 = (bf16[1,1024,256]{2,1,0:T(8,128)(2,1)S(1)}, bf16[1,1024,256]{2,1,0:T(8,128)(2,1)S(1)}, u32[]{:S(2)}, u32[]{:S(2)}) collective-permute-start(bf16[1,1024,256]{2,1,0:T(8,128)(2,1)S(1)} %get-tuple-element.167), channel_id=1, source_target_pairs={{0,16},{4,20},{8,24},{12,28},{16,0},{20,4},{24,8},{28,12},{1,17},{... | collective-permute-start | bytes 1572872 | tf_op jit(solution)/shard_map/ppermute | solution.py:34
  90.9 20.6 %collective-permute-done.15 = bf16[1,1024,256]{2,1,0:T(8,128)(2,1)S(1)} collective-permute-done((bf16[1,1024,256]{2,1,0:T(8,128)(2,1)S(1)}, bf16[1,1024,256]{2,1,0:T(8,128)(2,1)S(1)}, u32[]{:S(2)}, u32[]{:S(2)}) %collective-permute-start.15) | collective-permute-done | bytes 524320 | tf_op jit(solution)/shard_map/ppermute | solution.py:34
  114.9 15.1 %collective-permute-done.17 = bf16[1,512,256]{2,1,0:T(8,128)(2,1)S(1)} collective-permute-done((bf16[1,512,256]{2,1,0:T(8,128)(2,1)S(1)}, bf16[1,512,256]{2,1,0:T(8,128)(2,1)S(1)}, u32[]{:S(2)}, u32[]{:S(2)}) %collective-permute-start.17) | collective-permute-done | bytes 262176 | tf_op jit(solution)/shard_map/ppermute | solution.py:34
  131.0 3.4 %collective-permute-start.18 = (bf16[1,512,256]{2,1,0:T(8,128)(2,1)S(1)}, bf16[1,512,256]{2,1,0:T(8,128)(2,1)S(1)}, u32[]{:S(2)}, u32[]{:S(2)}) collective-permute-start(bf16[1,512,256]{2,1,0:T(8,128)(2,1)S(1)} %get-tuple-element.176), channel_id=1, source_target_pairs={{0,16},{4,20},{8,24},{12,28},{16,0},{20,4},{24,8},{28,12},{1,17},{... | collective-permute-start | bytes 786440 | tf_op jit(solution)/shard_map/ppermute | solution.py:34
  135.8 9.1 %collective-permute-done.18 = bf16[1,512,256]{2,1,0:T(8,128)(2,1)S(1)} collective-permute-done((bf16[1,512,256]{2,1,0:T(8,128)(2,1)S(1)}, bf16[1,512,256]{2,1,0:T(8,128)(2,1)S(1)}, u32[]{:S(2)}, u32[]{:S(2)}) %collective-permute-start.18) | collective-permute-done | bytes 262176 | tf_op jit(solution)/shard_map/ppermute | solution.py:34
  (58 shorter events, 29.2 us)
Async XLA Ops:
  0.6 21.3 %copy-start = (bf16[512,2048]{1,0:T(8,128)(2,1)S(1)}, bf16[512,2048]{1,0:T(8,128)(2,1)}, u32[]{:S(2)}) copy-start(bf16[512,2048]{1,0:T(8,128)(2,1)} %param.10) | copy-start | bytes 6291460
  11.4 7.2 %collective-permute-start = (bf16[4,128,128]{2,1,0:T(8,128)(2,1)S(1)}, bf16[4,128,128]{2,1,0:T(8,128)(2,1)S(1)}, u32[]{:S(2)}, u32[]{:S(2)}) collective-permute-start(bf16[4,128,128]{2,1,0:T(8,128)(2,1)S(1)} %get-tuple-element.97), channel_id=1, source_target_pairs={{0,4},{4,0},{8,12},{12,8},{16,20},{20,16},{24,28},{28,24},{1,5},{5... | collective-permute-start | bytes 393224 | tf_op jit(solution)/shard_map/ppermute | solution.py:34
  16.3 5.7 %copy-start.4 = (bf16[1024,2048]{1,0:T(8,128)(2,1)S(1)}, bf16[1024,2048]{1,0:T(8,128)(2,1)}, u32[]{:S(2)}) copy-start(bf16[1024,2048]{1,0:T(8,128)(2,1)} %refs_1_.2) | copy-start | bytes 12582916
  19.2 7.0 %collective-permute-start.1 = (bf16[4,128,128]{2,1,0:T(8,128)(2,1)S(1)}, bf16[4,128,128]{2,1,0:T(8,128)(2,1)S(1)}, u32[]{:S(2)}, u32[]{:S(2)}) collective-permute-start(bf16[4,128,128]{2,1,0:T(8,128)(2,1)S(1)} %get-tuple-element.103), channel_id=1, source_target_pairs={{0,8},{4,12},{8,0},{12,4},{16,24},{20,28},{24,16},{28,20},{1,9},{5... | collective-permute-start | bytes 393224 | tf_op jit(solution)/shard_map/ppermute | solution.py:34
  20.9 27.2 %collective-permute-start.4 = (bf16[4,512,256]{2,1,0:T(8,128)(2,1)S(1)}, bf16[4,512,256]{2,1,0:T(8,128)(2,1)S(1)}, u32[]{:S(2)}, u32[]{:S(2)}) collective-permute-start(bf16[4,512,256]{2,1,0:T(8,128)(2,1)S(1)} %gradient_terms.6), channel_id=1, source_target_pairs={{0,4},{4,0},{8,12},{12,8},{16,20},{20,16},{24,28},{28,24},{1,5},{5... | collective-permute-start | bytes 3145736 | tf_op jit(solution)/shard_map/ppermute | solution.py:34
  24.3 5.6 %copy-start.6 = (bf16[512]{0:T(512)(128)(2,1)S(1)}, bf16[512]{0:T(512)(128)(2,1)}, u32[]{:S(2)}) copy-start(bf16[512]{0:T(512)(128)(2,1)} %param.11) | copy-start | bytes 3076
  24.3 11.3 %copy-start.5 = (s32[1024]{0:T(1024)S(1)}, s32[1024]{0:T(1024)}, u32[]{:S(2)}) copy-start(s32[1024]{0:T(1024)} %param.8) | copy-start | bytes 12292
  26.8 7.5 %collective-permute-start.2 = (bf16[4,128,128]{2,1,0:T(8,128)(2,1)S(1)}, bf16[4,128,128]{2,1,0:T(8,128)(2,1)S(1)}, u32[]{:S(2)}, u32[]{:S(2)}) collective-permute-start(bf16[4,128,128]{2,1,0:T(8,128)(2,1)S(1)} %get-tuple-element.109), channel_id=1, source_target_pairs={{0,16},{4,20},{8,24},{12,28},{16,0},{20,4},{24,8},{28,12},{1,17},{... | collective-permute-start | bytes 393224 | tf_op jit(solution)/shard_map/ppermute | solution.py:34
  29.5 26.8 %collective-permute-start.6 = (bf16[4,512,256]{2,1,0:T(8,128)(2,1)S(1)}, bf16[4,512,256]{2,1,0:T(8,128)(2,1)S(1)}, u32[]{:S(2)}, u32[]{:S(2)}) collective-permute-start(bf16[4,512,256]{2,1,0:T(8,128)(2,1)S(1)} %gradient_terms.7), channel_id=1, source_target_pairs={{0,8},{4,12},{8,0},{12,4},{16,24},{20,28},{24,16},{28,20},{1,9},{5... | collective-permute-start | bytes 3145736 | tf_op jit(solution)/shard_map/ppermute | solution.py:34
  40.3 7.8 %collective-permute-start.3 = (bf16[4,128,128]{2,1,0:T(8,128)(2,1)S(1)}, bf16[4,128,128]{2,1,0:T(8,128)(2,1)S(1)}, u32[]{:S(2)}, u32[]{:S(2)}) collective-permute-start(bf16[4,128,128]{2,1,0:T(8,128)(2,1)S(1)} %get-tuple-element.118), channel_id=1, source_target_pairs={{0,4},{4,0},{8,12},{12,8},{16,20},{20,16},{24,28},{28,24},{1,5},{5... | collective-permute-start | bytes 393224 | tf_op jit(solution)/shard_map/ppermute | solution.py:34
  48.7 35.7 %collective-permute-start.8 = (bf16[4,512,256]{2,1,0:T(8,128)(2,1)S(1)}, bf16[4,512,256]{2,1,0:T(8,128)(2,1)S(1)}, u32[]{:S(2)}, u32[]{:S(2)}) collective-permute-start(bf16[4,512,256]{2,1,0:T(8,128)(2,1)S(1)} %get-tuple-element.151), channel_id=1, source_target_pairs={{0,4},{4,0},{8,12},{12,8},{16,20},{20,16},{24,28},{28,24},{1,5},{5... | collective-permute-start | bytes 3145736 | tf_op jit(solution)/shard_map/ppermute | solution.py:34
  49.3 11.7 %collective-permute-start.5 = (bf16[2,4,128,128]{3,2,1,0:T(8,128)(2,1)S(1)}, bf16[2,4,128,128]{3,2,1,0:T(8,128)(2,1)S(1)}, u32[]{:S(2)}, u32[]{:S(2)}) collective-permute-start(bf16[2,4,128,128]{3,2,1,0:T(8,128)(2,1)S(1)} %get-tuple-element.127), channel_id=1, source_target_pairs={{0,8},{4,12},{8,0},{12,4},{16,24},{20,28},{24,16},{28,20},{1,9},{5... | collective-permute-start | bytes 786440 | tf_op jit(solution)/shard_map/ppermute | solution.py:34
  61.6 7.3 %collective-permute-start.7 = (bf16[4,128,128]{2,1,0:T(8,128)(2,1)S(1)}, bf16[4,128,128]{2,1,0:T(8,128)(2,1)S(1)}, u32[]{:S(2)}, u32[]{:S(2)}) collective-permute-start(bf16[4,128,128]{2,1,0:T(8,128)(2,1)S(1)} %get-tuple-element.137), channel_id=1, source_target_pairs={{0,16},{4,20},{8,24},{12,28},{16,0},{20,4},{24,8},{28,12},{1,17},{... | collective-permute-start | bytes 393224 | tf_op jit(solution)/shard_map/ppermute | solution.py:34
  71.6 12.5 %collective-permute-start.9 = (bf16[2,512,256]{2,1,0:T(8,128)(2,1)S(1)}, bf16[2,512,256]{2,1,0:T(8,128)(2,1)S(1)}, u32[]{:S(2)}, u32[]{:S(2)}) collective-permute-start(bf16[2,512,256]{2,1,0:T(8,128)(2,1)S(1)} %get-tuple-element.152), channel_id=1, source_target_pairs={{0,8},{4,12},{8,0},{12,4},{16,24},{20,28},{24,16},{28,20},{1,9},{5... | collective-permute-start | bytes 1572872 | tf_op jit(solution)/shard_map/ppermute | solution.py:34
  71.7 12.4 %collective-permute-start.10 = (bf16[2,512,256]{2,1,0:T(8,128)(2,1)S(1)}, bf16[2,512,256]{2,1,0:T(8,128)(2,1)S(1)}, u32[]{:S(2)}, u32[]{:S(2)}) collective-permute-start(bf16[2,512,256]{2,1,0:T(8,128)(2,1)S(1)} %get-tuple-element.153), channel_id=1, source_target_pairs={{0,4},{4,0},{8,12},{12,8},{16,20},{20,16},{24,28},{28,24},{1,5},{5... | collective-permute-start | bytes 1572872 | tf_op jit(solution)/shard_map/ppermute | solution.py:34
  84.6 4.2 %collective-permute-start.11 = (bf16[2,256,2048]{2,1,0:T(8,128)(2,1)S(1)}, bf16[2,256,2048]{2,1,0:T(8,128)(2,1)S(1)}, u32[]{:S(2)}, u32[]{:S(2)}) collective-permute-start(bf16[2,256,2048]{2,1,0:T(8,128)(2,1)S(1)} %get-tuple-element.160), channel_id=1, source_target_pairs={{0,1},{1,0},{2,3},{3,2},{4,5},{5,4},{6,7},{7,6},{8,9},{9,8},{10,11... | collective-permute-start | bytes 6291464 | tf_op jit(solution)/shard_map/ppermute | solution.py:34
  84.7 26.9 %collective-permute-start.13 = (bf16[4,512,256]{2,1,0:T(8,128)(2,1)S(1)}, bf16[4,512,256]{2,1,0:T(8,128)(2,1)S(1)}, u32[]{:S(2)}, u32[]{:S(2)}) collective-permute-start(bf16[4,512,256]{2,1,0:T(8,128)(2,1)S(1)} %get-tuple-element.165), channel_id=1, source_target_pairs={{0,4},{4,0},{8,12},{12,8},{16,20},{20,16},{24,28},{28,24},{1,5},{5... | collective-permute-start | bytes 3145736 | tf_op jit(solution)/shard_map/ppermute | solution.py:34
  85.3 26.2 %collective-permute-start.15 = (bf16[1,1024,256]{2,1,0:T(8,128)(2,1)S(1)}, bf16[1,1024,256]{2,1,0:T(8,128)(2,1)S(1)}, u32[]{:S(2)}, u32[]{:S(2)}) collective-permute-start(bf16[1,1024,256]{2,1,0:T(8,128)(2,1)S(1)} %get-tuple-element.167), channel_id=1, source_target_pairs={{0,16},{4,20},{8,24},{12,28},{16,0},{20,4},{24,8},{28,12},{1,17},{... | collective-permute-start | bytes 1572872 | tf_op jit(solution)/shard_map/ppermute | solution.py:34
  88.0 23.5 %collective-permute-start.14 = (bf16[2,512,256]{2,1,0:T(8,128)(2,1)S(1)}, bf16[2,512,256]{2,1,0:T(8,128)(2,1)S(1)}, u32[]{:S(2)}, u32[]{:S(2)}) collective-permute-start(bf16[2,512,256]{2,1,0:T(8,128)(2,1)S(1)} %get-tuple-element.166), channel_id=1, source_target_pairs={{0,8},{4,12},{8,0},{12,4},{16,24},{20,28},{24,16},{28,20},{1,9},{5... | collective-permute-start | bytes 1572872 | tf_op jit(solution)/shard_map/ppermute | solution.py:34
  89.4 41.5 %collective-permute-start.12 = (bf16[1,256,2048]{2,1,0:T(8,128)(2,1)S(1)}, bf16[1,256,2048]{2,1,0:T(8,128)(2,1)S(1)}, u32[]{:S(2)}, u32[]{:S(2)}) collective-permute-start(bf16[1,256,2048]{2,1,0:T(8,128)(2,1)S(1)} %get-tuple-element.163), channel_id=1, source_target_pairs={{0,2},{1,3},{2,0},{3,1},{4,6},{5,7},{6,4},{7,5},{8,10},{9,11},{10,... | collective-permute-start | bytes 3145736 | tf_op jit(solution)/shard_map/ppermute | solution.py:34
  111.9 19.0 %collective-permute-start.16 = (bf16[2,512,256]{2,1,0:T(8,128)(2,1)S(1)}, bf16[2,512,256]{2,1,0:T(8,128)(2,1)S(1)}, u32[]{:S(2)}, u32[]{:S(2)}) collective-permute-start(bf16[2,512,256]{2,1,0:T(8,128)(2,1)S(1)} %get-tuple-element.172), channel_id=1, source_target_pairs={{0,8},{4,12},{8,0},{12,4},{16,24},{20,28},{24,16},{28,20},{1,9},{5... | collective-permute-start | bytes 1572872 | tf_op jit(solution)/shard_map/ppermute | solution.py:34
  113.7 16.3 %collective-permute-start.17 = (bf16[1,512,256]{2,1,0:T(8,128)(2,1)S(1)}, bf16[1,512,256]{2,1,0:T(8,128)(2,1)S(1)}, u32[]{:S(2)}, u32[]{:S(2)}) collective-permute-start(bf16[1,512,256]{2,1,0:T(8,128)(2,1)S(1)} %get-tuple-element.173), channel_id=1, source_target_pairs={{0,16},{4,20},{8,24},{12,28},{16,0},{20,4},{24,8},{28,12},{1,17},{... | collective-permute-start | bytes 786440 | tf_op jit(solution)/shard_map/ppermute | solution.py:34
  131.0 13.9 %collective-permute-start.18 = (bf16[1,512,256]{2,1,0:T(8,128)(2,1)S(1)}, bf16[1,512,256]{2,1,0:T(8,128)(2,1)S(1)}, u32[]{:S(2)}, u32[]{:S(2)}) collective-permute-start(bf16[1,512,256]{2,1,0:T(8,128)(2,1)S(1)} %get-tuple-element.176), channel_id=1, source_target_pairs={{0,16},{4,20},{8,24},{12,28},{16,0},{20,4},{24,8},{28,12},{1,17},{... | collective-permute-start | bytes 786440 | tf_op jit(solution)/shard_map/ppermute | solution.py:34
  134.4 12.1 %copy-start.1 = (bf16[512,2048]{1,0:T(8,128)(2,1)S(1)}, bf16[512,2048]{1,0:T(8,128)(2,1)}, u32[]{:S(2)}) copy-start(bf16[512,2048]{1,0:T(8,128)(2,1)} %param.10) | copy-start | bytes 6291460
  (2 other events, 5.1 us)

commit v8 on v7

--- a/solution.py
+++ b/solution.py
@@ -41,44 +41,48 @@
     return order
 
 
-def states_kernel(rows_ref, weight_ref, key_ref, value_ref, state_ref, sent_ref, key_t_ref, value_t_ref):
+def states_kernel(parts, rows_ref, weight_ref, key_ref, value_ref, state_ref, sent_ref, key_t_ref, value_t_ref, copy_ref, held_ref, sems):
     heads = state_ref.shape[0]
-    product = dot(rows_ref[...], weight_ref[0]).astype(bf16)
-
-    @pl.when(pl.program_id(0) == 0)
-    def _():
-        value_ref[...] = product
-        for h in range(heads):
-            columns = slice(h * HD, (h + 1) * HD)
-            value_t_ref[columns, :] = value_ref[:, columns].T
-
-    @pl.when(pl.program_id(0) == 1)
-    def _():
-        key_ref[...] = product
-        for h in range(heads):
-            columns = slice(h * HD, (h + 1) * HD)
-            key_t = key_ref[:, columns].T
-            key_t_ref[columns, :] = key_t
-            state = dot(key_t, value_ref[:, columns])
-            state_ref[h] = state
-            sent_ref[h] = state.astype(bf16)
-
-
-def block_states(rows, weights):
+    step = copy_ref.shape[0] // parts
+    value_copy = pltpu.make_async_copy(weight_ref.at[2], held_ref.at[0], sems.at[0])
+    key_copy = pltpu.make_async_copy(weight_ref.at[1], held_ref.at[1], sems.at[1])
+    row_copies = []
+    for part in range(parts):
+        chunk = pl.ds(part * step, step)
+        row_copies.append(pltpu.make_async_copy(rows_ref.at[chunk], copy_ref.at[chunk], sems.at[2 + part]))
+    value_copy.start()
+    for copy in row_copies:
+        copy.start()
+    key_copy.start()
+    value_copy.wait()
+    for part in range(parts):
+        row_copies[part].wait()
+        chunk = slice(part * step, (part + 1) * step)
+        value_ref[chunk, :] = dot(copy_ref[chunk, :], held_ref[0]).astype(bf16)
+    for h in range(heads):
+        columns = slice(h * HD, (h + 1) * HD)
+        value_t_ref[columns, :] = value_ref[:, columns].T
+    key_copy.wait()
+    key_ref[...] = dot(copy_ref[...], held_ref[1]).astype(bf16)
+    for h in range(heads):
+        columns = slice(h * HD, (h + 1) * HD)
+        key_t = key_ref[:, columns].T
+        key_t_ref[columns, :] = key_t
+        state = dot(key_t, value_ref[:, columns])
+        state_ref[h] = state
+        sent_ref[h] = state.astype(bf16)
+
+
+def block_states(rows, weights, parts=2):
     count, depth = rows.shape
     width = weights.shape[2]
     heads = width // HD
-    full = pl.BlockSpec((count, width), lambda i: (0, 0))
-    full_t = pl.BlockSpec((width, count), lambda i: (0, 0))
-    squares = pl.BlockSpec((heads, HD, HD), lambda i: (0, 0, 0))
-    return pl.pallas_call(
-        states_kernel,
-        grid=(2,),
-        in_specs=[
-            pl.BlockSpec((count, depth), lambda i: (0, 0)),
-            pl.BlockSpec((1, depth, width), lambda i: (2 - i, 0, 0)),
-        ],
-        out_specs=[full, full, squares, squares, full_t, full_t],
+    hbm = pl.BlockSpec(memory_space=pltpu.HBM)
+    vmem = pl.BlockSpec(memory_space=pltpu.VMEM)
+    return pl.pallas_call(
+        functools.partial(states_kernel, parts),
+        in_specs=[hbm, hbm],
+        out_specs=[vmem] * 7,
         out_shape=[
             jax.ShapeDtypeStruct((count, width), bf16),
             jax.ShapeDtypeStruct((count, width), bf16),
@@ -86,8 +90,10 @@
             jax.ShapeDtypeStruct((heads, HD, HD), bf16),
             jax.ShapeDtypeStruct((width, count), bf16),
             jax.ShapeDtypeStruct((width, count), bf16),
+            jax.ShapeDtypeStruct((count, depth), bf16),
         ],
-        compiler_params=params(32),
+        scratch_shapes=[pltpu.VMEM((2, depth, width), bf16), pltpu.SemaphoreType.DMA((2 + parts,))],
+        compiler_params=params(44),
         cost_estimate=COST,
         name="block_states",
     )(rows, weights)
@@ -443,7 +449,7 @@
         outputs = [(0, 0, left.shape[0], slots) for slots in parts]
         return gradient_terms([left], right, info, outputs)
 
-    keys, values, own_state, sent, keys_t, values_t = block_states(layer_input, weights)
+    keys, values, own_state, sent, keys_t, values_t, layer_input = block_states(layer_input, weights)
 
     got = exchange(sent, "seq", 0)
     (value_send,) = terms(values_t, after(layer_input, own_state), order[half:])

time: 147 us -> 145 us (0.986)
  local copies, waits for them, and re-layouts: 5.14 us -> 0.99 us
  starting transfers between devices: 24.9 us -> 22.5 us
  waiting for transfers between devices: 64.9 us -> 67.3 us
  Pallas kernels: 43.7 us -> 46 us
    unnamed x14 -> x12, local copies, waits for them, and re-layouts: 5.14 us -> 0.98 us
    ppermute x19, starting transfers between devices: 24.9 us -> 22.5 us  [exchange(): return lax.ppermute(arr, axis, [(i, i ^ 1 << bit) for i in range(count)])]
    ppermute x19, waiting for transfers between devices: 64.9 us -> 67.3 us  [exchange(): return lax.ppermute(arr, axis, [(i, i ^ 1 << bit) for i in range(count)])]
    pallas_call x1, Pallas kernels: 5.57 us -> 7.89 us  [block_states(): pl.pallas_call(functools.partial(states_kernel, parts), in_specs=[hbm, hb...]
  transfers between devices with their start and end apart: 19 -> 19, of which waited for: 9 -> 10; matrix products, arithmetic and copies ran while one was open for 5% -> 5% of each run, Pallas kernels for 24% -> 25%
where the time goes in v8:
time: 145 us
  waiting for transfers between devices  67.3 us (46%)
  Pallas kernels  46 us (32%)
  starting transfers between devices  22.5 us (16%)
  matrix products  4.72 us (3%)
  other arithmetic  2.28 us (2%)
    ppermute x19, waiting for transfers between devices, exchange(): return lax.ppermute(arr, axis, [(i, i ^ 1 << bit) for i in range(count)])  67.3 us
    ppermute x19, starting transfers between devices, exchange(): return lax.ppermute(arr, axis, [(i, i ^ 1 << bit) for i in range(count)])  22.5 us
    pallas_call x6, Pallas kernels, gradient_terms(): pl.pallas_call(functools.partial(terms_kernel, len(lefts), outputs), in_s...  13.1 us
    pallas_call x1, Pallas kernels, input_terms(): pl.pallas_call(functools.partial(input_kernel, order), grid_spec=pltpu.Pr...  9.12 us
    pallas_call x1, Pallas kernels, block_states(): pl.pallas_call(functools.partial(states_kernel, parts), in_specs=[hbm, hb...  7.89 us
    pallas_call x6, Pallas kernels, small(): pl.pallas_call(kernel, in_specs=[pl.BlockSpec(memory_space=pltpu.SMEM)] +...  5.17 us
    pallas_call x1, Pallas kernels, middle(): pl.pallas_call(middle_kernel, grid=(heads,), in_specs=[column, column, pl...  4.46 us
  transfers between devices with their start and end apart: 19, of which 10 were waited for; matrix products, arithmetic and copies ran while one was open for 5% of the time, Pallas kernels for 25%

profile of v8, /device:TPU:0, one launch (start us, length us, event | category | flops | bytes accessed | tf_op | source)
XLA Modules:
  0.0 144.7 jit_solution(14464453357213468916)
XLA Ops:
  0.7 7.9 %block_states.1 = (bf16[1024,512]{1,0:T(8,128)(2,1)S(1)}, bf16[1024,512]{1,0:T(8,128)(2,1)S(1)}, f32[4,128,128]{2,1,0:T(8,128)S(1)}, bf16[4,128,128]{2,1,0:T(8,1...) custom-call(bf16[1024,2048]{1,0:T(8,128)(2,1)} %rows_ref, ...), custom_call_target="tpu_custom_call" | custom-call | flops 1000000 | bytes 1 | tf_op jit(solution)/shard_map/block_states/pallas_call | solution.py:82
  8.6 3.0 %collective-permute-start = (bf16[4,128,128]{2,1,0:T(8,128)(2,1)S(1)}, bf16[4,128,128]{2,1,0:T(8,128)(2,1)S(1)}, u32[]{:S(2)}, u32[]{:S(2)}) collective-permute-start(bf16[4,128,128]{2,1,0:T(8,128)(2,1)S(1)} %get-tuple-element.99), channel_id=1, source_target_pairs={{0,4},{4,0},{8,12},{12,8},{16,20},{20,16},{24,28},{28,24},{1,5},{5... | collective-permute-start | bytes 393224 | tf_op jit(solution)/shard_map/ppermute | solution.py:34
  11.7 1.8 %gradient_terms.6 = bf16[4,512,256]{2,1,0:T(8,128)(2,1)S(1)} custom-call(s32[2]{0:T(128)S(1)} %pad_add_fusion.position_ref.info_ref.place_ref, bf16[512,1024]{1,0:T(8,128)(2,1)S(1)} %get-tuple-element.94.refs_0_, bf16[1024,2048]{1,0:T(8,128)(2,1)S(1)} %get-tuple-element.141.refs_1_), custom_call_target="tpu_custom_call" | custom-call | flops 1000000 | bytes 1 | tf_op jit(solution)/shard_map/gradient_terms/pallas_call | solution.py:130
  14.4 2.3 %fusion.1.query_ref = bf16[1024,512]{1,0:T(8,128)(2,1)S(1)} fusion(bf16[1024,2048]{1,0:T(8,128)(2,1)S(1)} %get-tuple-element.141.refs_1_, bf16[3,2048,512]{2,1,0:T(8,128)(2,1)S(1)} %bitcast.22), kind=kOutput, calls=%fused_computation.3 | convolution fusion | flops 2148007936 | bytes 7340032 | tf_op jit(solution)/shard_map/dot_general | solution.py:446
  19.5 2.4 %fusion.3.grad_ref = f32[1024,512]{1,0:T(8,128)S(1)} fusion(bf16[1024,2048]{1,0:T(8,128)(2,1)S(1)} %copy-done.3, bf16[512,2048]{1,0:T(8,128)(2,1)S(1)} %copy-done), kind=kOutput, calls=%fused_computation.7 | convolution fusion | flops 2147483648 | bytes 8388608 | tf_op jit(solution)/shard_map/dot_general | solution.py:29
  22.0 1.8 %gradient_terms.7 = bf16[4,512,256]{2,1,0:T(8,128)(2,1)S(1)} custom-call(s32[2]{0:T(128)S(1)} %pad_add_fusion.position_ref.info_ref.place_ref, bf16[512,1024]{1,0:T(8,128)(2,1)S(1)} %get-tuple-element.106.refs_0_, bf16[1024,2048]{1,0:T(8,128)(2,1)S(1)} %get-tuple-element.141.refs_1_), custom_call_target="tpu_custom_call" | custom-call | flops 1000000 | bytes 1 | tf_op jit(solution)/shard_map/gradient_terms/pallas_call | solution.py:130
  24.4 2.7 %collective-permute-start.2 = (bf16[4,128,128]{2,1,0:T(8,128)(2,1)S(1)}, bf16[4,128,128]{2,1,0:T(8,128)(2,1)S(1)}, u32[]{:S(2)}, u32[]{:S(2)}) collective-permute-start(bf16[4,128,128]{2,1,0:T(8,128)(2,1)S(1)} %get-tuple-element.111), channel_id=1, source_target_pairs={{0,16},{4,20},{8,24},{12,28},{16,0},{20,4},{24,8},{28,12},{1,17},{... | collective-permute-start | bytes 393224 | tf_op jit(solution)/shard_map/ppermute | solution.py:34
  27.5 5.0 %collective-permute-done.2.refs_1_ = bf16[4,128,128]{2,1,0:T(8,128)(2,1)S(1)} collective-permute-done((bf16[4,128,128]{2,1,0:T(8,128)(2,1)S(1)}, bf16[4,128,128]{2,1,0:T(8,128)(2,1)S(1)}, u32[]{:S(2)}, u32[]{:S(2)}) %collective-permute-start.2) | collective-permute-done | bytes 131104 | tf_op jit(solution)/shard_map/ppermute | solution.py:34
  33.8 4.5 %norm_backward.1 = (bf16[512,1024]{1,0:T(8,128)(2,1)S(1)}, bf16[1024,512]{1,0:T(8,128)(2,1)S(1)}, bf16[512,1024]{1,0:T(8,128)(2,1)S(1)}, f32[4,128,128]{2,1,0:T(8,128)S(1)}, bf16[4,128,128]{2,1,0:T(8,128)(2,1)S(1)}) custom-call(bf16[1024,512]{1,0:T(8,128)(2,1)S(1)} %fusion.1.query_ref, f32[1024,512]{1,0:T(8,128)S(1)} %fusion.3.grad_ref, ...), custom_call_target="tpu_custom_call" | custom-call | flops 4294967296 | bytes 1 | tf_op jit(solution)/shard_map/norm_backward/pallas_call | solution.py:289
  39.9 2.9 %gradient_terms.8 = (bf16[4,512,256]{2,1,0:T(8,128)(2,1)S(1)}, bf16[4,512,256]{2,1,0:T(8,128)(2,1)S(1)}) custom-call(s32[2]{0:T(128)S(1)} %pad_add_fusion.position_ref.info_ref.place_ref, bf16[512,1024]{1,0:T(8,128)(2,1)S(1)} %get-tuple-element.121.refs_0_, bf16[1024,2048]{1,0:T(8,128)(2,1)S(1)} %copy-done.3), custom_call_target="tpu_custom_call" | custom-call | flops 1000000 | bytes 1 | tf_op jit(solution)/shard_map/gradient_terms/pallas_call | solution.py:130
  42.8 3.4 %collective-permute-done.3.got_ref = bf16[4,128,128]{2,1,0:T(8,128)(2,1)S(1)} collective-permute-done((bf16[4,128,128]{2,1,0:T(8,128)(2,1)S(1)}, bf16[4,128,128]{2,1,0:T(8,128)(2,1)S(1)}, u32[]{:S(2)}, u32[]{:S(2)}) %collective-permute-start.3) | collective-permute-done | bytes 131104 | tf_op jit(solution)/shard_map/ppermute | solution.py:34
  47.8 2.9 %gradient_terms.9 = (bf16[4,512,256]{2,1,0:T(8,128)(2,1)S(1)}, bf16[4,512,256]{2,1,0:T(8,128)(2,1)S(1)}) custom-call(s32[2]{0:T(128)S(1)} %pad_add_fusion.position_ref.info_ref.place_ref, bf16[512,1024]{1,0:T(8,128)(2,1)S(1)} %get-tuple-element.130.refs_0_, bf16[1024,2048]{1,0:T(8,128)(2,1)S(1)} %get-tuple-element.141.refs_1_), custom_call_target="tpu_custom_call" | custom-call | flops 1000000 | bytes 1 | tf_op jit(solution)/shard_map/gradient_terms/pallas_call | solution.py:130
  50.7 3.8 %collective-permute-done.6.refs_3_ = bf16[4,512,256]{2,1,0:T(8,128)(2,1)S(1)} collective-permute-done((bf16[4,512,256]{2,1,0:T(8,128)(2,1)S(1)}, bf16[4,512,256]{2,1,0:T(8,128)(2,1)S(1)}, u32[]{:S(2)}, u32[]{:S(2)}) %collective-permute-start.6) | collective-permute-done | bytes 1048608 | tf_op jit(solution)/shard_map/ppermute | solution.py:34
  54.6 4.6 %collective-permute-done.5.refs_3_ = bf16[2,4,128,128]{3,2,1,0:T(8,128)(2,1)S(1)} collective-permute-done((bf16[2,4,128,128]{3,2,1,0:T(8,128)(2,1)S(1)}, bf16[2,4,128,128]{3,2,1,0:T(8,128)(2,1)S(1)}, u32[]{:S(2)}, u32[]{:S(2)}) %collective-permute-start.5) | collective-permute-done | bytes 262176 | tf_op jit(solution)/shard_map/ppermute | solution.py:34
  59.8 1.8 %gradient_terms.10.refs_0_ = bf16[4,512,256]{2,1,0:T(8,128)(2,1)S(1)} custom-call(s32[2]{0:T(128)S(1)} %pad_add_fusion.position_ref.info_ref.place_ref, bf16[512,1024]{1,0:T(8,128)(2,1)S(1)} %get-tuple-element.94.refs_0_, bf16[1024,2048]{1,0:T(8,128)(2,1)S(1)} %get-tuple-element.141.refs_1_), custom_call_target="tpu_custom_call" | custom-call | flops 1000000 | bytes 1 | tf_op jit(solution)/shard_map/gradient_terms/pallas_call | solution.py:130
  61.7 1.8 %gradient_terms.11.refs_2_ = bf16[4,512,256]{2,1,0:T(8,128)(2,1)S(1)} custom-call(s32[2]{0:T(128)S(1)} %pad_add_fusion.position_ref.info_ref.place_ref, bf16[512,1024]{1,0:T(8,128)(2,1)S(1)} %get-tuple-element.106.refs_0_, bf16[1024,2048]{1,0:T(8,128)(2,1)S(1)} %get-tuple-element.141.refs_1_), custom_call_target="tpu_custom_call" | custom-call | flops 1000000 | bytes 1 | tf_op jit(solution)/shard_map/gradient_terms/pallas_call | solution.py:130
  63.5 3.5 %collective-permute-done.7.refs_4_ = bf16[4,128,128]{2,1,0:T(8,128)(2,1)S(1)} collective-permute-done((bf16[4,128,128]{2,1,0:T(8,128)(2,1)S(1)}, bf16[4,128,128]{2,1,0:T(8,128)(2,1)S(1)}, u32[]{:S(2)}, u32[]{:S(2)}) %collective-permute-start.7) | collective-permute-done | bytes 131104 | tf_op jit(solution)/shard_map/ppermute | solution.py:34
  69.8 1.7 %collective-permute-start.10 = (bf16[2,512,256]{2,1,0:T(8,128)(2,1)S(1)}, bf16[2,512,256]{2,1,0:T(8,128)(2,1)S(1)}, u32[]{:S(2)}, u32[]{:S(2)}) collective-permute-start(bf16[2,512,256]{2,1,0:T(8,128)(2,1)S(1)} %get-tuple-element.155), channel_id=1, source_target_pairs={{0,4},{4,0},{8,12},{12,8},{16,20},{20,16},{24,28},{28,24},{1,5},{5... | collective-permute-start | bytes 1572872 | tf_op jit(solution)/shard_map/ppermute | solution.py:34
  71.4 1.9 %key_value_grads.1 = (bf16[1024,512]{1,0:T(8,128)(2,1)S(1)}, bf16[1024,512]{1,0:T(8,128)(2,1)S(1)}) custom-call(bf16[1024,512]{1,0:T(8,128)(2,1)S(1)} %get-tuple-element.117.key_ref, bf16[1024,512]{1,0:T(8,128)(2,1)S(1)} %get-tuple-element.118.value_ref, f32[4,128,128]{2,1,0:T(8,128)S(1)} %get-tuple-element.147.mine_ref.grad_ref), custom_call_target="tpu_custom_call" | custom-call | flops 1000000 | bytes 1 | tf_op jit(solution)/shard_map/key_value_grads/pallas_call | solution.py:359
  73.3 9.1 %input_terms.1 = (bf16[2,256,2048]{2,1,0:T(8,128)(2,1)S(1)}, bf16[2,256,2048]{2,1,0:T(8,128)(2,1)S(1)}) custom-call(s32[2]{0:T(128)S(1)} %pad_add_fusion.position_ref.info_ref.place_ref, bf16[1024,512]{1,0:T(8,128)(2,1)S(1)} %get-tuple-element.116.query_ref, bf16[1024,512]{1,0:T(8,128)(2,1)S(1)} %get-tuple-element.148.key_ref, ...), custom_call_target="tpu_custom_call" | custom-call | flops 1000000 | bytes 1 | tf_op jit(solution)/shard_map/input_terms/pallas_call | solution.py:391
  89.3 21.2 %collective-permute-done.15 = bf16[1,1024,256]{2,1,0:T(8,128)(2,1)S(1)} collective-permute-done((bf16[1,1024,256]{2,1,0:T(8,128)(2,1)S(1)}, bf16[1,1024,256]{2,1,0:T(8,128)(2,1)S(1)}, u32[]{:S(2)}, u32[]{:S(2)}) %collective-permute-start.15) | collective-permute-done | bytes 524320 | tf_op jit(solution)/shard_map/ppermute | solution.py:34
  113.1 14.9 %collective-permute-done.17 = bf16[1,512,256]{2,1,0:T(8,128)(2,1)S(1)} collective-permute-done((bf16[1,512,256]{2,1,0:T(8,128)(2,1)S(1)}, bf16[1,512,256]{2,1,0:T(8,128)(2,1)S(1)}, u32[]{:S(2)}, u32[]{:S(2)}) %collective-permute-start.17) | collective-permute-done | bytes 262176 | tf_op jit(solution)/shard_map/ppermute | solution.py:34
  129.8 2.6 %collective-permute-start.18 = (bf16[1,512,256]{2,1,0:T(8,128)(2,1)S(1)}, bf16[1,512,256]{2,1,0:T(8,128)(2,1)S(1)}, u32[]{:S(2)}, u32[]{:S(2)}) collective-permute-start(bf16[1,512,256]{2,1,0:T(8,128)(2,1)S(1)} %get-tuple-element.178), channel_id=1, source_target_pairs={{0,16},{4,20},{8,24},{12,28},{16,0},{20,4},{24,8},{28,12},{1,17},{... | collective-permute-start | bytes 786440 | tf_op jit(solution)/shard_map/ppermute | solution.py:34
  133.8 9.3 %collective-permute-done.18 = bf16[1,512,256]{2,1,0:T(8,128)(2,1)S(1)} collective-permute-done((bf16[1,512,256]{2,1,0:T(8,128)(2,1)S(1)}, bf16[1,512,256]{2,1,0:T(8,128)(2,1)S(1)}, u32[]{:S(2)}, u32[]{:S(2)}) %collective-permute-start.18) | collective-permute-done | bytes 262176 | tf_op jit(solution)/shard_map/ppermute | solution.py:34
  (56 shorter events, 27.0 us)
Async XLA Ops:
  0.6 18.9 %copy-start = (bf16[512,2048]{1,0:T(8,128)(2,1)S(1)}, bf16[512,2048]{1,0:T(8,128)(2,1)}, u32[]{:S(2)}) copy-start(bf16[512,2048]{1,0:T(8,128)(2,1)} %param.10) | copy-start | bytes 6291460
  8.6 8.2 %collective-permute-start = (bf16[4,128,128]{2,1,0:T(8,128)(2,1)S(1)}, bf16[4,128,128]{2,1,0:T(8,128)(2,1)S(1)}, u32[]{:S(2)}, u32[]{:S(2)}) collective-permute-start(bf16[4,128,128]{2,1,0:T(8,128)(2,1)S(1)} %get-tuple-element.99), channel_id=1, source_target_pairs={{0,4},{4,0},{8,12},{12,8},{16,20},{20,16},{24,28},{28,24},{1,5},{5... | collective-permute-start | bytes 393224 | tf_op jit(solution)/shard_map/ppermute | solution.py:34
  14.4 5.1 %copy-start.3 = (bf16[1024,2048]{1,0:T(8,128)(2,1)S(1)}, bf16[1024,2048]{1,0:T(8,128)(2,1)}, u32[]{:S(2)}) copy-start(bf16[1024,2048]{1,0:T(8,128)(2,1)} %refs_1_) | copy-start | bytes 12582916
  17.4 6.4 %collective-permute-start.1 = (bf16[4,128,128]{2,1,0:T(8,128)(2,1)S(1)}, bf16[4,128,128]{2,1,0:T(8,128)(2,1)S(1)}, u32[]{:S(2)}, u32[]{:S(2)}) collective-permute-start(bf16[4,128,128]{2,1,0:T(8,128)(2,1)S(1)} %get-tuple-element.105), channel_id=1, source_target_pairs={{0,8},{4,12},{8,0},{12,4},{16,24},{20,28},{24,16},{28,20},{1,9},{5... | collective-permute-start | bytes 393224 | tf_op jit(solution)/shard_map/ppermute | solution.py:34
  19.0 27.2 %collective-permute-start.4 = (bf16[4,512,256]{2,1,0:T(8,128)(2,1)S(1)}, bf16[4,512,256]{2,1,0:T(8,128)(2,1)S(1)}, u32[]{:S(2)}, u32[]{:S(2)}) collective-permute-start(bf16[4,512,256]{2,1,0:T(8,128)(2,1)S(1)} %gradient_terms.6), channel_id=1, source_target_pairs={{0,4},{4,0},{8,12},{12,8},{16,20},{20,16},{24,28},{28,24},{1,5},{5... | collective-permute-start | bytes 3145736 | tf_op jit(solution)/shard_map/ppermute | solution.py:34
  21.9 5.6 %copy-start.5 = (bf16[512]{0:T(512)(128)(2,1)S(1)}, bf16[512]{0:T(512)(128)(2,1)}, u32[]{:S(2)}) copy-start(bf16[512]{0:T(512)(128)(2,1)} %param.11) | copy-start | bytes 3076
  21.9 11.9 %copy-start.4 = (s32[1024]{0:T(1024)S(1)}, s32[1024]{0:T(1024)}, u32[]{:S(2)}) copy-start(s32[1024]{0:T(1024)} %param.8) | copy-start | bytes 12292
  24.4 8.1 %collective-permute-start.2 = (bf16[4,128,128]{2,1,0:T(8,128)(2,1)S(1)}, bf16[4,128,128]{2,1,0:T(8,128)(2,1)S(1)}, u32[]{:S(2)}, u32[]{:S(2)}) collective-permute-start(bf16[4,128,128]{2,1,0:T(8,128)(2,1)S(1)} %get-tuple-element.111), channel_id=1, source_target_pairs={{0,16},{4,20},{8,24},{12,28},{16,0},{20,4},{24,8},{28,12},{1,17},{... | collective-permute-start | bytes 393224 | tf_op jit(solution)/shard_map/ppermute | solution.py:34
  27.1 27.5 %collective-permute-start.6 = (bf16[4,512,256]{2,1,0:T(8,128)(2,1)S(1)}, bf16[4,512,256]{2,1,0:T(8,128)(2,1)S(1)}, u32[]{:S(2)}, u32[]{:S(2)}) collective-permute-start(bf16[4,512,256]{2,1,0:T(8,128)(2,1)S(1)} %gradient_terms.7), channel_id=1, source_target_pairs={{0,8},{4,12},{8,0},{12,4},{16,24},{20,28},{24,16},{28,20},{1,9},{5... | collective-permute-start | bytes 3145736 | tf_op jit(solution)/shard_map/ppermute | solution.py:34
  38.3 7.9 %collective-permute-start.3 = (bf16[4,128,128]{2,1,0:T(8,128)(2,1)S(1)}, bf16[4,128,128]{2,1,0:T(8,128)(2,1)S(1)}, u32[]{:S(2)}, u32[]{:S(2)}) collective-permute-start(bf16[4,128,128]{2,1,0:T(8,128)(2,1)S(1)} %get-tuple-element.120), channel_id=1, source_target_pairs={{0,4},{4,0},{8,12},{12,8},{16,20},{20,16},{24,28},{28,24},{1,5},{5... | collective-permute-start | bytes 393224 | tf_op jit(solution)/shard_map/ppermute | solution.py:34
  46.9 35.9 %collective-permute-start.8 = (bf16[4,512,256]{2,1,0:T(8,128)(2,1)S(1)}, bf16[4,512,256]{2,1,0:T(8,128)(2,1)S(1)}, u32[]{:S(2)}, u32[]{:S(2)}) collective-permute-start(bf16[4,512,256]{2,1,0:T(8,128)(2,1)S(1)} %get-tuple-element.153), channel_id=1, source_target_pairs={{0,4},{4,0},{8,12},{12,8},{16,20},{20,16},{24,28},{28,24},{1,5},{5... | collective-permute-start | bytes 3145736 | tf_op jit(solution)/shard_map/ppermute | solution.py:34
  47.4 11.7 %collective-permute-start.5 = (bf16[2,4,128,128]{3,2,1,0:T(8,128)(2,1)S(1)}, bf16[2,4,128,128]{3,2,1,0:T(8,128)(2,1)S(1)}, u32[]{:S(2)}, u32[]{:S(2)}) collective-permute-start(bf16[2,4,128,128]{3,2,1,0:T(8,128)(2,1)S(1)} %get-tuple-element.129), channel_id=1, source_target_pairs={{0,8},{4,12},{8,0},{12,4},{16,24},{20,28},{24,16},{28,20},{1,9},{5... | collective-permute-start | bytes 786440 | tf_op jit(solution)/shard_map/ppermute | solution.py:34
  59.8 7.3 %collective-permute-start.7 = (bf16[4,128,128]{2,1,0:T(8,128)(2,1)S(1)}, bf16[4,128,128]{2,1,0:T(8,128)(2,1)S(1)}, u32[]{:S(2)}, u32[]{:S(2)}) collective-permute-start(bf16[4,128,128]{2,1,0:T(8,128)(2,1)S(1)} %get-tuple-element.139), channel_id=1, source_target_pairs={{0,16},{4,20},{8,24},{12,28},{16,0},{20,4},{24,8},{28,12},{1,17},{... | collective-permute-start | bytes 393224 | tf_op jit(solution)/shard_map/ppermute | solution.py:34
  69.7 12.8 %collective-permute-start.9 = (bf16[2,512,256]{2,1,0:T(8,128)(2,1)S(1)}, bf16[2,512,256]{2,1,0:T(8,128)(2,1)S(1)}, u32[]{:S(2)}, u32[]{:S(2)}) collective-permute-start(bf16[2,512,256]{2,1,0:T(8,128)(2,1)S(1)} %get-tuple-element.154), channel_id=1, source_target_pairs={{0,8},{4,12},{8,0},{12,4},{16,24},{20,28},{24,16},{28,20},{1,9},{5... | collective-permute-start | bytes 1572872 | tf_op jit(solution)/shard_map/ppermute | solution.py:34
  69.8 12.7 %collective-permute-start.10 = (bf16[2,512,256]{2,1,0:T(8,128)(2,1)S(1)}, bf16[2,512,256]{2,1,0:T(8,128)(2,1)S(1)}, u32[]{:S(2)}, u32[]{:S(2)}) collective-permute-start(bf16[2,512,256]{2,1,0:T(8,128)(2,1)S(1)} %get-tuple-element.155), channel_id=1, source_target_pairs={{0,4},{4,0},{8,12},{12,8},{16,20},{20,16},{24,28},{28,24},{1,5},{5... | collective-permute-start | bytes 1572872 | tf_op jit(solution)/shard_map/ppermute | solution.py:34
  83.0 4.2 %collective-permute-start.11 = (bf16[2,256,2048]{2,1,0:T(8,128)(2,1)S(1)}, bf16[2,256,2048]{2,1,0:T(8,128)(2,1)S(1)}, u32[]{:S(2)}, u32[]{:S(2)}) collective-permute-start(bf16[2,256,2048]{2,1,0:T(8,128)(2,1)S(1)} %get-tuple-element.162), channel_id=1, source_target_pairs={{0,1},{1,0},{2,3},{3,2},{4,5},{5,4},{6,7},{7,6},{8,9},{9,8},{10,11... | collective-permute-start | bytes 6291464 | tf_op jit(solution)/shard_map/ppermute | solution.py:34
  83.1 27.5 %collective-permute-start.13 = (bf16[4,512,256]{2,1,0:T(8,128)(2,1)S(1)}, bf16[4,512,256]{2,1,0:T(8,128)(2,1)S(1)}, u32[]{:S(2)}, u32[]{:S(2)}) collective-permute-start(bf16[4,512,256]{2,1,0:T(8,128)(2,1)S(1)} %get-tuple-element.167), channel_id=1, source_target_pairs={{0,4},{4,0},{8,12},{12,8},{16,20},{20,16},{24,28},{28,24},{1,5},{5... | collective-permute-start | bytes 3145736 | tf_op jit(solution)/shard_map/ppermute | solution.py:34
  84.3 26.1 %collective-permute-start.15 = (bf16[1,1024,256]{2,1,0:T(8,128)(2,1)S(1)}, bf16[1,1024,256]{2,1,0:T(8,128)(2,1)S(1)}, u32[]{:S(2)}, u32[]{:S(2)}) collective-permute-start(bf16[1,1024,256]{2,1,0:T(8,128)(2,1)S(1)} %get-tuple-element.169), channel_id=1, source_target_pairs={{0,16},{4,20},{8,24},{12,28},{16,0},{20,4},{24,8},{28,12},{1,17},{... | collective-permute-start | bytes 1572872 | tf_op jit(solution)/shard_map/ppermute | solution.py:34
  86.0 24.4 %collective-permute-start.14 = (bf16[2,512,256]{2,1,0:T(8,128)(2,1)S(1)}, bf16[2,512,256]{2,1,0:T(8,128)(2,1)S(1)}, u32[]{:S(2)}, u32[]{:S(2)}) collective-permute-start(bf16[2,512,256]{2,1,0:T(8,128)(2,1)S(1)} %get-tuple-element.168), channel_id=1, source_target_pairs={{0,8},{4,12},{8,0},{12,4},{16,24},{20,28},{24,16},{28,20},{1,9},{5... | collective-permute-start | bytes 1572872 | tf_op jit(solution)/shard_map/ppermute | solution.py:34
  87.7 42.0 %collective-permute-start.12 = (bf16[1,256,2048]{2,1,0:T(8,128)(2,1)S(1)}, bf16[1,256,2048]{2,1,0:T(8,128)(2,1)S(1)}, u32[]{:S(2)}, u32[]{:S(2)}) collective-permute-start(bf16[1,256,2048]{2,1,0:T(8,128)(2,1)S(1)} %get-tuple-element.165), channel_id=1, source_target_pairs={{0,2},{1,3},{2,0},{3,1},{4,6},{5,7},{6,4},{7,5},{8,10},{9,11},{10,... | collective-permute-start | bytes 3145736 | tf_op jit(solution)/shard_map/ppermute | solution.py:34
  110.8 18.8 %collective-permute-start.16 = (bf16[2,512,256]{2,1,0:T(8,128)(2,1)S(1)}, bf16[2,512,256]{2,1,0:T(8,128)(2,1)S(1)}, u32[]{:S(2)}, u32[]{:S(2)}) collective-permute-start(bf16[2,512,256]{2,1,0:T(8,128)(2,1)S(1)} %get-tuple-element.174), channel_id=1, source_target_pairs={{0,8},{4,12},{8,0},{12,4},{16,24},{20,28},{24,16},{28,20},{1,9},{5... | collective-permute-start | bytes 1572872 | tf_op jit(solution)/shard_map/ppermute | solution.py:34
  111.7 16.3 %collective-permute-start.17 = (bf16[1,512,256]{2,1,0:T(8,128)(2,1)S(1)}, bf16[1,512,256]{2,1,0:T(8,128)(2,1)S(1)}, u32[]{:S(2)}, u32[]{:S(2)}) collective-permute-start(bf16[1,512,256]{2,1,0:T(8,128)(2,1)S(1)} %get-tuple-element.175), channel_id=1, source_target_pairs={{0,16},{4,20},{8,24},{12,28},{16,0},{20,4},{24,8},{28,12},{1,17},{... | collective-permute-start | bytes 786440 | tf_op jit(solution)/shard_map/ppermute | solution.py:34
  129.8 13.3 %collective-permute-start.18 = (bf16[1,512,256]{2,1,0:T(8,128)(2,1)S(1)}, bf16[1,512,256]{2,1,0:T(8,128)(2,1)S(1)}, u32[]{:S(2)}, u32[]{:S(2)}) collective-permute-start(bf16[1,512,256]{2,1,0:T(8,128)(2,1)S(1)} %get-tuple-element.178), channel_id=1, source_target_pairs={{0,16},{4,20},{8,24},{12,28},{16,0},{20,4},{24,8},{28,12},{1,17},{... | collective-permute-start | bytes 786440 | tf_op jit(solution)/shard_map/ppermute | solution.py:34
  132.5 12.3 %copy-start.1 = (bf16[512,2048]{1,0:T(8,128)(2,1)S(1)}, bf16[512,2048]{1,0:T(8,128)(2,1)}, u32[]{:S(2)}) copy-start(bf16[512,2048]{1,0:T(8,128)(2,1)} %param.10) | copy-start | bytes 6291460
  (1 other events, 2.8 us)

commit v9 on v8

--- a/solution.py
+++ b/solution.py
@@ -449,6 +449,14 @@
         outputs = [(0, 0, left.shape[0], slots) for slots in parts]
         return gradient_terms([left], right, info, outputs)
 
+    side = proj_weight.shape[2] // 2
+
+    def both_terms(left, right):
+        outputs = []
+        for low, slots in ((0, order), (side, swapped)):
+            outputs += [(0, low, low + side, slots[:half]), (0, low, low + side, slots[half:])]
+        return gradient_terms([left], right, info, outputs)
+
     keys, values, own_state, sent, keys_t, values_t, layer_input = block_states(layer_input, weights)
 
     got = exchange(sent, "seq", 0)
@@ -480,15 +488,15 @@
     out_got = exchange(after(out_send, total), "seq", 0)
 
     got = exchange(sent, "seq", 1)
-    query_keep, query_send = terms(query_grad_t, after(layer_input, total), order[:half], order[half:])
-    got = after(got, query_keep, key_got)
+    first_keep, first_send, second_keep, second_send = both_terms(query_grad_t, after(layer_input, total))
+    got = after(got, first_keep, key_got)
     suffix = suffix_step(info, 1, [total, mine, mate, got])
-    query_got = exchange(after(query_send, suffix[0]), "seq", 0)
 
     for bit in stages[2:]:
         got = exchange(suffix[4], "seq", bit)
         if bit == 2:
             (value_keep,) = terms(values_t, after(layer_input, suffix[0]), order[:half])
+            second_got = exchange(after(second_send, value_keep), "seq", 1)
             (key_keep,) = terms(keys_t, after(layer_input, value_keep), swapped[:half])
             got = after(got, key_keep)
         suffix = suffix_step(info, bit, list(suffix[:4]) + [got])
@@ -501,9 +509,6 @@
     key_got = exchange(key_send, "seq", 0)
 
     key_grad, value_grad = key_value_grads(keys, values, after(mine, value_keep))
-    grads = (query_grad, key_grad, value_grad)
-    input_keep, input_send = input_terms(grads, weights, info, head_order, 0, 1)
-
     def stage(keep, got, token, bit, axis="seq"):
         keep, send = sums([(keep, after(got, token))])
         return keep, exchange(send, axis, bit)
@@ -513,16 +518,23 @@
             keep, got = stage(keep, got, keep, bit)
         return keep[0], got[0]
 
+    second_keep, second_got = stage(second_keep, second_got, key_grad, 0)
+    grads = after((query_grad, key_grad, value_grad), second_keep)
+    input_keep, input_send = input_terms(grads, weights, info, head_order, 0, 1)
     value_got, key_got = after((value_got, key_got), input_keep)
+    key_half = key_keep
     late_keep, late_send = sums([(value_keep, value_got), (key_keep, key_got)], merge=True)
     late_got = exchange(late_send, "seq", 2)
     out_keep, out_got = stage(out_keep, out_got, late_keep, 1)
+    first_got = exchange(after(first_send, key_half), "seq", 0)
     input_got = exchange(after(input_send, out_keep), "head", 0)
     for bit in range(1, head_bits):
         input_keep, input_got = stage(input_keep, input_got, out_keep, bit, "head")
     out_keep, out_got = stage(out_keep, out_got, (input_keep, late_got), 2)
-    query_keep, query_got = stage(query_keep, query_got, out_keep, 1)
-    query_keep, query_got = stage(query_keep, query_got, (query_keep, out_got, input_got), 2)
+    first_keep, first_got = stage(first_keep, first_got, out_keep, 1)
+    first_got = after(first_got, first_keep, out_got)
+    query_keep, query_send = sums([(first_keep, first_got), (second_keep, second_got)], merge=True)
+    query_got = exchange(query_send, "seq", 2)
 
     out_pair = rest(out_keep, out_got, stages[3:])
     late_pair = rest(late_keep, late_got, stages[3:])

time: 145 us -> 145 us (level)
    ppermute x19 -> x21, starting transfers between devices: 22.5 us -> 23.9 us  [exchange(): return lax.ppermute(arr, axis, [(i, i ^ 1 << bit) for i in range(count)])]
    ppermute x19 -> x21, waiting for transfers between devices: 67.3 us -> 66.5 us  [exchange(): return lax.ppermute(arr, axis, [(i, i ^ 1 << bit) for i in range(count)])]
  transfers between devices with their start and end apart: 19 -> 21, of which waited for: 10 -> 13; matrix products, arithmetic and copies ran while one was open for 5% -> 4% of each run, Pallas kernels for 25% -> 26%
where the time goes in v9:
time: 145 us
  waiting for transfers between devices  66.5 us (46%)
  Pallas kernels  46 us (32%)
  starting transfers between devices  23.9 us (16%)
  matrix products  4.72 us (3%)
  other arithmetic  2.28 us (2%)
    ppermute x21, waiting for transfers between devices, exchange(): return lax.ppermute(arr, axis, [(i, i ^ 1 << bit) for i in range(count)])  66.5 us
    ppermute x21, starting transfers between devices, exchange(): return lax.ppermute(arr, axis, [(i, i ^ 1 << bit) for i in range(count)])  23.9 us
    pallas_call x6, Pallas kernels, gradient_terms(): pl.pallas_call(functools.partial(terms_kernel, len(lefts), outputs), in_s...  13.1 us
    pallas_call x1, Pallas kernels, input_terms(): pl.pallas_call(functools.partial(input_kernel, order), grid_spec=pltpu.Pr...  9.12 us
    pallas_call x1, Pallas kernels, block_states(): pl.pallas_call(functools.partial(states_kernel, parts), in_specs=[hbm, hb...  7.89 us
    pallas_call x6, Pallas kernels, small(): pl.pallas_call(kernel, in_specs=[pl.BlockSpec(memory_space=pltpu.SMEM)] +...  5.17 us
    pallas_call x1, Pallas kernels, middle(): pl.pallas_call(middle_kernel, grid=(heads,), in_specs=[column, column, pl...  4.46 us
  transfers between devices with their start and end apart: 21, of which 13 were waited for; matrix products, arithmetic and copies ran while one was open for 4% of the time, Pallas kernels for 26%

profile of v9, /device:TPU:0, one launch (start us, length us, event | category | flops | bytes accessed | tf_op | source)
XLA Modules:
  0.0 145.3 jit_solution(12412791340993085090)
XLA Ops:
  0.7 7.9 %block_states.1 = (bf16[1024,512]{1,0:T(8,128)(2,1)S(1)}, bf16[1024,512]{1,0:T(8,128)(2,1)S(1)}, f32[4,128,128]{2,1,0:T(8,128)S(1)}, bf16[4,128,128]{2,1,0:T(8,1...) custom-call(bf16[1024,2048]{1,0:T(8,128)(2,1)} %rows_ref, ...), custom_call_target="tpu_custom_call" | custom-call | flops 1000000 | bytes 1 | tf_op jit(solution)/shard_map/block_states/pallas_call | solution.py:82
  8.6 3.0 %collective-permute-start = (bf16[4,128,128]{2,1,0:T(8,128)(2,1)S(1)}, bf16[4,128,128]{2,1,0:T(8,128)(2,1)S(1)}, u32[]{:S(2)}, u32[]{:S(2)}) collective-permute-start(bf16[4,128,128]{2,1,0:T(8,128)(2,1)S(1)} %get-tuple-element.108), channel_id=1, source_target_pairs={{0,4},{4,0},{8,12},{12,8},{16,20},{20,16},{24,28},{28,24},{1,5},{5... | collective-permute-start | bytes 393224 | tf_op jit(solution)/shard_map/ppermute | solution.py:34
  11.7 1.8 %gradient_terms.6 = bf16[4,512,256]{2,1,0:T(8,128)(2,1)S(1)} custom-call(s32[2]{0:T(128)S(1)} %pad_add_fusion.position_ref.info_ref.place_ref, bf16[512,1024]{1,0:T(8,128)(2,1)S(1)} %get-tuple-element.103.refs_0_, bf16[1024,2048]{1,0:T(8,128)(2,1)S(1)} %get-tuple-element.150.refs_1_), custom_call_target="tpu_custom_call" | custom-call | flops 1000000 | bytes 1 | tf_op jit(solution)/shard_map/gradient_terms/pallas_call | solution.py:130
  14.4 2.3 %fusion.1.query_ref = bf16[1024,512]{1,0:T(8,128)(2,1)S(1)} fusion(bf16[1024,2048]{1,0:T(8,128)(2,1)S(1)} %get-tuple-element.150.refs_1_, bf16[3,2048,512]{2,1,0:T(8,128)(2,1)S(1)} %bitcast.22), kind=kOutput, calls=%fused_computation.3 | convolution fusion | flops 2148007936 | bytes 7340032 | tf_op jit(solution)/shard_map/dot_general | solution.py:446
  19.5 2.4 %fusion.3.grad_ref = f32[1024,512]{1,0:T(8,128)S(1)} fusion(bf16[1024,2048]{1,0:T(8,128)(2,1)S(1)} %copy-done.3, bf16[512,2048]{1,0:T(8,128)(2,1)S(1)} %copy-done), kind=kOutput, calls=%fused_computation.7 | convolution fusion | flops 2147483648 | bytes 8388608 | tf_op jit(solution)/shard_map/dot_general | solution.py:29
  22.0 1.8 %gradient_terms.7 = bf16[4,512,256]{2,1,0:T(8,128)(2,1)S(1)} custom-call(s32[2]{0:T(128)S(1)} %pad_add_fusion.position_ref.info_ref.place_ref, bf16[512,1024]{1,0:T(8,128)(2,1)S(1)} %get-tuple-element.115.refs_0_, bf16[1024,2048]{1,0:T(8,128)(2,1)S(1)} %get-tuple-element.150.refs_1_), custom_call_target="tpu_custom_call" | custom-call | flops 1000000 | bytes 1 | tf_op jit(solution)/shard_map/gradient_terms/pallas_call | solution.py:130
  24.4 2.7 %collective-permute-start.2 = (bf16[4,128,128]{2,1,0:T(8,128)(2,1)S(1)}, bf16[4,128,128]{2,1,0:T(8,128)(2,1)S(1)}, u32[]{:S(2)}, u32[]{:S(2)}) collective-permute-start(bf16[4,128,128]{2,1,0:T(8,128)(2,1)S(1)} %get-tuple-element.120), channel_id=1, source_target_pairs={{0,16},{4,20},{8,24},{12,28},{16,0},{20,4},{24,8},{28,12},{1,17},{... | collective-permute-start | bytes 393224 | tf_op jit(solution)/shard_map/ppermute | solution.py:34
  27.5 5.0 %collective-permute-done.2.refs_1_ = bf16[4,128,128]{2,1,0:T(8,128)(2,1)S(1)} collective-permute-done((bf16[4,128,128]{2,1,0:T(8,128)(2,1)S(1)}, bf16[4,128,128]{2,1,0:T(8,128)(2,1)S(1)}, u32[]{:S(2)}, u32[]{:S(2)}) %collective-permute-start.2) | collective-permute-done | bytes 131104 | tf_op jit(solution)/shard_map/ppermute | solution.py:34
  33.8 4.5 %norm_backward.1 = (bf16[512,1024]{1,0:T(8,128)(2,1)S(1)}, bf16[1024,512]{1,0:T(8,128)(2,1)S(1)}, bf16[512,1024]{1,0:T(8,128)(2,1)S(1)}, f32[4,128,128]{2,1,0:T(8,128)S(1)}, bf16[4,128,128]{2,1,0:T(8,128)(2,1)S(1)}) custom-call(bf16[1024,512]{1,0:T(8,128)(2,1)S(1)} %fusion.1.query_ref, f32[1024,512]{1,0:T(8,128)S(1)} %fusion.3.grad_ref, ...), custom_call_target="tpu_custom_call" | custom-call | flops 4294967296 | bytes 1 | tf_op jit(solution)/shard_map/norm_backward/pallas_call | solution.py:289
  39.9 2.9 %gradient_terms.8 = (bf16[4,512,256]{2,1,0:T(8,128)(2,1)S(1)}, bf16[4,512,256]{2,1,0:T(8,128)(2,1)S(1)}) custom-call(s32[2]{0:T(128)S(1)} %pad_add_fusion.position_ref.info_ref.place_ref, bf16[512,1024]{1,0:T(8,128)(2,1)S(1)} %get-tuple-element.130.refs_0_, bf16[1024,2048]{1,0:T(8,128)(2,1)S(1)} %copy-done.3), custom_call_target="tpu_custom_call" | custom-call | flops 1000000 | bytes 1 | tf_op jit(solution)/shard_map/gradient_terms/pallas_call | solution.py:130
  42.8 3.4 %collective-permute-done.3.got_ref = bf16[4,128,128]{2,1,0:T(8,128)(2,1)S(1)} collective-permute-done((bf16[4,128,128]{2,1,0:T(8,128)(2,1)S(1)}, bf16[4,128,128]{2,1,0:T(8,128)(2,1)S(1)}, u32[]{:S(2)}, u32[]{:S(2)}) %collective-permute-start.3) | collective-permute-done | bytes 131104 | tf_op jit(solution)/shard_map/ppermute | solution.py:34
  47.8 2.9 %gradient_terms.9 = (bf16[4,256,256]{2,1,0:T(8,128)(2,1)S(1)}, bf16[4,256,256]{2,1,0:T(8,128)(2,1)S(1)}, bf16[4,256,256]{2,1,0:T(8,128)(2,1)S(1)}, bf16[4,256,256]{2,1,0:T(8,128)(2,1)S(1)}) custom-call(s32[2]{0:T(128)S(1)} %pad_add_fusion.position_ref.info_ref.place_ref, bf16[512,1024]{1,0:T(8,128)(2,1)S(1)} %get-tuple-element.139.refs_0_, ...), custom_call_target="tpu_custom_call" | custom-call | flops 1000000 | bytes 1 | tf_op jit(solution)/shard_map/gradient_terms/pallas_call | solution.py:130
  50.7 3.9 %collective-permute-done.6.refs_3_ = bf16[4,512,256]{2,1,0:T(8,128)(2,1)S(1)} collective-permute-done((bf16[4,512,256]{2,1,0:T(8,128)(2,1)S(1)}, bf16[4,512,256]{2,1,0:T(8,128)(2,1)S(1)}, u32[]{:S(2)}, u32[]{:S(2)}) %collective-permute-start.6) | collective-permute-done | bytes 1048608 | tf_op jit(solution)/shard_map/ppermute | solution.py:34
  54.6 4.6 %collective-permute-done.5.refs_3_ = bf16[2,4,128,128]{3,2,1,0:T(8,128)(2,1)S(1)} collective-permute-done((bf16[2,4,128,128]{3,2,1,0:T(8,128)(2,1)S(1)}, bf16[2,4,128,128]{3,2,1,0:T(8,128)(2,1)S(1)}, u32[]{:S(2)}, u32[]{:S(2)}) %collective-permute-start.5) | collective-permute-done | bytes 262176 | tf_op jit(solution)/shard_map/ppermute | solution.py:34
  62.7 1.8 %gradient_terms.11.refs_2_ = bf16[4,512,256]{2,1,0:T(8,128)(2,1)S(1)} custom-call(s32[2]{0:T(128)S(1)} %pad_add_fusion.position_ref.info_ref.place_ref, bf16[512,1024]{1,0:T(8,128)(2,1)S(1)} %get-tuple-element.115.refs_0_, bf16[1024,2048]{1,0:T(8,128)(2,1)S(1)} %get-tuple-element.150.refs_1_), custom_call_target="tpu_custom_call" | custom-call | flops 1000000 | bytes 1 | tf_op jit(solution)/shard_map/gradient_terms/pallas_call | solution.py:130
  64.5 2.6 %collective-permute-done.7.refs_4_ = bf16[4,128,128]{2,1,0:T(8,128)(2,1)S(1)} collective-permute-done((bf16[4,128,128]{2,1,0:T(8,128)(2,1)S(1)}, bf16[4,128,128]{2,1,0:T(8,128)(2,1)S(1)}, u32[]{:S(2)}, u32[]{:S(2)}) %collective-permute-start.7) | collective-permute-done | bytes 131104 | tf_op jit(solution)/shard_map/ppermute | solution.py:34
  71.5 1.9 %key_value_grads.1 = (bf16[1024,512]{1,0:T(8,128)(2,1)S(1)}, bf16[1024,512]{1,0:T(8,128)(2,1)S(1)}) custom-call(bf16[1024,512]{1,0:T(8,128)(2,1)S(1)} %get-tuple-element.126.key_ref, bf16[1024,512]{1,0:T(8,128)(2,1)S(1)} %get-tuple-element.127.value_ref, f32[4,128,128]{2,1,0:T(8,128)S(1)} %get-tuple-element.156.mine_ref.grad_ref), custom_call_target="tpu_custom_call" | custom-call | flops 1000000 | bytes 1 | tf_op jit(solution)/shard_map/key_value_grads/pallas_call | solution.py:359
  73.4 4.5 %collective-permute-done.8.refs_1_ = bf16[4,256,256]{2,1,0:T(8,128)(2,1)S(1)} collective-permute-done((bf16[4,256,256]{2,1,0:T(8,128)(2,1)S(1)}, bf16[4,256,256]{2,1,0:T(8,128)(2,1)S(1)}, u32[]{:S(2)}, u32[]{:S(2)}) %collective-permute-start.8) | collective-permute-done | bytes 524320 | tf_op jit(solution)/shard_map/ppermute | solution.py:34
  78.0 9.1 %input_terms.1 = (bf16[2,256,2048]{2,1,0:T(8,128)(2,1)S(1)}, bf16[2,256,2048]{2,1,0:T(8,128)(2,1)S(1)}) custom-call(s32[2]{0:T(128)S(1)} %pad_add_fusion.position_ref.info_ref.place_ref, bf16[1024,512]{1,0:T(8,128)(2,1)S(1)} %get-tuple-element.164.query_ref, bf16[1024,512]{1,0:T(8,128)(2,1)S(1)} %get-tuple-element.165.key_ref, ...), custom_call_target="tpu_custom_call" | custom-call | flops 1000000 | bytes 1 | tf_op jit(solution)/shard_map/input_terms/pallas_call | solution.py:391
  89.4 1.9 %collective-permute-start.15 = (bf16[2,512,256]{2,1,0:T(8,128)(2,1)S(1)}, bf16[2,512,256]{2,1,0:T(8,128)(2,1)S(1)}, u32[]{:S(2)}, u32[]{:S(2)}) collective-permute-start(bf16[2,512,256]{2,1,0:T(8,128)(2,1)S(1)} %get-tuple-element.185), channel_id=1, source_target_pairs={{0,8},{4,12},{8,0},{12,4},{16,24},{20,28},{24,16},{28,20},{1,9},{5... | collective-permute-start | bytes 1572872 | tf_op jit(solution)/shard_map/ppermute | solution.py:34
  95.0 19.6 %collective-permute-done.16 = bf16[1,1024,256]{2,1,0:T(8,128)(2,1)S(1)} collective-permute-done((bf16[1,1024,256]{2,1,0:T(8,128)(2,1)S(1)}, bf16[1,1024,256]{2,1,0:T(8,128)(2,1)S(1)}, u32[]{:S(2)}, u32[]{:S(2)}) %collective-permute-start.16) | collective-permute-done | bytes 524320 | tf_op jit(solution)/shard_map/ppermute | solution.py:34
  115.3 2.3 %collective-permute-start.18 = (bf16[1,512,256]{2,1,0:T(8,128)(2,1)S(1)}, bf16[1,512,256]{2,1,0:T(8,128)(2,1)S(1)}, u32[]{:S(2)}, u32[]{:S(2)}) collective-permute-start(bf16[1,512,256]{2,1,0:T(8,128)(2,1)S(1)} %get-tuple-element.192), channel_id=1, source_target_pairs={{0,16},{4,20},{8,24},{12,28},{16,0},{20,4},{24,8},{28,12},{1,17},{... | collective-permute-start | bytes 786440 | tf_op jit(solution)/shard_map/ppermute | solution.py:34
  119.2 9.1 %collective-permute-done.17.refs_1_ = bf16[2,256,256]{2,1,0:T(8,128)(2,1)S(1)} collective-permute-done((bf16[2,256,256]{2,1,0:T(8,128)(2,1)S(1)}, bf16[2,256,256]{2,1,0:T(8,128)(2,1)S(1)}, u32[]{:S(2)}, u32[]{:S(2)}) %collective-permute-start.17) | collective-permute-done | bytes 262176 | tf_op jit(solution)/shard_map/ppermute | solution.py:34
  131.1 11.2 %collective-permute-done.20 = bf16[1,512,256]{2,1,0:T(8,128)(2,1)S(1)} collective-permute-done((bf16[1,512,256]{2,1,0:T(8,128)(2,1)S(1)}, bf16[1,512,256]{2,1,0:T(8,128)(2,1)S(1)}, u32[]{:S(2)}, u32[]{:S(2)}) %collective-permute-start.20) | collective-permute-done | bytes 262176 | tf_op jit(solution)/shard_map/ppermute | solution.py:34
  (61 shorter events, 31.5 us)
Async XLA Ops:
  0.6 18.9 %copy-start = (bf16[512,2048]{1,0:T(8,128)(2,1)S(1)}, bf16[512,2048]{1,0:T(8,128)(2,1)}, u32[]{:S(2)}) copy-start(bf16[512,2048]{1,0:T(8,128)(2,1)} %param.10) | copy-start | bytes 6291460
  8.6 8.2 %collective-permute-start = (bf16[4,128,128]{2,1,0:T(8,128)(2,1)S(1)}, bf16[4,128,128]{2,1,0:T(8,128)(2,1)S(1)}, u32[]{:S(2)}, u32[]{:S(2)}) collective-permute-start(bf16[4,128,128]{2,1,0:T(8,128)(2,1)S(1)} %get-tuple-element.108), channel_id=1, source_target_pairs={{0,4},{4,0},{8,12},{12,8},{16,20},{20,16},{24,28},{28,24},{1,5},{5... | collective-permute-start | bytes 393224 | tf_op jit(solution)/shard_map/ppermute | solution.py:34
  17.4 6.4 %collective-permute-start.1 = (bf16[4,128,128]{2,1,0:T(8,128)(2,1)S(1)}, bf16[4,128,128]{2,1,0:T(8,128)(2,1)S(1)}, u32[]{:S(2)}, u32[]{:S(2)}) collective-permute-start(bf16[4,128,128]{2,1,0:T(8,128)(2,1)S(1)} %get-tuple-element.114), channel_id=1, source_target_pairs={{0,8},{4,12},{8,0},{12,4},{16,24},{20,28},{24,16},{28,20},{1,9},{5... | collective-permute-start | bytes 393224 | tf_op jit(solution)/shard_map/ppermute | solution.py:34
  19.0 27.2 %collective-permute-start.4 = (bf16[4,512,256]{2,1,0:T(8,128)(2,1)S(1)}, bf16[4,512,256]{2,1,0:T(8,128)(2,1)S(1)}, u32[]{:S(2)}, u32[]{:S(2)}) collective-permute-start(bf16[4,512,256]{2,1,0:T(8,128)(2,1)S(1)} %gradient_terms.6), channel_id=1, source_target_pairs={{0,4},{4,0},{8,12},{12,8},{16,20},{20,16},{24,28},{28,24},{1,5},{5... | collective-permute-start | bytes 3145736 | tf_op jit(solution)/shard_map/ppermute | solution.py:34
  21.9 5.6 %copy-start.5 = (bf16[512]{0:T(512)(128)(2,1)S(1)}, bf16[512]{0:T(512)(128)(2,1)}, u32[]{:S(2)}) copy-start(bf16[512]{0:T(512)(128)(2,1)} %param.11) | copy-start | bytes 3076
  21.9 11.9 %copy-start.4 = (s32[1024]{0:T(1024)S(1)}, s32[1024]{0:T(1024)}, u32[]{:S(2)}) copy-start(s32[1024]{0:T(1024)} %param.8) | copy-start | bytes 12292
  24.4 8.1 %collective-permute-start.2 = (bf16[4,128,128]{2,1,0:T(8,128)(2,1)S(1)}, bf16[4,128,128]{2,1,0:T(8,128)(2,1)S(1)}, u32[]{:S(2)}, u32[]{:S(2)}) collective-permute-start(bf16[4,128,128]{2,1,0:T(8,128)(2,1)S(1)} %get-tuple-element.120), channel_id=1, source_target_pairs={{0,16},{4,20},{8,24},{12,28},{16,0},{20,4},{24,8},{28,12},{1,17},{... | collective-permute-start | bytes 393224 | tf_op jit(solution)/shard_map/ppermute | solution.py:34
  27.1 27.5 %collective-permute-start.6 = (bf16[4,512,256]{2,1,0:T(8,128)(2,1)S(1)}, bf16[4,512,256]{2,1,0:T(8,128)(2,1)S(1)}, u32[]{:S(2)}, u32[]{:S(2)}) collective-permute-start(bf16[4,512,256]{2,1,0:T(8,128)(2,1)S(1)} %gradient_terms.7), channel_id=1, source_target_pairs={{0,8},{4,12},{8,0},{12,4},{16,24},{20,28},{24,16},{28,20},{1,9},{5... | collective-permute-start | bytes 3145736 | tf_op jit(solution)/shard_map/ppermute | solution.py:34
  38.3 7.9 %collective-permute-start.3 = (bf16[4,128,128]{2,1,0:T(8,128)(2,1)S(1)}, bf16[4,128,128]{2,1,0:T(8,128)(2,1)S(1)}, u32[]{:S(2)}, u32[]{:S(2)}) collective-permute-start(bf16[4,128,128]{2,1,0:T(8,128)(2,1)S(1)} %get-tuple-element.129), channel_id=1, source_target_pairs={{0,4},{4,0},{8,12},{12,8},{16,20},{20,16},{24,28},{28,24},{1,5},{5... | collective-permute-start | bytes 393224 | tf_op jit(solution)/shard_map/ppermute | solution.py:34
  46.9 41.5 %collective-permute-start.9 = (bf16[4,512,256]{2,1,0:T(8,128)(2,1)S(1)}, bf16[4,512,256]{2,1,0:T(8,128)(2,1)S(1)}, u32[]{:S(2)}, u32[]{:S(2)}) collective-permute-start(bf16[4,512,256]{2,1,0:T(8,128)(2,1)S(1)} %get-tuple-element.170), channel_id=1, source_target_pairs={{0,4},{4,0},{8,12},{12,8},{16,20},{20,16},{24,28},{28,24},{1,5},{5... | collective-permute-start | bytes 3145736 | tf_op jit(solution)/shard_map/ppermute | solution.py:34
  47.4 11.7 %collective-permute-start.5 = (bf16[2,4,128,128]{3,2,1,0:T(8,128)(2,1)S(1)}, bf16[2,4,128,128]{3,2,1,0:T(8,128)(2,1)S(1)}, u32[]{:S(2)}, u32[]{:S(2)}) collective-permute-start(bf16[2,4,128,128]{3,2,1,0:T(8,128)(2,1)S(1)} %get-tuple-element.138), channel_id=1, source_target_pairs={{0,8},{4,12},{8,0},{12,4},{16,24},{20,28},{24,16},{28,20},{1,9},{5... | collective-permute-start | bytes 786440 | tf_op jit(solution)/shard_map/ppermute | solution.py:34
  59.8 7.3 %collective-permute-start.7 = (bf16[4,128,128]{2,1,0:T(8,128)(2,1)S(1)}, bf16[4,128,128]{2,1,0:T(8,128)(2,1)S(1)}, u32[]{:S(2)}, u32[]{:S(2)}) collective-permute-start(bf16[4,128,128]{2,1,0:T(8,128)(2,1)S(1)} %get-tuple-element.148), channel_id=1, source_target_pairs={{0,16},{4,20},{8,24},{12,28},{16,0},{20,4},{24,8},{28,12},{1,17},{... | collective-permute-start | bytes 393224 | tf_op jit(solution)/shard_map/ppermute | solution.py:34
  61.7 16.2 %collective-permute-start.8 = (bf16[4,256,256]{2,1,0:T(8,128)(2,1)S(1)}, bf16[4,256,256]{2,1,0:T(8,128)(2,1)S(1)}, u32[]{:S(2)}, u32[]{:S(2)}) collective-permute-start(bf16[4,256,256]{2,1,0:T(8,128)(2,1)S(1)} %get-tuple-element.161), channel_id=1, source_target_pairs={{0,8},{4,12},{8,0},{12,4},{16,24},{20,28},{24,16},{28,20},{1,9},{5... | collective-permute-start | bytes 1572872 | tf_op jit(solution)/shard_map/ppermute | solution.py:34
  69.7 18.3 %collective-permute-start.10 = (bf16[2,512,256]{2,1,0:T(8,128)(2,1)S(1)}, bf16[2,512,256]{2,1,0:T(8,128)(2,1)S(1)}, u32[]{:S(2)}, u32[]{:S(2)}) collective-permute-start(bf16[2,512,256]{2,1,0:T(8,128)(2,1)S(1)} %get-tuple-element.171), channel_id=1, source_target_pairs={{0,8},{4,12},{8,0},{12,4},{16,24},{20,28},{24,16},{28,20},{1,9},{5... | collective-permute-start | bytes 1572872 | tf_op jit(solution)/shard_map/ppermute | solution.py:34
  69.8 18.2 %collective-permute-start.11 = (bf16[2,512,256]{2,1,0:T(8,128)(2,1)S(1)}, bf16[2,512,256]{2,1,0:T(8,128)(2,1)S(1)}, u32[]{:S(2)}, u32[]{:S(2)}) collective-permute-start(bf16[2,512,256]{2,1,0:T(8,128)(2,1)S(1)} %get-tuple-element.172), channel_id=1, source_target_pairs={{0,4},{4,0},{8,12},{12,8},{16,20},{20,16},{24,28},{28,24},{1,5},{5... | collective-permute-start | bytes 1572872 | tf_op jit(solution)/shard_map/ppermute | solution.py:34
  88.6 4.2 %collective-permute-start.12 = (bf16[2,256,2048]{2,1,0:T(8,128)(2,1)S(1)}, bf16[2,256,2048]{2,1,0:T(8,128)(2,1)S(1)}, u32[]{:S(2)}, u32[]{:S(2)}) collective-permute-start(bf16[2,256,2048]{2,1,0:T(8,128)(2,1)S(1)} %get-tuple-element.179), channel_id=1, source_target_pairs={{0,1},{1,0},{2,3},{3,2},{4,5},{5,4},{6,7},{7,6},{8,9},{9,8},{10,11... | collective-permute-start | bytes 6291464 | tf_op jit(solution)/shard_map/ppermute | solution.py:34
  88.6 26.0 %collective-permute-start.16 = (bf16[1,1024,256]{2,1,0:T(8,128)(2,1)S(1)}, bf16[1,1024,256]{2,1,0:T(8,128)(2,1)S(1)}, u32[]{:S(2)}, u32[]{:S(2)}) collective-permute-start(bf16[1,1024,256]{2,1,0:T(8,128)(2,1)S(1)} %get-tuple-element.186), channel_id=1, source_target_pairs={{0,16},{4,20},{8,24},{12,28},{16,0},{20,4},{24,8},{28,12},{1,17},{... | collective-permute-start | bytes 1572872 | tf_op jit(solution)/shard_map/ppermute | solution.py:34
  89.4 25.3 %collective-permute-start.15 = (bf16[2,512,256]{2,1,0:T(8,128)(2,1)S(1)}, bf16[2,512,256]{2,1,0:T(8,128)(2,1)S(1)}, u32[]{:S(2)}, u32[]{:S(2)}) collective-permute-start(bf16[2,512,256]{2,1,0:T(8,128)(2,1)S(1)} %get-tuple-element.185), channel_id=1, source_target_pairs={{0,8},{4,12},{8,0},{12,4},{16,24},{20,28},{24,16},{28,20},{1,9},{5... | collective-permute-start | bytes 1572872 | tf_op jit(solution)/shard_map/ppermute | solution.py:34
  91.3 23.6 %collective-permute-start.14 = (bf16[4,256,256]{2,1,0:T(8,128)(2,1)S(1)}, bf16[4,256,256]{2,1,0:T(8,128)(2,1)S(1)}, u32[]{:S(2)}, u32[]{:S(2)}) collective-permute-start(bf16[4,256,256]{2,1,0:T(8,128)(2,1)S(1)} %get-tuple-element.184), channel_id=1, source_target_pairs={{0,4},{4,0},{8,12},{12,8},{16,20},{20,16},{24,28},{28,24},{1,5},{5... | collective-permute-start | bytes 1572872 | tf_op jit(solution)/shard_map/ppermute | solution.py:34
  93.3 50.6 %collective-permute-start.13 = (bf16[1,256,2048]{2,1,0:T(8,128)(2,1)S(1)}, bf16[1,256,2048]{2,1,0:T(8,128)(2,1)S(1)}, u32[]{:S(2)}, u32[]{:S(2)}) collective-permute-start(bf16[1,256,2048]{2,1,0:T(8,128)(2,1)S(1)} %get-tuple-element.182), channel_id=1, source_target_pairs={{0,2},{1,3},{2,0},{3,1},{4,6},{5,7},{6,4},{7,5},{8,10},{9,11},{10,... | collective-permute-start | bytes 3145736 | tf_op jit(solution)/shard_map/ppermute | solution.py:34
  115.1 13.3 %collective-permute-start.17 = (bf16[2,256,256]{2,1,0:T(8,128)(2,1)S(1)}, bf16[2,256,256]{2,1,0:T(8,128)(2,1)S(1)}, u32[]{:S(2)}, u32[]{:S(2)}) collective-permute-start(bf16[2,256,256]{2,1,0:T(8,128)(2,1)S(1)} %get-tuple-element.191), channel_id=1, source_target_pairs={{0,8},{4,12},{8,0},{12,4},{16,24},{20,28},{24,16},{28,20},{1,9},{5... | collective-permute-start | bytes 786440 | tf_op jit(solution)/shard_map/ppermute | solution.py:34
  115.3 14.5 %collective-permute-start.18 = (bf16[1,512,256]{2,1,0:T(8,128)(2,1)S(1)}, bf16[1,512,256]{2,1,0:T(8,128)(2,1)S(1)}, u32[]{:S(2)}, u32[]{:S(2)}) collective-permute-start(bf16[1,512,256]{2,1,0:T(8,128)(2,1)S(1)} %get-tuple-element.192), channel_id=1, source_target_pairs={{0,16},{4,20},{8,24},{12,28},{16,0},{20,4},{24,8},{28,12},{1,17},{... | collective-permute-start | bytes 786440 | tf_op jit(solution)/shard_map/ppermute | solution.py:34
  117.7 12.1 %collective-permute-start.19 = (bf16[2,256,256]{2,1,0:T(8,128)(2,1)S(1)}, bf16[2,256,256]{2,1,0:T(8,128)(2,1)S(1)}, u32[]{:S(2)}, u32[]{:S(2)}) collective-permute-start(bf16[2,256,256]{2,1,0:T(8,128)(2,1)S(1)} %get-tuple-element.194), channel_id=1, source_target_pairs={{0,4},{4,0},{8,12},{12,8},{16,20},{20,16},{24,28},{28,24},{1,5},{5... | collective-permute-start | bytes 786440 | tf_op jit(solution)/shard_map/ppermute | solution.py:34
  129.9 12.3 %collective-permute-start.20 = (bf16[1,512,256]{2,1,0:T(8,128)(2,1)S(1)}, bf16[1,512,256]{2,1,0:T(8,128)(2,1)S(1)}, u32[]{:S(2)}, u32[]{:S(2)}) collective-permute-start(bf16[1,512,256]{2,1,0:T(8,128)(2,1)S(1)} %get-tuple-element.196), channel_id=1, source_target_pairs={{0,16},{4,20},{8,24},{12,28},{16,0},{20,4},{24,8},{28,12},{1,17},{... | collective-permute-start | bytes 786440 | tf_op jit(solution)/shard_map/ppermute | solution.py:34
  (3 other events, 10.9 us)

commit v10 on v8

--- a/solution.py
+++ b/solution.py
@@ -177,7 +177,7 @@
     return ((info_ref[0] >> bit) & 1).astype(f32)
 
 
-def small(kernel, info, arrays, shapes, name):
+def small(kernel, info, arrays, shapes, name, flops=1000000):
     vmem = pl.BlockSpec(memory_space=pltpu.VMEM)
     return pl.pallas_call(
         kernel,
@@ -185,7 +185,7 @@
         out_specs=[vmem] * len(shapes),
         out_shape=[jax.ShapeDtypeStruct(shape, kind) for shape, kind in shapes],
         compiler_params=params(),
-        cost_estimate=COST,
+        cost_estimate=pl.CostEstimate(flops=flops, bytes_accessed=1, transcendentals=0),
         name=name,
     )(info, *arrays)
 
@@ -251,7 +251,7 @@
 def suffix_step(info, bit, arrays):
     shape = arrays[0].shape
     shapes = [(shape, f32)] * 4 + [(shape, bf16)]
-    return small(functools.partial(suffix_kernel, bit), info, arrays, shapes, "suffix_step")
+    return small(functools.partial(suffix_kernel, bit), info, arrays, shapes, "suffix_step", 4000000000 if bit == 2 else 1000000)
 
 
 def middle_kernel(query_ref, grad_ref, mask_ref, gain_ref, own_ref, before_ref, normed_t_ref, query_grad_ref, query_grad_t_ref, block_grad_ref, sent_ref, held_ref):
@@ -314,36 +314,35 @@
     )(queries, normed_grad, mask, gain, own, before)
 
 
-def late_kernel(mine_ref, mate_ref, other_ref, *refs):
-    for side, state_ref, parts in ((0, mate_ref, refs[0:2] + refs[4:6]), (1, other_ref, refs[2:4] + refs[6:8])):
-        own, got, keep, send = parts
-        half = keep.shape[0]
-
-        def times(state, block):
-            return lax.dot_general(state, block, (((side,), (0,)), ((), ())), preferred_element_type=f32)
-
-        for slot in range(2 * half):
-            out = keep if slot < half else send
-            for h in range(mine_ref.shape[0]):
-                rows = slice(h * HD, (h + 1) * HD)
-                total = times(mine_ref[h].astype(bf16), own[slot, rows, :])
-                total += times(state_ref[h].astype(bf16), got[slot, rows, :])
-                out[slot % half, rows, :] = total.astype(bf16)
-
-
-def late_terms(mine, mate, other, value_keep, value_got, key_keep, key_got):
-    slots, rows, width = value_keep.shape
+def late_kernel(side, cut, mine_ref, state_ref, own_ref, low_ref, high_ref, keep_ref, send_ref):
+    half = keep_ref.shape[0]
+
+    def times(state, block):
+        return lax.dot_general(state, block, (((side,), (0,)), ((), ())), preferred_element_type=f32)
+
+    for slot in range(2 * half):
+        out = keep_ref if slot < half else send_ref
+        for h in range(mine_ref.shape[0]):
+            rows = slice(h * HD, (h + 1) * HD)
+            got = low_ref[slot, rows, :] if slot < cut else high_ref[slot - cut, rows, :]
+            total = times(mine_ref[h].astype(bf16), own_ref[slot, rows, :])
+            total += times(state_ref[h].astype(bf16), got)
+            out[slot % half, rows, :] = total.astype(bf16)
+
+
+def late_terms(side, mine, state, own, low, high):
+    slots, rows, width = own.shape
     vmem = pl.BlockSpec(memory_space=pltpu.VMEM)
     shape = jax.ShapeDtypeStruct((slots // 2, rows, width), bf16)
     return pl.pallas_call(
-        late_kernel,
-        in_specs=[vmem] * 7,
-        out_specs=[vmem] * 4,
-        out_shape=[shape] * 4,
+        functools.partial(late_kernel, side, low.shape[0]),
+        in_specs=[vmem] * 5,
+        out_specs=[vmem] * 2,
+        out_shape=[shape] * 2,
         compiler_params=params(),
         cost_estimate=COST,
         name="late_terms",
-    )(mine, mate, other, value_keep, value_got, key_keep, key_got)
+    )(mine, state, own, low, high)
 
 
 def key_value_kernel(key_ref, value_ref, grad_ref, key_grad_ref, value_grad_ref):
@@ -404,23 +403,22 @@
     )(info, *grads, weight)
 
 
-def finish_kernel(query_keep_ref, query_got_ref, late_keep_ref, late_got_ref, out_ref):
-    width = query_keep_ref.shape[0]
-    out_ref[0] = (query_keep_ref[...].astype(f32) + query_got_ref[...].astype(f32)).T
-    for index in range(2):
-        rows = slice(index * width, (index + 1) * width)
-        out_ref[1 + index] = (late_keep_ref[rows, :].astype(f32) + late_got_ref[rows, :].astype(f32)).T
-
-
-def finish(query_keep, query_got, late_keep, late_got):
-    rows, width = query_keep.shape
+def finish_kernel(*refs):
+    out = refs[-1]
+    for index in range(3):
+        keep, got = refs[2 * index], refs[2 * index + 1]
+        out[index] = (keep[...].astype(f32) + got[...].astype(f32)).T
+
+
+def finish(*arrays):
+    rows, width = arrays[0].shape
     return pl.pallas_call(
         finish_kernel,
         out_shape=jax.ShapeDtypeStruct((3, width, rows), f32),
         compiler_params=params(),
         cost_estimate=COST,
         name="finish",
-    )(query_keep, query_got, late_keep, late_got)
+    )(*arrays)
 
 
 def after(value, *others):
@@ -452,7 +450,8 @@
     keys, values, own_state, sent, keys_t, values_t, layer_input = block_states(layer_input, weights)
 
     got = exchange(sent, "seq", 0)
-    (value_send,) = terms(values_t, after(layer_input, own_state), order[half:])
+    cut = half + 3 * half // 4
+    value_send, value_rest = terms(values_t, after(layer_input, own_state), order[half:cut], order[cut:])
     queries = project(after(layer_input, value_send), 0)
     got = after(got, queries)
     before, total, sent = prefix_step(info, 0, [own_state, got])
@@ -461,7 +460,9 @@
         got = exchange(sent, "seq", bit)
         if bit == 1:
             normed_grad = dot_t(after(output_grad, total), out_weight)
-            (key_send,) = terms(keys_t, after(layer_input, normed_grad), swapped[half:])
+            key_send, key_rest = terms(
+                keys_t, after(layer_input, normed_grad), swapped[half:cut], swapped[cut:]
+            )
             got = after(got, key_send)
         elif bit == 2:
             (mark,) = small(mark_kernel, after(info, total), [], [((8, 128), f32)], "mark")
@@ -477,11 +478,13 @@
     out_keep, out_send = terms(normed_t, after(output_grad, own_grad), order[:half], order[half:])
     got = after(got, out_keep, value_got)
     total, mine, mate, sent = suffix_first(info, own_grad, got)
-    out_got = exchange(after(out_send, total), "seq", 0)
+    value_rest = exchange(after(value_rest, total), "seq", 0)
 
     got = exchange(sent, "seq", 1)
     query_keep, query_send = terms(query_grad_t, after(layer_input, total), order[:half], order[half:])
-    got = after(got, query_keep, key_got)
+    value_rest = after(value_rest, query_keep)
+    out_got = exchange(after(out_send, value_rest), "seq", 0)
+    got = after(got, query_keep, key_got, value_rest)
     suffix = suffix_step(info, 1, [total, mine, mate, got])
     query_got = exchange(after(query_send, suffix[0]), "seq", 0)
 
@@ -489,20 +492,20 @@
         got = exchange(suffix[4], "seq", bit)
         if bit == 2:
             (value_keep,) = terms(values_t, after(layer_input, suffix[0]), order[:half])
+            key_rest = exchange(after(key_rest, value_keep), "seq", 1)
             (key_keep,) = terms(keys_t, after(layer_input, value_keep), swapped[:half])
             got = after(got, key_keep)
         suffix = suffix_step(info, bit, list(suffix[:4]) + [got])
     total, mine, mate, other, sent = suffix
 
-    value_keep, value_send, key_keep, key_send = late_terms(
-        mine, mate, other, value_keep, value_got, key_keep, key_got
-    )
+    value_keep, value_send = late_terms(0, mine, mate, after(value_keep, key_rest), value_got, value_rest)
     value_got = exchange(value_send, "seq", 1)
+    key_grad, value_grad = key_value_grads(keys, values, after(mine, value_keep))
+    key_keep, key_send = late_terms(1, mine, other, after(key_keep, key_grad), key_got, key_rest)
     key_got = exchange(key_send, "seq", 0)
-
-    key_grad, value_grad = key_value_grads(keys, values, after(mine, value_keep))
-    grads = (query_grad, key_grad, value_grad)
-    input_keep, input_send = input_terms(grads, weights, info, head_order, 0, 1)
+    grads = after((query_grad, key_grad, value_grad), key_keep)
+    grads, out_got = after((grads, out_got), key_keep)
+    first_keep, first_send = input_terms(grads, weights, info, head_order, 0, 2)
 
     def stage(keep, got, token, bit, axis="seq"):
         keep, send = sums([(keep, after(got, token))])
@@ -513,23 +516,33 @@
             keep, got = stage(keep, got, keep, bit)
         return keep[0], got[0]
 
-    value_got, key_got = after((value_got, key_got), input_keep)
-    late_keep, late_send = sums([(value_keep, value_got), (key_keep, key_got)], merge=True)
-    late_got = exchange(late_send, "seq", 2)
-    out_keep, out_got = stage(out_keep, out_got, late_keep, 1)
-    input_got = exchange(after(input_send, out_keep), "head", 0)
+    value_keep, value_got = stage(value_keep, value_got, first_keep, 2)
+    out_keep, out_send = sums([(out_keep, after(out_got, value_keep))])
+    second_keep, second_send = input_terms(grads, after(weights, out_keep), info, head_order, 1, 2)
+    out_got = exchange(out_send, "seq", 1)
+    key_keep, key_got = stage(key_keep, key_got, (second_keep, value_got), 2)
+    first_got = exchange(after(first_send, key_keep), "head", 0)
+    second_got = exchange(after(second_send, key_keep), "head", 0)
     for bit in range(1, head_bits):
-        input_keep, input_got = stage(input_keep, input_got, out_keep, bit, "head")
-    out_keep, out_got = stage(out_keep, out_got, (input_keep, late_got), 2)
-    query_keep, query_got = stage(query_keep, query_got, out_keep, 1)
-    query_keep, query_got = stage(query_keep, query_got, (query_keep, out_got, input_got), 2)
+        first_keep, first_got = stage(first_keep, first_got, key_keep, bit, "head")
+        second_keep, second_got = stage(second_keep, second_got, first_keep, bit, "head")
+    out_keep, out_got = stage(out_keep, out_got, second_keep, 2)
+    query_keep, query_got = stage(query_keep, query_got, (out_keep, key_got), 1)
+    query_keep, query_got = stage(query_keep, query_got, (query_keep, out_got), 2)
 
     out_pair = rest(out_keep, out_got, stages[3:])
-    late_pair = rest(late_keep, late_got, stages[3:])
+    value_pair = rest(value_keep, value_got, stages[3:])
+    key_pair = rest(key_keep, key_got, stages[3:])
     query_pair = rest(query_keep, query_got, stages[3:])
-    input_grad = (input_keep[0].astype(f32) + input_got[0].astype(f32)).astype(bf16)
+    input_grad = jnp.concatenate(
+        [
+            (keep[0].astype(f32) + got[0].astype(f32)).astype(bf16)
+            for keep, got in ((first_keep, first_got), (second_keep, second_got))
+        ],
+        1,
+    )
     out_weight_grad = out_pair[0].astype(f32) + out_pair[1].astype(f32)
-    proj_weight_grad = finish(*query_pair, *late_pair)
+    proj_weight_grad = finish(*query_pair, *value_pair, *key_pair)
     return (input_grad, jnp.transpose(proj_weight_grad, (1, 0, 2)), out_weight_grad)
 
 

time: 145 us -> 150 us (1.034)
  starting transfers between devices: 22.5 us -> 36 us
  waiting for transfers between devices: 67.3 us -> 58.9 us
    ppermute x19 -> x24, starting transfers between devices: 22.5 us -> 36 us  [exchange(): return lax.ppermute(arr, axis, [(i, i ^ 1 << bit) for i in range(count)])]
    ppermute x19 -> x24, waiting for transfers between devices: 67.3 us -> 58.9 us  [exchange(): return lax.ppermute(arr, axis, [(i, i ^ 1 << bit) for i in range(count)])]
    pallas_call x1 -> x2, Pallas kernels: 9.12 us -> 9.71 us  [input_terms(): pl.pallas_call(functools.partial(input_kernel, order), grid_spec=pltpu.Pr...]
  transfers between devices with their start and end apart: 19 -> 24, of which waited for: 10 -> 13; matrix products, arithmetic and copies ran while one was open for 5% -> 5% of each run, Pallas kernels for 25% -> 24%
where the time goes in v10:
time: 150 us
  waiting for transfers between devices  58.9 us (39%)
  Pallas kernels  46.9 us (31%)
  starting transfers between devices  36 us (24%)
  matrix products  4.72 us (3%)
  other arithmetic  2.36 us (2%)
    ppermute x24, waiting for transfers between devices, exchange(): return lax.ppermute(arr, axis, [(i, i ^ 1 << bit) for i in range(count)])  58.9 us
    ppermute x24, starting transfers between devices, exchange(): return lax.ppermute(arr, axis, [(i, i ^ 1 << bit) for i in range(count)])  36 us
    pallas_call x6, Pallas kernels, gradient_terms(): pl.pallas_call(functools.partial(terms_kernel, len(lefts), outputs), in_s...  13.1 us
    pallas_call x2, Pallas kernels, input_terms(): pl.pallas_call(functools.partial(input_kernel, order), grid_spec=pltpu.Pr...  9.71 us
    pallas_call x1, Pallas kernels, block_states(): pl.pallas_call(functools.partial(states_kernel, parts), in_specs=[hbm, hb...  7.91 us
    pallas_call x6, Pallas kernels, small(): pl.pallas_call(kernel, in_specs=[pl.BlockSpec(memory_space=pltpu.SMEM)] +...  5.17 us
    pallas_call x1, Pallas kernels, middle(): pl.pallas_call(middle_kernel, grid=(heads,), in_specs=[column, column, pl...  4.47 us
  transfers between devices with their start and end apart: 24, of which 13 were waited for; matrix products, arithmetic and copies ran while one was open for 5% of the time, Pallas kernels for 24%

profile of v10, /device:TPU:0, one launch (start us, length us, event | category | flops | bytes accessed | tf_op | source)
XLA Modules:
  0.0 149.8 jit_solution(13167704288219569139)
XLA Ops:
  0.7 7.9 %block_states.1 = (bf16[1024,512]{1,0:T(8,128)(2,1)S(1)}, bf16[1024,512]{1,0:T(8,128)(2,1)S(1)}, f32[4,128,128]{2,1,0:T(8,128)S(1)}, bf16[4,128,128]{2,1,0:T(8,1...) custom-call(bf16[1024,2048]{1,0:T(8,128)(2,1)} %rows_ref, ...), custom_call_target="tpu_custom_call" | custom-call | flops 1000000 | bytes 1 | tf_op jit(solution)/shard_map/block_states/pallas_call | solution.py:82
  8.6 3.0 %collective-permute-start = (bf16[4,128,128]{2,1,0:T(8,128)(2,1)S(1)}, bf16[4,128,128]{2,1,0:T(8,128)(2,1)S(1)}, u32[]{:S(2)}, u32[]{:S(2)}) collective-permute-start(bf16[4,128,128]{2,1,0:T(8,128)(2,1)S(1)} %get-tuple-element.125), channel_id=1, source_target_pairs={{0,4},{4,0},{8,12},{12,8},{16,20},{20,16},{24,28},{28,24},{1,5},{5... | collective-permute-start | bytes 393224 | tf_op jit(solution)/shard_map/ppermute | solution.py:34
  13.5 2.3 %fusion.1.query_ref = bf16[1024,512]{1,0:T(8,128)(2,1)S(1)} fusion(bf16[1024,2048]{1,0:T(8,128)(2,1)S(1)} %get-tuple-element.171.refs_1_, bf16[3,2048,512]{2,1,0:T(8,128)(2,1)S(1)} %bitcast.26), kind=kOutput, calls=%fused_computation.2 | convolution fusion | flops 2148007936 | bytes 7340032 | tf_op jit(solution)/shard_map/dot_general | solution.py:444
  19.2 2.4 %fusion.4.grad_ref = f32[1024,512]{1,0:T(8,128)S(1)} fusion(bf16[1024,2048]{1,0:T(8,128)(2,1)S(1)} %copy-done.3, bf16[512,2048]{1,0:T(8,128)(2,1)S(1)} %copy-done), kind=kOutput, calls=%fused_computation.10 | convolution fusion | flops 2147483648 | bytes 8388608 | tf_op jit(solution)/shard_map/dot_general | solution.py:29
  24.0 2.7 %collective-permute-start.2 = (bf16[4,128,128]{2,1,0:T(8,128)(2,1)S(1)}, bf16[4,128,128]{2,1,0:T(8,128)(2,1)S(1)}, u32[]{:S(2)}, u32[]{:S(2)}) collective-permute-start(bf16[4,128,128]{2,1,0:T(8,128)(2,1)S(1)} %get-tuple-element.138), channel_id=1, source_target_pairs={{0,16},{4,20},{8,24},{12,28},{16,0},{20,4},{24,8},{28,12},{1,17},{... | collective-permute-start | bytes 393224 | tf_op jit(solution)/shard_map/ppermute | solution.py:34
  27.1 4.4 %collective-permute-done.2.refs_1_ = bf16[4,128,128]{2,1,0:T(8,128)(2,1)S(1)} collective-permute-done((bf16[4,128,128]{2,1,0:T(8,128)(2,1)S(1)}, bf16[4,128,128]{2,1,0:T(8,128)(2,1)S(1)}, u32[]{:S(2)}, u32[]{:S(2)}) %collective-permute-start.2) | collective-permute-done | bytes 131104 | tf_op jit(solution)/shard_map/ppermute | solution.py:34
  32.8 4.5 %norm_backward.1 = (bf16[512,1024]{1,0:T(8,128)(2,1)S(1)}, bf16[1024,512]{1,0:T(8,128)(2,1)S(1)}, bf16[512,1024]{1,0:T(8,128)(2,1)S(1)}, f32[4,128,128]{2,1,0:T(8,128)S(1)}, bf16[4,128,128]{2,1,0:T(8,128)(2,1)S(1)}) custom-call(bf16[1024,512]{1,0:T(8,128)(2,1)S(1)} %fusion.1.query_ref, f32[1024,512]{1,0:T(8,128)S(1)} %fusion.4.grad_ref, ...), custom_call_target="tpu_custom_call" | custom-call | flops 4294967296 | bytes 1 | tf_op jit(solution)/shard_map/norm_backward/pallas_call | solution.py:289
  39.0 2.9 %gradient_terms.8 = (bf16[4,512,256]{2,1,0:T(8,128)(2,1)S(1)}, bf16[4,512,256]{2,1,0:T(8,128)(2,1)S(1)}) custom-call(s32[2]{0:T(128)S(1)} %pad_add_fusion.position_ref.info_ref.place_ref, bf16[512,1024]{1,0:T(8,128)(2,1)S(1)} %get-tuple-element.148.refs_0_, bf16[1024,2048]{1,0:T(8,128)(2,1)S(1)} %copy-done.3), custom_call_target="tpu_custom_call" | custom-call | flops 1000000 | bytes 1 | tf_op jit(solution)/shard_map/gradient_terms/pallas_call | solution.py:130
  44.7 2.9 %gradient_terms.9 = (bf16[4,512,256]{2,1,0:T(8,128)(2,1)S(1)}, bf16[4,512,256]{2,1,0:T(8,128)(2,1)S(1)}) custom-call(s32[2]{0:T(128)S(1)} %pad_add_fusion.position_ref.info_ref.place_ref, bf16[512,1024]{1,0:T(8,128)(2,1)S(1)} %get-tuple-element.157.refs_0_, bf16[1024,2048]{1,0:T(8,128)(2,1)S(1)} %get-tuple-element.171.refs_1_), custom_call_target="tpu_custom_call" | custom-call | flops 1000000 | bytes 1 | tf_op jit(solution)/shard_map/gradient_terms/pallas_call | solution.py:130
  47.7 2.3 %collective-permute-done.7.high_ref = bf16[1,512,256]{2,1,0:T(8,128)(2,1)S(1)} collective-permute-done((bf16[1,512,256]{2,1,0:T(8,128)(2,1)S(1)}, bf16[1,512,256]{2,1,0:T(8,128)(2,1)S(1)}, u32[]{:S(2)}, u32[]{:S(2)}) %collective-permute-start.7) | collective-permute-done | bytes 262176 | tf_op jit(solution)/shard_map/ppermute | solution.py:34
  53.2 4.1 %collective-permute-start.8 = (bf16[4,128,128]{2,1,0:T(8,128)(2,1)S(1)}, bf16[4,128,128]{2,1,0:T(8,128)(2,1)S(1)}, u32[]{:S(2)}, u32[]{:S(2)}) collective-permute-start(bf16[4,128,128]{2,1,0:T(8,128)(2,1)S(1)} %get-tuple-element.169), channel_id=1, source_target_pairs={{0,16},{4,20},{8,24},{12,28},{16,0},{20,4},{24,8},{28,12},{1,17},{... | collective-permute-start | bytes 393224 | tf_op jit(solution)/shard_map/ppermute | solution.py:34
  62.4 3.2 %collective-permute-done.9.high_ref = bf16[1,512,256]{2,1,0:T(8,128)(2,1)S(1)} collective-permute-done((bf16[1,512,256]{2,1,0:T(8,128)(2,1)S(1)}, bf16[1,512,256]{2,1,0:T(8,128)(2,1)S(1)}, u32[]{:S(2)}, u32[]{:S(2)}) %collective-permute-start.9) | collective-permute-done | bytes 262176 | tf_op jit(solution)/shard_map/ppermute | solution.py:34
  69.9 6.1 %collective-permute-done.10.refs_1_ = bf16[4,512,256]{2,1,0:T(8,128)(2,1)S(1)} collective-permute-done((bf16[4,512,256]{2,1,0:T(8,128)(2,1)S(1)}, bf16[4,512,256]{2,1,0:T(8,128)(2,1)S(1)}, u32[]{:S(2)}, u32[]{:S(2)}) %collective-permute-start.10) | collective-permute-done | bytes 1048608 | tf_op jit(solution)/shard_map/ppermute | solution.py:34
  76.0 4.7 %input_terms.2 = (bf16[2,256,1024]{2,1,0:T(8,128)(2,1)S(1)}, bf16[2,256,1024]{2,1,0:T(8,128)(2,1)S(1)}) custom-call(s32[2]{0:T(128)S(1)} %pad_add_fusion.position_ref.info_ref.place_ref, bf16[1024,512]{1,0:T(8,128)(2,1)S(1)} %get-tuple-element.190.query_ref, bf16[1024,512]{1,0:T(8,128)(2,1)S(1)} %get-tuple-element.191.key_ref, ...), custom_call_target="tpu_custom_call" | custom-call | flops 1000000 | bytes 1 | tf_op jit(solution)/shard_map/input_terms/pallas_call | solution.py:390
  80.9 3.7 %collective-permute-start.13 = (bf16[1,512,256]{2,1,0:T(8,128)(2,1)S(1)}, bf16[1,512,256]{2,1,0:T(8,128)(2,1)S(1)}, u32[]{:S(2)}, u32[]{:S(2)}) collective-permute-start(bf16[1,512,256]{2,1,0:T(8,128)(2,1)S(1)} %get-tuple-element.204), channel_id=1, source_target_pairs={{0,16},{4,20},{8,24},{12,28},{16,0},{20,4},{24,8},{28,12},{1,17},{... | collective-permute-start | bytes 786440 | tf_op jit(solution)/shard_map/ppermute | solution.py:34
  84.9 5.0 %input_terms.3 = (bf16[2,256,1024]{2,1,0:T(8,128)(2,1)S(1)}, bf16[2,256,1024]{2,1,0:T(8,128)(2,1)S(1)}) custom-call(s32[2]{0:T(128)S(1)} %pad_add_fusion.position_ref.info_ref.place_ref, bf16[1024,512]{1,0:T(8,128)(2,1)S(1)} %get-tuple-element.190.query_ref, bf16[1024,512]{1,0:T(8,128)(2,1)S(1)} %get-tuple-element.191.key_ref, ...), custom_call_target="tpu_custom_call" | custom-call | flops 1000000 | bytes 1 | tf_op jit(solution)/shard_map/input_terms/pallas_call | solution.py:390
  92.6 3.4 %collective-permute-start.20 = (bf16[1,512,256]{2,1,0:T(8,128)(2,1)S(1)}, bf16[1,512,256]{2,1,0:T(8,128)(2,1)S(1)}, u32[]{:S(2)}, u32[]{:S(2)}) collective-permute-start(bf16[1,512,256]{2,1,0:T(8,128)(2,1)S(1)} %get-tuple-element.221), channel_id=1, source_target_pairs={{0,16},{4,20},{8,24},{12,28},{16,0},{20,4},{24,8},{28,12},{1,17},{... | collective-permute-start | bytes 786440 | tf_op jit(solution)/shard_map/ppermute | solution.py:34
  96.5 15.3 %collective-permute-done.19.refs_1_ = bf16[2,512,256]{2,1,0:T(8,128)(2,1)S(1)} collective-permute-done((bf16[2,512,256]{2,1,0:T(8,128)(2,1)S(1)}, bf16[2,512,256]{2,1,0:T(8,128)(2,1)S(1)}, u32[]{:S(2)}, u32[]{:S(2)}) %collective-permute-start.19) | collective-permute-done | bytes 524320 | tf_op jit(solution)/shard_map/ppermute | solution.py:34
  111.9 4.0 %collective-permute-done.18.refs_1_ = bf16[4,512,256]{2,1,0:T(8,128)(2,1)S(1)} collective-permute-done((bf16[4,512,256]{2,1,0:T(8,128)(2,1)S(1)}, bf16[4,512,256]{2,1,0:T(8,128)(2,1)S(1)}, u32[]{:S(2)}, u32[]{:S(2)}) %collective-permute-start.18) | collective-permute-done | bytes 1048608 | tf_op jit(solution)/shard_map/ppermute | solution.py:34
  117.8 3.4 %collective-permute-start.22 = (bf16[1,512,256]{2,1,0:T(8,128)(2,1)S(1)}, bf16[1,512,256]{2,1,0:T(8,128)(2,1)S(1)}, u32[]{:S(2)}, u32[]{:S(2)}) collective-permute-start(bf16[1,512,256]{2,1,0:T(8,128)(2,1)S(1)} %get-tuple-element.225), channel_id=1, source_target_pairs={{0,16},{4,20},{8,24},{12,28},{16,0},{20,4},{24,8},{28,12},{1,17},{... | collective-permute-start | bytes 786440 | tf_op jit(solution)/shard_map/ppermute | solution.py:34
  121.8 11.1 %collective-permute-done.22 = bf16[1,512,256]{2,1,0:T(8,128)(2,1)S(1)} collective-permute-done((bf16[1,512,256]{2,1,0:T(8,128)(2,1)S(1)}, bf16[1,512,256]{2,1,0:T(8,128)(2,1)S(1)}, u32[]{:S(2)}, u32[]{:S(2)}) %collective-permute-start.22) | collective-permute-done | bytes 262176 | tf_op jit(solution)/shard_map/ppermute | solution.py:34
  135.1 2.2 %collective-permute-start.23 = (bf16[1,512,256]{2,1,0:T(8,128)(2,1)S(1)}, bf16[1,512,256]{2,1,0:T(8,128)(2,1)S(1)}, u32[]{:S(2)}, u32[]{:S(2)}) collective-permute-start(bf16[1,512,256]{2,1,0:T(8,128)(2,1)S(1)} %get-tuple-element.228), channel_id=1, source_target_pairs={{0,16},{4,20},{8,24},{12,28},{16,0},{20,4},{24,8},{28,12},{1,17},{... | collective-permute-start | bytes 786440 | tf_op jit(solution)/shard_map/ppermute | solution.py:34
  137.5 3.2 %collective-permute-done.17 = bf16[1,256,1024]{2,1,0:T(8,128)(2,1)S(1)} collective-permute-done((bf16[1,256,1024]{2,1,0:T(8,128)(2,1)S(1)}, bf16[1,256,1024]{2,1,0:T(8,128)(2,1)S(1)}, u32[]{:S(2)}, u32[]{:S(2)}) %collective-permute-start.17) | collective-permute-done | bytes 524320 | tf_op jit(solution)/shard_map/ppermute | solution.py:34
  142.0 6.3 %collective-permute-done.23 = bf16[1,512,256]{2,1,0:T(8,128)(2,1)S(1)} collective-permute-done((bf16[1,512,256]{2,1,0:T(8,128)(2,1)S(1)}, bf16[1,512,256]{2,1,0:T(8,128)(2,1)S(1)}, u32[]{:S(2)}, u32[]{:S(2)}) %collective-permute-start.23) | collective-permute-done | bytes 262176 | tf_op jit(solution)/shard_map/ppermute | solution.py:34
  (72 shorter events, 37.9 us)
Async XLA Ops:
  8.6 7.2 %collective-permute-start = (bf16[4,128,128]{2,1,0:T(8,128)(2,1)S(1)}, bf16[4,128,128]{2,1,0:T(8,128)(2,1)S(1)}, u32[]{:S(2)}, u32[]{:S(2)}) collective-permute-start(bf16[4,128,128]{2,1,0:T(8,128)(2,1)S(1)} %get-tuple-element.125), channel_id=1, source_target_pairs={{0,4},{4,0},{8,12},{12,8},{16,20},{20,16},{24,28},{28,24},{1,5},{5... | collective-permute-start | bytes 393224 | tf_op jit(solution)/shard_map/ppermute | solution.py:34
  16.5 6.9 %collective-permute-start.1 = (bf16[4,128,128]{2,1,0:T(8,128)(2,1)S(1)}, bf16[4,128,128]{2,1,0:T(8,128)(2,1)S(1)}, u32[]{:S(2)}, u32[]{:S(2)}) collective-permute-start(bf16[4,128,128]{2,1,0:T(8,128)(2,1)S(1)} %get-tuple-element.131), channel_id=1, source_target_pairs={{0,8},{4,12},{8,0},{12,4},{16,24},{20,28},{24,16},{28,20},{1,9},{5... | collective-permute-start | bytes 393224 | tf_op jit(solution)/shard_map/ppermute | solution.py:34
  18.1 24.3 %collective-permute-start.4 = (bf16[3,512,256]{2,1,0:T(8,128)(2,1)S(1)}, bf16[3,512,256]{2,1,0:T(8,128)(2,1)S(1)}, u32[]{:S(2)}, u32[]{:S(2)}) collective-permute-start(bf16[3,512,256]{2,1,0:T(8,128)(2,1)S(1)} %get-tuple-element.151), channel_id=1, source_target_pairs={{0,4},{4,0},{8,12},{12,8},{16,20},{20,16},{24,28},{28,24},{1,5},{5... | collective-permute-start | bytes 2359304 | tf_op jit(solution)/shard_map/ppermute | solution.py:34
  24.0 7.5 %collective-permute-start.2 = (bf16[4,128,128]{2,1,0:T(8,128)(2,1)S(1)}, bf16[4,128,128]{2,1,0:T(8,128)(2,1)S(1)}, u32[]{:S(2)}, u32[]{:S(2)}) collective-permute-start(bf16[4,128,128]{2,1,0:T(8,128)(2,1)S(1)} %get-tuple-element.138), channel_id=1, source_target_pairs={{0,16},{4,20},{8,24},{12,28},{16,0},{20,4},{24,8},{28,12},{1,17},{... | collective-permute-start | bytes 393224 | tf_op jit(solution)/shard_map/ppermute | solution.py:34
  26.7 24.7 %collective-permute-start.6 = (bf16[3,512,256]{2,1,0:T(8,128)(2,1)S(1)}, bf16[3,512,256]{2,1,0:T(8,128)(2,1)S(1)}, u32[]{:S(2)}, u32[]{:S(2)}) collective-permute-start(bf16[3,512,256]{2,1,0:T(8,128)(2,1)S(1)} %get-tuple-element.160), channel_id=1, source_target_pairs={{0,8},{4,12},{8,0},{12,4},{16,24},{20,28},{24,16},{28,20},{1,9},{5... | collective-permute-start | bytes 2359304 | tf_op jit(solution)/shard_map/ppermute | solution.py:34
  37.3 5.0 %collective-permute-start.3 = (bf16[4,128,128]{2,1,0:T(8,128)(2,1)S(1)}, bf16[4,128,128]{2,1,0:T(8,128)(2,1)S(1)}, u32[]{:S(2)}, u32[]{:S(2)}) collective-permute-start(bf16[4,128,128]{2,1,0:T(8,128)(2,1)S(1)} %get-tuple-element.147), channel_id=1, source_target_pairs={{0,4},{4,0},{8,12},{12,8},{16,20},{20,16},{24,28},{28,24},{1,5},{5... | collective-permute-start | bytes 393224 | tf_op jit(solution)/shard_map/ppermute | solution.py:34
  43.0 6.9 %collective-permute-start.7 = (bf16[1,512,256]{2,1,0:T(8,128)(2,1)S(1)}, bf16[1,512,256]{2,1,0:T(8,128)(2,1)S(1)}, u32[]{:S(2)}, u32[]{:S(2)}) collective-permute-start(bf16[1,512,256]{2,1,0:T(8,128)(2,1)S(1)} %get-tuple-element.162), channel_id=1, source_target_pairs={{0,4},{4,0},{8,12},{12,8},{16,20},{20,16},{24,28},{28,24},{1,5},{5... | collective-permute-start | bytes 786440 | tf_op jit(solution)/shard_map/ppermute | solution.py:34
  44.7 7.9 %collective-permute-start.5 = (bf16[2,4,128,128]{3,2,1,0:T(8,128)(2,1)S(1)}, bf16[2,4,128,128]{3,2,1,0:T(8,128)(2,1)S(1)}, u32[]{:S(2)}, u32[]{:S(2)}) collective-permute-start(bf16[2,4,128,128]{3,2,1,0:T(8,128)(2,1)S(1)} %get-tuple-element.156), channel_id=1, source_target_pairs={{0,8},{4,12},{8,0},{12,4},{16,24},{20,28},{24,16},{28,20},{1,9},{5... | collective-permute-start | bytes 786440 | tf_op jit(solution)/shard_map/ppermute | solution.py:34
  50.0 26.1 %collective-permute-start.10 = (bf16[4,512,256]{2,1,0:T(8,128)(2,1)S(1)}, bf16[4,512,256]{2,1,0:T(8,128)(2,1)S(1)}, u32[]{:S(2)}, u32[]{:S(2)}) collective-permute-start(bf16[4,512,256]{2,1,0:T(8,128)(2,1)S(1)} %get-tuple-element.189), channel_id=1, source_target_pairs={{0,4},{4,0},{8,12},{12,8},{16,20},{20,16},{24,28},{28,24},{1,5},{5... | collective-permute-start | bytes 3145736 | tf_op jit(solution)/shard_map/ppermute | solution.py:34
  53.2 7.9 %collective-permute-start.8 = (bf16[4,128,128]{2,1,0:T(8,128)(2,1)S(1)}, bf16[4,128,128]{2,1,0:T(8,128)(2,1)S(1)}, u32[]{:S(2)}, u32[]{:S(2)}) collective-permute-start(bf16[4,128,128]{2,1,0:T(8,128)(2,1)S(1)} %get-tuple-element.169), channel_id=1, source_target_pairs={{0,16},{4,20},{8,24},{12,28},{16,0},{20,4},{24,8},{28,12},{1,17},{... | collective-permute-start | bytes 393224 | tf_op jit(solution)/shard_map/ppermute | solution.py:34
  59.2 6.4 %collective-permute-start.9 = (bf16[1,512,256]{2,1,0:T(8,128)(2,1)S(1)}, bf16[1,512,256]{2,1,0:T(8,128)(2,1)S(1)}, u32[]{:S(2)}, u32[]{:S(2)}) collective-permute-start(bf16[1,512,256]{2,1,0:T(8,128)(2,1)S(1)} %get-tuple-element.176), channel_id=1, source_target_pairs={{0,8},{4,12},{8,0},{12,4},{16,24},{20,28},{24,16},{28,20},{1,9},{5... | collective-permute-start | bytes 786440 | tf_op jit(solution)/shard_map/ppermute | solution.py:34
  66.4 14.4 %collective-permute-start.12 = (bf16[2,512,256]{2,1,0:T(8,128)(2,1)S(1)}, bf16[2,512,256]{2,1,0:T(8,128)(2,1)S(1)}, u32[]{:S(2)}, u32[]{:S(2)}) collective-permute-start(bf16[2,512,256]{2,1,0:T(8,128)(2,1)S(1)} %get-tuple-element.197), channel_id=1, source_target_pairs={{0,8},{4,12},{8,0},{12,4},{16,24},{20,28},{24,16},{28,20},{1,9},{5... | collective-permute-start | bytes 1572872 | tf_op jit(solution)/shard_map/ppermute | solution.py:34
  69.1 20.8 %collective-permute-start.11 = (bf16[2,512,256]{2,1,0:T(8,128)(2,1)S(1)}, bf16[2,512,256]{2,1,0:T(8,128)(2,1)S(1)}, u32[]{:S(2)}, u32[]{:S(2)}) collective-permute-start(bf16[2,512,256]{2,1,0:T(8,128)(2,1)S(1)} %get-tuple-element.195), channel_id=1, source_target_pairs={{0,4},{4,0},{8,12},{12,8},{16,20},{20,16},{24,28},{28,24},{1,5},{5... | collective-permute-start | bytes 1572872 | tf_op jit(solution)/shard_map/ppermute | solution.py:34
  80.9 9.1 %collective-permute-start.13 = (bf16[1,512,256]{2,1,0:T(8,128)(2,1)S(1)}, bf16[1,512,256]{2,1,0:T(8,128)(2,1)S(1)}, u32[]{:S(2)}, u32[]{:S(2)}) collective-permute-start(bf16[1,512,256]{2,1,0:T(8,128)(2,1)S(1)} %get-tuple-element.204), channel_id=1, source_target_pairs={{0,16},{4,20},{8,24},{12,28},{16,0},{20,4},{24,8},{28,12},{1,17},{... | collective-permute-start | bytes 786440 | tf_op jit(solution)/shard_map/ppermute | solution.py:34
  90.2 5.8 %collective-permute-start.14 = (bf16[2,256,1024]{2,1,0:T(8,128)(2,1)S(1)}, bf16[2,256,1024]{2,1,0:T(8,128)(2,1)S(1)}, u32[]{:S(2)}, u32[]{:S(2)}) collective-permute-start(bf16[2,256,1024]{2,1,0:T(8,128)(2,1)S(1)} %get-tuple-element.207), channel_id=1, source_target_pairs={{0,1},{1,0},{2,3},{3,2},{4,5},{5,4},{6,7},{7,6},{8,9},{9,8},{10,11... | collective-permute-start | bytes 3145736 | tf_op jit(solution)/shard_map/ppermute | solution.py:34
  90.3 6.0 %collective-permute-start.16 = (bf16[2,256,1024]{2,1,0:T(8,128)(2,1)S(1)}, bf16[2,256,1024]{2,1,0:T(8,128)(2,1)S(1)}, u32[]{:S(2)}, u32[]{:S(2)}) collective-permute-start(bf16[2,256,1024]{2,1,0:T(8,128)(2,1)S(1)} %get-tuple-element.212), channel_id=1, source_target_pairs={{0,1},{1,0},{2,3},{3,2},{4,5},{5,4},{6,7},{7,6},{8,9},{9,8},{10,11... | collective-permute-start | bytes 3145736 | tf_op jit(solution)/shard_map/ppermute | solution.py:34
  90.8 25.2 %collective-permute-start.18 = (bf16[4,512,256]{2,1,0:T(8,128)(2,1)S(1)}, bf16[4,512,256]{2,1,0:T(8,128)(2,1)S(1)}, u32[]{:S(2)}, u32[]{:S(2)}) collective-permute-start(bf16[4,512,256]{2,1,0:T(8,128)(2,1)S(1)} %get-tuple-element.217), channel_id=1, source_target_pairs={{0,4},{4,0},{8,12},{12,8},{16,20},{20,16},{24,28},{28,24},{1,5},{5... | collective-permute-start | bytes 3145736 | tf_op jit(solution)/shard_map/ppermute | solution.py:34
  92.5 19.2 %collective-permute-start.19 = (bf16[2,512,256]{2,1,0:T(8,128)(2,1)S(1)}, bf16[2,512,256]{2,1,0:T(8,128)(2,1)S(1)}, u32[]{:S(2)}, u32[]{:S(2)}) collective-permute-start(bf16[2,512,256]{2,1,0:T(8,128)(2,1)S(1)} %get-tuple-element.218), channel_id=1, source_target_pairs={{0,8},{4,12},{8,0},{12,4},{16,24},{20,28},{24,16},{28,20},{1,9},{5... | collective-permute-start | bytes 1572872 | tf_op jit(solution)/shard_map/ppermute | solution.py:34
  92.6 23.3 %collective-permute-start.20 = (bf16[1,512,256]{2,1,0:T(8,128)(2,1)S(1)}, bf16[1,512,256]{2,1,0:T(8,128)(2,1)S(1)}, u32[]{:S(2)}, u32[]{:S(2)}) collective-permute-start(bf16[1,512,256]{2,1,0:T(8,128)(2,1)S(1)} %get-tuple-element.221), channel_id=1, source_target_pairs={{0,16},{4,20},{8,24},{12,28},{16,0},{20,4},{24,8},{28,12},{1,17},{... | collective-permute-start | bytes 786440 | tf_op jit(solution)/shard_map/ppermute | solution.py:34
  116.2 18.8 %collective-permute-start.21 = (bf16[2,512,256]{2,1,0:T(8,128)(2,1)S(1)}, bf16[2,512,256]{2,1,0:T(8,128)(2,1)S(1)}, u32[]{:S(2)}, u32[]{:S(2)}) collective-permute-start(bf16[2,512,256]{2,1,0:T(8,128)(2,1)S(1)} %get-tuple-element.224), channel_id=1, source_target_pairs={{0,8},{4,12},{8,0},{12,4},{16,24},{20,28},{24,16},{28,20},{1,9},{5... | collective-permute-start | bytes 1572872 | tf_op jit(solution)/shard_map/ppermute | solution.py:34
  116.4 20.9 %collective-permute-start.15 = (bf16[1,256,1024]{2,1,0:T(8,128)(2,1)S(1)}, bf16[1,256,1024]{2,1,0:T(8,128)(2,1)S(1)}, u32[]{:S(2)}, u32[]{:S(2)}) collective-permute-start(bf16[1,256,1024]{2,1,0:T(8,128)(2,1)S(1)} %get-tuple-element.210), channel_id=1, source_target_pairs={{0,2},{1,3},{2,0},{3,1},{4,6},{5,7},{6,4},{7,5},{8,10},{9,11},{10,... | collective-permute-start | bytes 1572872 | tf_op jit(solution)/shard_map/ppermute | solution.py:34
  117.8 15.0 %collective-permute-start.22 = (bf16[1,512,256]{2,1,0:T(8,128)(2,1)S(1)}, bf16[1,512,256]{2,1,0:T(8,128)(2,1)S(1)}, u32[]{:S(2)}, u32[]{:S(2)}) collective-permute-start(bf16[1,512,256]{2,1,0:T(8,128)(2,1)S(1)} %get-tuple-element.225), channel_id=1, source_target_pairs={{0,16},{4,20},{8,24},{12,28},{16,0},{20,4},{24,8},{28,12},{1,17},{... | collective-permute-start | bytes 786440 | tf_op jit(solution)/shard_map/ppermute | solution.py:34
  121.2 19.5 %collective-permute-start.17 = (bf16[1,256,1024]{2,1,0:T(8,128)(2,1)S(1)}, bf16[1,256,1024]{2,1,0:T(8,128)(2,1)S(1)}, u32[]{:S(2)}, u32[]{:S(2)}) collective-permute-start(bf16[1,256,1024]{2,1,0:T(8,128)(2,1)S(1)} %get-tuple-element.215), channel_id=1, source_target_pairs={{0,2},{1,3},{2,0},{3,1},{4,6},{5,7},{6,4},{7,5},{8,10},{9,11},{10,... | collective-permute-start | bytes 1572872 | tf_op jit(solution)/shard_map/ppermute | solution.py:34
  135.1 13.1 %collective-permute-start.23 = (bf16[1,512,256]{2,1,0:T(8,128)(2,1)S(1)}, bf16[1,512,256]{2,1,0:T(8,128)(2,1)S(1)}, u32[]{:S(2)}, u32[]{:S(2)}) collective-permute-start(bf16[1,512,256]{2,1,0:T(8,128)(2,1)S(1)} %get-tuple-element.228), channel_id=1, source_target_pairs={{0,16},{4,20},{8,24},{12,28},{16,0},{20,4},{24,8},{28,12},{1,17},{... | collective-permute-start | bytes 786440 | tf_op jit(solution)/shard_map/ppermute | solution.py:34
  (6 other events, 62.3 us)

commit v11 on v8

--- a/solution.py
+++ b/solution.py
@@ -194,20 +194,22 @@
     out_ref[...] = jnp.full(out_ref.shape, flag(info_ref, 0))
 
 
-def prefix_kernel(bit, info_ref, *refs):
-    before_ref, total_ref, sent_ref = refs[-3:]
-    total, got = refs[0][...], refs[1][...].astype(f32)
+def prefix_kernel(bit, info_ref, total_ref, got_ref, *refs):
+    got = got_ref[...].astype(f32)
     before = got * flag(info_ref, bit)
     if bit:
-        before += refs[2][...]
-    before_ref[...] = before
-    total_ref[...] = total + got
-    sent_ref[...] = (total + got).astype(bf16)
-
-
-def prefix_step(info, bit, arrays):
+        before += refs[0][...]
+        refs = refs[1:]
+    refs[0][...] = before
+    if len(refs) > 1:
+        total = total_ref[...] + got
+        refs[1][...] = total
+        refs[2][...] = total.astype(bf16)
+
+
+def prefix_step(info, bit, arrays, last):
     shape = arrays[0].shape
-    shapes = [(shape, f32), (shape, f32), (shape, bf16)]
+    shapes = [(shape, f32)] if last else [(shape, f32), (shape, f32), (shape, bf16)]
     return small(functools.partial(prefix_kernel, bit), info, arrays, shapes, "prefix_step")
 
 
@@ -229,8 +231,8 @@
     return small(suffix_first_kernel, info, [own, got], shapes, "suffix_first")
 
 
-def suffix_kernel(bit, info_ref, *refs):
-    arrays, (total_ref, mine_ref, mate_ref, other_ref, sent_ref) = refs[:-5], refs[-5:]
+def suffix_kernel(bit, inputs, info_ref, *refs):
+    arrays, outs = refs[:inputs], refs[inputs:]
     upper = flag(info_ref, bit)
     total = arrays[0][...]
     if bit == 1:
@@ -241,17 +243,18 @@
         got = arrays[4][...].astype(f32)
         later = got * (1.0 - upper)
         other = arrays[3][...] + later
-    total_ref[...] = total + got
-    mine_ref[...] = arrays[1][...] + later
-    mate_ref[...] = arrays[2][...] + later
-    other_ref[...] = other
-    sent_ref[...] = (total + got).astype(bf16)
-
-
-def suffix_step(info, bit, arrays):
+    outs[0][...] = arrays[1][...] + later
+    outs[1][...] = arrays[2][...] + later
+    outs[2][...] = other
+    if len(outs) > 3:
+        outs[3][...] = total + got
+        outs[4][...] = (total + got).astype(bf16)
+
+
+def suffix_step(info, bit, arrays, last):
     shape = arrays[0].shape
-    shapes = [(shape, f32)] * 4 + [(shape, bf16)]
-    return small(functools.partial(suffix_kernel, bit), info, arrays, shapes, "suffix_step")
+    shapes = [(shape, f32)] * 3 if last else [(shape, f32)] * 4 + [(shape, bf16)]
+    return small(functools.partial(suffix_kernel, bit, len(arrays)), info, arrays, shapes, "suffix_step")
 
 
 def middle_kernel(query_ref, grad_ref, mask_ref, gain_ref, own_ref, before_ref, normed_t_ref, query_grad_ref, query_grad_t_ref, block_grad_ref, sent_ref, held_ref):
@@ -455,7 +458,7 @@
     (value_send,) = terms(values_t, after(layer_input, own_state), order[half:])
     queries = project(after(layer_input, value_send), 0)
     got = after(got, queries)
-    before, total, sent = prefix_step(info, 0, [own_state, got])
+    before, total, sent = prefix_step(info, 0, [own_state, got], False)
     value_got = exchange(after(value_send, total), "seq", 0)
     for bit in stages[1:]:
         got = exchange(sent, "seq", bit)
@@ -467,7 +470,9 @@
             (mark,) = small(mark_kernel, after(info, total), [], [((8, 128), f32)], "mark")
             key_got = exchange(after(key_send, mark), "seq", 1)
             got = after(got, mark)
-        before, total, sent = prefix_step(info, bit, [total, got, before])
+        before, *sums_on = prefix_step(info, bit, [total, got, before], bit == stages[-1])
+        if sums_on:
+            total, sent = sums_on
 
     normed_t, query_grad, query_grad_t, own_grad, sent = middle(
         queries, normed_grad, mask, norm_gain[None, :], own_state, before
@@ -482,17 +487,21 @@
     got = exchange(sent, "seq", 1)
     query_keep, query_send = terms(query_grad_t, after(layer_input, total), order[:half], order[half:])
     got = after(got, query_keep, key_got)
-    suffix = suffix_step(info, 1, [total, mine, mate, got])
-    query_got = exchange(after(query_send, suffix[0]), "seq", 0)
+    mine, mate, other, *sums_on = suffix_step(info, 1, [total, mine, mate, got], False)
+    total, sent = sums_on
+    query_got = exchange(after(query_send, total), "seq", 0)
 
     for bit in stages[2:]:
-        got = exchange(suffix[4], "seq", bit)
+        got = exchange(sent, "seq", bit)
         if bit == 2:
-            (value_keep,) = terms(values_t, after(layer_input, suffix[0]), order[:half])
+            (value_keep,) = terms(values_t, after(layer_input, total), order[:half])
             (key_keep,) = terms(keys_t, after(layer_input, value_keep), swapped[:half])
             got = after(got, key_keep)
-        suffix = suffix_step(info, bit, list(suffix[:4]) + [got])
-    total, mine, mate, other, sent = suffix
+        mine, mate, other, *sums_on = suffix_step(
+            info, bit, [total, mine, mate, other, got], bit == stages[-1]
+        )
+        if sums_on:
+            total, sent = sums_on
 
     value_keep, value_send, key_keep, key_send = late_terms(
         mine, mate, other, value_keep, value_got, key_keep, key_got

time: 145 us -> 144 us (level)
  transfers between devices with their start and end apart: 19 -> 19, of which waited for: 10 -> 10; matrix products, arithmetic and copies ran while one was open for 5% -> 5% of each run, Pallas kernels for 25% -> 24%
where the time goes in v11:
time: 144 us
  waiting for transfers between devices  67.8 us (47%)
  Pallas kernels  44.8 us (31%)
  starting transfers between devices  22.6 us (16%)
  matrix products  4.72 us (3%)
  other arithmetic  2.28 us (2%)
    ppermute x19, waiting for transfers between devices, exchange(): return lax.ppermute(arr, axis, [(i, i ^ 1 << bit) for i in range(count)])  67.8 us
    ppermute x19, starting transfers between devices, exchange(): return lax.ppermute(arr, axis, [(i, i ^ 1 << bit) for i in range(count)])  22.6 us
    pallas_call x6, Pallas kernels, gradient_terms(): pl.pallas_call(functools.partial(terms_kernel, len(lefts), outputs), in_s...  13.1 us
    pallas_call x1, Pallas kernels, input_terms(): pl.pallas_call(functools.partial(input_kernel, order), grid_spec=pltpu.Pr...  9.12 us
    pallas_call x1, Pallas kernels, block_states(): pl.pallas_call(functools.partial(states_kernel, parts), in_specs=[hbm, hb...  7.89 us
    pallas_call x1, Pallas kernels, middle(): pl.pallas_call(middle_kernel, grid=(heads,), in_specs=[column, column, pl...  4.66 us
    pallas_call x6, Pallas kernels, small(): pl.pallas_call(kernel, in_specs=[pl.BlockSpec(memory_space=pltpu.SMEM)] +...  3.73 us
  transfers between devices with their start and end apart: 19, of which 10 were waited for; matrix products, arithmetic and copies ran while one was open for 5% of the time, Pallas kernels for 24%

profile of v11, /device:TPU:0, one launch (start us, length us, event | category | flops | bytes accessed | tf_op | source)
XLA Modules:
  0.0 144.1 jit_solution(1146008423986151304)
XLA Ops:
  0.7 7.9 %block_states.1 = (bf16[1024,512]{1,0:T(8,128)(2,1)S(1)}, bf16[1024,512]{1,0:T(8,128)(2,1)S(1)}, f32[4,128,128]{2,1,0:T(8,128)S(1)}, bf16[4,128,128]{2,1,0:T(8,1...) custom-call(bf16[1024,2048]{1,0:T(8,128)(2,1)} %rows_ref, ...), custom_call_target="tpu_custom_call" | custom-call | flops 1000000 | bytes 1 | tf_op jit(solution)/shard_map/block_states/pallas_call | solution.py:82
  8.6 3.0 %collective-permute-start = (bf16[4,128,128]{2,1,0:T(8,128)(2,1)S(1)}, bf16[4,128,128]{2,1,0:T(8,128)(2,1)S(1)}, u32[]{:S(2)}, u32[]{:S(2)}) collective-permute-start(bf16[4,128,128]{2,1,0:T(8,128)(2,1)S(1)} %get-tuple-element.98), channel_id=1, source_target_pairs={{0,4},{4,0},{8,12},{12,8},{16,20},{20,16},{24,28},{28,24},{1,5},{5... | collective-permute-start | bytes 393224 | tf_op jit(solution)/shard_map/ppermute | solution.py:34
  11.7 1.8 %gradient_terms.6 = bf16[4,512,256]{2,1,0:T(8,128)(2,1)S(1)} custom-call(s32[2]{0:T(128)S(1)} %pad_add_fusion.position_ref.info_ref.place_ref, bf16[512,1024]{1,0:T(8,128)(2,1)S(1)} %get-tuple-element.93.refs_0_, bf16[1024,2048]{1,0:T(8,128)(2,1)S(1)} %get-tuple-element.139.refs_1_), custom_call_target="tpu_custom_call" | custom-call | flops 1000000 | bytes 1 | tf_op jit(solution)/shard_map/gradient_terms/pallas_call | solution.py:130
  14.4 2.3 %fusion.1.query_ref = bf16[1024,512]{1,0:T(8,128)(2,1)S(1)} fusion(bf16[1024,2048]{1,0:T(8,128)(2,1)S(1)} %get-tuple-element.139.refs_1_, bf16[3,2048,512]{2,1,0:T(8,128)(2,1)S(1)} %bitcast.22), kind=kOutput, calls=%fused_computation.3 | convolution fusion | flops 2148007936 | bytes 7340032 | tf_op jit(solution)/shard_map/dot_general | solution.py:449
  19.5 2.4 %fusion.3.grad_ref = f32[1024,512]{1,0:T(8,128)S(1)} fusion(bf16[1024,2048]{1,0:T(8,128)(2,1)S(1)} %copy-done.3, bf16[512,2048]{1,0:T(8,128)(2,1)S(1)} %copy-done), kind=kOutput, calls=%fused_computation.7 | convolution fusion | flops 2147483648 | bytes 8388608 | tf_op jit(solution)/shard_map/dot_general | solution.py:29
  22.0 1.8 %gradient_terms.7 = bf16[4,512,256]{2,1,0:T(8,128)(2,1)S(1)} custom-call(s32[2]{0:T(128)S(1)} %pad_add_fusion.position_ref.info_ref.place_ref, bf16[512,1024]{1,0:T(8,128)(2,1)S(1)} %get-tuple-element.105.refs_0_, bf16[1024,2048]{1,0:T(8,128)(2,1)S(1)} %get-tuple-element.139.refs_1_), custom_call_target="tpu_custom_call" | custom-call | flops 1000000 | bytes 1 | tf_op jit(solution)/shard_map/gradient_terms/pallas_call | solution.py:130
  24.4 2.7 %collective-permute-start.2 = (bf16[4,128,128]{2,1,0:T(8,128)(2,1)S(1)}, bf16[4,128,128]{2,1,0:T(8,128)(2,1)S(1)}, u32[]{:S(2)}, u32[]{:S(2)}) collective-permute-start(bf16[4,128,128]{2,1,0:T(8,128)(2,1)S(1)} %get-tuple-element.110), channel_id=1, source_target_pairs={{0,16},{4,20},{8,24},{12,28},{16,0},{20,4},{24,8},{28,12},{1,17},{... | collective-permute-start | bytes 393224 | tf_op jit(solution)/shard_map/ppermute | solution.py:34
  27.5 4.9 %collective-permute-done.2.got_ref = bf16[4,128,128]{2,1,0:T(8,128)(2,1)S(1)} collective-permute-done((bf16[4,128,128]{2,1,0:T(8,128)(2,1)S(1)}, bf16[4,128,128]{2,1,0:T(8,128)(2,1)S(1)}, u32[]{:S(2)}, u32[]{:S(2)}) %collective-permute-start.2) | collective-permute-done | bytes 131104 | tf_op jit(solution)/shard_map/ppermute | solution.py:34
  33.1 4.7 %norm_backward.1 = (bf16[512,1024]{1,0:T(8,128)(2,1)S(1)}, bf16[1024,512]{1,0:T(8,128)(2,1)S(1)}, bf16[512,1024]{1,0:T(8,128)(2,1)S(1)}, f32[4,128,128]{2,1,0:T(8,128)S(1)}, bf16[4,128,128]{2,1,0:T(8,128)(2,1)S(1)}) custom-call(bf16[1024,512]{1,0:T(8,128)(2,1)S(1)} %fusion.1.query_ref, f32[1024,512]{1,0:T(8,128)S(1)} %fusion.3.grad_ref, ...), custom_call_target="tpu_custom_call" | custom-call | flops 4294967296 | bytes 1 | tf_op jit(solution)/shard_map/norm_backward/pallas_call | solution.py:292
  39.4 2.9 %gradient_terms.8 = (bf16[4,512,256]{2,1,0:T(8,128)(2,1)S(1)}, bf16[4,512,256]{2,1,0:T(8,128)(2,1)S(1)}) custom-call(s32[2]{0:T(128)S(1)} %pad_add_fusion.position_ref.info_ref.place_ref, bf16[512,1024]{1,0:T(8,128)(2,1)S(1)} %get-tuple-element.119.refs_0_, bf16[1024,2048]{1,0:T(8,128)(2,1)S(1)} %copy-done.3), custom_call_target="tpu_custom_call" | custom-call | flops 1000000 | bytes 1 | tf_op jit(solution)/shard_map/gradient_terms/pallas_call | solution.py:130
  42.3 3.9 %collective-permute-done.3.got_ref = bf16[4,128,128]{2,1,0:T(8,128)(2,1)S(1)} collective-permute-done((bf16[4,128,128]{2,1,0:T(8,128)(2,1)S(1)}, bf16[4,128,128]{2,1,0:T(8,128)(2,1)S(1)}, u32[]{:S(2)}, u32[]{:S(2)}) %collective-permute-start.3) | collective-permute-done | bytes 131104 | tf_op jit(solution)/shard_map/ppermute | solution.py:34
  47.8 2.9 %gradient_terms.9 = (bf16[4,512,256]{2,1,0:T(8,128)(2,1)S(1)}, bf16[4,512,256]{2,1,0:T(8,128)(2,1)S(1)}) custom-call(s32[2]{0:T(128)S(1)} %pad_add_fusion.position_ref.info_ref.place_ref, bf16[512,1024]{1,0:T(8,128)(2,1)S(1)} %get-tuple-element.128.refs_0_, bf16[1024,2048]{1,0:T(8,128)(2,1)S(1)} %get-tuple-element.139.refs_1_), custom_call_target="tpu_custom_call" | custom-call | flops 1000000 | bytes 1 | tf_op jit(solution)/shard_map/gradient_terms/pallas_call | solution.py:130
  50.7 3.9 %collective-permute-done.6.refs_3_ = bf16[4,512,256]{2,1,0:T(8,128)(2,1)S(1)} collective-permute-done((bf16[4,512,256]{2,1,0:T(8,128)(2,1)S(1)}, bf16[4,512,256]{2,1,0:T(8,128)(2,1)S(1)}, u32[]{:S(2)}, u32[]{:S(2)}) %collective-permute-start.6) | collective-permute-done | bytes 1048608 | tf_op jit(solution)/shard_map/ppermute | solution.py:34
  54.6 4.5 %collective-permute-done.5.refs_3_ = bf16[2,4,128,128]{3,2,1,0:T(8,128)(2,1)S(1)} collective-permute-done((bf16[2,4,128,128]{3,2,1,0:T(8,128)(2,1)S(1)}, bf16[2,4,128,128]{3,2,1,0:T(8,128)(2,1)S(1)}, u32[]{:S(2)}, u32[]{:S(2)}) %collective-permute-start.5) | collective-permute-done | bytes 262176 | tf_op jit(solution)/shard_map/ppermute | solution.py:34
  59.9 1.8 %gradient_terms.10.refs_0_ = bf16[4,512,256]{2,1,0:T(8,128)(2,1)S(1)} custom-call(s32[2]{0:T(128)S(1)} %pad_add_fusion.position_ref.info_ref.place_ref, bf16[512,1024]{1,0:T(8,128)(2,1)S(1)} %get-tuple-element.93.refs_0_, bf16[1024,2048]{1,0:T(8,128)(2,1)S(1)} %get-tuple-element.139.refs_1_), custom_call_target="tpu_custom_call" | custom-call | flops 1000000 | bytes 1 | tf_op jit(solution)/shard_map/gradient_terms/pallas_call | solution.py:130
  61.7 1.8 %gradient_terms.11.refs_2_ = bf16[4,512,256]{2,1,0:T(8,128)(2,1)S(1)} custom-call(s32[2]{0:T(128)S(1)} %pad_add_fusion.position_ref.info_ref.place_ref, bf16[512,1024]{1,0:T(8,128)(2,1)S(1)} %get-tuple-element.105.refs_0_, bf16[1024,2048]{1,0:T(8,128)(2,1)S(1)} %get-tuple-element.139.refs_1_), custom_call_target="tpu_custom_call" | custom-call | flops 1000000 | bytes 1 | tf_op jit(solution)/shard_map/gradient_terms/pallas_call | solution.py:130
  63.5 3.5 %collective-permute-done.7.refs_4_ = bf16[4,128,128]{2,1,0:T(8,128)(2,1)S(1)} collective-permute-done((bf16[4,128,128]{2,1,0:T(8,128)(2,1)S(1)}, bf16[4,128,128]{2,1,0:T(8,128)(2,1)S(1)}, u32[]{:S(2)}, u32[]{:S(2)}) %collective-permute-start.7) | collective-permute-done | bytes 131104 | tf_op jit(solution)/shard_map/ppermute | solution.py:34
  69.1 1.7 %collective-permute-start.10 = (bf16[2,512,256]{2,1,0:T(8,128)(2,1)S(1)}, bf16[2,512,256]{2,1,0:T(8,128)(2,1)S(1)}, u32[]{:S(2)}, u32[]{:S(2)}) collective-permute-start(bf16[2,512,256]{2,1,0:T(8,128)(2,1)S(1)} %get-tuple-element.153), channel_id=1, source_target_pairs={{0,4},{4,0},{8,12},{12,8},{16,20},{20,16},{24,28},{28,24},{1,5},{5... | collective-permute-start | bytes 1572872 | tf_op jit(solution)/shard_map/ppermute | solution.py:34
  70.8 1.9 %key_value_grads.1 = (bf16[1024,512]{1,0:T(8,128)(2,1)S(1)}, bf16[1024,512]{1,0:T(8,128)(2,1)S(1)}) custom-call(bf16[1024,512]{1,0:T(8,128)(2,1)S(1)} %get-tuple-element.115.key_ref, bf16[1024,512]{1,0:T(8,128)(2,1)S(1)} %get-tuple-element.116.value_ref, f32[4,128,128]{2,1,0:T(8,128)S(1)} %get-tuple-element.145.mine_ref.grad_ref), custom_call_target="tpu_custom_call" | custom-call | flops 1000000 | bytes 1 | tf_op jit(solution)/shard_map/key_value_grads/pallas_call | solution.py:362
  72.7 9.1 %input_terms.1 = (bf16[2,256,2048]{2,1,0:T(8,128)(2,1)S(1)}, bf16[2,256,2048]{2,1,0:T(8,128)(2,1)S(1)}) custom-call(s32[2]{0:T(128)S(1)} %pad_add_fusion.position_ref.info_ref.place_ref, bf16[1024,512]{1,0:T(8,128)(2,1)S(1)} %get-tuple-element.114.query_ref, bf16[1024,512]{1,0:T(8,128)(2,1)S(1)} %get-tuple-element.146.key_ref, ...), custom_call_target="tpu_custom_call" | custom-call | flops 1000000 | bytes 1 | tf_op jit(solution)/shard_map/input_terms/pallas_call | solution.py:394
  88.6 21.2 %collective-permute-done.15 = bf16[1,1024,256]{2,1,0:T(8,128)(2,1)S(1)} collective-permute-done((bf16[1,1024,256]{2,1,0:T(8,128)(2,1)S(1)}, bf16[1,1024,256]{2,1,0:T(8,128)(2,1)S(1)}, u32[]{:S(2)}, u32[]{:S(2)}) %collective-permute-start.15) | collective-permute-done | bytes 524320 | tf_op jit(solution)/shard_map/ppermute | solution.py:34
  112.5 14.9 %collective-permute-done.17 = bf16[1,512,256]{2,1,0:T(8,128)(2,1)S(1)} collective-permute-done((bf16[1,512,256]{2,1,0:T(8,128)(2,1)S(1)}, bf16[1,512,256]{2,1,0:T(8,128)(2,1)S(1)}, u32[]{:S(2)}, u32[]{:S(2)}) %collective-permute-start.17) | collective-permute-done | bytes 262176 | tf_op jit(solution)/shard_map/ppermute | solution.py:34
  129.2 2.6 %collective-permute-start.18 = (bf16[1,512,256]{2,1,0:T(8,128)(2,1)S(1)}, bf16[1,512,256]{2,1,0:T(8,128)(2,1)S(1)}, u32[]{:S(2)}, u32[]{:S(2)}) collective-permute-start(bf16[1,512,256]{2,1,0:T(8,128)(2,1)S(1)} %get-tuple-element.176), channel_id=1, source_target_pairs={{0,16},{4,20},{8,24},{12,28},{16,0},{20,4},{24,8},{28,12},{1,17},{... | collective-permute-start | bytes 786440 | tf_op jit(solution)/shard_map/ppermute | solution.py:34
  133.2 9.3 %collective-permute-done.18 = bf16[1,512,256]{2,1,0:T(8,128)(2,1)S(1)} collective-permute-done((bf16[1,512,256]{2,1,0:T(8,128)(2,1)S(1)}, bf16[1,512,256]{2,1,0:T(8,128)(2,1)S(1)}, u32[]{:S(2)}, u32[]{:S(2)}) %collective-permute-start.18) | collective-permute-done | bytes 262176 | tf_op jit(solution)/shard_map/ppermute | solution.py:34
  (56 shorter events, 25.6 us)
Async XLA Ops:
  0.6 18.9 %copy-start = (bf16[512,2048]{1,0:T(8,128)(2,1)S(1)}, bf16[512,2048]{1,0:T(8,128)(2,1)}, u32[]{:S(2)}) copy-start(bf16[512,2048]{1,0:T(8,128)(2,1)} %param.10) | copy-start | bytes 6291460
  8.6 8.2 %collective-permute-start = (bf16[4,128,128]{2,1,0:T(8,128)(2,1)S(1)}, bf16[4,128,128]{2,1,0:T(8,128)(2,1)S(1)}, u32[]{:S(2)}, u32[]{:S(2)}) collective-permute-start(bf16[4,128,128]{2,1,0:T(8,128)(2,1)S(1)} %get-tuple-element.98), channel_id=1, source_target_pairs={{0,4},{4,0},{8,12},{12,8},{16,20},{20,16},{24,28},{28,24},{1,5},{5... | collective-permute-start | bytes 393224 | tf_op jit(solution)/shard_map/ppermute | solution.py:34
  14.4 5.1 %copy-start.3 = (bf16[1024,2048]{1,0:T(8,128)(2,1)S(1)}, bf16[1024,2048]{1,0:T(8,128)(2,1)}, u32[]{:S(2)}) copy-start(bf16[1024,2048]{1,0:T(8,128)(2,1)} %refs_1_) | copy-start | bytes 12582916
  17.4 6.4 %collective-permute-start.1 = (bf16[4,128,128]{2,1,0:T(8,128)(2,1)S(1)}, bf16[4,128,128]{2,1,0:T(8,128)(2,1)S(1)}, u32[]{:S(2)}, u32[]{:S(2)}) collective-permute-start(bf16[4,128,128]{2,1,0:T(8,128)(2,1)S(1)} %get-tuple-element.104), channel_id=1, source_target_pairs={{0,8},{4,12},{8,0},{12,4},{16,24},{20,28},{24,16},{28,20},{1,9},{5... | collective-permute-start | bytes 393224 | tf_op jit(solution)/shard_map/ppermute | solution.py:34
  19.0 27.2 %collective-permute-start.4 = (bf16[4,512,256]{2,1,0:T(8,128)(2,1)S(1)}, bf16[4,512,256]{2,1,0:T(8,128)(2,1)S(1)}, u32[]{:S(2)}, u32[]{:S(2)}) collective-permute-start(bf16[4,512,256]{2,1,0:T(8,128)(2,1)S(1)} %gradient_terms.6), channel_id=1, source_target_pairs={{0,4},{4,0},{8,12},{12,8},{16,20},{20,16},{24,28},{28,24},{1,5},{5... | collective-permute-start | bytes 3145736 | tf_op jit(solution)/shard_map/ppermute | solution.py:34
  21.9 5.6 %copy-start.5 = (bf16[512]{0:T(512)(128)(2,1)S(1)}, bf16[512]{0:T(512)(128)(2,1)}, u32[]{:S(2)}) copy-start(bf16[512]{0:T(512)(128)(2,1)} %param.11) | copy-start | bytes 3076
  21.9 11.1 %copy-start.4 = (s32[1024]{0:T(1024)S(1)}, s32[1024]{0:T(1024)}, u32[]{:S(2)}) copy-start(s32[1024]{0:T(1024)} %param.8) | copy-start | bytes 12292
  24.4 8.1 %collective-permute-start.2 = (bf16[4,128,128]{2,1,0:T(8,128)(2,1)S(1)}, bf16[4,128,128]{2,1,0:T(8,128)(2,1)S(1)}, u32[]{:S(2)}, u32[]{:S(2)}) collective-permute-start(bf16[4,128,128]{2,1,0:T(8,128)(2,1)S(1)} %get-tuple-element.110), channel_id=1, source_target_pairs={{0,16},{4,20},{8,24},{12,28},{16,0},{20,4},{24,8},{28,12},{1,17},{... | collective-permute-start | bytes 393224 | tf_op jit(solution)/shard_map/ppermute | solution.py:34
  27.1 27.5 %collective-permute-start.6 = (bf16[4,512,256]{2,1,0:T(8,128)(2,1)S(1)}, bf16[4,512,256]{2,1,0:T(8,128)(2,1)S(1)}, u32[]{:S(2)}, u32[]{:S(2)}) collective-permute-start(bf16[4,512,256]{2,1,0:T(8,128)(2,1)S(1)} %gradient_terms.7), channel_id=1, source_target_pairs={{0,8},{4,12},{8,0},{12,4},{16,24},{20,28},{24,16},{28,20},{1,9},{5... | collective-permute-start | bytes 3145736 | tf_op jit(solution)/shard_map/ppermute | solution.py:34
  37.7 8.5 %collective-permute-start.3 = (bf16[4,128,128]{2,1,0:T(8,128)(2,1)S(1)}, bf16[4,128,128]{2,1,0:T(8,128)(2,1)S(1)}, u32[]{:S(2)}, u32[]{:S(2)}) collective-permute-start(bf16[4,128,128]{2,1,0:T(8,128)(2,1)S(1)} %get-tuple-element.118), channel_id=1, source_target_pairs={{0,4},{4,0},{8,12},{12,8},{16,20},{20,16},{24,28},{28,24},{1,5},{5... | collective-permute-start | bytes 393224 | tf_op jit(solution)/shard_map/ppermute | solution.py:34
  46.9 35.2 %collective-permute-start.8 = (bf16[4,512,256]{2,1,0:T(8,128)(2,1)S(1)}, bf16[4,512,256]{2,1,0:T(8,128)(2,1)S(1)}, u32[]{:S(2)}, u32[]{:S(2)}) collective-permute-start(bf16[4,512,256]{2,1,0:T(8,128)(2,1)S(1)} %get-tuple-element.151), channel_id=1, source_target_pairs={{0,4},{4,0},{8,12},{12,8},{16,20},{20,16},{24,28},{28,24},{1,5},{5... | collective-permute-start | bytes 3145736 | tf_op jit(solution)/shard_map/ppermute | solution.py:34
  47.4 11.7 %collective-permute-start.5 = (bf16[2,4,128,128]{3,2,1,0:T(8,128)(2,1)S(1)}, bf16[2,4,128,128]{3,2,1,0:T(8,128)(2,1)S(1)}, u32[]{:S(2)}, u32[]{:S(2)}) collective-permute-start(bf16[2,4,128,128]{3,2,1,0:T(8,128)(2,1)S(1)} %get-tuple-element.127), channel_id=1, source_target_pairs={{0,8},{4,12},{8,0},{12,4},{16,24},{20,28},{24,16},{28,20},{1,9},{5... | collective-permute-start | bytes 786440 | tf_op jit(solution)/shard_map/ppermute | solution.py:34
  59.8 7.3 %collective-permute-start.7 = (bf16[4,128,128]{2,1,0:T(8,128)(2,1)S(1)}, bf16[4,128,128]{2,1,0:T(8,128)(2,1)S(1)}, u32[]{:S(2)}, u32[]{:S(2)}) collective-permute-start(bf16[4,128,128]{2,1,0:T(8,128)(2,1)S(1)} %get-tuple-element.137), channel_id=1, source_target_pairs={{0,16},{4,20},{8,24},{12,28},{16,0},{20,4},{24,8},{28,12},{1,17},{... | collective-permute-start | bytes 393224 | tf_op jit(solution)/shard_map/ppermute | solution.py:34
  69.0 12.8 %collective-permute-start.9 = (bf16[2,512,256]{2,1,0:T(8,128)(2,1)S(1)}, bf16[2,512,256]{2,1,0:T(8,128)(2,1)S(1)}, u32[]{:S(2)}, u32[]{:S(2)}) collective-permute-start(bf16[2,512,256]{2,1,0:T(8,128)(2,1)S(1)} %get-tuple-element.152), channel_id=1, source_target_pairs={{0,8},{4,12},{8,0},{12,4},{16,24},{20,28},{24,16},{28,20},{1,9},{5... | collective-permute-start | bytes 1572872 | tf_op jit(solution)/shard_map/ppermute | solution.py:34
  69.1 12.8 %collective-permute-start.10 = (bf16[2,512,256]{2,1,0:T(8,128)(2,1)S(1)}, bf16[2,512,256]{2,1,0:T(8,128)(2,1)S(1)}, u32[]{:S(2)}, u32[]{:S(2)}) collective-permute-start(bf16[2,512,256]{2,1,0:T(8,128)(2,1)S(1)} %get-tuple-element.153), channel_id=1, source_target_pairs={{0,4},{4,0},{8,12},{12,8},{16,20},{20,16},{24,28},{28,24},{1,5},{5... | collective-permute-start | bytes 1572872 | tf_op jit(solution)/shard_map/ppermute | solution.py:34
  82.3 4.2 %collective-permute-start.11 = (bf16[2,256,2048]{2,1,0:T(8,128)(2,1)S(1)}, bf16[2,256,2048]{2,1,0:T(8,128)(2,1)S(1)}, u32[]{:S(2)}, u32[]{:S(2)}) collective-permute-start(bf16[2,256,2048]{2,1,0:T(8,128)(2,1)S(1)} %get-tuple-element.160), channel_id=1, source_target_pairs={{0,1},{1,0},{2,3},{3,2},{4,5},{5,4},{6,7},{7,6},{8,9},{9,8},{10,11... | collective-permute-start | bytes 6291464 | tf_op jit(solution)/shard_map/ppermute | solution.py:34
  82.4 27.5 %collective-permute-start.13 = (bf16[4,512,256]{2,1,0:T(8,128)(2,1)S(1)}, bf16[4,512,256]{2,1,0:T(8,128)(2,1)S(1)}, u32[]{:S(2)}, u32[]{:S(2)}) collective-permute-start(bf16[4,512,256]{2,1,0:T(8,128)(2,1)S(1)} %get-tuple-element.165), channel_id=1, source_target_pairs={{0,4},{4,0},{8,12},{12,8},{16,20},{20,16},{24,28},{28,24},{1,5},{5... | collective-permute-start | bytes 3145736 | tf_op jit(solution)/shard_map/ppermute | solution.py:34
  83.7 26.1 %collective-permute-start.15 = (bf16[1,1024,256]{2,1,0:T(8,128)(2,1)S(1)}, bf16[1,1024,256]{2,1,0:T(8,128)(2,1)S(1)}, u32[]{:S(2)}, u32[]{:S(2)}) collective-permute-start(bf16[1,1024,256]{2,1,0:T(8,128)(2,1)S(1)} %get-tuple-element.167), channel_id=1, source_target_pairs={{0,16},{4,20},{8,24},{12,28},{16,0},{20,4},{24,8},{28,12},{1,17},{... | collective-permute-start | bytes 1572872 | tf_op jit(solution)/shard_map/ppermute | solution.py:34
  85.3 24.5 %collective-permute-start.14 = (bf16[2,512,256]{2,1,0:T(8,128)(2,1)S(1)}, bf16[2,512,256]{2,1,0:T(8,128)(2,1)S(1)}, u32[]{:S(2)}, u32[]{:S(2)}) collective-permute-start(bf16[2,512,256]{2,1,0:T(8,128)(2,1)S(1)} %get-tuple-element.166), channel_id=1, source_target_pairs={{0,8},{4,12},{8,0},{12,4},{16,24},{20,28},{24,16},{28,20},{1,9},{5... | collective-permute-start | bytes 1572872 | tf_op jit(solution)/shard_map/ppermute | solution.py:34
  87.0 42.0 %collective-permute-start.12 = (bf16[1,256,2048]{2,1,0:T(8,128)(2,1)S(1)}, bf16[1,256,2048]{2,1,0:T(8,128)(2,1)S(1)}, u32[]{:S(2)}, u32[]{:S(2)}) collective-permute-start(bf16[1,256,2048]{2,1,0:T(8,128)(2,1)S(1)} %get-tuple-element.163), channel_id=1, source_target_pairs={{0,2},{1,3},{2,0},{3,1},{4,6},{5,7},{6,4},{7,5},{8,10},{9,11},{10,... | collective-permute-start | bytes 3145736 | tf_op jit(solution)/shard_map/ppermute | solution.py:34
  110.2 18.8 %collective-permute-start.16 = (bf16[2,512,256]{2,1,0:T(8,128)(2,1)S(1)}, bf16[2,512,256]{2,1,0:T(8,128)(2,1)S(1)}, u32[]{:S(2)}, u32[]{:S(2)}) collective-permute-start(bf16[2,512,256]{2,1,0:T(8,128)(2,1)S(1)} %get-tuple-element.172), channel_id=1, source_target_pairs={{0,8},{4,12},{8,0},{12,4},{16,24},{20,28},{24,16},{28,20},{1,9},{5... | collective-permute-start | bytes 1572872 | tf_op jit(solution)/shard_map/ppermute | solution.py:34
  111.1 16.3 %collective-permute-start.17 = (bf16[1,512,256]{2,1,0:T(8,128)(2,1)S(1)}, bf16[1,512,256]{2,1,0:T(8,128)(2,1)S(1)}, u32[]{:S(2)}, u32[]{:S(2)}) collective-permute-start(bf16[1,512,256]{2,1,0:T(8,128)(2,1)S(1)} %get-tuple-element.173), channel_id=1, source_target_pairs={{0,16},{4,20},{8,24},{12,28},{16,0},{20,4},{24,8},{28,12},{1,17},{... | collective-permute-start | bytes 786440 | tf_op jit(solution)/shard_map/ppermute | solution.py:34
  129.2 13.3 %collective-permute-start.18 = (bf16[1,512,256]{2,1,0:T(8,128)(2,1)S(1)}, bf16[1,512,256]{2,1,0:T(8,128)(2,1)S(1)}, u32[]{:S(2)}, u32[]{:S(2)}) collective-permute-start(bf16[1,512,256]{2,1,0:T(8,128)(2,1)S(1)} %get-tuple-element.176), channel_id=1, source_target_pairs={{0,16},{4,20},{8,24},{12,28},{16,0},{20,4},{24,8},{28,12},{1,17},{... | collective-permute-start | bytes 786440 | tf_op jit(solution)/shard_map/ppermute | solution.py:34
  131.8 12.3 %copy-start.1 = (bf16[512,2048]{1,0:T(8,128)(2,1)S(1)}, bf16[512,2048]{1,0:T(8,128)(2,1)}, u32[]{:S(2)}) copy-start(bf16[512,2048]{1,0:T(8,128)(2,1)} %param.10) | copy-start | bytes 6291460
  (1 other events, 2.8 us)

commit v12 on v11

--- a/solution.py
+++ b/solution.py
@@ -531,7 +531,9 @@
         input_keep, input_got = stage(input_keep, input_got, out_keep, bit, "head")
     out_keep, out_got = stage(out_keep, out_got, (input_keep, late_got), 2)
     query_keep, query_got = stage(query_keep, query_got, out_keep, 1)
-    query_keep, query_got = stage(query_keep, query_got, (query_keep, out_got, input_got), 2)
+    query_keep, query_send = sums([(query_keep, after(query_got, query_keep))])
+    out_got, input_got = after((out_got, input_got), query_keep)
+    query_got = after(exchange(query_send, "seq", 2), out_got, input_got)
 
     out_pair = rest(out_keep, out_got, stages[3:])
     late_pair = rest(late_keep, late_got, stages[3:])

time: 144 us -> 143 us (level)
  starting transfers between devices: 22.6 us -> 20 us
  waiting for transfers between devices: 67.8 us -> 69.3 us
    ppermute x19, starting transfers between devices: 22.6 us -> 20 us  [exchange(): return lax.ppermute(arr, axis, [(i, i ^ 1 << bit) for i in range(count)])]
    ppermute x19, waiting for transfers between devices: 67.8 us -> 69.3 us  [exchange(): return lax.ppermute(arr, axis, [(i, i ^ 1 << bit) for i in range(count)])]
  transfers between devices with their start and end apart: 19 -> 19, of which waited for: 10 -> 9; matrix products, arithmetic and copies ran while one was open for 5% -> 5% of each run, Pallas kernels for 24% -> 24%
where the time goes in v12:
time: 143 us
  waiting for transfers between devices  69.3 us (48%)
  Pallas kernels  44.8 us (31%)
  starting transfers between devices  20 us (14%)
  matrix products  4.72 us (3%)
  other arithmetic  2.29 us (2%)
    ppermute x19, waiting for transfers between devices, exchange(): return lax.ppermute(arr, axis, [(i, i ^ 1 << bit) for i in range(count)])  69.3 us
    ppermute x19, starting transfers between devices, exchange(): return lax.ppermute(arr, axis, [(i, i ^ 1 << bit) for i in range(count)])  20 us
    pallas_call x6, Pallas kernels, gradient_terms(): pl.pallas_call(functools.partial(terms_kernel, len(lefts), outputs), in_s...  13.1 us
    pallas_call x1, Pallas kernels, input_terms(): pl.pallas_call(functools.partial(input_kernel, order), grid_spec=pltpu.Pr...  9.12 us
    pallas_call x1, Pallas kernels, block_states(): pl.pallas_call(functools.partial(states_kernel, parts), in_specs=[hbm, hb...  7.89 us
    pallas_call x1, Pallas kernels, middle(): pl.pallas_call(middle_kernel, grid=(heads,), in_specs=[column, column, pl...  4.66 us
    pallas_call x6, Pallas kernels, small(): pl.pallas_call(kernel, in_specs=[pl.BlockSpec(memory_space=pltpu.SMEM)] +...  3.73 us
  transfers between devices with their start and end apart: 19, of which 9 were waited for; matrix products, arithmetic and copies ran while one was open for 5% of the time, Pallas kernels for 24%

profile of v12, /device:TPU:0, one launch (start us, length us, event | category | flops | bytes accessed | tf_op | source)
XLA Modules:
  0.0 143.1 jit_solution(4765672334086834053)
XLA Ops:
  0.7 7.9 %block_states.1 = (bf16[1024,512]{1,0:T(8,128)(2,1)S(1)}, bf16[1024,512]{1,0:T(8,128)(2,1)S(1)}, f32[4,128,128]{2,1,0:T(8,128)S(1)}, bf16[4,128,128]{2,1,0:T(8,1...) custom-call(bf16[1024,2048]{1,0:T(8,128)(2,1)} %rows_ref, ...), custom_call_target="tpu_custom_call" | custom-call | flops 1000000 | bytes 1 | tf_op jit(solution)/shard_map/block_states/pallas_call | solution.py:82
  8.6 3.0 %collective-permute-start = (bf16[4,128,128]{2,1,0:T(8,128)(2,1)S(1)}, bf16[4,128,128]{2,1,0:T(8,128)(2,1)S(1)}, u32[]{:S(2)}, u32[]{:S(2)}) collective-permute-start(bf16[4,128,128]{2,1,0:T(8,128)(2,1)S(1)} %get-tuple-element.101), channel_id=1, source_target_pairs={{0,4},{4,0},{8,12},{12,8},{16,20},{20,16},{24,28},{28,24},{1,5},{5... | collective-permute-start | bytes 393224 | tf_op jit(solution)/shard_map/ppermute | solution.py:34
  11.7 1.8 %gradient_terms.6 = bf16[4,512,256]{2,1,0:T(8,128)(2,1)S(1)} custom-call(s32[2]{0:T(128)S(1)} %pad_add_fusion.position_ref.info_ref.place_ref, bf16[512,1024]{1,0:T(8,128)(2,1)S(1)} %get-tuple-element.96.refs_0_, bf16[1024,2048]{1,0:T(8,128)(2,1)S(1)} %get-tuple-element.142.refs_1_), custom_call_target="tpu_custom_call" | custom-call | flops 1000000 | bytes 1 | tf_op jit(solution)/shard_map/gradient_terms/pallas_call | solution.py:130
  14.4 2.3 %fusion.1.query_ref = bf16[1024,512]{1,0:T(8,128)(2,1)S(1)} fusion(bf16[1024,2048]{1,0:T(8,128)(2,1)S(1)} %get-tuple-element.142.refs_1_, bf16[3,2048,512]{2,1,0:T(8,128)(2,1)S(1)} %bitcast.22), kind=kOutput, calls=%fused_computation.3 | convolution fusion | flops 2148007936 | bytes 7340032 | tf_op jit(solution)/shard_map/dot_general | solution.py:449
  19.5 2.4 %fusion.3.grad_ref = f32[1024,512]{1,0:T(8,128)S(1)} fusion(bf16[1024,2048]{1,0:T(8,128)(2,1)S(1)} %copy-done.3, bf16[512,2048]{1,0:T(8,128)(2,1)S(1)} %copy-done), kind=kOutput, calls=%fused_computation.7 | convolution fusion | flops 2147483648 | bytes 8388608 | tf_op jit(solution)/shard_map/dot_general | solution.py:29
  22.0 1.8 %gradient_terms.7 = bf16[4,512,256]{2,1,0:T(8,128)(2,1)S(1)} custom-call(s32[2]{0:T(128)S(1)} %pad_add_fusion.position_ref.info_ref.place_ref, bf16[512,1024]{1,0:T(8,128)(2,1)S(1)} %get-tuple-element.108.refs_0_, bf16[1024,2048]{1,0:T(8,128)(2,1)S(1)} %get-tuple-element.142.refs_1_), custom_call_target="tpu_custom_call" | custom-call | flops 1000000 | bytes 1 | tf_op jit(solution)/shard_map/gradient_terms/pallas_call | solution.py:130
  24.4 2.7 %collective-permute-start.2 = (bf16[4,128,128]{2,1,0:T(8,128)(2,1)S(1)}, bf16[4,128,128]{2,1,0:T(8,128)(2,1)S(1)}, u32[]{:S(2)}, u32[]{:S(2)}) collective-permute-start(bf16[4,128,128]{2,1,0:T(8,128)(2,1)S(1)} %get-tuple-element.113), channel_id=1, source_target_pairs={{0,16},{4,20},{8,24},{12,28},{16,0},{20,4},{24,8},{28,12},{1,17},{... | collective-permute-start | bytes 393224 | tf_op jit(solution)/shard_map/ppermute | solution.py:34
  27.5 4.9 %collective-permute-done.2.got_ref = bf16[4,128,128]{2,1,0:T(8,128)(2,1)S(1)} collective-permute-done((bf16[4,128,128]{2,1,0:T(8,128)(2,1)S(1)}, bf16[4,128,128]{2,1,0:T(8,128)(2,1)S(1)}, u32[]{:S(2)}, u32[]{:S(2)}) %collective-permute-start.2) | collective-permute-done | bytes 131104 | tf_op jit(solution)/shard_map/ppermute | solution.py:34
  33.1 4.7 %norm_backward.1 = (bf16[512,1024]{1,0:T(8,128)(2,1)S(1)}, bf16[1024,512]{1,0:T(8,128)(2,1)S(1)}, bf16[512,1024]{1,0:T(8,128)(2,1)S(1)}, f32[4,128,128]{2,1,0:T(8,128)S(1)}, bf16[4,128,128]{2,1,0:T(8,128)(2,1)S(1)}) custom-call(bf16[1024,512]{1,0:T(8,128)(2,1)S(1)} %fusion.1.query_ref, f32[1024,512]{1,0:T(8,128)S(1)} %fusion.3.grad_ref, ...), custom_call_target="tpu_custom_call" | custom-call | flops 4294967296 | bytes 1 | tf_op jit(solution)/shard_map/norm_backward/pallas_call | solution.py:292
  39.4 2.9 %gradient_terms.8 = (bf16[4,512,256]{2,1,0:T(8,128)(2,1)S(1)}, bf16[4,512,256]{2,1,0:T(8,128)(2,1)S(1)}) custom-call(s32[2]{0:T(128)S(1)} %pad_add_fusion.position_ref.info_ref.place_ref, bf16[512,1024]{1,0:T(8,128)(2,1)S(1)} %get-tuple-element.122.refs_0_, bf16[1024,2048]{1,0:T(8,128)(2,1)S(1)} %copy-done.3), custom_call_target="tpu_custom_call" | custom-call | flops 1000000 | bytes 1 | tf_op jit(solution)/shard_map/gradient_terms/pallas_call | solution.py:130
  42.3 3.9 %collective-permute-done.3.got_ref = bf16[4,128,128]{2,1,0:T(8,128)(2,1)S(1)} collective-permute-done((bf16[4,128,128]{2,1,0:T(8,128)(2,1)S(1)}, bf16[4,128,128]{2,1,0:T(8,128)(2,1)S(1)}, u32[]{:S(2)}, u32[]{:S(2)}) %collective-permute-start.3) | collective-permute-done | bytes 131104 | tf_op jit(solution)/shard_map/ppermute | solution.py:34
  47.8 2.9 %gradient_terms.9 = (bf16[4,512,256]{2,1,0:T(8,128)(2,1)S(1)}, bf16[4,512,256]{2,1,0:T(8,128)(2,1)S(1)}) custom-call(s32[2]{0:T(128)S(1)} %pad_add_fusion.position_ref.info_ref.place_ref, bf16[512,1024]{1,0:T(8,128)(2,1)S(1)} %get-tuple-element.131.refs_0_, bf16[1024,2048]{1,0:T(8,128)(2,1)S(1)} %get-tuple-element.142.refs_1_), custom_call_target="tpu_custom_call" | custom-call | flops 1000000 | bytes 1 | tf_op jit(solution)/shard_map/gradient_terms/pallas_call | solution.py:130
  50.7 3.9 %collective-permute-done.6.refs_3_ = bf16[4,512,256]{2,1,0:T(8,128)(2,1)S(1)} collective-permute-done((bf16[4,512,256]{2,1,0:T(8,128)(2,1)S(1)}, bf16[4,512,256]{2,1,0:T(8,128)(2,1)S(1)}, u32[]{:S(2)}, u32[]{:S(2)}) %collective-permute-start.6) | collective-permute-done | bytes 1048608 | tf_op jit(solution)/shard_map/ppermute | solution.py:34
  54.6 4.5 %collective-permute-done.5.refs_3_ = bf16[2,4,128,128]{3,2,1,0:T(8,128)(2,1)S(1)} collective-permute-done((bf16[2,4,128,128]{3,2,1,0:T(8,128)(2,1)S(1)}, bf16[2,4,128,128]{3,2,1,0:T(8,128)(2,1)S(1)}, u32[]{:S(2)}, u32[]{:S(2)}) %collective-permute-start.5) | collective-permute-done | bytes 262176 | tf_op jit(solution)/shard_map/ppermute | solution.py:34
  59.9 1.8 %gradient_terms.10.refs_0_ = bf16[4,512,256]{2,1,0:T(8,128)(2,1)S(1)} custom-call(s32[2]{0:T(128)S(1)} %pad_add_fusion.position_ref.info_ref.place_ref, bf16[512,1024]{1,0:T(8,128)(2,1)S(1)} %get-tuple-element.96.refs_0_, bf16[1024,2048]{1,0:T(8,128)(2,1)S(1)} %get-tuple-element.142.refs_1_), custom_call_target="tpu_custom_call" | custom-call | flops 1000000 | bytes 1 | tf_op jit(solution)/shard_map/gradient_terms/pallas_call | solution.py:130
  61.7 1.8 %gradient_terms.11.refs_2_ = bf16[4,512,256]{2,1,0:T(8,128)(2,1)S(1)} custom-call(s32[2]{0:T(128)S(1)} %pad_add_fusion.position_ref.info_ref.place_ref, bf16[512,1024]{1,0:T(8,128)(2,1)S(1)} %get-tuple-element.108.refs_0_, bf16[1024,2048]{1,0:T(8,128)(2,1)S(1)} %get-tuple-element.142.refs_1_), custom_call_target="tpu_custom_call" | custom-call | flops 1000000 | bytes 1 | tf_op jit(solution)/shard_map/gradient_terms/pallas_call | solution.py:130
  63.5 3.5 %collective-permute-done.7.refs_4_ = bf16[4,128,128]{2,1,0:T(8,128)(2,1)S(1)} collective-permute-done((bf16[4,128,128]{2,1,0:T(8,128)(2,1)S(1)}, bf16[4,128,128]{2,1,0:T(8,128)(2,1)S(1)}, u32[]{:S(2)}, u32[]{:S(2)}) %collective-permute-start.7) | collective-permute-done | bytes 131104 | tf_op jit(solution)/shard_map/ppermute | solution.py:34
  69.1 1.7 %collective-permute-start.10 = (bf16[2,512,256]{2,1,0:T(8,128)(2,1)S(1)}, bf16[2,512,256]{2,1,0:T(8,128)(2,1)S(1)}, u32[]{:S(2)}, u32[]{:S(2)}) collective-permute-start(bf16[2,512,256]{2,1,0:T(8,128)(2,1)S(1)} %get-tuple-element.156), channel_id=1, source_target_pairs={{0,4},{4,0},{8,12},{12,8},{16,20},{20,16},{24,28},{28,24},{1,5},{5... | collective-permute-start | bytes 1572872 | tf_op jit(solution)/shard_map/ppermute | solution.py:34
  70.8 1.9 %key_value_grads.1 = (bf16[1024,512]{1,0:T(8,128)(2,1)S(1)}, bf16[1024,512]{1,0:T(8,128)(2,1)S(1)}) custom-call(bf16[1024,512]{1,0:T(8,128)(2,1)S(1)} %get-tuple-element.118.key_ref, bf16[1024,512]{1,0:T(8,128)(2,1)S(1)} %get-tuple-element.119.value_ref, f32[4,128,128]{2,1,0:T(8,128)S(1)} %get-tuple-element.148.mine_ref.grad_ref), custom_call_target="tpu_custom_call" | custom-call | flops 1000000 | bytes 1 | tf_op jit(solution)/shard_map/key_value_grads/pallas_call | solution.py:362
  72.7 9.1 %input_terms.1 = (bf16[2,256,2048]{2,1,0:T(8,128)(2,1)S(1)}, bf16[2,256,2048]{2,1,0:T(8,128)(2,1)S(1)}) custom-call(s32[2]{0:T(128)S(1)} %pad_add_fusion.position_ref.info_ref.place_ref, bf16[1024,512]{1,0:T(8,128)(2,1)S(1)} %get-tuple-element.117.query_ref, bf16[1024,512]{1,0:T(8,128)(2,1)S(1)} %get-tuple-element.149.key_ref, ...), custom_call_target="tpu_custom_call" | custom-call | flops 1000000 | bytes 1 | tf_op jit(solution)/shard_map/input_terms/pallas_call | solution.py:394
  83.7 1.7 %collective-permute-start.13 = (bf16[1,1024,256]{2,1,0:T(8,128)(2,1)S(1)}, bf16[1,1024,256]{2,1,0:T(8,128)(2,1)S(1)}, u32[]{:S(2)}, u32[]{:S(2)}) collective-permute-start(bf16[1,1024,256]{2,1,0:T(8,128)(2,1)S(1)} %get-tuple-element.167), channel_id=1, source_target_pairs={{0,16},{4,20},{8,24},{12,28},{16,0},{20,4},{24,8},{28,12},{1,17},{... | collective-permute-start | bytes 1572872 | tf_op jit(solution)/shard_map/ppermute | solution.py:34
  88.6 21.2 %collective-permute-done.13 = bf16[1,1024,256]{2,1,0:T(8,128)(2,1)S(1)} collective-permute-done((bf16[1,1024,256]{2,1,0:T(8,128)(2,1)S(1)}, bf16[1,1024,256]{2,1,0:T(8,128)(2,1)S(1)}, u32[]{:S(2)}, u32[]{:S(2)}) %collective-permute-start.13) | collective-permute-done | bytes 524320 | tf_op jit(solution)/shard_map/ppermute | solution.py:34
  112.5 16.5 %collective-permute-done.17.refs_1_ = bf16[2,512,256]{2,1,0:T(8,128)(2,1)S(1)} collective-permute-done((bf16[2,512,256]{2,1,0:T(8,128)(2,1)S(1)}, bf16[2,512,256]{2,1,0:T(8,128)(2,1)S(1)}, u32[]{:S(2)}, u32[]{:S(2)}) %collective-permute-start.17) | collective-permute-done | bytes 524320 | tf_op jit(solution)/shard_map/ppermute | solution.py:34
  131.5 10.0 %collective-permute-done.18 = bf16[1,512,256]{2,1,0:T(8,128)(2,1)S(1)} collective-permute-done((bf16[1,512,256]{2,1,0:T(8,128)(2,1)S(1)}, bf16[1,512,256]{2,1,0:T(8,128)(2,1)S(1)}, u32[]{:S(2)}, u32[]{:S(2)}) %collective-permute-start.18) | collective-permute-done | bytes 262176 | tf_op jit(solution)/shard_map/ppermute | solution.py:34
  (56 shorter events, 23.2 us)
Async XLA Ops:
  0.6 18.9 %copy-start = (bf16[512,2048]{1,0:T(8,128)(2,1)S(1)}, bf16[512,2048]{1,0:T(8,128)(2,1)}, u32[]{:S(2)}) copy-start(bf16[512,2048]{1,0:T(8,128)(2,1)} %param.10) | copy-start | bytes 6291460
  8.6 8.2 %collective-permute-start = (bf16[4,128,128]{2,1,0:T(8,128)(2,1)S(1)}, bf16[4,128,128]{2,1,0:T(8,128)(2,1)S(1)}, u32[]{:S(2)}, u32[]{:S(2)}) collective-permute-start(bf16[4,128,128]{2,1,0:T(8,128)(2,1)S(1)} %get-tuple-element.101), channel_id=1, source_target_pairs={{0,4},{4,0},{8,12},{12,8},{16,20},{20,16},{24,28},{28,24},{1,5},{5... | collective-permute-start | bytes 393224 | tf_op jit(solution)/shard_map/ppermute | solution.py:34
  14.4 5.1 %copy-start.3 = (bf16[1024,2048]{1,0:T(8,128)(2,1)S(1)}, bf16[1024,2048]{1,0:T(8,128)(2,1)}, u32[]{:S(2)}) copy-start(bf16[1024,2048]{1,0:T(8,128)(2,1)} %refs_1_) | copy-start | bytes 12582916
  17.4 6.4 %collective-permute-start.1 = (bf16[4,128,128]{2,1,0:T(8,128)(2,1)S(1)}, bf16[4,128,128]{2,1,0:T(8,128)(2,1)S(1)}, u32[]{:S(2)}, u32[]{:S(2)}) collective-permute-start(bf16[4,128,128]{2,1,0:T(8,128)(2,1)S(1)} %get-tuple-element.107), channel_id=1, source_target_pairs={{0,8},{4,12},{8,0},{12,4},{16,24},{20,28},{24,16},{28,20},{1,9},{5... | collective-permute-start | bytes 393224 | tf_op jit(solution)/shard_map/ppermute | solution.py:34
  19.0 27.2 %collective-permute-start.4 = (bf16[4,512,256]{2,1,0:T(8,128)(2,1)S(1)}, bf16[4,512,256]{2,1,0:T(8,128)(2,1)S(1)}, u32[]{:S(2)}, u32[]{:S(2)}) collective-permute-start(bf16[4,512,256]{2,1,0:T(8,128)(2,1)S(1)} %gradient_terms.6), channel_id=1, source_target_pairs={{0,4},{4,0},{8,12},{12,8},{16,20},{20,16},{24,28},{28,24},{1,5},{5... | collective-permute-start | bytes 3145736 | tf_op jit(solution)/shard_map/ppermute | solution.py:34
  21.9 5.6 %copy-start.5 = (bf16[512]{0:T(512)(128)(2,1)S(1)}, bf16[512]{0:T(512)(128)(2,1)}, u32[]{:S(2)}) copy-start(bf16[512]{0:T(512)(128)(2,1)} %param.11) | copy-start | bytes 3076
  21.9 11.1 %copy-start.4 = (s32[1024]{0:T(1024)S(1)}, s32[1024]{0:T(1024)}, u32[]{:S(2)}) copy-start(s32[1024]{0:T(1024)} %param.8) | copy-start | bytes 12292
  24.4 8.1 %collective-permute-start.2 = (bf16[4,128,128]{2,1,0:T(8,128)(2,1)S(1)}, bf16[4,128,128]{2,1,0:T(8,128)(2,1)S(1)}, u32[]{:S(2)}, u32[]{:S(2)}) collective-permute-start(bf16[4,128,128]{2,1,0:T(8,128)(2,1)S(1)} %get-tuple-element.113), channel_id=1, source_target_pairs={{0,16},{4,20},{8,24},{12,28},{16,0},{20,4},{24,8},{28,12},{1,17},{... | collective-permute-start | bytes 393224 | tf_op jit(solution)/shard_map/ppermute | solution.py:34
  27.1 27.5 %collective-permute-start.6 = (bf16[4,512,256]{2,1,0:T(8,128)(2,1)S(1)}, bf16[4,512,256]{2,1,0:T(8,128)(2,1)S(1)}, u32[]{:S(2)}, u32[]{:S(2)}) collective-permute-start(bf16[4,512,256]{2,1,0:T(8,128)(2,1)S(1)} %gradient_terms.7), channel_id=1, source_target_pairs={{0,8},{4,12},{8,0},{12,4},{16,24},{20,28},{24,16},{28,20},{1,9},{5... | collective-permute-start | bytes 3145736 | tf_op jit(solution)/shard_map/ppermute | solution.py:34
  37.7 8.5 %collective-permute-start.3 = (bf16[4,128,128]{2,1,0:T(8,128)(2,1)S(1)}, bf16[4,128,128]{2,1,0:T(8,128)(2,1)S(1)}, u32[]{:S(2)}, u32[]{:S(2)}) collective-permute-start(bf16[4,128,128]{2,1,0:T(8,128)(2,1)S(1)} %get-tuple-element.121), channel_id=1, source_target_pairs={{0,4},{4,0},{8,12},{12,8},{16,20},{20,16},{24,28},{28,24},{1,5},{5... | collective-permute-start | bytes 393224 | tf_op jit(solution)/shard_map/ppermute | solution.py:34
  46.9 35.2 %collective-permute-start.8 = (bf16[4,512,256]{2,1,0:T(8,128)(2,1)S(1)}, bf16[4,512,256]{2,1,0:T(8,128)(2,1)S(1)}, u32[]{:S(2)}, u32[]{:S(2)}) collective-permute-start(bf16[4,512,256]{2,1,0:T(8,128)(2,1)S(1)} %get-tuple-element.154), channel_id=1, source_target_pairs={{0,4},{4,0},{8,12},{12,8},{16,20},{20,16},{24,28},{28,24},{1,5},{5... | collective-permute-start | bytes 3145736 | tf_op jit(solution)/shard_map/ppermute | solution.py:34
  47.4 11.7 %collective-permute-start.5 = (bf16[2,4,128,128]{3,2,1,0:T(8,128)(2,1)S(1)}, bf16[2,4,128,128]{3,2,1,0:T(8,128)(2,1)S(1)}, u32[]{:S(2)}, u32[]{:S(2)}) collective-permute-start(bf16[2,4,128,128]{3,2,1,0:T(8,128)(2,1)S(1)} %get-tuple-element.130), channel_id=1, source_target_pairs={{0,8},{4,12},{8,0},{12,4},{16,24},{20,28},{24,16},{28,20},{1,9},{5... | collective-permute-start | bytes 786440 | tf_op jit(solution)/shard_map/ppermute | solution.py:34
  59.8 7.3 %collective-permute-start.7 = (bf16[4,128,128]{2,1,0:T(8,128)(2,1)S(1)}, bf16[4,128,128]{2,1,0:T(8,128)(2,1)S(1)}, u32[]{:S(2)}, u32[]{:S(2)}) collective-permute-start(bf16[4,128,128]{2,1,0:T(8,128)(2,1)S(1)} %get-tuple-element.140), channel_id=1, source_target_pairs={{0,16},{4,20},{8,24},{12,28},{16,0},{20,4},{24,8},{28,12},{1,17},{... | collective-permute-start | bytes 393224 | tf_op jit(solution)/shard_map/ppermute | solution.py:34
  69.0 12.8 %collective-permute-start.9 = (bf16[2,512,256]{2,1,0:T(8,128)(2,1)S(1)}, bf16[2,512,256]{2,1,0:T(8,128)(2,1)S(1)}, u32[]{:S(2)}, u32[]{:S(2)}) collective-permute-start(bf16[2,512,256]{2,1,0:T(8,128)(2,1)S(1)} %get-tuple-element.155), channel_id=1, source_target_pairs={{0,8},{4,12},{8,0},{12,4},{16,24},{20,28},{24,16},{28,20},{1,9},{5... | collective-permute-start | bytes 1572872 | tf_op jit(solution)/shard_map/ppermute | solution.py:34
  69.1 12.8 %collective-permute-start.10 = (bf16[2,512,256]{2,1,0:T(8,128)(2,1)S(1)}, bf16[2,512,256]{2,1,0:T(8,128)(2,1)S(1)}, u32[]{:S(2)}, u32[]{:S(2)}) collective-permute-start(bf16[2,512,256]{2,1,0:T(8,128)(2,1)S(1)} %get-tuple-element.156), channel_id=1, source_target_pairs={{0,4},{4,0},{8,12},{12,8},{16,20},{20,16},{24,28},{28,24},{1,5},{5... | collective-permute-start | bytes 1572872 | tf_op jit(solution)/shard_map/ppermute | solution.py:34
  82.3 4.2 %collective-permute-start.11 = (bf16[2,256,2048]{2,1,0:T(8,128)(2,1)S(1)}, bf16[2,256,2048]{2,1,0:T(8,128)(2,1)S(1)}, u32[]{:S(2)}, u32[]{:S(2)}) collective-permute-start(bf16[2,256,2048]{2,1,0:T(8,128)(2,1)S(1)} %get-tuple-element.163), channel_id=1, source_target_pairs={{0,1},{1,0},{2,3},{3,2},{4,5},{5,4},{6,7},{7,6},{8,9},{9,8},{10,11... | collective-permute-start | bytes 6291464 | tf_op jit(solution)/shard_map/ppermute | solution.py:34
  82.4 27.5 %collective-permute-start.16 = (bf16[4,512,256]{2,1,0:T(8,128)(2,1)S(1)}, bf16[4,512,256]{2,1,0:T(8,128)(2,1)S(1)}, u32[]{:S(2)}, u32[]{:S(2)}) collective-permute-start(bf16[4,512,256]{2,1,0:T(8,128)(2,1)S(1)} %get-tuple-element.172), channel_id=1, source_target_pairs={{0,4},{4,0},{8,12},{12,8},{16,20},{20,16},{24,28},{28,24},{1,5},{5... | collective-permute-start | bytes 3145736 | tf_op jit(solution)/shard_map/ppermute | solution.py:34
  83.7 26.1 %collective-permute-start.13 = (bf16[1,1024,256]{2,1,0:T(8,128)(2,1)S(1)}, bf16[1,1024,256]{2,1,0:T(8,128)(2,1)S(1)}, u32[]{:S(2)}, u32[]{:S(2)}) collective-permute-start(bf16[1,1024,256]{2,1,0:T(8,128)(2,1)S(1)} %get-tuple-element.167), channel_id=1, source_target_pairs={{0,16},{4,20},{8,24},{12,28},{16,0},{20,4},{24,8},{28,12},{1,17},{... | collective-permute-start | bytes 1572872 | tf_op jit(solution)/shard_map/ppermute | solution.py:34
  85.3 24.5 %collective-permute-start.12 = (bf16[2,512,256]{2,1,0:T(8,128)(2,1)S(1)}, bf16[2,512,256]{2,1,0:T(8,128)(2,1)S(1)}, u32[]{:S(2)}, u32[]{:S(2)}) collective-permute-start(bf16[2,512,256]{2,1,0:T(8,128)(2,1)S(1)} %get-tuple-element.166), channel_id=1, source_target_pairs={{0,8},{4,12},{8,0},{12,4},{16,24},{20,28},{24,16},{28,20},{1,9},{5... | collective-permute-start | bytes 1572872 | tf_op jit(solution)/shard_map/ppermute | solution.py:34
  87.0 42.2 %collective-permute-start.15 = (bf16[1,256,2048]{2,1,0:T(8,128)(2,1)S(1)}, bf16[1,256,2048]{2,1,0:T(8,128)(2,1)S(1)}, u32[]{:S(2)}, u32[]{:S(2)}) collective-permute-start(bf16[1,256,2048]{2,1,0:T(8,128)(2,1)S(1)} %get-tuple-element.170), channel_id=1, source_target_pairs={{0,2},{1,3},{2,0},{3,1},{4,6},{5,7},{6,4},{7,5},{8,10},{9,11},{10,... | collective-permute-start | bytes 3145736 | tf_op jit(solution)/shard_map/ppermute | solution.py:34
  110.2 18.8 %collective-permute-start.17 = (bf16[2,512,256]{2,1,0:T(8,128)(2,1)S(1)}, bf16[2,512,256]{2,1,0:T(8,128)(2,1)S(1)}, u32[]{:S(2)}, u32[]{:S(2)}) collective-permute-start(bf16[2,512,256]{2,1,0:T(8,128)(2,1)S(1)} %get-tuple-element.176), channel_id=1, source_target_pairs={{0,8},{4,12},{8,0},{12,4},{16,24},{20,28},{24,16},{28,20},{1,9},{5... | collective-permute-start | bytes 1572872 | tf_op jit(solution)/shard_map/ppermute | solution.py:34
  111.1 18.2 %collective-permute-start.14 = (bf16[1,512,256]{2,1,0:T(8,128)(2,1)S(1)}, bf16[1,512,256]{2,1,0:T(8,128)(2,1)S(1)}, u32[]{:S(2)}, u32[]{:S(2)}) collective-permute-start(bf16[1,512,256]{2,1,0:T(8,128)(2,1)S(1)} %get-tuple-element.169), channel_id=1, source_target_pairs={{0,16},{4,20},{8,24},{12,28},{16,0},{20,4},{24,8},{28,12},{1,17},{... | collective-permute-start | bytes 786440 | tf_op jit(solution)/shard_map/ppermute | solution.py:34
  129.2 12.3 %collective-permute-start.18 = (bf16[1,512,256]{2,1,0:T(8,128)(2,1)S(1)}, bf16[1,512,256]{2,1,0:T(8,128)(2,1)S(1)}, u32[]{:S(2)}, u32[]{:S(2)}) collective-permute-start(bf16[1,512,256]{2,1,0:T(8,128)(2,1)S(1)} %get-tuple-element.180), channel_id=1, source_target_pairs={{0,16},{4,20},{8,24},{12,28},{16,0},{20,4},{24,8},{28,12},{1,17},{... | collective-permute-start | bytes 786440 | tf_op jit(solution)/shard_map/ppermute | solution.py:34
  129.3 13.8 %copy-start.1 = (bf16[512,2048]{1,0:T(8,128)(2,1)S(1)}, bf16[512,2048]{1,0:T(8,128)(2,1)}, u32[]{:S(2)}) copy-start(bf16[512,2048]{1,0:T(8,128)(2,1)} %param.10) | copy-start | bytes 6291460
  (1 other events, 2.8 us)

commit v13 on v12

--- a/solution.py
+++ b/solution.py
@@ -73,7 +73,7 @@
         sent_ref[h] = state.astype(bf16)
 
 
-def block_states(rows, weights, parts=2):
+def block_states(rows, weights, parts=4):
     count, depth = rows.shape
     width = weights.shape[2]
     heads = width // HD

time: 143 us -> 143 us (level)
  no operation moved by 1% of the time
where the time goes in v13:
time: 143 us
  waiting for transfers between devices  69.3 us (48%)
  Pallas kernels  44.7 us (31%)
  starting transfers between devices  20 us (14%)
  matrix products  4.71 us (3%)
  other arithmetic  2.29 us (2%)
    ppermute x19, waiting for transfers between devices, exchange(): return lax.ppermute(arr, axis, [(i, i ^ 1 << bit) for i in range(count)])  69.3 us
    ppermute x19, starting transfers between devices, exchange(): return lax.ppermute(arr, axis, [(i, i ^ 1 << bit) for i in range(count)])  20 us
    pallas_call x6, Pallas kernels, gradient_terms(): pl.pallas_call(functools.partial(terms_kernel, len(lefts), outputs), in_s...  13.1 us
    pallas_call x1, Pallas kernels, input_terms(): pl.pallas_call(functools.partial(input_kernel, order), grid_spec=pltpu.Pr...  9.12 us
    pallas_call x1, Pallas kernels, block_states(): pl.pallas_call(functools.partial(states_kernel, parts), in_specs=[hbm, hb...  7.85 us
    pallas_call x1, Pallas kernels, middle(): pl.pallas_call(middle_kernel, grid=(heads,), in_specs=[column, column, pl...  4.66 us
    pallas_call x6, Pallas kernels, small(): pl.pallas_call(kernel, in_specs=[pl.BlockSpec(memory_space=pltpu.SMEM)] +...  3.73 us
  transfers between devices with their start and end apart: 19, of which 9 were waited for; matrix products, arithmetic and copies ran while one was open for 5% of the time, Pallas kernels for 24%

profile of v13, /device:TPU:0, one launch (start us, length us, event | category | flops | bytes accessed | tf_op | source)
XLA Modules:
  0.0 143.0 jit_solution(11984917031640974858)
XLA Ops:
  0.7 7.8 %block_states.1 = (bf16[1024,512]{1,0:T(8,128)(2,1)S(1)}, bf16[1024,512]{1,0:T(8,128)(2,1)S(1)}, f32[4,128,128]{2,1,0:T(8,128)S(1)}, bf16[4,128,128]{2,1,0:T(8,1...) custom-call(bf16[1024,2048]{1,0:T(8,128)(2,1)} %rows_ref, ...), custom_call_target="tpu_custom_call" | custom-call | flops 1000000 | bytes 1 | tf_op jit(solution)/shard_map/block_states/pallas_call | solution.py:82
  8.6 3.0 %collective-permute-start = (bf16[4,128,128]{2,1,0:T(8,128)(2,1)S(1)}, bf16[4,128,128]{2,1,0:T(8,128)(2,1)S(1)}, u32[]{:S(2)}, u32[]{:S(2)}) collective-permute-start(bf16[4,128,128]{2,1,0:T(8,128)(2,1)S(1)} %get-tuple-element.101), channel_id=1, source_target_pairs={{0,4},{4,0},{8,12},{12,8},{16,20},{20,16},{24,28},{28,24},{1,5},{5... | collective-permute-start | bytes 393224 | tf_op jit(solution)/shard_map/ppermute | solution.py:34
  11.6 1.8 %gradient_terms.6 = bf16[4,512,256]{2,1,0:T(8,128)(2,1)S(1)} custom-call(s32[2]{0:T(128)S(1)} %pad_add_fusion.position_ref.info_ref.place_ref, bf16[512,1024]{1,0:T(8,128)(2,1)S(1)} %get-tuple-element.96.refs_0_, bf16[1024,2048]{1,0:T(8,128)(2,1)S(1)} %get-tuple-element.142.refs_1_), custom_call_target="tpu_custom_call" | custom-call | flops 1000000 | bytes 1 | tf_op jit(solution)/shard_map/gradient_terms/pallas_call | solution.py:130
  14.4 2.3 %fusion.1.query_ref = bf16[1024,512]{1,0:T(8,128)(2,1)S(1)} fusion(bf16[1024,2048]{1,0:T(8,128)(2,1)S(1)} %get-tuple-element.142.refs_1_, bf16[3,2048,512]{2,1,0:T(8,128)(2,1)S(1)} %bitcast.22), kind=kOutput, calls=%fused_computation.3 | convolution fusion | flops 2148007936 | bytes 7340032 | tf_op jit(solution)/shard_map/dot_general | solution.py:449
  19.5 2.4 %fusion.3.grad_ref = f32[1024,512]{1,0:T(8,128)S(1)} fusion(bf16[1024,2048]{1,0:T(8,128)(2,1)S(1)} %copy-done.3, bf16[512,2048]{1,0:T(8,128)(2,1)S(1)} %copy-done), kind=kOutput, calls=%fused_computation.7 | convolution fusion | flops 2147483648 | bytes 8388608 | tf_op jit(solution)/shard_map/dot_general | solution.py:29
  21.9 1.8 %gradient_terms.7 = bf16[4,512,256]{2,1,0:T(8,128)(2,1)S(1)} custom-call(s32[2]{0:T(128)S(1)} %pad_add_fusion.position_ref.info_ref.place_ref, bf16[512,1024]{1,0:T(8,128)(2,1)S(1)} %get-tuple-element.108.refs_0_, bf16[1024,2048]{1,0:T(8,128)(2,1)S(1)} %get-tuple-element.142.refs_1_), custom_call_target="tpu_custom_call" | custom-call | flops 1000000 | bytes 1 | tf_op jit(solution)/shard_map/gradient_terms/pallas_call | solution.py:130
  24.4 2.7 %collective-permute-start.2 = (bf16[4,128,128]{2,1,0:T(8,128)(2,1)S(1)}, bf16[4,128,128]{2,1,0:T(8,128)(2,1)S(1)}, u32[]{:S(2)}, u32[]{:S(2)}) collective-permute-start(bf16[4,128,128]{2,1,0:T(8,128)(2,1)S(1)} %get-tuple-element.113), channel_id=1, source_target_pairs={{0,16},{4,20},{8,24},{12,28},{16,0},{20,4},{24,8},{28,12},{1,17},{... | collective-permute-start | bytes 393224 | tf_op jit(solution)/shard_map/ppermute | solution.py:34
  27.5 5.0 %collective-permute-done.2.got_ref = bf16[4,128,128]{2,1,0:T(8,128)(2,1)S(1)} collective-permute-done((bf16[4,128,128]{2,1,0:T(8,128)(2,1)S(1)}, bf16[4,128,128]{2,1,0:T(8,128)(2,1)S(1)}, u32[]{:S(2)}, u32[]{:S(2)}) %collective-permute-start.2) | collective-permute-done | bytes 131104 | tf_op jit(solution)/shard_map/ppermute | solution.py:34
  33.0 4.7 %norm_backward.1 = (bf16[512,1024]{1,0:T(8,128)(2,1)S(1)}, bf16[1024,512]{1,0:T(8,128)(2,1)S(1)}, bf16[512,1024]{1,0:T(8,128)(2,1)S(1)}, f32[4,128,128]{2,1,0:T(8,128)S(1)}, bf16[4,128,128]{2,1,0:T(8,128)(2,1)S(1)}) custom-call(bf16[1024,512]{1,0:T(8,128)(2,1)S(1)} %fusion.1.query_ref, f32[1024,512]{1,0:T(8,128)S(1)} %fusion.3.grad_ref, ...), custom_call_target="tpu_custom_call" | custom-call | flops 4294967296 | bytes 1 | tf_op jit(solution)/shard_map/norm_backward/pallas_call | solution.py:292
  39.3 2.9 %gradient_terms.8 = (bf16[4,512,256]{2,1,0:T(8,128)(2,1)S(1)}, bf16[4,512,256]{2,1,0:T(8,128)(2,1)S(1)}) custom-call(s32[2]{0:T(128)S(1)} %pad_add_fusion.position_ref.info_ref.place_ref, bf16[512,1024]{1,0:T(8,128)(2,1)S(1)} %get-tuple-element.122.refs_0_, bf16[1024,2048]{1,0:T(8,128)(2,1)S(1)} %copy-done.3), custom_call_target="tpu_custom_call" | custom-call | flops 1000000 | bytes 1 | tf_op jit(solution)/shard_map/gradient_terms/pallas_call | solution.py:130
  42.2 3.9 %collective-permute-done.3.got_ref = bf16[4,128,128]{2,1,0:T(8,128)(2,1)S(1)} collective-permute-done((bf16[4,128,128]{2,1,0:T(8,128)(2,1)S(1)}, bf16[4,128,128]{2,1,0:T(8,128)(2,1)S(1)}, u32[]{:S(2)}, u32[]{:S(2)}) %collective-permute-start.3) | collective-permute-done | bytes 131104 | tf_op jit(solution)/shard_map/ppermute | solution.py:34
  47.7 2.9 %gradient_terms.9 = (bf16[4,512,256]{2,1,0:T(8,128)(2,1)S(1)}, bf16[4,512,256]{2,1,0:T(8,128)(2,1)S(1)}) custom-call(s32[2]{0:T(128)S(1)} %pad_add_fusion.position_ref.info_ref.place_ref, bf16[512,1024]{1,0:T(8,128)(2,1)S(1)} %get-tuple-element.131.refs_0_, bf16[1024,2048]{1,0:T(8,128)(2,1)S(1)} %get-tuple-element.142.refs_1_), custom_call_target="tpu_custom_call" | custom-call | flops 1000000 | bytes 1 | tf_op jit(solution)/shard_map/gradient_terms/pallas_call | solution.py:130
  50.7 3.8 %collective-permute-done.6.refs_3_ = bf16[4,512,256]{2,1,0:T(8,128)(2,1)S(1)} collective-permute-done((bf16[4,512,256]{2,1,0:T(8,128)(2,1)S(1)}, bf16[4,512,256]{2,1,0:T(8,128)(2,1)S(1)}, u32[]{:S(2)}, u32[]{:S(2)}) %collective-permute-start.6) | collective-permute-done | bytes 1048608 | tf_op jit(solution)/shard_map/ppermute | solution.py:34
  54.5 4.6 %collective-permute-done.5.refs_3_ = bf16[2,4,128,128]{3,2,1,0:T(8,128)(2,1)S(1)} collective-permute-done((bf16[2,4,128,128]{3,2,1,0:T(8,128)(2,1)S(1)}, bf16[2,4,128,128]{3,2,1,0:T(8,128)(2,1)S(1)}, u32[]{:S(2)}, u32[]{:S(2)}) %collective-permute-start.5) | collective-permute-done | bytes 262176 | tf_op jit(solution)/shard_map/ppermute | solution.py:34
  59.8 1.8 %gradient_terms.10.refs_0_ = bf16[4,512,256]{2,1,0:T(8,128)(2,1)S(1)} custom-call(s32[2]{0:T(128)S(1)} %pad_add_fusion.position_ref.info_ref.place_ref, bf16[512,1024]{1,0:T(8,128)(2,1)S(1)} %get-tuple-element.96.refs_0_, bf16[1024,2048]{1,0:T(8,128)(2,1)S(1)} %get-tuple-element.142.refs_1_), custom_call_target="tpu_custom_call" | custom-call | flops 1000000 | bytes 1 | tf_op jit(solution)/shard_map/gradient_terms/pallas_call | solution.py:130
  61.6 1.8 %gradient_terms.11.refs_2_ = bf16[4,512,256]{2,1,0:T(8,128)(2,1)S(1)} custom-call(s32[2]{0:T(128)S(1)} %pad_add_fusion.position_ref.info_ref.place_ref, bf16[512,1024]{1,0:T(8,128)(2,1)S(1)} %get-tuple-element.108.refs_0_, bf16[1024,2048]{1,0:T(8,128)(2,1)S(1)} %get-tuple-element.142.refs_1_), custom_call_target="tpu_custom_call" | custom-call | flops 1000000 | bytes 1 | tf_op jit(solution)/shard_map/gradient_terms/pallas_call | solution.py:130
  63.5 3.5 %collective-permute-done.7.refs_4_ = bf16[4,128,128]{2,1,0:T(8,128)(2,1)S(1)} collective-permute-done((bf16[4,128,128]{2,1,0:T(8,128)(2,1)S(1)}, bf16[4,128,128]{2,1,0:T(8,128)(2,1)S(1)}, u32[]{:S(2)}, u32[]{:S(2)}) %collective-permute-start.7) | collective-permute-done | bytes 131104 | tf_op jit(solution)/shard_map/ppermute | solution.py:34
  69.0 1.7 %collective-permute-start.10 = (bf16[2,512,256]{2,1,0:T(8,128)(2,1)S(1)}, bf16[2,512,256]{2,1,0:T(8,128)(2,1)S(1)}, u32[]{:S(2)}, u32[]{:S(2)}) collective-permute-start(bf16[2,512,256]{2,1,0:T(8,128)(2,1)S(1)} %get-tuple-element.156), channel_id=1, source_target_pairs={{0,4},{4,0},{8,12},{12,8},{16,20},{20,16},{24,28},{28,24},{1,5},{5... | collective-permute-start | bytes 1572872 | tf_op jit(solution)/shard_map/ppermute | solution.py:34
  70.7 1.9 %key_value_grads.1 = (bf16[1024,512]{1,0:T(8,128)(2,1)S(1)}, bf16[1024,512]{1,0:T(8,128)(2,1)S(1)}) custom-call(bf16[1024,512]{1,0:T(8,128)(2,1)S(1)} %get-tuple-element.118.key_ref, bf16[1024,512]{1,0:T(8,128)(2,1)S(1)} %get-tuple-element.119.value_ref, f32[4,128,128]{2,1,0:T(8,128)S(1)} %get-tuple-element.148.mine_ref.grad_ref), custom_call_target="tpu_custom_call" | custom-call | flops 1000000 | bytes 1 | tf_op jit(solution)/shard_map/key_value_grads/pallas_call | solution.py:362
  72.6 9.1 %input_terms.1 = (bf16[2,256,2048]{2,1,0:T(8,128)(2,1)S(1)}, bf16[2,256,2048]{2,1,0:T(8,128)(2,1)S(1)}) custom-call(s32[2]{0:T(128)S(1)} %pad_add_fusion.position_ref.info_ref.place_ref, bf16[1024,512]{1,0:T(8,128)(2,1)S(1)} %get-tuple-element.117.query_ref, bf16[1024,512]{1,0:T(8,128)(2,1)S(1)} %get-tuple-element.149.key_ref, ...), custom_call_target="tpu_custom_call" | custom-call | flops 1000000 | bytes 1 | tf_op jit(solution)/shard_map/input_terms/pallas_call | solution.py:394
  83.6 1.7 %collective-permute-start.13 = (bf16[1,1024,256]{2,1,0:T(8,128)(2,1)S(1)}, bf16[1,1024,256]{2,1,0:T(8,128)(2,1)S(1)}, u32[]{:S(2)}, u32[]{:S(2)}) collective-permute-start(bf16[1,1024,256]{2,1,0:T(8,128)(2,1)S(1)} %get-tuple-element.167), channel_id=1, source_target_pairs={{0,16},{4,20},{8,24},{12,28},{16,0},{20,4},{24,8},{28,12},{1,17},{... | collective-permute-start | bytes 1572872 | tf_op jit(solution)/shard_map/ppermute | solution.py:34
  88.5 21.2 %collective-permute-done.13 = bf16[1,1024,256]{2,1,0:T(8,128)(2,1)S(1)} collective-permute-done((bf16[1,1024,256]{2,1,0:T(8,128)(2,1)S(1)}, bf16[1,1024,256]{2,1,0:T(8,128)(2,1)S(1)}, u32[]{:S(2)}, u32[]{:S(2)}) %collective-permute-start.13) | collective-permute-done | bytes 524320 | tf_op jit(solution)/shard_map/ppermute | solution.py:34
  112.4 16.5 %collective-permute-done.17.refs_1_ = bf16[2,512,256]{2,1,0:T(8,128)(2,1)S(1)} collective-permute-done((bf16[2,512,256]{2,1,0:T(8,128)(2,1)S(1)}, bf16[2,512,256]{2,1,0:T(8,128)(2,1)S(1)}, u32[]{:S(2)}, u32[]{:S(2)}) %collective-permute-start.17) | collective-permute-done | bytes 524320 | tf_op jit(solution)/shard_map/ppermute | solution.py:34
  131.4 9.9 %collective-permute-done.18 = bf16[1,512,256]{2,1,0:T(8,128)(2,1)S(1)} collective-permute-done((bf16[1,512,256]{2,1,0:T(8,128)(2,1)S(1)}, bf16[1,512,256]{2,1,0:T(8,128)(2,1)S(1)}, u32[]{:S(2)}, u32[]{:S(2)}) %collective-permute-start.18) | collective-permute-done | bytes 262176 | tf_op jit(solution)/shard_map/ppermute | solution.py:34
  (56 shorter events, 23.1 us)
Async XLA Ops:
  0.6 18.9 %copy-start = (bf16[512,2048]{1,0:T(8,128)(2,1)S(1)}, bf16[512,2048]{1,0:T(8,128)(2,1)}, u32[]{:S(2)}) copy-start(bf16[512,2048]{1,0:T(8,128)(2,1)} %param.10) | copy-start | bytes 6291460
  8.6 8.1 %collective-permute-start = (bf16[4,128,128]{2,1,0:T(8,128)(2,1)S(1)}, bf16[4,128,128]{2,1,0:T(8,128)(2,1)S(1)}, u32[]{:S(2)}, u32[]{:S(2)}) collective-permute-start(bf16[4,128,128]{2,1,0:T(8,128)(2,1)S(1)} %get-tuple-element.101), channel_id=1, source_target_pairs={{0,4},{4,0},{8,12},{12,8},{16,20},{20,16},{24,28},{28,24},{1,5},{5... | collective-permute-start | bytes 393224 | tf_op jit(solution)/shard_map/ppermute | solution.py:34
  14.4 5.1 %copy-start.3 = (bf16[1024,2048]{1,0:T(8,128)(2,1)S(1)}, bf16[1024,2048]{1,0:T(8,128)(2,1)}, u32[]{:S(2)}) copy-start(bf16[1024,2048]{1,0:T(8,128)(2,1)} %refs_1_) | copy-start | bytes 12582916
  17.3 6.4 %collective-permute-start.1 = (bf16[4,128,128]{2,1,0:T(8,128)(2,1)S(1)}, bf16[4,128,128]{2,1,0:T(8,128)(2,1)S(1)}, u32[]{:S(2)}, u32[]{:S(2)}) collective-permute-start(bf16[4,128,128]{2,1,0:T(8,128)(2,1)S(1)} %get-tuple-element.107), channel_id=1, source_target_pairs={{0,8},{4,12},{8,0},{12,4},{16,24},{20,28},{24,16},{28,20},{1,9},{5... | collective-permute-start | bytes 393224 | tf_op jit(solution)/shard_map/ppermute | solution.py:34
  19.0 27.2 %collective-permute-start.4 = (bf16[4,512,256]{2,1,0:T(8,128)(2,1)S(1)}, bf16[4,512,256]{2,1,0:T(8,128)(2,1)S(1)}, u32[]{:S(2)}, u32[]{:S(2)}) collective-permute-start(bf16[4,512,256]{2,1,0:T(8,128)(2,1)S(1)} %gradient_terms.6), channel_id=1, source_target_pairs={{0,4},{4,0},{8,12},{12,8},{16,20},{20,16},{24,28},{28,24},{1,5},{5... | collective-permute-start | bytes 3145736 | tf_op jit(solution)/shard_map/ppermute | solution.py:34
  21.9 5.6 %copy-start.5 = (bf16[512]{0:T(512)(128)(2,1)S(1)}, bf16[512]{0:T(512)(128)(2,1)}, u32[]{:S(2)}) copy-start(bf16[512]{0:T(512)(128)(2,1)} %param.11) | copy-start | bytes 3076
  21.9 11.1 %copy-start.4 = (s32[1024]{0:T(1024)S(1)}, s32[1024]{0:T(1024)}, u32[]{:S(2)}) copy-start(s32[1024]{0:T(1024)} %param.8) | copy-start | bytes 12292
  24.4 8.1 %collective-permute-start.2 = (bf16[4,128,128]{2,1,0:T(8,128)(2,1)S(1)}, bf16[4,128,128]{2,1,0:T(8,128)(2,1)S(1)}, u32[]{:S(2)}, u32[]{:S(2)}) collective-permute-start(bf16[4,128,128]{2,1,0:T(8,128)(2,1)S(1)} %get-tuple-element.113), channel_id=1, source_target_pairs={{0,16},{4,20},{8,24},{12,28},{16,0},{20,4},{24,8},{28,12},{1,17},{... | collective-permute-start | bytes 393224 | tf_op jit(solution)/shard_map/ppermute | solution.py:34
  27.0 27.5 %collective-permute-start.6 = (bf16[4,512,256]{2,1,0:T(8,128)(2,1)S(1)}, bf16[4,512,256]{2,1,0:T(8,128)(2,1)S(1)}, u32[]{:S(2)}, u32[]{:S(2)}) collective-permute-start(bf16[4,512,256]{2,1,0:T(8,128)(2,1)S(1)} %gradient_terms.7), channel_id=1, source_target_pairs={{0,8},{4,12},{8,0},{12,4},{16,24},{20,28},{24,16},{28,20},{1,9},{5... | collective-permute-start | bytes 3145736 | tf_op jit(solution)/shard_map/ppermute | solution.py:34
  37.7 8.4 %collective-permute-start.3 = (bf16[4,128,128]{2,1,0:T(8,128)(2,1)S(1)}, bf16[4,128,128]{2,1,0:T(8,128)(2,1)S(1)}, u32[]{:S(2)}, u32[]{:S(2)}) collective-permute-start(bf16[4,128,128]{2,1,0:T(8,128)(2,1)S(1)} %get-tuple-element.121), channel_id=1, source_target_pairs={{0,4},{4,0},{8,12},{12,8},{16,20},{20,16},{24,28},{28,24},{1,5},{5... | collective-permute-start | bytes 393224 | tf_op jit(solution)/shard_map/ppermute | solution.py:34
  46.8 35.2 %collective-permute-start.8 = (bf16[4,512,256]{2,1,0:T(8,128)(2,1)S(1)}, bf16[4,512,256]{2,1,0:T(8,128)(2,1)S(1)}, u32[]{:S(2)}, u32[]{:S(2)}) collective-permute-start(bf16[4,512,256]{2,1,0:T(8,128)(2,1)S(1)} %get-tuple-element.154), channel_id=1, source_target_pairs={{0,4},{4,0},{8,12},{12,8},{16,20},{20,16},{24,28},{28,24},{1,5},{5... | collective-permute-start | bytes 3145736 | tf_op jit(solution)/shard_map/ppermute | solution.py:34
  47.4 11.7 %collective-permute-start.5 = (bf16[2,4,128,128]{3,2,1,0:T(8,128)(2,1)S(1)}, bf16[2,4,128,128]{3,2,1,0:T(8,128)(2,1)S(1)}, u32[]{:S(2)}, u32[]{:S(2)}) collective-permute-start(bf16[2,4,128,128]{3,2,1,0:T(8,128)(2,1)S(1)} %get-tuple-element.130), channel_id=1, source_target_pairs={{0,8},{4,12},{8,0},{12,4},{16,24},{20,28},{24,16},{28,20},{1,9},{5... | collective-permute-start | bytes 786440 | tf_op jit(solution)/shard_map/ppermute | solution.py:34
  59.7 7.3 %collective-permute-start.7 = (bf16[4,128,128]{2,1,0:T(8,128)(2,1)S(1)}, bf16[4,128,128]{2,1,0:T(8,128)(2,1)S(1)}, u32[]{:S(2)}, u32[]{:S(2)}) collective-permute-start(bf16[4,128,128]{2,1,0:T(8,128)(2,1)S(1)} %get-tuple-element.140), channel_id=1, source_target_pairs={{0,16},{4,20},{8,24},{12,28},{16,0},{20,4},{24,8},{28,12},{1,17},{... | collective-permute-start | bytes 393224 | tf_op jit(solution)/shard_map/ppermute | solution.py:34
  69.0 12.8 %collective-permute-start.9 = (bf16[2,512,256]{2,1,0:T(8,128)(2,1)S(1)}, bf16[2,512,256]{2,1,0:T(8,128)(2,1)S(1)}, u32[]{:S(2)}, u32[]{:S(2)}) collective-permute-start(bf16[2,512,256]{2,1,0:T(8,128)(2,1)S(1)} %get-tuple-element.155), channel_id=1, source_target_pairs={{0,8},{4,12},{8,0},{12,4},{16,24},{20,28},{24,16},{28,20},{1,9},{5... | collective-permute-start | bytes 1572872 | tf_op jit(solution)/shard_map/ppermute | solution.py:34
  69.0 12.7 %collective-permute-start.10 = (bf16[2,512,256]{2,1,0:T(8,128)(2,1)S(1)}, bf16[2,512,256]{2,1,0:T(8,128)(2,1)S(1)}, u32[]{:S(2)}, u32[]{:S(2)}) collective-permute-start(bf16[2,512,256]{2,1,0:T(8,128)(2,1)S(1)} %get-tuple-element.156), channel_id=1, source_target_pairs={{0,4},{4,0},{8,12},{12,8},{16,20},{20,16},{24,28},{28,24},{1,5},{5... | collective-permute-start | bytes 1572872 | tf_op jit(solution)/shard_map/ppermute | solution.py:34
  82.3 4.2 %collective-permute-start.11 = (bf16[2,256,2048]{2,1,0:T(8,128)(2,1)S(1)}, bf16[2,256,2048]{2,1,0:T(8,128)(2,1)S(1)}, u32[]{:S(2)}, u32[]{:S(2)}) collective-permute-start(bf16[2,256,2048]{2,1,0:T(8,128)(2,1)S(1)} %get-tuple-element.163), channel_id=1, source_target_pairs={{0,1},{1,0},{2,3},{3,2},{4,5},{5,4},{6,7},{7,6},{8,9},{9,8},{10,11... | collective-permute-start | bytes 6291464 | tf_op jit(solution)/shard_map/ppermute | solution.py:34
  82.4 27.5 %collective-permute-start.16 = (bf16[4,512,256]{2,1,0:T(8,128)(2,1)S(1)}, bf16[4,512,256]{2,1,0:T(8,128)(2,1)S(1)}, u32[]{:S(2)}, u32[]{:S(2)}) collective-permute-start(bf16[4,512,256]{2,1,0:T(8,128)(2,1)S(1)} %get-tuple-element.172), channel_id=1, source_target_pairs={{0,4},{4,0},{8,12},{12,8},{16,20},{20,16},{24,28},{28,24},{1,5},{5... | collective-permute-start | bytes 3145736 | tf_op jit(solution)/shard_map/ppermute | solution.py:34
  83.6 26.1 %collective-permute-start.13 = (bf16[1,1024,256]{2,1,0:T(8,128)(2,1)S(1)}, bf16[1,1024,256]{2,1,0:T(8,128)(2,1)S(1)}, u32[]{:S(2)}, u32[]{:S(2)}) collective-permute-start(bf16[1,1024,256]{2,1,0:T(8,128)(2,1)S(1)} %get-tuple-element.167), channel_id=1, source_target_pairs={{0,16},{4,20},{8,24},{12,28},{16,0},{20,4},{24,8},{28,12},{1,17},{... | collective-permute-start | bytes 1572872 | tf_op jit(solution)/shard_map/ppermute | solution.py:34
  85.3 24.4 %collective-permute-start.12 = (bf16[2,512,256]{2,1,0:T(8,128)(2,1)S(1)}, bf16[2,512,256]{2,1,0:T(8,128)(2,1)S(1)}, u32[]{:S(2)}, u32[]{:S(2)}) collective-permute-start(bf16[2,512,256]{2,1,0:T(8,128)(2,1)S(1)} %get-tuple-element.166), channel_id=1, source_target_pairs={{0,8},{4,12},{8,0},{12,4},{16,24},{20,28},{24,16},{28,20},{1,9},{5... | collective-permute-start | bytes 1572872 | tf_op jit(solution)/shard_map/ppermute | solution.py:34
  87.0 42.2 %collective-permute-start.15 = (bf16[1,256,2048]{2,1,0:T(8,128)(2,1)S(1)}, bf16[1,256,2048]{2,1,0:T(8,128)(2,1)S(1)}, u32[]{:S(2)}, u32[]{:S(2)}) collective-permute-start(bf16[1,256,2048]{2,1,0:T(8,128)(2,1)S(1)} %get-tuple-element.170), channel_id=1, source_target_pairs={{0,2},{1,3},{2,0},{3,1},{4,6},{5,7},{6,4},{7,5},{8,10},{9,11},{10,... | collective-permute-start | bytes 3145736 | tf_op jit(solution)/shard_map/ppermute | solution.py:34
  110.1 18.8 %collective-permute-start.17 = (bf16[2,512,256]{2,1,0:T(8,128)(2,1)S(1)}, bf16[2,512,256]{2,1,0:T(8,128)(2,1)S(1)}, u32[]{:S(2)}, u32[]{:S(2)}) collective-permute-start(bf16[2,512,256]{2,1,0:T(8,128)(2,1)S(1)} %get-tuple-element.176), channel_id=1, source_target_pairs={{0,8},{4,12},{8,0},{12,4},{16,24},{20,28},{24,16},{28,20},{1,9},{5... | collective-permute-start | bytes 1572872 | tf_op jit(solution)/shard_map/ppermute | solution.py:34
  111.0 18.1 %collective-permute-start.14 = (bf16[1,512,256]{2,1,0:T(8,128)(2,1)S(1)}, bf16[1,512,256]{2,1,0:T(8,128)(2,1)S(1)}, u32[]{:S(2)}, u32[]{:S(2)}) collective-permute-start(bf16[1,512,256]{2,1,0:T(8,128)(2,1)S(1)} %get-tuple-element.169), channel_id=1, source_target_pairs={{0,16},{4,20},{8,24},{12,28},{16,0},{20,4},{24,8},{28,12},{1,17},{... | collective-permute-start | bytes 786440 | tf_op jit(solution)/shard_map/ppermute | solution.py:34
  129.1 12.3 %collective-permute-start.18 = (bf16[1,512,256]{2,1,0:T(8,128)(2,1)S(1)}, bf16[1,512,256]{2,1,0:T(8,128)(2,1)S(1)}, u32[]{:S(2)}, u32[]{:S(2)}) collective-permute-start(bf16[1,512,256]{2,1,0:T(8,128)(2,1)S(1)} %get-tuple-element.180), channel_id=1, source_target_pairs={{0,16},{4,20},{8,24},{12,28},{16,0},{20,4},{24,8},{28,12},{1,17},{... | collective-permute-start | bytes 786440 | tf_op jit(solution)/shard_map/ppermute | solution.py:34
  129.2 13.8 %copy-start.1 = (bf16[512,2048]{1,0:T(8,128)(2,1)S(1)}, bf16[512,2048]{1,0:T(8,128)(2,1)}, u32[]{:S(2)}) copy-start(bf16[512,2048]{1,0:T(8,128)(2,1)} %param.10) | copy-start | bytes 6291460
  (1 other events, 2.8 us)
